TPU v7x, 32 devices: a whole 2x2x4 slice. The times are simulated.
32 devices in a mesh: row: 8 (over z, x), col: 4 (over y, core).
Axes of the slice: x: 2, y: 2, z: 4, core: 2. Of those that a mesh axis runs over, the one named last changes fastest.
Arguments:
- latents: bfloat16 [1408, 24576], P('col', 'row'), may hold values from -6 to 6
- skip_input: bfloat16 [1408, 24576], P('col', 'row'), may hold values from -6 to 6
- condition: bfloat16 [24, 1408], P('row', 'col'), may hold values from -6 to 6
- text_states: bfloat16 [24, 333, 1024], P('row', None, 'col'), may hold values from -6 to 6
- text_lengths: int32 [24], P('row'), may hold values from 42 to 333
- positions: int32 [2, 24576], P(None, 'row'), may hold values from 0 to 31
- out_grad: float32 [1408, 24576], P('col', 'row'), may hold values from -6 to 6
- skip_weight: bfloat16 [2, 1408, 1408], P(None, 'row', 'col'), may hold values from -0.109375 to 0.109375
- modulation: bfloat16 [1408, 2, 1408], P('row', None, 'col'), may hold values from -0.15625 to 0.15625
- self_inputs: bfloat16 [1408, 3, 1408], P('row', None, 'col'), may hold values from -0.15625 to 0.15625
- self_output: bfloat16 [1408, 1408], P('col', 'row'), may hold values from -1.75 to 1.75
- cross_query: bfloat16 [1408, 1408], P('row', 'col'), may hold values from -0.15625 to 0.15625
- cross_keyvalue: bfloat16 [1024, 2, 1408], P('row', None, 'col'), may hold values from -0.1875 to 0.1875
- cross_output: bfloat16 [1408, 1408], P('col', 'row'), may hold values from -1 to 1
- expand_weight: bfloat16 [1408, 6144], P('row', 'col'), may hold values from -0.15625 to 0.15625
- reduce_weight: bfloat16 [6144, 1408], P('col', 'row'), may hold values from -0.078125 to 0.078125
- skip_gain: float32 [1408], P('col'), may hold values from 0.5 to 1.5
- skip_bias: float32 [1408], P('col'), may hold values from -3 to 3
- cross_gain: float32 [1408], P('col'), may hold values from 0.5 to 1.5
- cross_bias: float32 [1408], P('col'), may hold values from -3 to 3
- hidden_gain: float32 [1408], P('col'), may hold values from 0.5 to 1.5
- hidden_bias: float32 [1408], P('col'), may hold values from -3 to 3
- query_gain: float32 [88], replicated, may hold values from 0.5 to 1.5
- key_gain: float32 [88], replicated, may hold values from 0.5 to 1.5
- cross_query_gain: float32 [88], replicated, may hold values from 0.5 to 1.5
- text_key_gain: float32 [88], replicated, may hold values from 0.5 to 1.5
Outputs:
- output: float32 [1408, 24576], P('col', 'row')
- grad_latents: float32 [1408, 24576], P('col', 'row')
- grad_skip: float32 [1408, 24576], P('col', 'row')
- grad_skip_weight: float32 [2, 1408, 1408], P(None, 'row', 'col')
- grad_modulation: float32 [1408, 2, 1408], P('row', None, 'col')
- grad_self_inputs: float32 [1408, 3, 1408], P('row', None, 'col')
- grad_self_output: float32 [1408, 1408], P('col', 'row')
- grad_cross_query: float32 [1408, 1408], P('row', 'col')
- grad_cross_keyvalue: float32 [1024, 2, 1408], P('row', None, 'col')
- grad_cross_output: float32 [1408, 1408], P('col', 'row')
- grad_expand: float32 [1408, 6144], P('row', 'col')
- grad_reduce: float32 [6144, 1408], P('col', 'row')
- grad_skip_gain: float32 [1408], P('col')
- grad_skip_bias: float32 [1408], P('col')
- grad_cross_gain: float32 [1408], P('col')
- grad_cross_bias: float32 [1408], P('col')
- grad_hidden_gain: float32 [1408], P('col')
- grad_hidden_bias: float32 [1408], P('col')
- grad_query_gain: float32 [88], replicated
- grad_key_gain: float32 [88], replicated
- grad_cross_query_gain: float32 [88], replicated
- grad_text_key_gain: float32 [88], replicated
All inputs are finite; a program needn't handle non-finite values.
Results may differ from a plain program's by a relative error of at most 0.025.
Values may be sent and summed in bfloat16 or wider, within the bound.
A program may use at most 512 MiB of HBM per device.

v0:
```python
from functools import partial
import math

import jax
import jax.numpy as jnp
from jax import lax
from jax.sharding import PartitionSpec as P

L = 1024
MICRO = 3
SEQ_MB = 1


EPSILON = 1e-06
HALF_TYPE = jnp.bfloat16
FULL_TYPE = jnp.float32


def spread(values):
    return lax.all_gather(values, "col", axis=0, tiled=True)


def collect(partials):
    return lax.psum_scatter(
        partials.astype(jnp.bfloat16), "col", scatter_dimension=0, tiled=True
    ).astype(jnp.float32)


def own_features(operand, block_weight):
    whole = lax.all_gather(operand, "col", axis=2, tiled=True)
    return jnp.einsum("blc,dc->dbl", whole, block_weight, preferred_element_type=FULL_TYPE)


def row_sums(first, second):
    return lax.psum((first, second), "col")


def col_normalize(values):
    width = values.shape[0] * lax.axis_size("col")
    totals, squares = row_sums(jnp.sum(values, 0), jnp.sum(values * values, 0))
    average = totals / width
    inverse = lax.rsqrt(squares / width - average * average + EPSILON)
    return ((values - average[None]) * inverse[None], inverse)


def norm_spread(values, scaling, shifting):
    normal, inverse = col_normalize(values)
    whole = spread((normal * scaling + shifting).astype(HALF_TYPE))
    return (whole, normal, inverse)


def norm_back(grad_normal, normal, inverse):
    width = normal.shape[0] * lax.axis_size("col")
    totals, crossed = row_sums(jnp.sum(grad_normal, 0), jnp.sum(grad_normal * normal, 0))
    return inverse[None] * (grad_normal - (totals / width)[None] - normal * (crossed / width)[None])


def head_norm(values, gain):
    average = jnp.mean(values, -1, keepdims=True)
    centred = values - average
    variance = jnp.mean(centred * centred, -1, keepdims=True)
    return centred * lax.rsqrt(variance + EPSILON) * gain


def rope_tables(places, head_dim):
    quarter = head_dim // 4
    freqs = jnp.exp(jnp.arange(quarter, dtype=FULL_TYPE) * (-4.0 * math.log(10000.0) / head_dim))
    angle_rows = places[0].astype(FULL_TYPE)[:, None] * freqs[None, :]
    angle_cols = places[1].astype(FULL_TYPE)[:, None] * freqs[None, :]
    cosine = jnp.concatenate(
        [jnp.cos(angle_rows), jnp.cos(angle_rows), jnp.cos(angle_cols), jnp.cos(angle_cols)], 1
    )
    sine = jnp.concatenate(
        [jnp.sin(angle_rows), jnp.sin(angle_rows), jnp.sin(angle_cols), jnp.sin(angle_cols)], 1
    )
    return (cosine, sine)


def rotate(values):
    quarter = values.shape[-1] // 4
    part_one = values[..., :quarter]
    part_two = values[..., quarter : 2 * quarter]
    part_three = values[..., 2 * quarter : 3 * quarter]
    part_four = values[..., 3 * quarter :]
    return jnp.concatenate([-part_two, part_one, -part_four, part_three], -1)


def apply_rope(values, cosine, sine):
    return values * cosine + rotate(values) * sine


def masked_scores(query_in, key_in, valid):
    factor = query_in.shape[-1] ** (-0.5)
    scores = (
        jnp.einsum("bqhd,bkhd->bhqk", query_in, key_in, preferred_element_type=FULL_TYPE) * factor
    )
    if valid is not None:
        scores = jnp.where(valid[:, None, None, :], scores, -1000000000.0)
    return scores


def attend_forward(query_in, key_in, value_in, valid):
    scores = masked_scores(query_in, key_in, valid)
    maximum = jnp.max(scores, -1, keepdims=True)
    expo = jnp.exp(scores - maximum)
    totals = jnp.sum(expo, -1, keepdims=True)
    weights = (expo / totals).astype(HALF_TYPE)
    mixed = jnp.einsum("bhqk,bkhd->bqhd", weights, value_in, preferred_element_type=FULL_TYPE)
    return (mixed.astype(HALF_TYPE), maximum + jnp.log(totals))


def attend_backward(query_in, key_in, value_in, valid, logsum, grad_mixed):
    factor = query_in.shape[-1] ** (-0.5)
    probs = jnp.exp(masked_scores(query_in, key_in, valid) - logsum)
    grad_value = jnp.einsum(
        "bhqk,bqhd->bkhd", probs.astype(HALF_TYPE), grad_mixed, preferred_element_type=FULL_TYPE
    )
    grad_probs = jnp.einsum(
        "bqhd,bkhd->bhqk", grad_mixed, value_in, preferred_element_type=FULL_TYPE
    )
    delta = jnp.sum(probs * grad_probs, -1, keepdims=True)
    grad_prod = (probs * (grad_probs - delta) * factor).astype(HALF_TYPE)
    grad_query = jnp.einsum("bhqk,bkhd->bqhd", grad_prod, key_in, preferred_element_type=FULL_TYPE)
    grad_key = jnp.einsum("bhqk,bqhd->bkhd", grad_prod, query_in, preferred_element_type=FULL_TYPE)
    return (grad_query, grad_key, grad_value)


def accumulate(total, extra):
    if total is None:
        return extra
    return jax.tree.map(lambda left, right: left + right, total, extra)


def shards(
    latents,
    skip_input,
    condition,
    text_states,
    text_lengths,
    positions,
    out_grad,
    skip_weight,
    modulation,
    self_inputs,
    self_output,
    cross_query,
    cross_keyvalue,
    cross_output,
    expand_weight,
    reduce_weight,
    skip_gain,
    skip_bias,
    cross_gain,
    cross_bias,
    hidden_gain,
    hidden_bias,
    query_gain,
    key_gain,
    cross_query_gain,
    text_key_gain,
):
    width = latents.shape[0]
    head_dim = query_gain.shape[0]
    heads_here = width // head_dim
    text_count = text_states.shape[1]
    text_width = text_states.shape[2]
    w_skip, w_mod, w_self, w_attn, w_query, w_text, w_cross, w_expand, w_reduce = (
        lax.all_gather(skip_weight, "row", axis=1, tiled=True),
        lax.all_gather(modulation, "row", axis=0, tiled=True),
        lax.all_gather(self_inputs, "row", axis=0, tiled=True),
        lax.all_gather(self_output, "row", axis=1, tiled=True),
        lax.all_gather(cross_query, "row", axis=0, tiled=True),
        lax.all_gather(cross_keyvalue, "row", axis=0, tiled=True),
        lax.all_gather(cross_output, "row", axis=1, tiled=True),
        lax.all_gather(expand_weight, "row", axis=0, tiled=True),
        lax.all_gather(reduce_weight, "row", axis=1, tiled=True),
    )
    blocks = (
        lax.all_to_all(jnp.transpose(w_attn), "col", split_axis=0, concat_axis=1, tiled=True),
        lax.all_to_all(jnp.transpose(w_cross), "col", split_axis=0, concat_axis=1, tiled=True),
        lax.all_to_all(w_query, "col", split_axis=0, concat_axis=1, tiled=True),
        lax.all_to_all(w_skip[0], "col", split_axis=0, concat_axis=1, tiled=True),
        lax.all_to_all(w_skip[1], "col", split_axis=0, concat_axis=1, tiled=True),
    )
    block = SEQ_MB * L
    latent_all = latents.reshape(width, MICRO, SEQ_MB, L)
    skip_all = skip_input.reshape(width, MICRO, SEQ_MB, L)
    grad_all = out_grad.reshape(width, MICRO, SEQ_MB, L)
    cond_all = condition.reshape(MICRO, SEQ_MB, width)
    text_all = text_states.reshape(MICRO, SEQ_MB, text_count, text_width)
    length_all = text_lengths.reshape(MICRO, SEQ_MB)
    place_all = positions.reshape(2, MICRO, block)
    gain_skip = skip_gain[:, None, None]
    bias_skip = skip_bias[:, None, None]
    gain_cross = cross_gain[:, None, None]
    bias_cross = cross_bias[:, None, None]
    gain_hidden = hidden_gain[:, None, None]
    bias_hidden = hidden_bias[:, None, None]

    def micro_step(latent_mb, skip_mb, cond_mb, text_mb, length_mb, place_mb, grad_mb):
        both_in = spread(jnp.concatenate([latent_mb, skip_mb], 1))
        first_in = both_in[:, :SEQ_MB]
        second_in = both_in[:, SEQ_MB:]
        joined = jnp.einsum(
            "dbl,de->ebl", first_in, w_skip[0], preferred_element_type=FULL_TYPE
        ) + jnp.einsum("dbl,de->ebl", second_in, w_skip[1], preferred_element_type=FULL_TYPE)
        skip_normal, skip_inverse = col_normalize(joined)
        stream = skip_normal * gain_skip + bias_skip
        embed = spread(jax.nn.silu(cond_mb.T.astype(FULL_TYPE)).astype(HALF_TYPE))
        modul = jnp.einsum("db,dke->keb", embed, w_mod, preferred_element_type=FULL_TYPE)
        shifting = modul[0][:, :, None]
        scaling = 1.0 + modul[1][:, :, None]
        normed_one, normal_one, inverse_one = norm_spread(stream, scaling, shifting)
        triple = jnp.einsum("dbl,dke->blke", normed_one, w_self, preferred_element_type=FULL_TYPE)
        triple = triple.reshape(SEQ_MB, L, 3, heads_here, head_dim)
        cosine, sine = rope_tables(place_mb, head_dim)
        cosine = cosine.reshape(SEQ_MB, L, 1, head_dim)
        sine = sine.reshape(SEQ_MB, L, 1, head_dim)

        def self_piece(raw_query, raw_key, gain_query, gain_key):
            return (
                apply_rope(head_norm(raw_query, gain_query), cosine, sine),
                apply_rope(head_norm(raw_key, gain_key), cosine, sine),
            )

        (rot_query, rot_key), self_pull = jax.vjp(
            self_piece, triple[:, :, 0], triple[:, :, 1], query_gain, key_gain
        )
        query_one = rot_query.astype(HALF_TYPE)
        key_one = rot_key.astype(HALF_TYPE)
        value_one = triple[:, :, 2].astype(HALF_TYPE)
        attended_one, logsum_one = attend_forward(query_one, key_one, value_one, None)
        mixed_one = attended_one.reshape(SEQ_MB, L, width)
        added_one = own_features(mixed_one, blocks[0])
        stream = stream + added_one
        normed_two, normal_two, inverse_two = norm_spread(stream, gain_cross, bias_cross)
        raw_cross = jnp.einsum("dbl,dc->blc", normed_two, w_query, preferred_element_type=FULL_TYPE)
        raw_cross = raw_cross.reshape(SEQ_MB, L, heads_here, head_dim)
        text_whole = lax.all_gather(text_mb, "col", axis=2, tiled=True)
        text_pair = jnp.einsum(
            "btd,dke->btke", text_whole, w_text, preferred_element_type=FULL_TYPE
        )
        text_pair = text_pair.reshape(SEQ_MB, text_count, 2, heads_here, head_dim)

        def cross_piece(raw_query, raw_key, gain_query, gain_key):
            return (head_norm(raw_query, gain_query), head_norm(raw_key, gain_key))

        (norm_query, norm_key), cross_pull = jax.vjp(
            cross_piece, raw_cross, text_pair[:, :, 0], cross_query_gain, text_key_gain
        )
        query_two = norm_query.astype(HALF_TYPE)
        key_two = norm_key.astype(HALF_TYPE)
        value_two = text_pair[:, :, 1].astype(HALF_TYPE)
        valid = jnp.arange(text_count)[None, :] < length_mb[:, None]
        attended_two, logsum_two = attend_forward(query_two, key_two, value_two, valid)
        mixed_two = attended_two.reshape(SEQ_MB, L, width)
        added_two = own_features(mixed_two, blocks[1])
        stream = stream + added_two
        normed_three, normal_three, inverse_three = norm_spread(stream, gain_hidden, bias_hidden)
        inner = jnp.einsum("dbl,df->blf", normed_three, w_expand, preferred_element_type=FULL_TYPE)
        activated, gelu_pull = jax.vjp(partial(jax.nn.gelu, approximate=True), inner)
        activated_half = activated.astype(HALF_TYPE)
        output = stream + collect(
            jnp.einsum("blf,fd->dbl", activated_half, w_reduce, preferred_element_type=FULL_TYPE)
        )
        grad_stream = grad_mb
        grad_out_full = spread(grad_stream.astype(HALF_TYPE))
        grad_reduce = jnp.einsum(
            "blf,dbl->fd", activated_half, grad_out_full, preferred_element_type=FULL_TYPE
        )
        grad_act = jnp.einsum(
            "dbl,fd->blf", grad_out_full, w_reduce, preferred_element_type=FULL_TYPE
        )
        grad_inner = gelu_pull(grad_act)[0].astype(HALF_TYPE)
        grad_expand = jnp.einsum(
            "dbl,blf->df", normed_three, grad_inner, preferred_element_type=FULL_TYPE
        )
        grad_normed = collect(
            jnp.einsum("blf,df->dbl", grad_inner, w_expand, preferred_element_type=FULL_TYPE)
        )
        grad_hidden_gain = jnp.sum(grad_normed * normal_three, (1, 2))
        grad_hidden_bias = jnp.sum(grad_normed, (1, 2))
        grad_stream = grad_stream + norm_back(
            grad_normed * gain_hidden, normal_three, inverse_three
        )
        grad_cross_full = spread(grad_stream.astype(HALF_TYPE))
        grad_cross_out = jnp.einsum(
            "blc,dbl->cd", mixed_two, grad_cross_full, preferred_element_type=FULL_TYPE
        )
        grad_mixed_two = jnp.einsum(
            "dbl,cd->blc", grad_cross_full, w_cross, preferred_element_type=FULL_TYPE
        )
        grad_mixed_two = grad_mixed_two.astype(HALF_TYPE).reshape(SEQ_MB, L, heads_here, head_dim)
        grad_query_two, grad_key_two, grad_value_two = attend_backward(
            query_two, key_two, value_two, valid, logsum_two, grad_mixed_two
        )
        grad_raw_cross, grad_raw_text, grad_cq_gain, grad_tk_gain = cross_pull(
            (grad_query_two, grad_key_two)
        )
        grad_raw_cross = grad_raw_cross.astype(HALF_TYPE).reshape(SEQ_MB, L, width)
        grad_pair = (
            jnp.stack([grad_raw_text, grad_value_two], 2)
            .astype(HALF_TYPE)
            .reshape(SEQ_MB, text_count, 2, width)
        )
        grad_text = jnp.einsum(
            "btd,btke->dke", text_whole, grad_pair, preferred_element_type=FULL_TYPE
        )
        grad_query_weight = jnp.einsum(
            "dbl,blc->dc", normed_two, grad_raw_cross, preferred_element_type=FULL_TYPE
        )
        grad_normed = own_features(grad_raw_cross, blocks[2])
        grad_cross_gain = jnp.sum(grad_normed * normal_two, (1, 2))
        grad_cross_bias = jnp.sum(grad_normed, (1, 2))
        grad_stream = grad_stream + norm_back(grad_normed * gain_cross, normal_two, inverse_two)
        grad_self_full = spread(grad_stream.astype(HALF_TYPE))
        grad_self_out = jnp.einsum(
            "blc,dbl->cd", mixed_one, grad_self_full, preferred_element_type=FULL_TYPE
        )
        grad_mixed_one = jnp.einsum(
            "dbl,cd->blc", grad_self_full, w_attn, preferred_element_type=FULL_TYPE
        )
        grad_mixed_one = grad_mixed_one.astype(HALF_TYPE).reshape(SEQ_MB, L, heads_here, head_dim)
        grad_query_one, grad_key_one, grad_value_one = attend_backward(
            query_one, key_one, value_one, None, logsum_one, grad_mixed_one
        )
        grad_raw_query, grad_raw_key, grad_q_gain, grad_k_gain = self_pull(
            (grad_query_one, grad_key_one)
        )
        grad_triple = (
            jnp.stack([grad_raw_query, grad_raw_key, grad_value_one], 2)
            .astype(HALF_TYPE)
            .reshape(SEQ_MB, L, 3, width)
        )
        grad_self_in = jnp.einsum(
            "dbl,blke->dke", normed_one, grad_triple, preferred_element_type=FULL_TYPE
        )
        grad_normed = collect(
            jnp.einsum("blke,dke->dbl", grad_triple, w_self, preferred_element_type=FULL_TYPE)
        )
        grad_shift = jnp.sum(grad_normed, 2)
        grad_scale = jnp.sum(grad_normed * normal_one, 2)
        grad_modul = jnp.stack([grad_shift, grad_scale], 0).astype(HALF_TYPE)
        grad_mod_weight = jnp.einsum(
            "db,keb->dke", embed, grad_modul, preferred_element_type=FULL_TYPE
        )
        grad_stream = grad_stream + norm_back(grad_normed * scaling, normal_one, inverse_one)
        grad_skip_gain = jnp.sum(grad_stream * skip_normal, (1, 2))
        grad_skip_bias = jnp.sum(grad_stream, (1, 2))
        grad_joined = norm_back(grad_stream * gain_skip, skip_normal, skip_inverse).astype(
            HALF_TYPE
        )
        grad_skip_w = jnp.stack(
            [
                jnp.einsum("dbl,ebl->de", first_in, grad_joined, preferred_element_type=FULL_TYPE),
                jnp.einsum("dbl,ebl->de", second_in, grad_joined, preferred_element_type=FULL_TYPE),
            ],
            0,
        )
        joined_whole = lax.all_gather(grad_joined, "col", axis=0, tiled=True)
        grad_latent_mb = jnp.einsum(
            "ebl,de->dbl", joined_whole, blocks[3], preferred_element_type=FULL_TYPE
        )
        grad_skip_mb = jnp.einsum(
            "ebl,de->dbl", joined_whole, blocks[4], preferred_element_type=FULL_TYPE
        )
        weight_part = (
            grad_skip_w,
            grad_mod_weight,
            grad_self_in,
            grad_self_out,
            grad_query_weight,
            grad_text,
            grad_cross_out,
            grad_expand,
            grad_reduce,
        )
        gain_part = (
            grad_skip_gain,
            grad_skip_bias,
            grad_cross_gain,
            grad_cross_bias,
            grad_hidden_gain,
            grad_hidden_bias,
        )
        head_part = (grad_q_gain, grad_k_gain, grad_cq_gain, grad_tk_gain)
        return (output, grad_latent_mb, grad_skip_mb, weight_part, gain_part, head_part)

    outputs = []
    grads_latent = []
    grads_skip = []
    weight_sums = None
    gain_sums = None
    head_sums = None
    for micro_index in range(MICRO):
        output, grad_latent, grad_skipped, weight_part, gain_part, head_part = micro_step(
            latent_all[:, micro_index],
            skip_all[:, micro_index],
            cond_all[micro_index],
            text_all[micro_index],
            length_all[micro_index],
            place_all[:, micro_index],
            grad_all[:, micro_index],
        )
        outputs.append(output.reshape(width, block))
        grads_latent.append(grad_latent.reshape(width, block))
        grads_skip.append(grad_skipped.reshape(width, block))
        gain_sums = accumulate(gain_sums, gain_part)
        head_sums = accumulate(head_sums, head_part)
        weight_sums = accumulate(weight_sums, weight_part)
    weight_sums = (
        lax.psum_scatter(
            weight_sums[0].astype(jnp.bfloat16), "row", scatter_dimension=1, tiled=True
        ).astype(jnp.float32),
        lax.psum_scatter(
            weight_sums[1].astype(jnp.bfloat16), "row", scatter_dimension=0, tiled=True
        ).astype(jnp.float32),
        lax.psum_scatter(
            weight_sums[2].astype(jnp.bfloat16), "row", scatter_dimension=0, tiled=True
        ).astype(jnp.float32),
        lax.psum_scatter(
            weight_sums[3].astype(jnp.bfloat16), "row", scatter_dimension=1, tiled=True
        ).astype(jnp.float32),
        lax.psum_scatter(
            weight_sums[4].astype(jnp.bfloat16), "row", scatter_dimension=0, tiled=True
        ).astype(jnp.float32),
        lax.psum_scatter(
            weight_sums[5].astype(jnp.bfloat16), "row", scatter_dimension=0, tiled=True
        ).astype(jnp.float32),
        lax.psum_scatter(
            weight_sums[6].astype(jnp.bfloat16), "row", scatter_dimension=1, tiled=True
        ).astype(jnp.float32),
        lax.psum_scatter(
            weight_sums[7].astype(jnp.bfloat16), "row", scatter_dimension=0, tiled=True
        ).astype(jnp.float32),
        lax.psum_scatter(
            weight_sums[8].astype(jnp.bfloat16), "row", scatter_dimension=1, tiled=True
        ).astype(jnp.float32),
    )
    gain_total = lax.psum(gain_sums, "row")
    head_total = lax.psum(head_sums, ("row", "col"))
    result = jnp.concatenate(outputs, 1)
    grad_latents = jnp.concatenate(grads_latent, 1)
    grad_skip = jnp.concatenate(grads_skip, 1)
    return (
        result,
        grad_latents,
        grad_skip,
        weight_sums[0],
        weight_sums[1],
        weight_sums[2],
        weight_sums[3],
        weight_sums[4],
        weight_sums[5],
        weight_sums[6],
        weight_sums[7],
        weight_sums[8],
        gain_total[0],
        gain_total[1],
        gain_total[2],
        gain_total[3],
        gain_total[4],
        gain_total[5],
        head_total[0],
        head_total[1],
        head_total[2],
        head_total[3],
    )


def solution(mesh):
    return jax.shard_map(
        shards,
        mesh=mesh,
        in_specs=(
            P("col", "row"),
            P("col", "row"),
            P("row", "col"),
            P("row", None, "col"),
            P("row"),
            P(None, "row"),
            P("col", "row"),
            P(None, "row", "col"),
            P("row", None, "col"),
            P("row", None, "col"),
            P("col", "row"),
            P("row", "col"),
            P("row", None, "col"),
            P("col", "row"),
            P("row", "col"),
            P("col", "row"),
            P("col"),
            P("col"),
            P("col"),
            P("col"),
            P("col"),
            P("col"),
            P(),
            P(),
            P(),
            P(),
        ),
        out_specs=(
            P("col", "row"),
            P("col", "row"),
            P("col", "row"),
            P(None, "row", "col"),
            P("row", None, "col"),
            P("row", None, "col"),
            P("col", "row"),
            P("row", "col"),
            P("row", None, "col"),
            P("col", "row"),
            P("row", "col"),
            P("col", "row"),
            P("col"),
            P("col"),
            P("col"),
            P("col"),
            P("col"),
            P("col"),
            P(),
            P(),
            P(),
            P(),
        ),
        check_vma=False,
    )
```

profile of v0, /device:TPU:0, one launch (start us, length us, event | category | flops | bytes accessed | tf_op | source)
XLA Modules:
  0.0 2771.7 jit_solution(15906166652235944853)
XLA Ops:
  34.4 13.0 all-reduce.41
  48.1 14.8 all-gather.53.cloned.1.call-done
  71.0 36.0 %all-gather.49.cloned.1.call-done = bf16[1408,2,1024]{2,1,0:T(2,128)(2,1)} async-done(((bf16[352,2,1024]{2,1,0:T(2,128)(2,1)}), bf16[1408,2,1024]{2,1,0:T(2,128)(2,1)}) %all-gather.49.cloned.1.call-update) | async-done | bytes 5767184 | tf_op jit(solution)/shard_map/all_gather | solution.py:20
  107.0 12.7 fusion.674
  119.7 32.9 %all-gather.67.cloned.1.call-done = bf16[1408,2,1024]{2,1,0:T(2,128)(2,1)} async-done(((bf16[352,2,1024]{2,1,0:T(2,128)(2,1)}), bf16[1408,2,1024]{2,1,0:T(2,128)(2,1)}) %all-gather.67.cloned.1.call-update) | async-done | bytes 5767184 | tf_op jit(solution)/shard_map/all_gather | solution.py:20
  152.6 12.7 fusion.673
  165.3 39.5 %all-gather.51.cloned.1.call-done = bf16[2,1408,352]{2,1,0:T(8,128)(2,1)} async-done(((bf16[2,176,352]{2,1,0:T(8,128)(2,1)}), bf16[2,1408,352]{2,1,0:T(8,128)(2,1)}) %all-gather.51.cloned.1.call-update) | async-done | bytes 1982480 | tf_op jit(solution)/shard_map/all_gather | solution.py:168
  213.2 35.0 %all-gather.73.cloned.1.call-done = bf16[1408,2,1024]{2,1,0:T(2,128)(2,1)} async-done(((bf16[352,2,1024]{2,1,0:T(2,128)(2,1)}), bf16[1408,2,1024]{2,1,0:T(2,128)(2,1)}) %all-gather.73.cloned.1.call-update) | async-done | bytes 5767184 | tf_op jit(solution)/shard_map/all_gather | solution.py:20
  248.2 11.8 fusion.672
  289.3 11.1 all-reduce.38
  348.4 20.6 all-gather.109.cloned.1.call-done
  378.5 19.7 all-gather.121.cloned.1.call-done
  507.6 33.1 %all_gather.151 = bf16[352,1408]{0,1:T(8,128)(2,1)S(1)} all-gather(bf16[352,176]{0,1:T(8,128)(2,1)S(1)} %copy-done.243), channel_id=1, replica_groups=mesh['row'=8,'col'=4] {'row'}, dimensions={1}, use_global_device_ids=true | all-gather | bytes 1115136 | tf_op jit(solution)/shard_map/all_gather | solution.py:171
  547.4 13.9 all-to-all-done
  576.5 11.0 all-reduce.37
  601.7 35.0 %all_gather.155 = bf16[1408,352]{1,0:T(8,128)(2,1)} all-gather(bf16[176,352]{1,0:T(8,128)(2,1)S(1)} %copy-done.244), channel_id=1, replica_groups=mesh['row'=8,'col'=4] {'row'}, dimensions={0}, use_global_device_ids=true | all-gather | bytes 1115136 | tf_op jit(solution)/shard_map/all_gather | solution.py:172
  670.8 11.7 all_gather.173
  697.8 33.5 %all_gather.157 = bf16[352,1408]{0,1:T(8,128)(2,1)S(1)} all-gather(bf16[352,176]{0,1:T(8,128)(2,1)S(1)} %copy-done.245), channel_id=1, replica_groups=mesh['row'=8,'col'=4] {'row'}, dimensions={1}, use_global_device_ids=true | all-gather | bytes 1115136 | tf_op jit(solution)/shard_map/all_gather | solution.py:174
  733.6 21.3 all_to_all.95
  816.2 30.3 %all-gather.63.cloned.1.call-done = bf16[1408,1536]{1,0:T(8,128)(2,1)} async-done(((bf16[176,1536]{1,0:T(8,128)(2,1)}), bf16[1408,1536]{1,0:T(8,128)(2,1)}) %all-gather.63.cloned.1.call-update) | async-done | bytes 4325392 | tf_op jit(solution)/shard_map/all_gather | solution.py:175
  846.6 26.9 all-gather.125.cloned.1.call-done
  883.0 19.1 all-gather.99.cloned.1.call-done
  902.1 77.2 %all-gather.65.cloned.1.call-done = bf16[1536,1408]{0,1:T(8,128)(2,1)} async-done(((bf16[1536,176]{0,1:T(8,128)(2,1)}), bf16[1536,1408]{0,1:T(8,128)(2,1)}) %all-gather.65.cloned.1.call-update) | async-done | bytes 4325392 | tf_op jit(solution)/shard_map/all_gather | solution.py:176
  979.3 12.1 fusion.58
  1015.6 19.1 all-gather.89.cloned.1.call-done
  1034.7 12.1 fusion.51
  1073.5 18.8 all-gather.79.cloned.1.call-done
  1092.3 12.1 fusion.44
  1114.4 16.7 reduce-scatter.33.cloned.1.call-done
  1131.2 39.1 %reduce-scatter.29.cloned.1.call-done = bf16[352,1,1024]{2,0,1:T(8,128)(2,1)} async-done(((bf16[1408,1,1024]{2,0,1:T(8,128)(2,1)}), bf16[352,1,1024]{2,0,1:T(8,128)(2,1)}) %reduce-scatter.29.cloned.1.call-update) | async-done | bytes 720912 | tf_op jit(solution)/shard_map/reduce_scatter | solution.py:24
  1170.2 38.7 %reduce-scatter.25.cloned.1.call-done = bf16[352,1,1024]{2,0,1:T(8,128)(2,1)} async-done(((bf16[1408,1,1024]{2,0,1:T(8,128)(2,1)}), bf16[352,1,1024]{2,0,1:T(8,128)(2,1)}) %reduce-scatter.25.cloned.1.call-update) | async-done | bytes 720912 | tf_op jit(solution)/shard_map/reduce_scatter | solution.py:24
  1233.8 24.2 all-gather.81.cloned.1.call-done
  1261.4 25.9 all-gather.91.cloned.1.call-done
  1297.5 18.3 all-gather.101.cloned.1.call-done
  1323.3 11.7 multiply_reduce_fusion.21
  1335.1 11.8 fusion.283
  1347.0 14.7 multiply_reduce_fusion.9
  1403.1 29.3 %all_to_all.96 = bf16[4,352,352]{1,2,0:T(8,128)(2,1)S(1)} all-to-all(bf16[4,352,352]{1,2,0:T(8,128)(2,1)S(1)} %copy.205), channel_id=1, replica_groups=mesh['row'=8,'col'=4] {'col'}, dimensions={0} | all-to-all | bytes 1982464 | tf_op jit(solution)/shard_map/all_to_all | solution.py:181
  1442.6 22.0 all-gather.93.cloned.1.call-done
  1483.1 20.5 reduce-scatter.23.cloned.1.call-done
  1509.2 33.2 %reduce-scatter.19.cloned.1.call-done = bf16[352,1,1024]{2,0,1:T(8,128)(2,1)} async-done(((bf16[1408,1,1024]{2,0,1:T(8,128)(2,1)}), bf16[352,1,1024]{2,0,1:T(8,128)(2,1)}) %reduce-scatter.19.cloned.1.call-update) | async-done | bytes 720912 | tf_op jit(solution)/shard_map/reduce_scatter | solution.py:24
  1548.3 33.1 %reduce-scatter.21.cloned.1.call-done = bf16[352,1,1024]{2,0,1:T(8,128)(2,1)} async-done(((bf16[1408,1,1024]{2,0,1:T(8,128)(2,1)}), bf16[352,1,1024]{2,0,1:T(8,128)(2,1)}) %reduce-scatter.21.cloned.1.call-update) | async-done | bytes 720912 | tf_op jit(solution)/shard_map/reduce_scatter | solution.py:24
  1587.0 23.6 all-gather.105.cloned.1.call-done
  1624.0 24.5 fusion.265
  1648.5 25.8 broadcast_multiply_fusion.1
  1692.7 23.9 fusion.277
  1719.4 25.5 broadcast_multiply_fusion.5
  1772.5 23.9 fusion.271
  1796.4 25.5 broadcast_multiply_fusion.3
  1851.0 10.8 fusion.445
  1887.0 12.0 fusion.180
  1984.9 11.2 multiply_reduce_fusion.54
  2079.9 11.1 all-reduce.31
  2157.9 57.8 %reduce-scatter.43.cloned.1.call-done = bf16[352,176]{0,1:T(8,128)(2,1)} async-done(((bf16[352,1408]{0,1:T(8,128)(2,1)}), bf16[352,176]{0,1:T(8,128)(2,1)}) %reduce-scatter.43.cloned.1.call-update) | async-done | bytes 123920 | tf_op jit(solution)/shard_map/reduce_scatter | solution.py:430
  2217.4 62.8 %reduce-scatter.41.cloned.1.call-done = bf16[176,352]{1,0:T(8,128)(2,1)} async-done(((bf16[1408,352]{1,0:T(8,128)(2,1)}), bf16[176,352]{1,0:T(8,128)(2,1)}) %reduce-scatter.41.cloned.1.call-update) | async-done | bytes 123920 | tf_op jit(solution)/shard_map/reduce_scatter | solution.py:424
  2281.8 65.9 %reduce-scatter.49.cloned.1.call-done = bf16[128,704]{1,0:T(8,128)(2,1)} async-done(((bf16[1024,704]{1,0:T(8,128)(2,1)}), bf16[128,704]{1,0:T(8,128)(2,1)}) %reduce-scatter.49.cloned.1.call-update) | async-done | bytes 180240
  2354.2 40.1 %all-reduce.29 = (f32[88]{0:T(128)}, f32[88]{0:T(128)}, f32[88]{0:T(128)}, f32[88]{0:T(128)}) all-reduce(f32[88]{0:T(128)S(1)} %add_add_fusion.21, f32[88]{0:T(128)S(1)} %add_add_fusion.20, f32[88]{0:T(128)S(1)} %add_add_fusion.19, f32[88]{0:T(128)S(1)} %add_add_fusion.18), channel_id=1, replica_groups=mesh['row'=8,'col'=4] {'row','col'}, use_global_device_ids=true, to_apply=%region_213.214 | all-reduce | flops 352 | bytes 2816 | tf_op jit(solution)/shard_map/psum | solution.py:441
  2394.3 17.6 reduce-scatter.39.cloned.1.call-done
  2413.6 36.0 %all-reduce.30 = (f32[352]{0:T(512)}, f32[352]{0:T(512)}, f32[352]{0:T(512)}, f32[352]{0:T(512)}, f32[352]{0:T(512)}, /*index=5*/f32[352]{0:T(512)}) all-reduce(f32[352]{0:T(512)S(1)} %add_add_fusion.17, f32[352]{0:T(512)S(1)} %add_add_fusion.16, f32[352]{0:T(512)S(1)} %add_add_fusion.15, ...), channel_id=1, replica_groups=mesh['row'=8,'col'=4] {'row'}, use_global_device_ids=true, to_apply=%region_189.190 | all-reduce | flops 2112 | bytes 16896 | tf_op jit(solution)/shard_map/psum | solution.py:440
  2449.6 39.8 %reduce-scatter.37.cloned.1.call-done = bf16[176,3,352]{2,0,1:T(8,128)(2,1)} async-done(((bf16[1408,3,352]{2,0,1:T(8,128)(2,1)}), bf16[176,3,352]{2,0,1:T(8,128)(2,1)}) %reduce-scatter.37.cloned.1.call-update) | async-done | bytes 371728 | tf_op jit(solution)/shard_map/reduce_scatter | solution.py:418
  2491.4 160.4 %all-reduce.44.cloned.1.call-done = (bf16[2,1408,352]{2,0,1:T(2,128)(2,1)}, bf16[1408,2,352]{2,1,0:T(2,128)(2,1)}) async-done(((bf16[2,1408,352]{2,0,1:T(2,128)(2,1)}, bf16[1408,2,352]{2,1,0:T(2,128)(2,1)}), (bf16[2,1408,352]{2,0,1:T(2,128)(2,1)}, bf16[1408,2,352]{2,1,0:T(2,128)(2,1)})) %all-reduce.44.cloned.1.call-update) | async-done | bytes 3964944
  2660.0 31.0 %all-gather.97.cloned.1.call-done = bf16[1408,1,1024]{2,0,1:T(8,128)(2,1)} async-done(((bf16[352,1,1024]{2,0,1:T(8,128)(2,1)}), bf16[1408,1,1024]{2,0,1:T(8,128)(2,1)}) %all-gather.97.cloned.1.call-update) | async-done | bytes 2883600 | tf_op jit(solution)/shard_map/all_gather | solution.py:360
  2694.4 24.0 all-gather.107.cloned.1.call-done
  2721.9 25.2 all-gather.87.cloned.1.call-done
  (1274 shorter events, 984.7 us)
Async XLA Ops:
  7.2 55.7 %all-gather.53.cloned.1.call-start = ((), (), s32[]{:S(2)}) async-start(), calls=%async_computation.23 | async-start | bytes 2433024 | tf_op jit(solution)/shard_map/all_gather | solution.py:169
  7.9 99.1 %all-gather.49.cloned.1.call-start = ((), (), s32[]{:S(2)}) async-start(), calls=%async_computation.21 | async-start | bytes 7208960 | tf_op jit(solution)/shard_map/all_gather | solution.py:20
  21.7 130.9 %all-gather.67.cloned.1.call-start = ((), (), s32[]{:S(2)}) async-start(), calls=%async_computation.31 | async-start | bytes 7208960 | tf_op jit(solution)/shard_map/all_gather | solution.py:20
  27.2 177.6 %all-gather.51.cloned.1.call-start = ((), (), s32[]{:S(2)}) async-start(), calls=%async_computation.22 | async-start | bytes 2433024 | tf_op jit(solution)/shard_map/all_gather | solution.py:168
  27.8 220.4 %all-gather.73.cloned.1.call-start = ((), (), s32[]{:S(2)}) async-start(), calls=%async_computation.35 | async-start | bytes 7208960 | tf_op jit(solution)/shard_map/all_gather | solution.py:20
  31.8 280.1 %all-gather.55.cloned.1.call-start = ((), (), s32[]{:S(2)}) async-start(), calls=%async_computation.24 | async-start | bytes 3649536 | tf_op jit(solution)/shard_map/all_gather | solution.py:170
  32.4 307.4 %all-gather.115.cloned.1.call-start = ((), (), s32[]{:S(2)}) async-start(), calls=%async_computation.69 | async-start | bytes 3604480 | tf_op jit(solution)/shard_map/all_gather | solution.py:20
  304.0 64.9 %all-gather.109.cloned.1.call-start = ((), (), s32[]{:S(2)}) async-start(), calls=%async_computation.66 | async-start | bytes 3604480 | tf_op jit(solution)/shard_map/all_gather | solution.py:20
  304.8 93.4 %all-gather.121.cloned.1.call-start = ((), (), s32[]{:S(2)}) async-start(), calls=%async_computation.72 | async-start | bytes 3604480 | tf_op jit(solution)/shard_map/all_gather | solution.py:20
  320.6 240.7 %all-gather.57.cloned.1.call-start = ((), (), s32[]{:S(2)}) async-start(), calls=%async_computation.25 | async-start | bytes 3604480 | tf_op jit(solution)/shard_map/all_gather | solution.py:30
  440.5 126.0 %all-gather.75.cloned.1.call-start = ((), (), s32[]{:S(2)}) async-start(), calls=%async_computation.36 | async-start | bytes 3604480 | tf_op jit(solution)/shard_map/all_gather | solution.py:30
  476.1 95.7 %all-gather.69.cloned.1.call-start = ((), (), s32[]{:S(2)}) async-start(), calls=%async_computation.32 | async-start | bytes 3604480 | tf_op jit(solution)/shard_map/all_gather | solution.py:30
  542.1 19.2 all-to-all-start
  546.4 90.3 %all-gather.59.cloned.1.call-start = ((), (), s32[]{:S(2)}) async-start(), calls=%async_computation.26 | async-start | bytes 1622016 | tf_op jit(solution)/shard_map/all_gather | solution.py:173
  547.2 92.8 %all-gather.111.cloned.1.call-start = ((), (), s32[]{:S(2)}) async-start(), calls=%async_computation.67 | async-start | bytes 3604480 | tf_op jit(solution)/shard_map/all_gather | solution.py:20
  592.0 68.0 %all-gather.117.cloned.1.call-start = ((), (), s32[]{:S(2)}) async-start(), calls=%async_computation.70 | async-start | bytes 3604480 | tf_op jit(solution)/shard_map/all_gather | solution.py:20
  592.6 93.6 %all-gather.123.cloned.1.call-start = ((), (), s32[]{:S(2)}) async-start(), calls=%async_computation.73 | async-start | bytes 3604480 | tf_op jit(solution)/shard_map/all_gather | solution.py:20
  593.3 161.6 %all-gather.61.cloned.1.call-start = ((), (), s32[]{:S(2)}) async-start(), calls=%async_computation.27 | async-start | bytes 3604480 | tf_op jit(solution)/shard_map/all_gather | solution.py:30
  650.5 109.1 %all-gather.71.cloned.1.call-start = ((), (), s32[]{:S(2)}) async-start(), calls=%async_computation.33 | async-start | bytes 3604480 | tf_op jit(solution)/shard_map/all_gather | solution.py:30
  659.8 675.2 %copy-start.211 = (f32[333,4]{0,1:T(4,128)}, f32[333,4]{0,1:T(4,128)S(1)}, u32[]{:S(2)}) copy-start(f32[333,4]{0,1:T(4,128)S(1)} %broadcast_multiply_fusion.16) | copy-start | bytes 15988
  659.9 675.1 %copy-start.258 = (f32[333,4]{0,1:T(4,128)}, f32[333,4]{0,1:T(4,128)S(1)}, u32[]{:S(2)}) copy-start(f32[333,4]{0,1:T(4,128)S(1)} %fusion.565) | copy-start | bytes 15988
  663.9 701.5 %copy-start.11 = (f32[1024,352]{0,1:T(8,128)}, f32[1024,352]{0,1:T(8,128)S(1)}, u32[]{:S(2)}) copy-start(f32[1024,352]{0,1:T(8,128)S(1)} %fusion.702) | copy-start | bytes 4325380
  664.1 701.4 %copy-start.187 = (f32[1024,4]{0,1:T(4,128)}, f32[1024,4]{0,1:T(4,128)S(1)}, u32[]{:S(2)}) copy-start(f32[1024,4]{0,1:T(4,128)S(1)} %broadcast_multiply_fusion.9) | copy-start | bytes 49156
  670.1 99.7 %all-gather.77.cloned.1.call-start = ((), (), s32[]{:S(2)}) async-start(), calls=%async_computation.37 | async-start | bytes 3604480 | tf_op jit(solution)/shard_map/all_gather | solution.py:30
  689.8 675.7 %copy-start.198 = (f32[1024,4]{0,1:T(4,128)}, f32[1024,4]{0,1:T(4,128)S(1)}, u32[]{:S(2)}) copy-start(f32[1024,4]{0,1:T(4,128)S(1)} %broadcast_multiply_fusion.6) | copy-start | bytes 49156
  697.1 149.5 %all-gather.63.cloned.1.call-start = ((), (), s32[]{:S(2)}) async-start(), calls=%async_computation.28 | async-start | bytes 4866048 | tf_op jit(solution)/shard_map/all_gather | solution.py:175
  697.7 175.7 %all-gather.125.cloned.1.call-start = ((), (), s32[]{:S(2)}) async-start(), calls=%async_computation.74 | async-start | bytes 3604480 | tf_op jit(solution)/shard_map/all_gather | solution.py:20
  789.5 112.6 %all-gather.99.cloned.1.call-start = ((), (), s32[]{:S(2)}) async-start(), calls=%async_computation.53 | async-start | bytes 3604480 | tf_op jit(solution)/shard_map/all_gather | solution.py:20
  803.3 176.0 %all-gather.65.cloned.1.call-start = ((), (), s32[]{:S(2)}) async-start(), calls=%async_computation.29 | async-start | bytes 4866048 | tf_op jit(solution)/shard_map/all_gather | solution.py:176
  804.1 202.0 %all-gather.119.cloned.1.call-start = ((), (), s32[]{:S(2)}) async-start(), calls=%async_computation.71 | async-start | bytes 3604480 | tf_op jit(solution)/shard_map/all_gather | solution.py:20
  804.6 230.1 %all-gather.89.cloned.1.call-start = ((), (), s32[]{:S(2)}) async-start(), calls=%async_computation.46 | async-start | bytes 3604480 | tf_op jit(solution)/shard_map/all_gather | solution.py:20
  810.2 253.6 %all-gather.113.cloned.1.call-start = ((), (), s32[]{:S(2)}) async-start(), calls=%async_computation.68 | async-start | bytes 3604480 | tf_op jit(solution)/shard_map/all_gather | solution.py:20
  810.7 281.5 %all-gather.79.cloned.1.call-start = ((), (), s32[]{:S(2)}) async-start(), calls=%async_computation.39 | async-start | bytes 3604480 | tf_op jit(solution)/shard_map/all_gather | solution.py:20
  816.2 315.0 %reduce-scatter.33.cloned.1.call-start = ((), (), s32[]{:S(2)}) async-start(), calls=%async_computation.54 | async-start | bytes 3604480 | tf_op jit(solution)/shard_map/reduce_scatter | solution.py:24
  1001.5 168.7 %reduce-scatter.29.cloned.1.call-start = ((), (), s32[]{:S(2)}) async-start(), calls=%async_computation.47 | async-start | bytes 3604480 | tf_op jit(solution)/shard_map/reduce_scatter | solution.py:24
  1056.9 152.0 %reduce-scatter.25.cloned.1.call-start = ((), (), s32[]{:S(2)}) async-start(), calls=%async_computation.40 | async-start | bytes 3604480 | tf_op jit(solution)/shard_map/reduce_scatter | solution.py:24
  1114.4 143.6 %all-gather.81.cloned.1.call-start = ((), (), s32[]{:S(2)}) async-start(), calls=%async_computation.41 | async-start | bytes 3604480 | tf_op jit(solution)/shard_map/all_gather | solution.py:20
  1229.6 57.6 %all-gather.91.cloned.1.call-start = ((), (), s32[]{:S(2)}) async-start(), calls=%async_computation.48 | async-start | bytes 3604480 | tf_op jit(solution)/shard_map/all_gather | solution.py:20
  1230.4 85.4 %all-gather.101.cloned.1.call-start = ((), (), s32[]{:S(2)}) async-start(), calls=%async_computation.55 | async-start | bytes 3604480 | tf_op jit(solution)/shard_map/all_gather | solution.py:20
  1233.4 199.0 %all-gather.83.cloned.1.call-start = ((), (), s32[]{:S(2)}) async-start(), calls=%async_computation.42 | async-start | bytes 3604480 | tf_op jit(solution)/shard_map/all_gather | solution.py:30
  1368.0 69.7 %all-gather.103.cloned.1.call-start = ((), (), s32[]{:S(2)}) async-start(), calls=%async_computation.56 | async-start | bytes 3604480 | tf_op jit(solution)/shard_map/all_gather | solution.py:30
  1368.8 95.9 %all-gather.93.cloned.1.call-start = ((), (), s32[]{:S(2)}) async-start(), calls=%async_computation.49 | async-start | bytes 3604480 | tf_op jit(solution)/shard_map/all_gather | solution.py:30
  1369.3 134.2 %reduce-scatter.23.cloned.1.call-start = ((), (), s32[]{:S(2)}) async-start(), calls=%async_computation.38 | async-start | bytes 3604480 | tf_op jit(solution)/shard_map/reduce_scatter | solution.py:24
  1379.8 162.6 %reduce-scatter.19.cloned.1.call-start = ((), (), s32[]{:S(2)}) async-start(), calls=%async_computation.30 | async-start | bytes 3604480 | tf_op jit(solution)/shard_map/reduce_scatter | solution.py:24
  1390.5 190.8 %reduce-scatter.21.cloned.1.call-start = ((), (), s32[]{:S(2)}) async-start(), calls=%async_computation.34 | async-start | bytes 3604480 | tf_op jit(solution)/shard_map/reduce_scatter | solution.py:24
  1401.1 209.5 %all-gather.105.cloned.1.call-start = ((), (), s32[]{:S(2)}) async-start(), calls=%async_computation.57 | async-start | bytes 3604480 | tf_op jit(solution)/shard_map/all_gather | solution.py:20
  1509.2 169.2 %all-gather.85.cloned.1.call-start = ((), (), s32[]{:S(2)}) async-start(), calls=%async_computation.43 | async-start | bytes 3604480 | tf_op jit(solution)/shard_map/all_gather | solution.py:20
  1548.1 210.4 %all-gather.95.cloned.1.call-start = ((), (), s32[]{:S(2)}) async-start(), calls=%async_computation.50 | async-start | bytes 3604480 | tf_op jit(solution)/shard_map/all_gather | solution.py:20
  1586.9 455.8 %reduce-scatter.35.cloned.1.call-start = ((), (), s32[]{:S(2)}) async-start(), calls=%async_computation.58 | async-start | bytes 3604480 | tf_op jit(solution)/shard_map/reduce_scatter | solution.py:24
  1847.3 195.5 %reduce-scatter.27.cloned.1.call-start = ((), (), s32[]{:S(2)}) async-start(), calls=%async_computation.44 | async-start | bytes 3604480 | tf_op jit(solution)/shard_map/reduce_scatter | solution.py:24
  1867.1 186.9 %reduce-scatter.31.cloned.1.call-start = ((), (), s32[]{:S(2)}) async-start(), calls=%async_computation.51 | async-start | bytes 3604480 | tf_op jit(solution)/shard_map/reduce_scatter | solution.py:24
  1886.8 266.7 %reduce-scatter.47.cloned.1.call-start = ((), (), s32[]{:S(2)}) async-start(), calls=%async_computation.65 | async-start | bytes 4866048 | tf_op jit(solution)/shard_map/reduce_scatter | solution.py:436
  1920.0 235.6 %reduce-scatter.45.cloned.1.call-start = ((), (), s32[]{:S(2)}) async-start(), calls=%async_computation.64 | async-start | bytes 4866048 | tf_op jit(solution)/shard_map/reduce_scatter | solution.py:433
  1940.9 274.8 %reduce-scatter.43.cloned.1.call-start = ((), (), s32[]{:S(2)}) async-start(), calls=%async_computation.63 | async-start | bytes 1216512 | tf_op jit(solution)/shard_map/reduce_scatter | solution.py:430
  1984.6 295.6 %reduce-scatter.41.cloned.1.call-start = ((), (), s32[]{:S(2)}) async-start(), calls=%async_computation.62 | async-start | bytes 1216512 | tf_op jit(solution)/shard_map/reduce_scatter | solution.py:424
  2004.8 342.9 %reduce-scatter.49.cloned.1.call-start = ((), (), s32[]{:S(2)}) async-start(), calls=%async_computation.75 | async-start | bytes 1769472
  2016.9 395.0 %reduce-scatter.39.cloned.1.call-start = ((), (), s32[]{:S(2)}) async-start(), calls=%async_computation.61 | async-start | bytes 1216512 | tf_op jit(solution)/shard_map/reduce_scatter | solution.py:421
  2026.6 462.8 %reduce-scatter.37.cloned.1.call-start = ((), (), s32[]{:S(2)}) async-start(), calls=%async_computation.60 | async-start | bytes 3649536 | tf_op jit(solution)/shard_map/reduce_scatter | solution.py:418
  2042.7 609.1 %all-reduce.44.cloned.1.call-start = ((), (), s32[]{:S(2)}) async-start(), calls=%async_computation.76 | async-start | bytes 8650752
  2140.5 550.5 %all-gather.97.cloned.1.call-start = ((), (), s32[]{:S(2)}) async-start(), calls=%async_computation.52 | async-start | bytes 3604480 | tf_op jit(solution)/shard_map/all_gather | solution.py:360
  2141.3 577.2 %all-gather.107.cloned.1.call-start = ((), (), s32[]{:S(2)}) async-start(), calls=%async_computation.59 | async-start | bytes 3604480 | tf_op jit(solution)/shard_map/all_gather | solution.py:360
  2142.0 605.1 %all-gather.87.cloned.1.call-start = ((), (), s32[]{:S(2)}) async-start(), calls=%async_computation.45 | async-start | bytes 3604480 | tf_op jit(solution)/shard_map/all_gather | solution.py:360
  2148.7 507.0 %all-to-all-start.4 = ((bf16[4,352,352]{1,2,0:T(8,128)(2,1)}), bf16[4,352,352]{1,2,0:T(8,128)(2,1)}, u32[]{:S(2)}, u32[]{:S(2)}) async-start(bf16[4,352,352]{1,2,0:T(8,128)(2,1)} %copy.223), calls=%async_computation.13 | async-start | bytes 2162688 | tf_op jit(solution)/shard_map/all_to_all | solution.py:183
  2655.7 97.2 %all-to-all-start.3 = ((bf16[4,352,352]{1,2,0:T(8,128)(2,1)}), bf16[4,352,352]{1,2,0:T(8,128)(2,1)}, u32[]{:S(2)}, u32[]{:S(2)}) async-start(bf16[4,352,352]{1,2,0:T(8,128)(2,1)} %copy.210), calls=%async_computation.8 | async-start | bytes 2162688 | tf_op jit(solution)/shard_map/all_to_all | solution.py:182
  (373 other events, 9591.5 us)
Sparse Core Ops, SparseCore 0:
  10.2 52.6 all-gather.52
  65.0 41.9 all-gather.48
  109.1 43.3 all-gather.66
  154.7 50.1 all-gather.50
  206.3 41.8 all-gather.72
  250.3 61.5 all-gather.54
  314.0 25.6 all-gather.114
  341.9 27.0 all-gather.108
  371.1 27.0 all-gather.120
  440.5 27.0 all-gather.56
  476.2 27.0 all-gather.74
  507.8 27.2 all-gather.68
  549.3 45.0 all-gather.58
  596.4 25.4 all-gather.110
  623.9 27.0 all-gather.116
  652.4 30.4 all-gather.122
  684.3 26.5 all-gather.60
  712.3 27.1 all-gather.70
  741.1 28.6 all-gather.76
  771.8 74.7 all-gather.62
  848.1 25.2 all-gather.124
  875.0 27.0 all-gather.98
  904.3 74.9 all-gather.64
  980.7 25.2 all-gather.118
  1007.6 27.0 all-gather.88
  1036.7 27.0 all-gather.112
  1065.2 27.0 all-gather.78
  1094.8 36.3 reduce-scatter.32
  1133.9 36.3 reduce-scatter.28
  1172.6 36.3 reduce-scatter.24
  1229.8 28.1 all-gather.80
  1260.1 27.0 all-gather.90
  1288.7 27.0 all-gather.100
  1368.1 27.0 all-gather.82
  1396.8 38.6 all-gather.102
  1437.6 27.0 all-gather.92
  1467.2 36.3 reduce-scatter.22
  1506.1 36.3 reduce-scatter.18
  1545.0 36.3 reduce-scatter.20
  1583.5 27.0 all-gather.104
  1612.2 27.0 all-gather.84
  1640.8 27.0 all-gather.94
  1847.5 36.6 reduce-scatter.34
  1886.8 36.3 reduce-scatter.26
  1926.2 36.3 reduce-scatter.30
  1967.0 89.8 reduce-scatter.46
  2060.9 89.5 reduce-scatter.44
  2154.2 61.5 reduce-scatter.42
  2219.4 60.7 reduce-scatter.40
  2284.0 63.6 reduce-scatter.48
  2351.0 60.8 reduce-scatter.38
  2415.6 73.8 reduce-scatter.36
  2492.9 158.8 all-reduce.43
  2653.3 37.6 all-gather.96
  2692.6 25.8 all-gather.106
  2720.0 27.0 all-gather.86
where the time goes:
time: 2780 us; the launch traced here: 2770 us
  waiting for transfers between devices  1220 us (44%)
  matrix products  775 us (28%)
  blocking collectives  360 us (13%)
  other arithmetic  211 us (8%)
  local copies, waits for them, and re-layouts  153 us (6%)
    all_gather x21, waiting for transfers between devices, spread(): return lax.all_gather(values, 'col', axis=0, tiled=True)  341 us
    unnamed x58, waiting for transfers between devices  237 us
    reduce_scatter x9, waiting for transfers between devices, collect(): lax.psum_scatter(partials.astype(jnp.bfloat16), 'col', scatter_dimension=...  181 us
    dot_general x6, matrix products, attend_backward(): jnp.einsum('bhqk,bkhd->bqhd', grad_prod, key_in, preferred_element_type=F...  115 us
    dot_general x6, matrix products, attend_backward(): jnp.einsum('bhqk,bqhd->bkhd', grad_prod, query_in, preferred_element_type...  104 us
    psum x9, blocking collectives, row_sums(): return lax.psum((first, second), 'col')  91.8 us
    all_gather x3, waiting for transfers between devices, micro_step(): joined_whole = lax.all_gather(grad_joined, 'col', axis=0, tiled=True)  80.3 us
    all_gather x1, waiting for transfers between devices, shards(): lax.all_gather(reduce_weight, 'row', axis=1, tiled=True)  77.2 us
  transfers between devices with their start and end apart: 59, of which 39 were waited for; matrix products, arithmetic and copies ran while one was open for 33% of the time, Pallas kernels for 0%

commit v1 on v0

v1 whole, which is shorter than its diff:
```python
from functools import partial
import math

import jax
import jax.numpy as jnp
from jax import lax
from jax.experimental import pallas as pl
from jax.experimental.pallas import tpu as pltpu
from jax.sharding import PartitionSpec as P

L = 1024
EPSILON = 1e-06
BF = jnp.bfloat16
F32 = jnp.float32
KEYPAD = 128
DEVICES = ("col", "row")


def einsum(spec, left, right):
    return jnp.einsum(spec, left, right, preferred_element_type=F32)


def dot(left, right, dims):
    return lax.dot_general(left, right, (dims, ((), ())), preferred_element_type=F32)


def block_of(length):
    return 256 if length % 256 == 0 else length


def attend_kernel(masked, scale, length_ref, q_ref, k_ref, v_ref, o_ref, lse_ref):
    queries = q_ref.shape[2]
    keys = k_ref.shape[2]
    step = block_of(queries)
    key = k_ref[0]
    value = v_ref[0]
    for first in range(0, queries, step):
        query = q_ref[0, :, first : first + step]
        scores = dot(key, query, ((0,), (0,))) * scale
        if masked:
            place = lax.broadcasted_iota(jnp.int32, (keys, step), 0)
            scores = jnp.where(place < length_ref[0], scores, -1e9)
        peak = jnp.max(scores, 0, keepdims=True)
        expo = jnp.exp(scores - peak)
        total = jnp.sum(expo, 0, keepdims=True)
        probs = (expo * (1.0 / total)).astype(BF)
        o_ref[0, :, first : first + step] = dot(value, probs, ((1,), (0,))).astype(BF)
        lse_ref[0, :, first : first + step] = peak + jnp.log(total)


def attend_back_kernel(
    masked, scale, length_ref, q_ref, k_ref, v_ref, g_ref, lse_ref, dq_ref, dk_ref, dv_ref
):
    queries = q_ref.shape[2]
    keys = k_ref.shape[2]
    step = block_of(queries)
    key = k_ref[0]
    value = v_ref[0]
    grad_key = None
    grad_value = None
    for first in range(0, queries, step):
        query = q_ref[0, :, first : first + step]
        grad = g_ref[0, :, first : first + step]
        scores = dot(key, query, ((0,), (0,))) * scale
        if masked:
            place = lax.broadcasted_iota(jnp.int32, (keys, step), 0)
            scores = jnp.where(place < length_ref[0], scores, -1e9)
        probs = jnp.exp(scores - lse_ref[0, :, first : first + step])
        part_value = dot(grad, probs.astype(BF), ((1,), (1,)))
        grad_probs = dot(value, grad, ((0,), (0,)))
        crossed = probs * grad_probs
        delta = jnp.sum(crossed, 0, keepdims=True)
        product = ((crossed - probs * delta) * scale).astype(BF)
        dq_ref[0, :, first : first + step] = dot(key, product, ((1,), (0,))).astype(dq_ref.dtype)
        part_key = dot(query, product, ((1,), (1,)))
        grad_key = part_key if grad_key is None else grad_key + part_key
        grad_value = part_value if grad_value is None else grad_value + part_value
    dk_ref[0] = grad_key.astype(dk_ref.dtype)
    dv_ref[0] = grad_value.astype(dv_ref.dtype)


def costs(heads, queries, keys, dim, products, moved):
    return pl.CostEstimate(
        flops=2 * products * heads * queries * keys * dim,
        transcendentals=heads * queries * keys,
        bytes_accessed=moved,
    )


def attend(length, query, key, value, masked):
    heads, dim, queries = query.shape
    keys = key.shape[2]
    wide = pl.BlockSpec((1, dim, queries), lambda h: (h, 0, 0))
    narrow = pl.BlockSpec((1, dim, keys), lambda h: (h, 0, 0))
    line = pl.BlockSpec((1, 1, queries), lambda h: (h, 0, 0))
    return pl.pallas_call(
        partial(attend_kernel, masked, dim ** (-0.5)),
        grid=(heads,),
        in_specs=[pl.BlockSpec(memory_space=pltpu.SMEM), wide, narrow, narrow],
        out_specs=[wide, line],
        out_shape=[
            jax.ShapeDtypeStruct((heads, dim, queries), BF),
            jax.ShapeDtypeStruct((heads, 1, queries), F32),
        ],
        cost_estimate=costs(heads, queries, keys, dim, 2, 4 * heads * dim * (queries + keys)),
    )(length, query, key, value)


def attend_back(length, query, key, value, grad, logsum, masked, kind):
    heads, dim, queries = query.shape
    keys = key.shape[2]
    wide = pl.BlockSpec((1, dim, queries), lambda h: (h, 0, 0))
    narrow = pl.BlockSpec((1, dim, keys), lambda h: (h, 0, 0))
    line = pl.BlockSpec((1, 1, queries), lambda h: (h, 0, 0))
    return pl.pallas_call(
        partial(attend_back_kernel, masked, dim ** (-0.5)),
        grid=(heads,),
        in_specs=[pl.BlockSpec(memory_space=pltpu.SMEM), wide, narrow, narrow, wide, line],
        out_specs=[wide, narrow, narrow],
        out_shape=[
            jax.ShapeDtypeStruct((heads, dim, queries), kind),
            jax.ShapeDtypeStruct((heads, dim, keys), kind),
            jax.ShapeDtypeStruct((heads, dim, keys), kind),
        ],
        cost_estimate=costs(heads, queries, keys, dim, 5, 7 * heads * dim * (queries + keys)),
    )(length, query, key, value, grad, logsum)


def normalize(values):
    average = jnp.mean(values, 0, keepdims=True)
    centred = values - average
    inverse = lax.rsqrt(jnp.mean(centred * centred, 0, keepdims=True) + EPSILON)
    return centred * inverse, inverse


def norm_back(grad, normal, inverse):
    average = jnp.mean(grad, 0, keepdims=True)
    crossed = jnp.mean(grad * normal, 0, keepdims=True)
    return inverse * (grad - average - normal * crossed)


def head_norm(values, gain):
    average = jnp.mean(values, 1, keepdims=True)
    centred = values - average
    variance = jnp.mean(centred * centred, 1, keepdims=True)
    return centred * lax.rsqrt(variance + EPSILON) * gain[None, :, None]


def rope_tables(places, head_dim):
    quarter = head_dim // 4
    freqs = jnp.exp(jnp.arange(quarter, dtype=F32) * (-4.0 * math.log(10000.0) / head_dim))
    rows = freqs[:, None] * places[0].astype(F32)[None, :]
    cols = freqs[:, None] * places[1].astype(F32)[None, :]
    angles = jnp.concatenate([rows, rows, cols, cols], 0)
    return jnp.cos(angles), jnp.sin(angles)


def rotate(values):
    quarter = values.shape[1] // 4
    one, two, three, four = (values[:, i * quarter : (i + 1) * quarter] for i in range(4))
    return jnp.concatenate([-two, one, -four, three], 1)


class Piece:
    def __init__(self, start, count, group, sequence):
        self.start = start
        self.count = count
        self.group = group
        self.sequence = sequence


def pieces_of(cols, sequences):
    mine = lax.axis_index("col")
    if cols == 4 and sequences == 3:
        return [
            Piece(0, L // 2, 2, mine // 2),
            Piece(2 * L, L // 4, 4, jnp.int32(2)),
        ]
    return [Piece(s * L, L // cols, cols, jnp.int32(s)) for s in range(sequences)]


def groups_of(size, cols):
    return [list(range(i, i + size)) for i in range(0, cols, size)]


def exchange(values, size, cols):
    if size == cols:
        return lax.all_to_all(values, "col", 0, 0, tiled=True)
    return lax.all_to_all(
        values, "col", 0, 0, tiled=True, axis_index_groups=groups_of(size, cols)
    )


def to_tokens(values, pieces, cols):
    width = values.shape[0]
    parts = []
    for piece in pieces:
        region = values[:, piece.start : piece.start + cols * piece.count]
        parts.append(region.reshape(width, cols, piece.count).transpose(1, 0, 2))
    stacked = jnp.concatenate(parts, 2)
    return exchange(stacked, cols, cols).reshape(cols * width, -1)


def to_features(values, pieces, cols):
    width = values.shape[0] // cols
    got = exchange(values.reshape(cols, width, -1), cols, cols)
    parts = []
    at = 0
    for piece in pieces:
        part = got[:, :, at : at + piece.count]
        parts.append(part.transpose(1, 0, 2).reshape(width, cols * piece.count))
        at += piece.count
    return jnp.concatenate(parts, 1)


def to_heads(values, piece, cols):
    many, heads, dim, count = values.shape
    size = piece.group
    split = values.reshape(many, size, heads // size, dim, count).transpose(1, 0, 2, 3, 4)
    got = exchange(split, size, cols)
    return got.transpose(1, 2, 3, 0, 4).reshape(many, heads // size, dim, size * count)


def from_heads(values, piece, cols):
    many, heads, dim, total = values.shape
    size = piece.group
    split = values.reshape(many, heads, dim, size, total // size).transpose(3, 0, 1, 2, 4)
    got = exchange(split, size, cols)
    return got.transpose(1, 0, 2, 3, 4).reshape(many, size * heads, dim, total // size)


def gather_weights(blocks):
    cols = lax.axis_size("col")
    most = max(block.shape[0] for block in blocks)
    padded = [jnp.pad(b, ((0, most - b.shape[0]), (0, 0))) for b in blocks]
    whole = lax.all_gather(jnp.stack(padded, 0), DEVICES, axis=1, tiled=True)
    result = []
    for index, block in enumerate(blocks):
        part = whole[index].reshape(cols, -1, most, block.shape[1])[:, :, : block.shape[0]]
        result.append(part.reshape(cols, -1, block.shape[1]))
    return result


def pick(values, axis, index):
    return lax.dynamic_index_in_dim(values, index, axis, False)


def add(left, right):
    return (left.astype(F32) + right.astype(F32)).astype(BF)


def swap(values, axis, bit):
    size = lax.axis_size(axis)
    return lax.ppermute(values, axis, [(i, i ^ bit) for i in range(size)])


def halves(blocks):
    core = lax.axis_index("col") % 2
    split = blocks.reshape(blocks.shape[0] // 2, 2, *blocks.shape[1:])
    return pick(split, 1, core), pick(split, 1, 1 - core)


def scatter_grad(keep, send, across):
    cols = lax.axis_size("col")
    rows = lax.axis_size("row")
    if (rows, cols) != (8, 4):
        core = lax.axis_index("col") % 2
        pair = jnp.stack([keep, send], 1)
        pair = jnp.where(core == 0, pair, pair[:, ::-1])
        flat = pair.reshape(-1, keep.shape[2])
        return lax.psum_scatter(flat, DEVICES, scatter_dimension=0, tiled=True).astype(F32)
    up = lax.axis_index("col") // 2
    side = lax.axis_index("row") % 2
    level = lax.axis_index("row") // 2
    shape = (2, 4, 2, keep.shape[1] // 8, keep.shape[2])
    got = swap(send, "col", 1).reshape(shape)
    keep = keep.reshape(shape)

    def stage(kept, got, axis, index, name, bit):
        away = add(pick(kept, axis, 1 - index), pick(got, axis, 1 - index))
        here = add(pick(kept, axis, index), pick(got, axis, index))
        return here, swap(away, name, bit)

    if across:
        keep, got = stage(keep, got, 2, side, "row", 1)
        keep, got = stage(keep, got, 0, up, "col", 2)
    else:
        keep, got = stage(keep, got, 0, up, "col", 2)
        keep, got = stage(keep, got, 1, side, "row", 1)
    total = add(keep, got)
    result = pick(total, 0, level).astype(F32)
    for other in (1, 2, 3):
        result = result + swap(pick(total, 0, level ^ other), "row", 2 * other).astype(F32)
    return result


def weight_grad(spec, across, fixed, blocks):
    mine, others = halves(blocks)
    send = einsum(spec, fixed, others).astype(BF)
    keep = einsum(spec, fixed, mine).astype(BF)
    return scatter_grad(keep, send, across)


def shards(
    latents,
    skip_input,
    condition,
    text_states,
    text_lengths,
    positions,
    out_grad,
    skip_weight,
    modulation,
    self_inputs,
    self_output,
    cross_query,
    cross_keyvalue,
    cross_output,
    expand_weight,
    reduce_weight,
    skip_gain,
    skip_bias,
    cross_gain,
    cross_bias,
    hidden_gain,
    hidden_bias,
    query_gain,
    key_gain,
    cross_query_gain,
    text_key_gain,
):
    cols = lax.axis_size("col")
    rows = lax.axis_size("row")
    mine = lax.axis_index("col")
    my_row = lax.axis_index("row")
    width, row_tokens = latents.shape
    depth = width * cols
    dim = query_gain.shape[0]
    heads = depth // dim
    sequences = row_tokens // L
    tokens = row_tokens // cols
    texts = text_states.shape[1]
    keys = -(-texts // KEYPAD) * KEYPAD
    pieces = pieces_of(cols, sequences)
    starts = [sum(p.count for p in pieces[:i]) for i in range(len(pieces))]

    def cut(values, index):
        return values[..., starts[index] : starts[index] + pieces[index].count]

    first = gather_weights(
        [skip_weight[0], skip_weight[1], self_inputs[:, 0], self_inputs[:, 1], self_inputs[:, 2]]
    )
    w_skip, w_self = first[:2], first[2:]
    w_attn, w_query, w_cross, *w_text = gather_weights(
        [self_output.T, cross_query, cross_output.T, cross_keyvalue[:, 0], cross_keyvalue[:, 1]]
    )
    w_expand, w_reduce = gather_weights([expand_weight, reduce_weight.T])

    gains = jnp.stack(
        [skip_gain, skip_bias, cross_gain, cross_bias, hidden_gain, hidden_bias], 0
    )
    gains = lax.all_gather(gains, "col", axis=1, tiled=True)[:, :, None]
    gain_skip, bias_skip, gain_cross, bias_cross, gain_hidden, bias_hidden = gains

    latent = to_tokens(latents, pieces, cols)
    skipped = to_tokens(skip_input, pieces, cols)
    grad_out = to_tokens(out_grad.astype(BF), pieces, cols)
    text = lax.all_gather(
        jnp.pad(text_states, ((0, 0), (0, keys - texts), (0, 0))), "col", axis=2, tiled=True
    )
    places = jnp.concatenate(
        [
            lax.dynamic_slice_in_dim(positions, p.start + mine * p.count, p.count, 1)
            for p in pieces
        ],
        1,
    )

    embed = lax.all_gather(jax.nn.silu(condition.astype(F32)).astype(BF), "row", axis=0, tiled=True)
    embed_all = lax.all_gather(embed, "col", axis=1, tiled=True)
    block_rows = depth // rows
    embed_rows = lax.dynamic_slice_in_dim(embed_all, my_row * block_rows, block_rows, 1)
    modul_part = einsum("sd,dke->ske", embed_rows, modulation)
    modul = lax.psum(modul_part, "row")
    modul = lax.dynamic_slice_in_dim(modul, my_row * sequences, sequences, 0)
    modul = lax.all_gather(modul, "col", axis=2, tiled=True)
    token_index = lax.broadcasted_iota(jnp.int32, (1, tokens), 1)
    chosen = jnp.stack([lax.dynamic_index_in_dim(modul, p.sequence, 0, False) for p in pieces], 0)
    chosen = lax.optimization_barrier(chosen.reshape(-1, depth)).T

    def per_token(which):
        result = chosen[:, which : which + 1]
        for index in range(1, len(pieces)):
            column = chosen[:, 2 * index + which : 2 * index + which + 1]
            result = jnp.where(token_index >= starts[index], column, result)
        return jnp.broadcast_to(result, (depth, tokens))

    shifting = per_token(0)
    scaling = 1.0 + per_token(1)

    def project(weight, values):
        return einsum("ckn,kt->cnt", weight, values).reshape(-1, values.shape[1])

    def output_project(weight, values):
        return einsum("cnk,ckt->nt", weight, values.reshape(cols, -1, values.shape[1]))

    joined = project(w_skip[0], latent) + project(w_skip[1], skipped)
    skip_normal, skip_inverse = normalize(joined)
    stream = skip_normal * gain_skip + bias_skip
    normal_one, inverse_one = normalize(stream)
    normed_one = (normal_one * scaling + shifting).astype(BF)
    raw = [project(w, normed_one).reshape(heads, dim, tokens) for w in w_self]
    cosine, sine = rope_tables(places, dim)

    def self_piece(value, gain):
        normal = head_norm(value, gain)
        return normal * cosine[None] + rotate(normal) * sine[None]

    rot_query, query_pull = jax.vjp(self_piece, raw[0], query_gain)
    rot_key, key_pull = jax.vjp(self_piece, raw[1], key_gain)
    triple = jnp.stack([rot_query.astype(BF), rot_key.astype(BF), raw[2].astype(BF)], 0)
    none = jnp.zeros((1,), jnp.int32)
    saved_self = []
    mixed_parts = []
    for index, piece in enumerate(pieces):
        whole = to_heads(cut(triple, index), piece, cols)
        mixed, logsum = attend(none, whole[0], whole[1], whole[2], False)
        saved_self.append((whole, logsum))
        mixed_parts.append(from_heads(mixed[None], piece, cols)[0])
    mixed_one = jnp.concatenate(mixed_parts, 2).reshape(depth, tokens)
    stream = stream + output_project(w_attn, mixed_one)
    normal_two, inverse_two = normalize(stream)
    normed_two = (normal_two * gain_cross + bias_cross).astype(BF)
    raw_cross = project(w_query, normed_two).reshape(heads, dim, tokens)
    norm_query, cross_pull = jax.vjp(head_norm, raw_cross, cross_query_gain)
    query_two = norm_query.astype(BF)
    my_text = jnp.concatenate(
        [lax.dynamic_index_in_dim(text, p.sequence, 0, False) for p in pieces], 0
    )
    raw_text = einsum("ckn,tk->cnt", w_text[0], my_text).reshape(heads, dim, -1)
    norm_key, text_pull = jax.vjp(head_norm, raw_text, text_key_gain)
    key_two = norm_key.astype(BF)
    value_two = einsum("ckn,tk->cnt", w_text[1], my_text).reshape(heads, dim, -1).astype(BF)
    saved_cross = []
    mixed_parts = []
    for index, piece in enumerate(pieces):
        length = lax.dynamic_index_in_dim(text_lengths, piece.sequence, 0, True)
        here = slice(index * keys, (index + 1) * keys)
        inputs = (length, cut(query_two, index), key_two[:, :, here], value_two[:, :, here])
        mixed, logsum = attend(*inputs, True)
        saved_cross.append((inputs, logsum))
        mixed_parts.append(mixed)
    mixed_two = jnp.concatenate(mixed_parts, 2).reshape(depth, tokens)
    stream = stream + output_project(w_cross, mixed_two)
    normal_three, inverse_three = normalize(stream)
    normed_three = (normal_three * gain_hidden + bias_hidden).astype(BF)
    inner = einsum("ckn,kt->cnt", w_expand, normed_three)
    activated, gelu_pull = jax.vjp(partial(jax.nn.gelu, approximate=True), inner)
    act = activated.astype(BF)
    output = stream + einsum("cnk,ckt->nt", w_reduce, act)
    result = to_features(output.astype(BF), pieces, cols).astype(F32)

    g_reduce = weight_grad("nt,ckt->cnk", True, grad_out, act)
    g_act = einsum("cnk,nt->ckt", w_reduce, grad_out)
    g_inner = gelu_pull(g_act)[0].astype(BF)
    g_expand = weight_grad("kt,cnt->ckn", False, normed_three, g_inner)
    g_normed = einsum("ckn,cnt->kt", w_expand, g_inner)
    g_hidden_gain = jnp.sum(g_normed * normal_three, 1)
    g_hidden_bias = jnp.sum(g_normed, 1)
    g_stream = grad_out.astype(F32) + norm_back(g_normed * gain_hidden, normal_three, inverse_three)

    g_low = g_stream.astype(BF)
    by_block = lambda values: values.reshape(cols, width, -1)
    g_cross_out = weight_grad("nt,ckt->cnk", True, g_low, by_block(mixed_two))
    g_mixed = einsum("cnk,nt->ckt", w_cross, g_low).astype(BF).reshape(heads, dim, tokens)
    g_queries = []
    g_keys = []
    g_values = []
    for index, piece in enumerate(pieces):
        inputs, logsum = saved_cross[index]
        g_q, g_k, g_v = attend_back(*inputs, cut(g_mixed, index), logsum, True, F32)
        g_queries.append(g_q)
        g_keys.append(g_k)
        g_values.append(g_v)
    g_raw_cross, g_cq_gain = cross_pull(jnp.concatenate(g_queries, 2))
    g_raw_text, g_tk_gain = text_pull(jnp.concatenate(g_keys, 2))
    g_craw = g_raw_cross.astype(BF).reshape(depth, tokens)
    g_pair = [
        by_block(g_raw_text.astype(BF).reshape(depth, -1)),
        by_block(jnp.concatenate(g_values, 2).astype(BF).reshape(depth, -1)),
    ]
    g_text = [weight_grad("tk,cnt->ckn", a, my_text, g) for a, g in zip((True, False), g_pair)]
    g_query_weight = weight_grad("kt,cnt->ckn", False, normed_two, by_block(g_craw))
    g_normed = einsum("ckn,cnt->kt", w_query, by_block(g_craw))
    g_cross_gain = jnp.sum(g_normed * normal_two, 1)
    g_cross_bias = jnp.sum(g_normed, 1)
    g_stream = g_stream + norm_back(g_normed * gain_cross, normal_two, inverse_two)

    g_low = g_stream.astype(BF)
    g_self_out = weight_grad("nt,ckt->cnk", True, g_low, by_block(mixed_one))
    g_mixed = einsum("cnk,nt->ckt", w_attn, g_low).astype(BF).reshape(heads, dim, tokens)
    g_parts = []
    for index, piece in enumerate(pieces):
        whole, logsum = saved_self[index]
        grad = to_heads(cut(g_mixed, index)[None], piece, cols)[0]
        parts = attend_back(none, whole[0], whole[1], whole[2], grad, logsum, False, BF)
        g_parts.append(from_heads(jnp.stack(parts, 0), piece, cols))
    g_heads = jnp.concatenate(g_parts, 3)
    g_raw_q, g_q_gain = query_pull(g_heads[0].astype(F32))
    g_raw_k, g_k_gain = key_pull(g_heads[1].astype(F32))
    g_triple = [
        by_block(g.reshape(depth, tokens))
        for g in (g_raw_q.astype(BF), g_raw_k.astype(BF), g_heads[2])
    ]
    g_self_in = [
        weight_grad("kt,cnt->ckn", a, normed_one, g)
        for a, g in zip((True, False, False), g_triple)
    ]
    g_normed = sum(einsum("ckn,cnt->kt", w, g) for w, g in zip(w_self, g_triple))
    crossed = g_normed * normal_one
    sums = jnp.stack(
        [
            jnp.stack([jnp.sum(cut(g_normed, i), 1), jnp.sum(cut(crossed, i), 1)], 0)
            for i in range(len(pieces))
        ],
        0,
    )
    which = jnp.stack(
        [jnp.where(jnp.arange(sequences) == p.sequence, 1.0, 0.0) for p in pieces], 0
    )
    g_modul = jnp.sum(which[:, :, None, None] * sums[:, None], 0)
    g_modul = lax.psum_scatter(g_modul, "col", scatter_dimension=2, tiled=True).astype(BF)
    g_modul = lax.all_gather(g_modul, "row", axis=0, tiled=True)
    g_modulation = einsum("sd,ske->dke", embed_rows, g_modul)
    g_stream = g_stream + norm_back(g_normed * scaling, normal_one, inverse_one)

    g_skip_gain = jnp.sum(g_stream * skip_normal, 1)
    g_skip_bias = jnp.sum(g_stream, 1)
    g_joined = norm_back(g_stream * gain_skip, skip_normal, skip_inverse).astype(BF)
    g_blocks = by_block(g_joined)
    g_skip_weight = [
        weight_grad("kt,cnt->ckn", a, v, g_blocks)
        for a, v in ((True, latent), (False, skipped))
    ]
    g_latent = einsum("ckn,cnt->kt", w_skip[0], g_blocks)
    g_skipped = einsum("ckn,cnt->kt", w_skip[1], g_blocks)
    g_latents = to_features(g_latent.astype(BF), pieces, cols).astype(F32)
    g_skip = to_features(g_skipped.astype(BF), pieces, cols).astype(F32)

    g_gains = jnp.stack(
        [g_skip_gain, g_skip_bias, g_cross_gain, g_cross_bias, g_hidden_gain, g_hidden_bias], 0
    )
    g_gains = lax.psum(g_gains, ("row", "col"))
    g_gains = lax.dynamic_slice_in_dim(g_gains, mine * width, width, 1)
    g_head = lax.psum(jnp.stack([g_q_gain, g_k_gain, g_cq_gain, g_tk_gain], 0), ("row", "col"))
    return (
        result,
        g_latents,
        g_skip,
        jnp.stack(g_skip_weight, 0),
        g_modulation,
        jnp.stack(g_self_in, 1),
        g_self_out.T,
        g_query_weight,
        jnp.stack(g_text, 1),
        g_cross_out.T,
        g_expand,
        g_reduce.T,
        *[g_gains[i] for i in range(6)],
        *[g_head[i] for i in range(4)],
    )


def solution(mesh):
    return jax.shard_map(
        shards,
        mesh=mesh,
        in_specs=(
            P("col", "row"),
            P("col", "row"),
            P("row", "col"),
            P("row", None, "col"),
            P("row"),
            P(None, "row"),
            P("col", "row"),
            P(None, "row", "col"),
            P("row", None, "col"),
            P("row", None, "col"),
            P("col", "row"),
            P("row", "col"),
            P("row", None, "col"),
            P("col", "row"),
            P("row", "col"),
            P("col", "row"),
            P("col"),
            P("col"),
            P("col"),
            P("col"),
            P("col"),
            P("col"),
            P(),
            P(),
            P(),
            P(),
        ),
        out_specs=(
            P("col", "row"),
            P("col", "row"),
            P("col", "row"),
            P(None, "row", "col"),
            P("row", None, "col"),
            P("row", None, "col"),
            P("col", "row"),
            P("row", "col"),
            P("row", None, "col"),
            P("col", "row"),
            P("row", "col"),
            P("col", "row"),
            P("col"),
            P("col"),
            P("col"),
            P("col"),
            P("col"),
            P("col"),
            P(),
            P(),
            P(),
            P(),
        ),
        check_vma=False,
    )
```

time: 2780 us -> 1870 us (0.67)
  waiting for transfers between devices: 1220 us -> 336 us
  matrix products: 775 us -> 335 us
  local copies, waits for them, and re-layouts: 153 us -> 445 us
  blocking collectives: 360 us -> 176 us
  Pallas kernels: 0 us -> 167 us
  starting transfers between devices: 27.7 us -> 143 us
    all_gather x39 -> x4, waiting for transfers between devices: 613 us -> 89.8 us  [the longest x3 89.8 us: gather_weights(): whole = lax.all_gather(jnp.stack(padded, 0), DEVICES, axis=1, tiled=True)]
    dot_general x117 -> x48, matrix products: 775 us -> 335 us  [einsum(): return jnp.einsum(spec, left, right, preferred_element_type=F32)]
    reduce_scatter x15 -> x0, waiting for transfers between devices: 359 us -> none  [the longest x9 181 us: collect(): lax.psum_scatter(partials.astype(jnp.bfloat16), 'col', scatter_dimension=...]
    unnamed x58 -> x7, waiting for transfers between devices: 237 us -> 0.1 us
    ppermute x0 -> x72, waiting for transfers between devices: none -> 227 us  [swap(): return lax.ppermute(values, axis, [(i, i ^ bit) for i in range(size)])]
    pallas_call x0 -> x8, Pallas kernels: none -> 167 us  [the longest x4 89.8 us: attend_back(): pl.pallas_call(partial(attend_back_kernel, masked, dim ** (-0.5)), grid=(...]
    psum x11 -> x1, blocking collectives: 168 us -> 40.2 us  [shards(): g_gains = lax.psum(g_gains, ('row', 'col'))]
    ppermute x0 -> x72, starting transfers between devices: none -> 95 us  [swap(): return lax.ppermute(values, axis, [(i, i ^ bit) for i in range(size)])]
  transfers between devices with their start and end apart: 59 -> 89, of which waited for: 39 -> 27; matrix products, arithmetic and copies ran while one was open for 33% -> 40% of each run, Pallas kernels for 0% -> 5%
where the time goes in v1:
time: 1870 us; the launch traced here: 1850 us
  local copies, waits for them, and re-layouts  445 us (24%)
  waiting for transfers between devices  336 us (18%)
  matrix products  335 us (18%)
  other arithmetic  223 us (12%)
  blocking collectives  176 us (9%)
  Pallas kernels  167 us (9%)
  starting transfers between devices  143 us (8%)
  between operations  20 us (1%)
    dot_general x48, matrix products, einsum(): return jnp.einsum(spec, left, right, preferred_element_type=F32)  335 us
    ppermute x72, waiting for transfers between devices, swap(): return lax.ppermute(values, axis, [(i, i ^ bit) for i in range(size)])  227 us
    ppermute x72, starting transfers between devices, swap(): return lax.ppermute(values, axis, [(i, i ^ bit) for i in range(size)])  95 us
    pallas_call x4, Pallas kernels, attend_back(): pl.pallas_call(partial(attend_back_kernel, masked, dim ** (-0.5)), grid=(...  89.8 us
    all_gather x3, waiting for transfers between devices, gather_weights(): whole = lax.all_gather(jnp.stack(padded, 0), DEVICES, axis=1, tiled=True)  89.8 us
    convert_element_type x48, other arithmetic, add(): return (left.astype(F32) + right.astype(F32)).astype(BF)  87.4 us
    pallas_call x4, Pallas kernels, attend(): pl.pallas_call(partial(attend_kernel, masked, dim ** (-0.5)), grid=(heads...  77.3 us
    unnamed x528, local copies, waits for them, and re-layouts  63.3 us
  transfers between devices with their start and end apart: 89, of which 27 were waited for; matrix products, arithmetic and copies ran while one was open for 40% of the time, Pallas kernels for 5%

profile of v1, /device:TPU:0, one launch (start us, length us, event | category | flops | bytes accessed | tf_op | source)
XLA Modules:
  0.0 1845.9 jit_solution(15450491816342694490)
XLA Ops:
  8.9 32.1 %all-gather.1 = bf16[8,3,352]{2,1,0:T(4,128)(2,1)S(1)} all-gather(bf16[1,3,352]{2,1,0:T(4,128)(2,1)S(1)} %fusion.268), channel_id=1, replica_groups=mesh['row'=8,'col'=4] {'row'}, dimensions={0}, use_global_device_ids=true | all-gather | bytes 19008 | tf_op jit(solution)/shard_map/all_gather | solution.py:379
  70.1 27.0 %all-gather = f32[4,352,6]{1,2,0:T(8,128)S(1)} all-gather(f32[1,352,6]{1,2,0:T(8,128)S(1)} %bitcast.1076), channel_id=1, replica_groups=mesh['row'=8,'col'=4] {'col'}, dimensions={0}, use_global_device_ids=true | all-gather | bytes 42240 | tf_op jit(solution)/shard_map/all_gather | solution.py:362
  107.8 12.7 all-reduce.14.cloned.1.call-done
  121.5 20.2 %all_gather.32 = f32[3,2,1408]{0,1,2:T(2,128)S(1)} all-gather(f32[3,2,352]{0,1,2:T(2,128)S(1)} %copy.755), channel_id=1, replica_groups=mesh['row'=8,'col'=4] {'col'}, dimensions={2}, use_global_device_ids=true | all-gather | bytes 42240 | tf_op jit(solution)/shard_map/all_gather | solution.py:386
  154.2 89.7 %all-gather.8.cloned.1.call-done = bf16[5,5632,352]{2,1,0:T(8,128)(2,1)} async-done(((bf16[5,176,352]{2,1,0:T(8,128)(2,1)}), bf16[5,5632,352]{2,1,0:T(8,128)(2,1)}) %all-gather.8.cloned.1.call-update) | async-done | bytes 19824656 | tf_op jit(solution)/shard_map/all_gather | solution.py:236
  243.9 15.6 fusion.293
  259.5 8.7 copy.873
  272.7 8.8 copy.874
  285.9 8.7 copy.878
  299.3 8.6 copy.877
  312.4 8.8 copy.879
  325.9 6.6 fusion.307
  332.6 7.9 fusion.300
  372.0 6.6 fusion.78
  383.0 7.2 all_to_all.70
  417.1 29.2 %shard_map.417 = (bf16[8,88,1024]{2,1,0:T(8,128)(2,1)}, f32[8,1,1024]{2,1,0:T(1,128)}) custom-call(s32[1]{0:T(128)} %constant.612.clone.1.length_ref, bf16[8,88,1024]{2,1,0:T(8,128)(2,1)} %squeeze.382.q_ref, bf16[8,88,1024]{2,1,0:T(8,128)(2,1)} %squeeze.383.k_ref, bf16[8,88,1024]{2,1,0:T(8,128)(2,1)} %squeeze.384.v_ref), custom_call_target="tpu_custom_call" | custom-call | flops 2952790016 | bytes 5767168 | tf_op jit(solution)/shard_map/pallas_call | solution.py:96
  461.2 15.5 fusion.292
  476.7 8.9 copy.882
  527.9 15.4 shard_map.418
  553.9 7.0 all-to-all-done.5
  565.0 8.2 fusion.303
  586.8 14.3 shard_map.420
  601.1 18.4 shard_map.419
  621.1 8.1 fusion.306
  633.3 17.8 fusion.291
  657.0 24.9 %multiply_convert_fusion = (bf16[4,1536,768]{2,1,0:T(8,128)(2,1)}, f32[4,1536,768]{2,1,0:T(8,128)}) fusion(bf16[4,1408,1536]{2,1,0:T(8,128)(2,1)S(1)} %bitcast.920, bf16[1408,768,1]{1,0,2:T(8,128)(2,1)} %fusion.57), kind=kOutput, calls=%fused_computation.9 | convolution fusion | flops 13330022400 | bytes 47775744 | tf_op jit(solution)/shard_map/ckn,kt->cnt/dot_general | solution.py:20
  681.9 32.2 %fusion.6 = bf16[4,1536,768]{2,1,0:T(8,128)(2,1)} fusion(f32[4,1536,768]{2,1,0:T(8,128)} %get-tuple-element.398, bf16[4,1408,1536]{2,1,0:T(8,128)(2,1)} %bitcast.916, bf16[1408,768,1]{1,0,2:T(8,128)(2,1)S(1)} %bitcast.976), kind=kOutput, calls=%fused_computation.8 | convolution fusion | flops 13381926912 | bytes 47775744 | tf_op jit(solution)/shard_map/cnk,nt->ckt/dot_general | solution.py:20
  714.0 30.3 %fusion.32 = (f32[1408]{0:T(1024)}, f32[768]{0:T(1024)S(1)}, f32[768]{0:T(1024)S(1)}, f32[1408]{0:T(1024)}, f32[1408,768,1]{1,0,2:T(8,128)S(1)}) fusion(f32[1408,768]{1,0:T(8,128)S(1)} %copy-done.8, f32[768]{0:T(1024)S(1)} %add_rsqrt_fusion, f32[768]{0:T(1024)S(1)} %broadcast_multiply_fusion.14, f32[1408]{0:T(1024)S(1)} %copy-done.168, ...), kind=kOutput, calls=%fused_computation.75 | convolution fusion | flops 13297283072 | bytes 35418624 | tf_op jit(solution)/shard_map/ckn,cnt->kt/dot_general | solution.py:20
  745.7 7.5 fusion.79
  755.4 19.8 %shard_map.421 = (f32[16,88,512]{2,1,0:T(8,128)}, f32[16,88,384]{2,1,0:T(8,128)}, f32[16,88,384]{2,1,0:T(8,128)}) custom-call(s32[1]{0:T(128)} %get-tuple-element.380.length_ref, bf16[16,88,512]{2,1,0:T(8,128)(2,1)} %slice.373.q_ref, bf16[16,88,384]{2,1,0:T(8,128)(2,1)} %get-tuple-element.322.k_ref, bf16[16,88,384]{2,1,0:T(8,128)(2,1)} %get-tuple-element.320.v_ref, ...), custom_call_target="tpu_custom_call" | custom-call | flops 2768240640 | bytes 8830976 | tf_op jit(solution)/shard_map/pallas_call | solution.py:115
  778.9 15.7 shard_map.422
  812.7 10.1 fusion.31
  827.6 7.4 fusion.82
  837.2 12.4 fusion.8
  849.6 11.6 convolution_convert_fusion.1
  861.2 11.9 fusion.7
  873.2 11.8 convolution_convert_fusion.3
  905.0 17.2 fusion.33
  931.2 35.6 %shard_map.423 = (bf16[8,88,1024]{2,1,0:T(8,128)(2,1)}, bf16[8,88,1024]{2,1,0:T(8,128)(2,1)}, bf16[8,88,1024]{2,1,0:T(8,128)(2,1)}) custom-call(s32[1]{0:T(128)} %constant.612.clone.1.length_ref, bf16[8,88,1024]{2,1,0:T(8,128)(2,1)} %squeeze.382.q_ref, bf16[8,88,1024]{2,1,0:T(8,128)(2,1)} %squeeze.383.k_ref, bf16[8,88,1024]{2,1,0:T(8,128)(2,1)} %squeeze.384.v_ref, ...), custom_call_target="tpu_custom_call" | custom-call | flops 7381975040 | bytes 10092544 | tf_op jit(solution)/shard_map/pallas_call | solution.py:115
  981.7 7.4 all_to_all.72
  1046.2 18.7 %shard_map.424 = (bf16[4,88,1024]{2,1,0:T(8,128)(2,1)}, bf16[4,88,1024]{2,1,0:T(8,128)(2,1)}, bf16[4,88,1024]{2,1,0:T(8,128)(2,1)}) custom-call(s32[1]{0:T(128)} %constant.612.clone.1.length_ref, bf16[4,88,1024]{2,1,0:T(8,128)(2,1)} %squeeze.385.q_ref, bf16[4,88,1024]{2,1,0:T(8,128)(2,1)} %squeeze.386.k_ref, bf16[4,88,1024]{2,1,0:T(8,128)(2,1)} %squeeze.387.v_ref, ...), custom_call_target="tpu_custom_call" | custom-call | flops 3690987520 | bytes 5046272 | tf_op jit(solution)/shard_map/pallas_call | solution.py:115
  1142.5 10.2 multiply_reduce_fusion.9
  1194.9 6.8 fusion.54
  1204.0 10.8 multiply_reduce_fusion.4
  1220.4 40.2 %all-reduce.11 = (f32[6,1408]{1,0:T(8,128)S(1)}, f32[4,88]{1,0:T(4,128)S(1)}) all-reduce(f32[6,1408]{1,0:T(8,128)S(1)} %stack.261, f32[4,88]{1,0:T(4,128)S(1)} %pad_maximum_fusion.14), channel_id=1, replica_groups=mesh['row'=8,'col'=4] {'row','col'}, use_global_device_ids=true, to_apply=%region_45.46 | all-reduce | flops 8800 | bytes 70400 | tf_op jit(solution)/shard_map/psum | solution.py:553
  1343.4 30.7 %all_gather.35 = bf16[24,2,352]{2,1,0:T(2,128)(2,1)S(1)} all-gather(bf16[3,2,352]{2,1,0:T(2,128)(2,1)S(1)} %copy.820), channel_id=1, replica_groups=mesh['row'=8,'col'=4] {'row'}, dimensions={0}, use_global_device_ids=true | all-gather | bytes 38016 | tf_op jit(solution)/shard_map/all_gather | solution.py:533
  1388.4 9.7 collective-permute-done.31
  1492.8 12.3 copy.868
  1505.1 6.8 fusion.20
  1527.2 11.8 copy.863
  1539.1 7.2 fusion.19
  1550.8 79.1 %collective-permute-done.1 = bf16[2,4,176,352]{3,2,1,0:T(8,128)(2,1)} collective-permute-done((bf16[2,4,176,352]{3,2,1,0:T(8,128)(2,1)}, bf16[2,4,176,352]{3,2,1,0:T(8,128)(2,1)}, u32[]{:S(2)}, u32[]{:S(2)}) %collective-permute-start.1) | collective-permute-done | bytes 991264 | tf_op jit(solution)/shard_map/ppermute | solution.py:254
  1637.6 7.5 collective-permute-done.20
  1648.3 8.3 collective-permute-done.26
  1660.9 6.7 collective-permute-done.2
  1680.9 6.7 constant_dynamic-slice_fusion
  1704.8 8.1 collective-permute-done.22
  1718.0 6.3 collective-permute-done.28
  1724.9 9.2 collective-permute-start.10
  1736.5 6.9 collective-permute-start.9
  1758.2 14.0 collective-permute-done.69
  1779.2 11.3 collective-permute-done.70
  1791.7 7.0 collective-permute-done.63
  1798.7 38.1 %collective-permute-done.64 = bf16[176,1536]{1,0:T(8,128)(2,1)S(1)} collective-permute-done((bf16[176,1536]{1,0:T(8,128)(2,1)S(1)}, bf16[176,1536]{1,0:T(8,128)(2,1)S(1)}, u32[]{:S(2)}, u32[]{:S(2)}) %collective-permute-start.64) | collective-permute-done | bytes 540704 | tf_op jit(solution)/shard_map/ppermute | solution.py:254
  (1076 shorter events, 783.4 us)
Async XLA Ops:
  8.1 112.5 %all-reduce.14.cloned.1.call-start = ((), (), s32[]{:S(2)}) async-start(), calls=%async_computation.17 | async-start | bytes 147456 | tf_op jit(solution)/shard_map/psum | solution.py:384
  47.4 100.1 %all-gather.12.cloned.1.call-start = ((), (), s32[]{:S(2)}) async-start(), calls=%async_computation.18 | async-start | bytes 2949120 | tf_op jit(solution)/shard_map/all_gather | solution.py:368
  49.4 194.4 %all-gather.8.cloned.1.call-start = ((), (), s32[]{:S(2)}) async-start(), calls=%async_computation.15 | async-start | bytes 22302720 | tf_op jit(solution)/shard_map/all_gather | solution.py:236
  50.7 410.5 %all-gather.10.cloned.1.call-start = ((), (), s32[]{:S(2)}) async-start(), calls=%async_computation.16 | async-start | bytes 22302720 | tf_op jit(solution)/shard_map/all_gather | solution.py:236
  52.1 581.2 %all-gather.14.cloned.1.call-start = ((), (), s32[]{:S(2)}) async-start(), calls=%async_computation.19 | async-start | bytes 35684352 | tf_op jit(solution)/shard_map/all_gather | solution.py:236
  56.3 93.7 %all-to-all-start = ((bf16[4,352,768]{2,1,0:T(8,128)(2,1)}), bf16[4,352,768]{2,1,0:T(8,128)(2,1)}, u32[]{:S(2)}, u32[]{:S(2)}) async-start(bf16[4,352,768]{2,1,0:T(8,128)(2,1)} %pad_maximum_fusion.3), calls=%async_computation | async-start | bytes 4325376 | tf_op jit(solution)/shard_map/all_to_all | solution.py:188
  150.1 182.5 %all-to-all-start.1 = ((bf16[4,352,768]{2,1,0:T(8,128)(2,1)}), bf16[4,352,768]{2,1,0:T(8,128)(2,1)S(1)}, u32[]{:S(2)}, u32[]{:S(2)}) async-start(bf16[4,352,768]{2,1,0:T(8,128)(2,1)} %pad_maximum_fusion.4), calls=%async_computation.1 | async-start | bytes 4325376 | tf_op jit(solution)/shard_map/all_to_all | solution.py:188
  456.7 55.6 %all-to-all-start.4 = ((bf16[4,3,4,88,256]{4,3,2,1,0:T(8,128)(2,1)}), bf16[4,3,4,88,256]{4,3,2,1,0:T(8,128)(2,1)}, u32[]{:S(2)}, u32[]{:S(2)}) async-start(bf16[4,3,4,88,256]{4,3,2,1,0:T(8,128)(2,1)} %bitcast.861), calls=%async_computation.4 | async-start | bytes 4325376 | tf_op jit(solution)/shard_map/all_to_all | solution.py:188
  512.3 33.8 %all-to-all-start.3 = ((bf16[2,1,8,88,512]{4,3,2,1,0:T(8,128)(2,1)}), bf16[2,1,8,88,512]{4,3,2,1,0:T(8,128)(2,1)}, u32[]{:S(2)}, u32[]{:S(2)}) async-start(bf16[2,1,8,88,512]{4,3,2,1,0:T(8,128)(2,1)} %bitcast.999), calls=%async_computation.3 | async-start | bytes 2883584 | tf_op jit(solution)/shard_map/all_to_all | solution.py:189
  546.1 14.8 all-to-all-start.5
  560.9 120.9 %all-to-all-start.7 = ((bf16[4,352,768]{2,1,0:T(8,128)(2,1)}), bf16[4,352,768]{2,1,0:T(8,128)(2,1)S(1)}, u32[]{:S(2)}, u32[]{:S(2)}) async-start(bf16[4,352,768]{2,1,0:T(8,128)(2,1)} %pad_maximum_fusion.5), calls=%async_computation.7 | async-start | bytes 4325376 | tf_op jit(solution)/shard_map/all_to_all | solution.py:188
  991.4 46.9 %all-to-all-start.10 = ((bf16[4,1,4,88,256]{4,3,2,1,0:T(8,128)(2,1)}), bf16[4,1,4,88,256]{4,3,2,1,0:T(8,128)(2,1)}, u32[]{:S(2)}, u32[]{:S(2)}) async-start(bf16[4,1,4,88,256]{4,3,2,1,0:T(8,128)(2,1)} %bitcast.103), calls=%async_computation.10 | async-start | bytes 1441792 | tf_op jit(solution)/shard_map/all_to_all | solution.py:188
  995.7 496.1 %collective-permute-start.66 = (bf16[2,1408,1536]{1,2,0:T(8,128)(2,1)}, bf16[2,1408,1536]{1,2,0:T(8,128)(2,1)}, u32[]{:S(2)}, u32[]{:S(2)}) collective-permute-start(bf16[2,1408,1536]{1,2,0:T(8,128)(2,1)} %fusion.8), channel_id=1, source_target_pairs={{0,1},{1,0},{2,3},{3,2},{4,5},{5,4},{6,7},{7,6},{8,9},{9,8},{10,11... | collective-permute-start | bytes 25952264 | tf_op jit(solution)/shard_map/ppermute | solution.py:254
  996.2 527.4 %collective-permute-start.60 = (bf16[2,1408,1536]{1,2,0:T(8,128)(2,1)}, bf16[2,1408,1536]{1,2,0:T(8,128)(2,1)}, u32[]{:S(2)}, u32[]{:S(2)}) collective-permute-start(bf16[2,1408,1536]{1,2,0:T(8,128)(2,1)} %fusion.7), channel_id=1, source_target_pairs={{0,1},{1,0},{2,3},{3,2},{4,5},{5,4},{6,7},{7,6},{8,9},{9,8},{10,11... | collective-permute-start | bytes 25952264 | tf_op jit(solution)/shard_map/ppermute | solution.py:254
  996.3 105.7 %collective-permute-start.54 = (bf16[2,1408,352]{1,2,0:T(8,128)(2,1)}, bf16[2,1408,352]{1,2,0:T(8,128)(2,1)}, u32[]{:S(2)}, u32[]{:S(2)}) collective-permute-start(bf16[2,1408,352]{1,2,0:T(8,128)(2,1)} %fusion.52), channel_id=1, source_target_pairs={{0,1},{1,0},{2,3},{3,2},{4,5},{5,4},{6,7},{7,6},{8,9},{9,8},{10,11... | collective-permute-start | bytes 5947400 | tf_op jit(solution)/shard_map/ppermute | solution.py:254
  1003.2 71.3 %collective-permute-start.42 = (bf16[2,1024,352]{1,2,0:T(8,128)(2,1)}, bf16[2,1024,352]{1,2,0:T(8,128)(2,1)}, u32[]{:S(2)}, u32[]{:S(2)}) collective-permute-start(bf16[2,1024,352]{1,2,0:T(8,128)(2,1)} %fusion.86), channel_id=1, source_target_pairs={{0,1},{1,0},{2,3},{3,2},{4,5},{5,4},{6,7},{7,6},{8,9},{9,8},{10,11... | collective-permute-start | bytes 4325384 | tf_op jit(solution)/shard_map/ppermute | solution.py:254
  1005.2 73.5 %collective-permute-start.48 = (bf16[2,1024,352]{1,2,0:T(8,128)(2,1)}, bf16[2,1024,352]{1,2,0:T(8,128)(2,1)}, u32[]{:S(2)}, u32[]{:S(2)}) collective-permute-start(bf16[2,1024,352]{1,2,0:T(8,128)(2,1)} %fusion.88), channel_id=1, source_target_pairs={{0,1},{1,0},{2,3},{3,2},{4,5},{5,4},{6,7},{7,6},{8,9},{9,8},{10,11... | collective-permute-start | bytes 4325384 | tf_op jit(solution)/shard_map/ppermute | solution.py:254
  1038.3 53.6 %all-to-all-start.6 = ((bf16[4,352,768]{2,1,0:T(8,128)(2,1)}), bf16[4,352,768]{2,1,0:T(8,128)(2,1)}, u32[]{:S(2)}, u32[]{:S(2)}) async-start(bf16[4,352,768]{2,1,0:T(8,128)(2,1)} %bitcast.1037), calls=%async_computation.6 | async-start | bytes 4325376 | tf_op jit(solution)/shard_map/all_to_all | solution.py:188
  1074.5 33.0 %collective-permute-start.36 = (bf16[2,1408,352]{1,2,0:T(8,128)(2,1)}, bf16[2,1408,352]{1,2,0:T(8,128)(2,1)}, u32[]{:S(2)}, u32[]{:S(2)}) collective-permute-start(bf16[2,1408,352]{1,2,0:T(8,128)(2,1)} %fusion.50), channel_id=1, source_target_pairs={{0,1},{1,0},{2,3},{3,2},{4,5},{5,4},{6,7},{7,6},{8,9},{9,8},{10,11... | collective-permute-start | bytes 5947400 | tf_op jit(solution)/shard_map/ppermute | solution.py:254
  1078.8 37.2 %collective-permute-start.30 = (bf16[2,1408,352]{1,2,0:T(8,128)(2,1)}, bf16[2,1408,352]{1,2,0:T(8,128)(2,1)}, u32[]{:S(2)}, u32[]{:S(2)}) collective-permute-start(bf16[2,1408,352]{1,2,0:T(8,128)(2,1)} %fusion.48), channel_id=1, source_target_pairs={{0,1},{1,0},{2,3},{3,2},{4,5},{5,4},{6,7},{7,6},{8,9},{9,8},{10,11... | collective-permute-start | bytes 5947400 | tf_op jit(solution)/shard_map/ppermute | solution.py:254
  1091.9 38.4 %all-to-all-start.11 = ((bf16[4,3,4,88,256]{4,3,2,1,0:T(8,128)(2,1)}), bf16[4,3,4,88,256]{4,3,2,1,0:T(8,128)(2,1)}, u32[]{:S(2)}, u32[]{:S(2)}) async-start(bf16[4,3,4,88,256]{4,3,2,1,0:T(8,128)(2,1)} %maximum_bitcast_fusion.1), calls=%async_computation.11 | async-start | bytes 4325376 | tf_op jit(solution)/shard_map/all_to_all | solution.py:188
  1096.4 245.8 %reduce-scatter.4.cloned.1.call-start = ((), (), s32[]{:S(2)}) async-start(), calls=%async_computation.20 | async-start | bytes 901120
  1101.9 174.4 %collective-permute-start.43 = (bf16[2,4,128,352]{2,3,1,0:T(8,128)(2,1)}, bf16[2,4,128,352]{2,3,1,0:T(8,128)(2,1)}, u32[]{:S(2)}, u32[]{:S(2)}) collective-permute-start(bf16[2,4,128,352]{2,3,1,0:T(8,128)(2,1)} %fusion.170), channel_id=1, source_target_pairs={{0,4},{4,0},{8,12},{12,8},{16,20},{20,16},{24,28},{28,24},{1,5},{5... | collective-permute-start | bytes 2162696 | tf_op jit(solution)/shard_map/ppermute | solution.py:254
  1107.5 182.5 %collective-permute-start.49 = (bf16[4,2,128,352]{2,3,0,1:T(8,128)(2,1)}, bf16[4,2,128,352]{2,3,0,1:T(8,128)(2,1)}, u32[]{:S(2)}, u32[]{:S(2)}) collective-permute-start(bf16[4,2,128,352]{2,3,0,1:T(8,128)(2,1)} %fusion.171), channel_id=1, source_target_pairs={{0,2},{1,3},{2,0},{3,1},{4,6},{5,7},{6,4},{7,5},{8,10},{9,11},{10,... | collective-permute-start | bytes 2162696 | tf_op jit(solution)/shard_map/ppermute | solution.py:254
  1116.0 261.7 %collective-permute-start.55 = (bf16[2,4,176,352]{3,2,1,0:T(8,128)(2,1)}, bf16[2,4,176,352]{3,2,1,0:T(8,128)(2,1)}, u32[]{:S(2)}, u32[]{:S(2)}) collective-permute-start(bf16[2,4,176,352]{3,2,1,0:T(8,128)(2,1)} %fusion.96), channel_id=1, source_target_pairs={{0,4},{4,0},{8,12},{12,8},{16,20},{20,16},{24,28},{28,24},{1,5},{5... | collective-permute-start | bytes 2973704 | tf_op jit(solution)/shard_map/ppermute | solution.py:254
  1278.1 41.8 %collective-permute-start.44 = (bf16[4,128,352]{1,2,0:T(8,128)(2,1)}, bf16[4,128,352]{1,2,0:T(8,128)(2,1)}, u32[]{:S(2)}, u32[]{:S(2)}) collective-permute-start(bf16[4,128,352]{1,2,0:T(8,128)(2,1)} %fusion.195), channel_id=1, source_target_pairs={{0,2},{1,3},{2,0},{3,1},{4,6},{5,7},{6,4},{7,5},{8,10},{9,11},{10,... | collective-permute-start | bytes 1081352 | tf_op jit(solution)/shard_map/ppermute | solution.py:254
  1291.8 32.9 %collective-permute-start.50 = (bf16[4,128,352]{1,2,0:T(8,128)(2,1)}, bf16[4,128,352]{1,2,0:T(8,128)(2,1)}, u32[]{:S(2)}, u32[]{:S(2)}) collective-permute-start(bf16[4,128,352]{1,2,0:T(8,128)(2,1)} %fusion.197), channel_id=1, source_target_pairs={{0,4},{4,0},{8,12},{12,8},{16,20},{20,16},{24,28},{28,24},{1,5},{5... | collective-permute-start | bytes 1081352 | tf_op jit(solution)/shard_map/ppermute | solution.py:254
  1324.7 62.4 %collective-permute-start.37 = (bf16[4,2,176,352]{3,2,1,0:T(8,128)(2,1)}, bf16[4,2,176,352]{3,2,1,0:T(8,128)(2,1)}, u32[]{:S(2)}, u32[]{:S(2)}) collective-permute-start(bf16[4,2,176,352]{3,2,1,0:T(8,128)(2,1)} %fusion.95), channel_id=1, source_target_pairs={{0,2},{1,3},{2,0},{3,1},{4,6},{5,7},{6,4},{7,5},{8,10},{9,11},{10,... | collective-permute-start | bytes 2973704 | tf_op jit(solution)/shard_map/ppermute | solution.py:254
  1326.5 47.6 %collective-permute-start.46 = (bf16[128,352]{0,1:T(8,128)(2,1)}, bf16[128,352]{0,1:T(8,128)(2,1)}, u32[]{:S(2)}, u32[]{:S(2)}) collective-permute-start(bf16[128,352]{0,1:T(8,128)(2,1)} %get-tuple-element.367), channel_id=1, source_target_pairs={{0,16},{4,20},{8,24},{12,28},{16,0},{20,4},{24,8},{28,12},{1,17},{... | collective-permute-start | bytes 270344 | tf_op jit(solution)/shard_map/ppermute | solution.py:254
  1337.8 81.8 %all-to-all-start.13 = ((bf16[4,352,768]{2,1,0:T(8,128)(2,1)}), bf16[4,352,768]{2,1,0:T(8,128)(2,1)S(1)}, u32[]{:S(2)}, u32[]{:S(2)}) async-start(bf16[4,352,768]{2,1,0:T(8,128)(2,1)} %bitcast.1036), calls=%async_computation.13 | async-start | bytes 4325376 | tf_op jit(solution)/shard_map/all_to_all | solution.py:188
  1374.1 24.0 %collective-permute-start.31 = (bf16[2,4,176,352]{3,2,1,0:T(8,128)(2,1)}, bf16[2,4,176,352]{3,2,1,0:T(8,128)(2,1)S(1)}, u32[]{:S(2)}, u32[]{:S(2)}) collective-permute-start(bf16[2,4,176,352]{3,2,1,0:T(8,128)(2,1)} %fusion.94), channel_id=1, source_target_pairs={{0,4},{4,0},{8,12},{12,8},{16,20},{20,16},{24,28},{28,24},{1,5},{5... | collective-permute-start | bytes 2973704 | tf_op jit(solution)/shard_map/ppermute | solution.py:254
  1384.1 14.3 collective-permute-start.56
  1410.7 44.5 %collective-permute-start.12 = (bf16[2,1408,352]{1,2,0:T(8,128)(2,1)}, bf16[2,1408,352]{1,2,0:T(8,128)(2,1)}, u32[]{:S(2)}, u32[]{:S(2)}) collective-permute-start(bf16[2,1408,352]{1,2,0:T(8,128)(2,1)} %fusion.42), channel_id=1, source_target_pairs={{0,1},{1,0},{2,3},{3,2},{4,5},{5,4},{6,7},{7,6},{8,9},{9,8},{10,11... | collective-permute-start | bytes 5947400 | tf_op jit(solution)/shard_map/ppermute | solution.py:254
  1410.7 13.9 collective-permute-start.58
  1419.6 35.6 %all-to-all-start.12 = ((bf16[4,352,768]{2,1,0:T(8,128)(2,1)}), bf16[4,352,768]{2,1,0:T(8,128)(2,1)}, u32[]{:S(2)}, u32[]{:S(2)}) async-start(bf16[4,352,768]{2,1,0:T(8,128)(2,1)} %bitcast.1035), calls=%async_computation.12 | async-start | bytes 4325376 | tf_op jit(solution)/shard_map/all_to_all | solution.py:188
  1452.3 15.4 collective-permute-start.18
  1452.3 23.5 %collective-permute-start.24 = (bf16[2,1408,352]{1,2,0:T(8,128)(2,1)}, bf16[2,1408,352]{1,2,0:T(8,128)(2,1)}, u32[]{:S(2)}, u32[]{:S(2)}) collective-permute-start(bf16[2,1408,352]{1,2,0:T(8,128)(2,1)} %fusion.46), channel_id=1, source_target_pairs={{0,1},{1,0},{2,3},{3,2},{4,5},{5,4},{6,7},{7,6},{8,9},{9,8},{10,11... | collective-permute-start | bytes 5947400 | tf_op jit(solution)/shard_map/ppermute | solution.py:254
  1455.2 24.4 %collective-permute-start.6 = (bf16[2,1408,352]{1,2,0:T(8,128)(2,1)}, bf16[2,1408,352]{1,2,0:T(8,128)(2,1)}, u32[]{:S(2)}, u32[]{:S(2)}) collective-permute-start(bf16[2,1408,352]{1,2,0:T(8,128)(2,1)} %fusion.40), channel_id=1, source_target_pairs={{0,1},{1,0},{2,3},{3,2},{4,5},{5,4},{6,7},{7,6},{8,9},{9,8},{10,11... | collective-permute-start | bytes 5947400 | tf_op jit(solution)/shard_map/ppermute | solution.py:254
  1467.7 44.2 %collective-permute-start = (bf16[2,1408,352]{1,2,0:T(8,128)(2,1)}, bf16[2,1408,352]{1,2,0:T(8,128)(2,1)}, u32[]{:S(2)}, u32[]{:S(2)}) collective-permute-start(bf16[2,1408,352]{1,2,0:T(8,128)(2,1)} %fusion.38), channel_id=1, source_target_pairs={{0,1},{1,0},{2,3},{3,2},{4,5},{5,4},{6,7},{7,6},{8,9},{9,8},{10,11... | collective-permute-start | bytes 5947400 | tf_op jit(solution)/shard_map/ppermute | solution.py:254
  1475.8 45.4 %collective-permute-start.13 = (bf16[2,4,176,352]{3,2,1,0:T(8,128)(2,1)}, bf16[2,4,176,352]{3,2,1,0:T(8,128)(2,1)}, u32[]{:S(2)}, u32[]{:S(2)}) collective-permute-start(bf16[2,4,176,352]{3,2,1,0:T(8,128)(2,1)} %fusion.91), channel_id=1, source_target_pairs={{0,4},{4,0},{8,12},{12,8},{16,20},{20,16},{24,28},{28,24},{1,5},{5... | collective-permute-start | bytes 2973704 | tf_op jit(solution)/shard_map/ppermute | solution.py:254
  1479.6 66.6 %collective-permute-start.19 = (bf16[4,2,176,352]{3,2,0,1:T(8,128)(2,1)}, bf16[4,2,176,352]{3,2,0,1:T(8,128)(2,1)}, u32[]{:S(2)}, u32[]{:S(2)}) collective-permute-start(bf16[4,2,176,352]{3,2,0,1:T(8,128)(2,1)} %fusion.92), channel_id=1, source_target_pairs={{0,2},{1,3},{2,0},{3,1},{4,6},{5,7},{6,4},{7,5},{8,10},{9,11},{10,... | collective-permute-start | bytes 2973704 | tf_op jit(solution)/shard_map/ppermute | solution.py:254
  1491.8 55.4 %collective-permute-start.25 = (bf16[4,2,176,352]{3,2,0,1:T(8,128)(2,1)}, bf16[4,2,176,352]{3,2,0,1:T(8,128)(2,1)}, u32[]{:S(2)}, u32[]{:S(2)}) collective-permute-start(bf16[4,2,176,352]{3,2,0,1:T(8,128)(2,1)} %fusion.93), channel_id=1, source_target_pairs={{0,2},{1,3},{2,0},{3,1},{4,6},{5,7},{6,4},{7,5},{8,10},{9,11},{10,... | collective-permute-start | bytes 2973704 | tf_op jit(solution)/shard_map/ppermute | solution.py:254
  1511.9 175.8 %collective-permute-start.67 = (bf16[2,4,176,1536]{3,2,1,0:T(8,128)(2,1)}, bf16[2,4,176,1536]{3,2,1,0:T(8,128)(2,1)}, u32[]{:S(2)}, u32[]{:S(2)}) collective-permute-start(bf16[2,4,176,1536]{3,2,1,0:T(8,128)(2,1)} %fusion.20), channel_id=1, source_target_pairs={{0,4},{4,0},{8,12},{12,8},{16,20},{20,16},{24,28},{28,24},{1,5},{5... | collective-permute-start | bytes 12976136 | tf_op jit(solution)/shard_map/ppermute | solution.py:254
  1521.2 108.7 %collective-permute-start.1 = (bf16[2,4,176,352]{3,2,1,0:T(8,128)(2,1)}, bf16[2,4,176,352]{3,2,1,0:T(8,128)(2,1)}, u32[]{:S(2)}, u32[]{:S(2)}) collective-permute-start(bf16[2,4,176,352]{3,2,1,0:T(8,128)(2,1)} %fusion.89), channel_id=1, source_target_pairs={{0,4},{4,0},{8,12},{12,8},{16,20},{20,16},{24,28},{28,24},{1,5},{5... | collective-permute-start | bytes 2973704 | tf_op jit(solution)/shard_map/ppermute | solution.py:254
  1523.6 108.7 %collective-permute-start.7 = (bf16[4,2,176,352]{3,2,0,1:T(8,128)(2,1)}, bf16[4,2,176,352]{3,2,0,1:T(8,128)(2,1)}, u32[]{:S(2)}, u32[]{:S(2)}) collective-permute-start(bf16[4,2,176,352]{3,2,0,1:T(8,128)(2,1)} %fusion.90), channel_id=1, source_target_pairs={{0,2},{1,3},{2,0},{3,1},{4,6},{5,7},{6,4},{7,5},{8,10},{9,11},{10,... | collective-permute-start | bytes 2973704 | tf_op jit(solution)/shard_map/ppermute | solution.py:254
  1546.2 88.2 %collective-permute-start.14 = (bf16[4,176,352]{2,1,0:T(8,128)(2,1)S(1)}, bf16[4,176,352]{2,1,0:T(8,128)(2,1)S(1)}, u32[]{:S(2)}, u32[]{:S(2)}) collective-permute-start(bf16[4,176,352]{2,1,0:T(8,128)(2,1)S(1)} %fusion.183), channel_id=1, source_target_pairs={{0,2},{1,3},{2,0},{3,1},{4,6},{5,7},{6,4},{7,5},{8,10},{9,11},{10,... | collective-permute-start | bytes 1486856 | tf_op jit(solution)/shard_map/ppermute | solution.py:254
  1547.2 148.1 %collective-permute-start.61 = (bf16[4,2,176,1536]{3,2,1,0:T(8,128)(2,1)}, bf16[4,2,176,1536]{3,2,1,0:T(8,128)(2,1)}, u32[]{:S(2)}, u32[]{:S(2)}) collective-permute-start(bf16[4,2,176,1536]{3,2,1,0:T(8,128)(2,1)} %fusion.19), channel_id=1, source_target_pairs={{0,2},{1,3},{2,0},{3,1},{4,6},{5,7},{6,4},{7,5},{8,10},{9,11},{10,... | collective-permute-start | bytes 12976136 | tf_op jit(solution)/shard_map/ppermute | solution.py:254
  1629.9 15.2 collective-permute-start.20
  1632.3 24.4 %collective-permute-start.26 = (bf16[4,176,352]{2,1,0:T(8,128)(2,1)S(1)}, bf16[4,176,352]{2,1,0:T(8,128)(2,1)S(1)}, u32[]{:S(2)}, u32[]{:S(2)}) collective-permute-start(bf16[4,176,352]{2,1,0:T(8,128)(2,1)S(1)} %fusion.187), channel_id=1, source_target_pairs={{0,4},{4,0},{8,12},{12,8},{16,20},{20,16},{24,28},{28,24},{1,5},{5... | collective-permute-start | bytes 1486856 | tf_op jit(solution)/shard_map/ppermute | solution.py:254
  1634.4 33.2 %collective-permute-start.2 = (bf16[4,176,352]{2,1,0:T(8,128)(2,1)S(1)}, bf16[4,176,352]{2,1,0:T(8,128)(2,1)S(1)}, u32[]{:S(2)}, u32[]{:S(2)}) collective-permute-start(bf16[4,176,352]{2,1,0:T(8,128)(2,1)S(1)} %fusion.179), channel_id=1, source_target_pairs={{0,2},{1,3},{2,0},{3,1},{4,6},{5,7},{6,4},{7,5},{8,10},{9,11},{10,... | collective-permute-start | bytes 1486856 | tf_op jit(solution)/shard_map/ppermute | solution.py:254
  1645.1 27.0 %collective-permute-start.8 = (bf16[4,176,352]{2,1,0:T(8,128)(2,1)S(1)}, bf16[4,176,352]{2,1,0:T(8,128)(2,1)S(1)}, u32[]{:S(2)}, u32[]{:S(2)}) collective-permute-start(bf16[4,176,352]{2,1,0:T(8,128)(2,1)S(1)} %fusion.181), channel_id=1, source_target_pairs={{0,4},{4,0},{8,12},{12,8},{16,20},{20,16},{24,28},{28,24},{1,5},{5... | collective-permute-start | bytes 1486856 | tf_op jit(solution)/shard_map/ppermute | solution.py:254
  1656.7 41.2 %collective-permute-start.15 = (bf16[176,352]{1,0:T(8,128)(2,1)}, bf16[176,352]{1,0:T(8,128)(2,1)}, u32[]{:S(2)}, u32[]{:S(2)}) collective-permute-start(bf16[176,352]{1,0:T(8,128)(2,1)} %get-tuple-element.345), channel_id=1, source_target_pairs={{0,8},{4,12},{8,0},{12,4},{16,24},{20,28},{24,16},{28,20},{1,9},{5... | collective-permute-start | bytes 371720 | tf_op jit(solution)/shard_map/ppermute | solution.py:254
  1667.6 32.5 %collective-permute-start.16 = (bf16[176,352]{1,0:T(8,128)(2,1)S(1)}, bf16[176,352]{1,0:T(8,128)(2,1)}, u32[]{:S(2)}, u32[]{:S(2)}) collective-permute-start(bf16[176,352]{1,0:T(8,128)(2,1)S(1)} %get-tuple-element.347), channel_id=1, source_target_pairs={{0,16},{4,20},{8,24},{12,28},{16,0},{20,4},{24,8},{28,12},{1,17},{... | collective-permute-start | bytes 371720 | tf_op jit(solution)/shard_map/ppermute | solution.py:254
  1672.1 30.0 %collective-permute-start.17 = (bf16[176,352]{1,0:T(8,128)(2,1)S(1)}, bf16[176,352]{1,0:T(8,128)(2,1)}, u32[]{:S(2)}, u32[]{:S(2)}) collective-permute-start(bf16[176,352]{1,0:T(8,128)(2,1)S(1)} %get-tuple-element.346), channel_id=1, source_target_pairs={{0,24},{4,28},{8,16},{12,20},{16,8},{20,12},{24,0},{28,4},{1,25},{... | collective-permute-start | bytes 371720 | tf_op jit(solution)/shard_map/ppermute | solution.py:254
  1690.7 56.0 %collective-permute-start.68 = (bf16[4,176,1536]{2,1,0:T(8,128)(2,1)S(1)}, bf16[4,176,1536]{2,1,0:T(8,128)(2,1)S(1)}, u32[]{:S(2)}, u32[]{:S(2)}) collective-permute-start(bf16[4,176,1536]{2,1,0:T(8,128)(2,1)S(1)} %fusion.61), channel_id=1, source_target_pairs={{0,2},{1,3},{2,0},{3,1},{4,6},{5,7},{6,4},{7,5},{8,10},{9,11},{10,... | collective-permute-start | bytes 6488072 | tf_op jit(solution)/shard_map/ppermute | solution.py:254
  1697.8 15.1 collective-permute-start.22
  1702.1 51.6 %collective-permute-start.62 = (bf16[4,176,1536]{2,1,0:T(8,128)(2,1)S(1)}, bf16[4,176,1536]{2,1,0:T(8,128)(2,1)S(1)}, u32[]{:S(2)}, u32[]{:S(2)}) collective-permute-start(bf16[4,176,1536]{2,1,0:T(8,128)(2,1)S(1)} %fusion.59), channel_id=1, source_target_pairs={{0,4},{4,0},{8,12},{12,8},{16,20},{20,16},{24,28},{28,24},{1,5},{5... | collective-permute-start | bytes 6488072 | tf_op jit(solution)/shard_map/ppermute | solution.py:254
  1724.9 20.2 %collective-permute-start.10 = (bf16[176,352]{1,0:T(8,128)(2,1)S(1)}, bf16[176,352]{1,0:T(8,128)(2,1)S(1)}, u32[]{:S(2)}, u32[]{:S(2)}) collective-permute-start(bf16[176,352]{1,0:T(8,128)(2,1)S(1)} %get-tuple-element.359), channel_id=1, source_target_pairs={{0,16},{4,20},{8,24},{12,28},{16,0},{20,4},{24,8},{28,12},{1,17},{... | collective-permute-start | bytes 371720 | tf_op jit(solution)/shard_map/ppermute | solution.py:254
  1749.3 23.0 %collective-permute-start.69 = (bf16[176,1536]{1,0:T(8,128)(2,1)S(1)}, bf16[176,1536]{1,0:T(8,128)(2,1)S(1)}, u32[]{:S(2)}, u32[]{:S(2)}) collective-permute-start(bf16[176,1536]{1,0:T(8,128)(2,1)S(1)} %get-tuple-element.301), channel_id=1, source_target_pairs={{0,8},{4,12},{8,0},{12,4},{16,24},{20,28},{24,16},{28,20},{1,9},{5... | collective-permute-start | bytes 1622024 | tf_op jit(solution)/shard_map/ppermute | solution.py:254
  1751.2 39.3 %collective-permute-start.70 = (bf16[176,1536]{1,0:T(8,128)(2,1)S(1)}, bf16[176,1536]{1,0:T(8,128)(2,1)S(1)}, u32[]{:S(2)}, u32[]{:S(2)}) collective-permute-start(bf16[176,1536]{1,0:T(8,128)(2,1)S(1)} %get-tuple-element.303), channel_id=1, source_target_pairs={{0,16},{4,20},{8,24},{12,28},{16,0},{20,4},{24,8},{28,12},{1,17},{... | collective-permute-start | bytes 1622024 | tf_op jit(solution)/shard_map/ppermute | solution.py:254
  1751.2 39.3 %collective-permute-start.71 = (bf16[176,1536]{1,0:T(8,128)(2,1)S(1)}, bf16[176,1536]{1,0:T(8,128)(2,1)S(1)}, u32[]{:S(2)}, u32[]{:S(2)}) collective-permute-start(bf16[176,1536]{1,0:T(8,128)(2,1)S(1)} %get-tuple-element.302), channel_id=1, source_target_pairs={{0,24},{4,28},{8,16},{12,20},{16,8},{20,12},{24,0},{28,4},{1,25},{... | collective-permute-start | bytes 1622024 | tf_op jit(solution)/shard_map/ppermute | solution.py:254
  1756.3 42.4 %collective-permute-start.63 = (bf16[176,1536]{1,0:T(8,128)(2,1)S(1)}, bf16[176,1536]{1,0:T(8,128)(2,1)S(1)}, u32[]{:S(2)}, u32[]{:S(2)}) collective-permute-start(bf16[176,1536]{1,0:T(8,128)(2,1)S(1)} %get-tuple-element.304), channel_id=1, source_target_pairs={{0,8},{4,12},{8,0},{12,4},{16,24},{20,28},{24,16},{28,20},{1,9},{5... | collective-permute-start | bytes 1622024 | tf_op jit(solution)/shard_map/ppermute | solution.py:254
  1757.3 79.5 %collective-permute-start.64 = (bf16[176,1536]{1,0:T(8,128)(2,1)S(1)}, bf16[176,1536]{1,0:T(8,128)(2,1)S(1)}, u32[]{:S(2)}, u32[]{:S(2)}) collective-permute-start(bf16[176,1536]{1,0:T(8,128)(2,1)S(1)} %get-tuple-element.306), channel_id=1, source_target_pairs={{0,16},{4,20},{8,24},{12,28},{16,0},{20,4},{24,8},{28,12},{1,17},{... | collective-permute-start | bytes 1622024 | tf_op jit(solution)/shard_map/ppermute | solution.py:254
  1772.3 64.6 %collective-permute-start.65 = (bf16[176,1536]{1,0:T(8,128)(2,1)S(1)}, bf16[176,1536]{1,0:T(8,128)(2,1)S(1)}, u32[]{:S(2)}, u32[]{:S(2)}) collective-permute-start(bf16[176,1536]{1,0:T(8,128)(2,1)S(1)} %get-tuple-element.305), channel_id=1, source_target_pairs={{0,24},{4,28},{8,16},{12,20},{16,8},{20,12},{24,0},{28,4},{1,25},{... | collective-permute-start | bytes 1622024 | tf_op jit(solution)/shard_map/ppermute | solution.py:254
  (283 other events, 5206.6 us)
Sparse Core Ops, SparseCore 0:
  47.5 72.9 all-reduce.13
Sparse Core Ops, SparseCore 1:
  49.5 33.7 all-gather.11
  86.2 157.6 all-gather.7
  247.4 135.6 all-gather.9
  386.2 200.6 all-gather.13
  1305.5 20.9 reduce-scatter.3

commit v2 on v1

v2 whole, which is shorter than its diff:
```python
from functools import partial
import math

import jax
import jax.numpy as jnp
from jax import lax
from jax.experimental import pallas as pl
from jax.experimental.pallas import tpu as pltpu
from jax.sharding import PartitionSpec as P

L = 1024
EPSILON = 1e-06
BF = jnp.bfloat16
F32 = jnp.float32
KEYPAD = 128
DEVICES = ("col", "row")
LOG2E = math.log2(math.e)
VMEM = 60 << 20


def einsum(spec, left, right):
    return jnp.einsum(spec, left, right, preferred_element_type=F32)


def dot(left, right, dims):
    return lax.dot_general(left, right, (dims, ((), ())), preferred_element_type=F32)


def params():
    return pltpu.CompilerParams(vmem_limit_bytes=VMEM)


def step_of(count):
    return 256 if count % 256 == 0 else count


def wide(ref, head):
    parts = [ref[s, 0, head] for s in range(ref.shape[0])]
    return parts[0] if len(parts) == 1 else jnp.concatenate(parts, 1)


def valid_keys(length_ref, keys, step):
    return lax.broadcasted_iota(jnp.int32, (keys, step), 0) < length_ref[0]


def attend_kernel(masked, length_ref, q_ref, k_ref, v_ref, o_ref, l_ref):
    groups, _, heads, dim, count = q_ref.shape
    step = step_of(count)
    factor = dim ** (-0.5) * LOG2E
    for head in range(heads):
        key = wide(k_ref, head).T
        value = wide(v_ref, head)
        keys = key.shape[0]
        value = jnp.concatenate([value, jnp.ones((8, keys), BF)], 0)
        for place in range(0, groups * count, step):
            group, first = divmod(place, count)
            query = q_ref[group, 0, head, :, first : first + step]
            expo = jnp.exp2(dot(key, query, ((1,), (0,))) * factor)
            if masked:
                expo = jnp.where(valid_keys(length_ref, keys, step), expo, 0.0)
            both = dot(value, expo.astype(BF), ((1,), (0,)))
            total = both[dim : dim + 1]
            o_ref[group, head, :, first : first + step] = (both[:dim] * (1.0 / total)).astype(BF)
            l_ref[head, :, place : place + step] = jnp.log2(total)


def attend_back_kernel(
    masked, length_ref, q_ref, k_ref, v_ref, m_ref, g_ref, l_ref, *outs
):
    groups, _, heads, dim, count = q_ref.shape
    step = step_of(count)
    scale = dim ** (-0.5)
    for head in range(heads):
        key = wide(k_ref, head)
        keys = key.shape[1]
        turned = key.T
        value = jnp.concatenate([wide(v_ref, head), jnp.ones((8, keys), BF)], 0).T
        g_key = g_value = None
        for place in range(0, groups * count, step):
            group, first = divmod(place, count)
            here = slice(first, first + step)
            query = q_ref[group, 0, head, :, here]
            grad = g_ref[group, head, :, here]
            delta = -jnp.sum(
                grad.astype(F32) * m_ref[group, head, :, here].astype(F32), 0, keepdims=True
            )
            high = delta.astype(BF)
            rest = (delta - high.astype(F32)).astype(BF)
            more = jnp.concatenate([grad, high, rest, jnp.zeros((6, step), BF)], 0)
            probs = jnp.exp2(
                dot(turned, query, ((1,), (0,))) * (scale * LOG2E)
                - l_ref[head, :, place : place + step]
            )
            if masked:
                probs = jnp.where(valid_keys(length_ref, keys, step), probs, 0.0)
            product = (probs * dot(value, more, ((1,), (0,)))).astype(BF)
            g_query = dot(key, product, ((1,), (0,))) * scale
            part_value = dot(grad, probs.astype(BF), ((1,), (1,)))
            part_key = dot(query, product, ((1,), (1,)))
            g_value = part_value if g_value is None else g_value + part_value
            g_key = part_key if g_key is None else g_key + part_key
            outs[0][group, 0, head, :, here] = g_query.astype(outs[0].dtype)
        g_key = g_key * scale
        if len(outs) == 1:
            for group in range(groups):
                here = slice(group * count, (group + 1) * count)
                outs[0][group, 1, head] = g_key[:, here].astype(BF)
                outs[0][group, 2, head] = g_value[:, here].astype(BF)
        else:
            outs[1][0, 0, head] = g_key
            outs[2][0, 0, head] = g_value


def costs(heads, queries, keys, dim, products):
    return pl.CostEstimate(
        flops=2 * products * heads * queries * keys * 256,
        transcendentals=heads * queries * keys,
        bytes_accessed=2 * products * heads * dim * (queries + keys),
    )


def head_block(shape, count, kind=0):
    groups, _, _, dim, tokens = shape
    return pl.BlockSpec((groups, 1, count, dim, tokens), lambda h: (0, kind, h, 0, 0))


def mix_block(shape, count):
    groups, _, _, dim, tokens = shape
    return pl.BlockSpec((groups, count, dim, tokens), lambda h: (0, h, 0, 0))


def attend(length, query, key, value, kinds, masked, most):
    groups, _, heads, dim, count = query.shape
    many = math.gcd(heads, most)
    total = groups * count
    keys = key.shape[0] * key.shape[4]
    return pl.pallas_call(
        partial(attend_kernel, masked),
        grid=(heads // many,),
        in_specs=[pl.BlockSpec(memory_space=pltpu.SMEM)]
        + [head_block(a.shape, many, kind) for a, kind in zip((query, key, value), kinds)],
        out_specs=[
            mix_block(query.shape, many),
            pl.BlockSpec((many, 1, total), lambda h: (h, 0, 0)),
        ],
        out_shape=[
            jax.ShapeDtypeStruct((groups, heads, dim, count), BF),
            jax.ShapeDtypeStruct((heads, 1, total), F32),
        ],
        cost_estimate=costs(heads, total, keys, dim, 2),
        compiler_params=params(),
        name="attend",
    )(length, query, key, value)


def attend_back(length, query, key, value, kinds, mixed, grad, logs, masked, most, stacked):
    groups, _, heads, dim, count = query.shape
    many = math.gcd(heads, most)
    total = groups * count
    keys = key.shape[0] * key.shape[4]
    if stacked:
        out_specs = pl.BlockSpec((groups, 3, many, dim, count), lambda h: (0, 0, h, 0, 0))
        out_shape = jax.ShapeDtypeStruct((groups, 3, heads, dim, count), BF)
    else:
        out_specs = [head_block(a.shape, many) for a in (query, key, value)]
        out_shape = [jax.ShapeDtypeStruct(a.shape, F32) for a in (query, key, value)]
    return pl.pallas_call(
        partial(attend_back_kernel, masked),
        grid=(heads // many,),
        in_specs=[pl.BlockSpec(memory_space=pltpu.SMEM)]
        + [head_block(a.shape, many, kind) for a, kind in zip((query, key, value), kinds)]
        + [mix_block(query.shape, many)] * 2
        + [pl.BlockSpec((many, 1, total), lambda h: (h, 0, 0))],
        out_specs=out_specs,
        out_shape=out_shape,
        cost_estimate=costs(heads, total, keys, dim, 5),
        compiler_params=params(),
        name="attend_back",
    )(length, query, key, value, mixed, grad, logs)


def work(rows, depth, tokens, moved):
    return pl.CostEstimate(flops=2 * rows * depth * tokens, transcendentals=0, bytes_accessed=moved)


def full(shape):
    return pl.BlockSpec(shape, lambda *_: (0,) * len(shape))


def project(weight, kinds, values, dtypes, joined=False):
    _, cols, depth, width = weight.shape
    tokens = values[0].shape[1]
    outs = 1 if joined else len(kinds)

    def kernel(*refs):
        blocks = refs[: len(kinds)]
        given = refs[len(kinds) : -outs]
        total = None
        for index, block in enumerate(blocks):
            part = dot(block[0, 0], given[index % len(given)][...], ((0,), (0,)))
            if not joined:
                refs[index - outs][...] = part.astype(dtypes[index])
            total = part if total is None else total + part
        if joined:
            refs[-1][...] = total.astype(dtypes[0])

    return pl.pallas_call(
        kernel,
        grid=(cols,),
        in_specs=[
            pl.BlockSpec((1, 1, depth, width), partial(lambda k, c: (k, c, 0, 0), kind))
            for kind in kinds
        ]
        + [full(v.shape) for v in values],
        out_specs=[pl.BlockSpec((width, tokens), lambda c: (c, 0))] * outs,
        out_shape=[jax.ShapeDtypeStruct((cols * width, tokens), dtypes[i]) for i in range(outs)],
        cost_estimate=work(len(kinds) * cols * width, depth, tokens, 8 * depth * tokens),
        compiler_params=params(),
        name="project",
    )(*([weight] * len(kinds)), *values)


def rebuild(weight, kinds, values, dtype):
    _, cols, depth, width = weight.shape
    tokens = values[0].shape[1]
    tile = depth // 4

    def kernel(*refs):
        total = None
        for block, given in zip(refs[: len(kinds)], refs[len(kinds) : -1]):
            for col in range(cols):
                part = dot(block[0, col], given[col * width : (col + 1) * width, :], ((1,), (0,)))
                total = part if total is None else total + part
        refs[-1][...] = total.astype(dtype)

    return pl.pallas_call(
        kernel,
        grid=(4,),
        in_specs=[
            pl.BlockSpec((1, cols, tile, width), partial(lambda k, j: (k, 0, j, 0), kind))
            for kind in kinds
        ]
        + [full(v.shape) for v in values],
        out_specs=pl.BlockSpec((tile, tokens), lambda j: (j, 0)),
        out_shape=jax.ShapeDtypeStruct((depth, tokens), dtype),
        cost_estimate=work(depth, len(kinds) * cols * width, tokens, 8 * depth * tokens),
        compiler_params=params(),
        name="rebuild",
    )(*([weight] * len(kinds)), *values)


def outer(core, left, rights, flip):
    rows, tokens = left.shape
    cols = lax.axis_size("col")
    width = rights[0].shape[0] // cols

    def kernel(core_ref, left_ref, *refs):
        for index in range(len(rights)):
            part = dot(left_ref[...], refs[index][...], ((1,), (1,)))
            refs[-1][index, 0] = part.astype(BF)

    return pl.pallas_call(
        kernel,
        grid_spec=pltpu.PrefetchScalarGridSpec(
            num_scalar_prefetch=1,
            grid=(cols // 2,),
            in_specs=[pl.BlockSpec((rows, tokens), lambda y, core: (0, 0))]
            + [
                pl.BlockSpec((width, tokens), lambda y, core: (2 * y + (core[0] ^ flip), 0))
                for _ in rights
            ],
            out_specs=pl.BlockSpec(
                (len(rights), 1, rows, width), lambda y, core: (0, y, 0, 0)
            ),
        ),
        out_shape=jax.ShapeDtypeStruct((len(rights), cols // 2, rows, width), BF),
        cost_estimate=work(
            rows, tokens, len(rights) * cols // 2 * width, 3 * rows * cols * width * len(rights)
        ),
        compiler_params=params(),
        name="outer",
    )(core, left, *rights)


def expand(blocks, values):
    many = len(blocks)
    depth, hidden = blocks[0].shape
    tokens = values.shape[1]
    tile = 384 if hidden % 384 == 0 else hidden
    slope = 0.79788456
    cubic = 0.044715

    def kernel(*refs):
        values_ref, act_ref, slope_ref = refs[many:]
        for index in range(many):
            inner = dot(refs[index][...], values_ref[...], ((0,), (0,)))
            square = inner * inner
            bent = jnp.tanh(inner * (slope + slope * cubic * square))
            half = 0.5 + 0.5 * bent
            act_ref[index] = (inner * half).astype(BF)
            rise = slope + 3.0 * slope * cubic * square
            slope_ref[index] = (half + 0.5 * inner * (1.0 - bent * bent) * rise).astype(BF)

    return pl.pallas_call(
        kernel,
        grid=(hidden // tile,),
        in_specs=[pl.BlockSpec((depth, tile), lambda j: (0, j))] * many + [full(values.shape)],
        out_specs=[pl.BlockSpec((many, tile, tokens), lambda j: (0, j, 0))] * 2,
        out_shape=[jax.ShapeDtypeStruct((many, hidden, tokens), BF)] * 2,
        cost_estimate=work(many * hidden, depth, tokens, 3 * many * hidden * depth),
        compiler_params=params(),
        name="expand",
    )(*blocks, values)


def expand_back(blocks, values, slopes):
    many = len(blocks)
    depth, hidden = blocks[0].shape
    tokens = values.shape[1]
    tile = 384 if hidden % 384 == 0 else hidden

    def kernel(*refs):
        values_ref, slope_ref, out_ref = refs[many:]
        for index in range(many):
            part = dot(refs[index][...], values_ref[...], ((0,), (0,)))
            out_ref[index] = (part * slope_ref[index].astype(F32)).astype(BF)

    return pl.pallas_call(
        kernel,
        grid=(hidden // tile,),
        in_specs=[pl.BlockSpec((depth, tile), lambda j: (0, j))] * many
        + [full(values.shape), pl.BlockSpec((many, tile, tokens), lambda j: (0, j, 0))],
        out_specs=pl.BlockSpec((many, tile, tokens), lambda j: (0, j, 0)),
        out_shape=jax.ShapeDtypeStruct((many, hidden, tokens), BF),
        cost_estimate=work(many * hidden, depth, tokens, 3 * many * hidden * depth),
        compiler_params=params(),
        name="expand_back",
    )(*blocks, values, slopes)


def contract(blocks, values, added, dtype):
    many = len(blocks)
    depth, hidden = blocks[0].shape
    tokens = values.shape[2]
    tile = depth // 4
    extra = [] if added is None else [added]

    def kernel(*refs):
        values_ref = refs[many]
        total = refs[many + 1][...] if extra else None
        for index in range(many):
            part = dot(refs[index][...], values_ref[index], ((1,), (0,)))
            total = part if total is None else total + part
        refs[-1][...] = total.astype(dtype)

    line = pl.BlockSpec((tile, tokens), lambda j: (j, 0))
    return pl.pallas_call(
        kernel,
        grid=(4,),
        in_specs=[pl.BlockSpec((tile, hidden), lambda j: (j, 0))] * many
        + [full(values.shape)]
        + [line] * len(extra),
        out_specs=line,
        out_shape=jax.ShapeDtypeStruct((depth, tokens), dtype),
        cost_estimate=work(depth, many * hidden, tokens, 3 * many * hidden * depth),
        compiler_params=params(),
        name="contract",
    )(*blocks, values, *extra)


def hidden_outer(base, grad_out, act, normed, grad_inner):
    many, hidden, tokens = act.shape
    depth = grad_out.shape[0]
    parts = 2 if hidden % 256 == 0 else 1
    tile = hidden // parts

    def kernel(base_ref, out_ref, act_ref, normed_ref, inner_ref, grad_ref):
        kind = pl.program_id(0)

        @pl.when(kind == 0)
        def _():
            grad_ref[0, 0] = dot(normed_ref[...], inner_ref[0], ((1,), (1,))).astype(BF)

        @pl.when(kind == 1)
        def _():
            grad_ref[0, 0] = dot(out_ref[...], act_ref[0], ((1,), (1,))).astype(BF)

    return pl.pallas_call(
        kernel,
        grid_spec=pltpu.PrefetchScalarGridSpec(
            num_scalar_prefetch=1,
            grid=(2, many, parts),
            in_specs=[
                pl.BlockSpec((depth, tokens), lambda s, p, j, b: (0, 0)),
                pl.BlockSpec((1, tile, tokens), lambda s, p, j, b: (s * p, s * j, 0)),
                pl.BlockSpec((depth, tokens), lambda s, p, j, b: (0, 0)),
                pl.BlockSpec(
                    (1, tile, tokens),
                    lambda s, p, j, b: (p + s * (many - 1 - p), j + s * (parts - 1 - j), 0),
                ),
            ],
            out_specs=pl.BlockSpec((1, 1, depth, tile), lambda s, p, j, b: (s, p ^ b[0], 0, j)),
        ),
        out_shape=jax.ShapeDtypeStruct((2, many, depth, hidden), BF),
        cost_estimate=work(2 * depth, tokens, many * hidden, 5 * many * depth * hidden),
        compiler_params=params(),
        name="hidden_outer",
    )(base, grad_out, act, normed, grad_inner)


def assemble(place, own, got):
    _, rows, width = own.shape

    def kernel(place_ref, own_ref, got_ref, out_ref):
        @pl.when(pl.program_id(1) == place_ref[1])
        def _():
            out_ref[0, 0] = own_ref[0]

        @pl.when(pl.program_id(1) != place_ref[1])
        def _():
            out_ref[0, 0] = got_ref[0]

    spec = pl.BlockSpec((1, rows, width), lambda z, x, place: (z ^ place[0], 0, 0))
    return pl.pallas_call(
        kernel,
        grid_spec=pltpu.PrefetchScalarGridSpec(
            num_scalar_prefetch=1,
            grid=(4, 2),
            in_specs=[spec, spec],
            out_specs=pl.BlockSpec((1, 1, rows, width), lambda z, x, place: (z, x, 0, 0)),
        ),
        out_shape=jax.ShapeDtypeStruct((4, 2, rows, width), BF),
        cost_estimate=work(1, 1, 1, 48 * rows * width),
        name="assemble",
    )(place, own, got).reshape(8 * rows, width)


def normalize(values):
    average = jnp.mean(values, 0, keepdims=True)
    centred = values - average
    inverse = lax.rsqrt(jnp.mean(centred * centred, 0, keepdims=True) + EPSILON)
    return centred * inverse, inverse


def norm_back(grad, normal, inverse):
    average = jnp.mean(grad, 0, keepdims=True)
    crossed = jnp.mean(grad * normal, 0, keepdims=True)
    return inverse * (grad - average - normal * crossed)


def head_norm(values, gain):
    average = jnp.mean(values, 1, keepdims=True)
    centred = values - average
    variance = jnp.mean(centred * centred, 1, keepdims=True)
    return centred * lax.rsqrt(variance + EPSILON) * gain[None, :, None]


def rope_tables(places, head_dim):
    quarter = head_dim // 4
    freqs = jnp.exp(jnp.arange(quarter, dtype=F32) * (-4.0 * math.log(10000.0) / head_dim))
    rows = freqs[:, None] * places[0].astype(F32)[None, :]
    cols = freqs[:, None] * places[1].astype(F32)[None, :]
    angles = jnp.concatenate([rows, rows, cols, cols], 0)
    return jnp.cos(angles), jnp.sin(angles)


def rotate(values):
    quarter = values.shape[1] // 4
    one, two, three, four = (values[:, i * quarter : (i + 1) * quarter] for i in range(4))
    return jnp.concatenate([-two, one, -four, three], 1)


class Piece:
    def __init__(self, start, count, group, sequence):
        self.start = start
        self.count = count
        self.group = group
        self.sequence = sequence


def pieces_of(cols, sequences):
    mine = lax.axis_index("col")
    if cols == 4 and sequences == 3:
        return [
            Piece(0, L // 2, 2, mine // 2),
            Piece(2 * L, L // 4, 4, jnp.int32(2)),
        ]
    return [Piece(s * L, L // cols, cols, jnp.int32(s)) for s in range(sequences)]


def groups_of(size, cols):
    return [list(range(i, i + size)) for i in range(0, cols, size)]


def exchange(values, size, cols):
    if size == cols:
        return lax.all_to_all(values, "col", 0, 0, tiled=True)
    return lax.all_to_all(
        values, "col", 0, 0, tiled=True, axis_index_groups=groups_of(size, cols)
    )


def to_tokens(values, pieces, cols):
    width = values.shape[0]
    parts = []
    for piece in pieces:
        region = values[:, piece.start : piece.start + cols * piece.count]
        parts.append(region.reshape(width, cols, piece.count).transpose(1, 0, 2))
    stacked = jnp.concatenate(parts, 2)
    return exchange(stacked, cols, cols).reshape(cols * width, -1)


def to_features(values, pieces, cols):
    width = values.shape[0] // cols
    got = exchange(values.reshape(cols, width, -1), cols, cols)
    parts = []
    at = 0
    for piece in pieces:
        part = got[:, :, at : at + piece.count]
        parts.append(part.transpose(1, 0, 2).reshape(width, cols * piece.count))
        at += piece.count
    return jnp.concatenate(parts, 1)


def shared(values, axis):
    size = lax.axis_size(axis)
    return lax.all_to_all(
        jnp.broadcast_to(values[None], (size, *values.shape)), axis, 0, 0, tiled=True
    )


def swap(values, axis, bit):
    size = lax.axis_size(axis)
    return lax.ppermute(values, axis, [(i, i ^ bit) for i in range(size)])


def custom_mesh():
    return (lax.axis_size("row"), lax.axis_size("col")) == (8, 4)


def gather_weights(blocks):
    cols = lax.axis_size("col")
    most = max(block.shape[0] for block in blocks)
    padded = [jnp.pad(b, ((0, most - b.shape[0]), (0, 0))) for b in blocks]
    whole = lax.all_gather(jnp.stack(padded, 0), DEVICES, axis=1, tiled=True)
    return whole.reshape(len(blocks), cols, -1, blocks[0].shape[1])


def gather_blocks(block, across, place):
    if not custom_mesh():
        cols = lax.axis_size("col")
        whole = lax.all_gather(block, DEVICES, axis=0, tiled=True).reshape(cols, -1, block.shape[1])
        return [whole[i] for i in range(cols)]
    stack = jnp.stack([block] + [swap(block, "row", 2 * level) for level in (1, 2, 3)], 0)
    if across:
        mine = assemble(place, stack, swap(stack, "row", 1))
        other = swap(mine, "col", 2)
    else:
        up = swap(stack, "col", 2)
        mine = assemble(place, stack, swap(stack, "row", 1))
        other = assemble(place, up, swap(up, "row", 1))
    return [mine, swap(mine, "col", 1), other, swap(other, "col", 1)]


def pick(values, axis, index):
    return lax.dynamic_index_in_dim(values, index, axis, False)


def add(left, right):
    return (left.astype(F32) + right.astype(F32)).astype(BF)


class Reduction:
    def __init__(self, core, left, rights, across):
        self.across = across
        self.many = len(rights)
        self.stage = 0
        if not custom_mesh():
            cols = lax.axis_size("col")
            whole = jnp.stack(
                [einsum("kt,cnt->ckn", left, r.reshape(cols, -1, r.shape[1])) for r in rights], 0
            )
            flat = whole.reshape(self.many, -1, whole.shape[3]).astype(BF)
            self.state = [lax.psum_scatter(flat, DEVICES, scatter_dimension=1, tiled=True)]
            return
        shape = (self.many, 2, 4, 2, left.shape[0] // 8, rights[0].shape[0] // 4)
        send = outer(core, left, rights, 1)
        got = swap(send, "col", 1)
        keep = outer(core, left, rights, 0)
        self.state = [keep.reshape(shape), got.reshape(shape)]

    def half(self, side):
        kept, got = self.state
        axis = (3 if kept.ndim == 6 else 2) if side else 1
        name, bit = ("row", 1) if side else ("col", 2)
        index = lax.axis_index("row") % 2 if side else lax.axis_index("col") // 2
        away = add(pick(kept, axis, 1 - index), pick(got, axis, 1 - index))
        here = add(pick(kept, axis, index), pick(got, axis, index))
        self.state = [here, swap(away, name, bit)]

    def advance(self):
        if not custom_mesh() or self.stage == 4:
            return
        self.stage += 1
        if self.stage <= 2:
            self.half(self.across == (self.stage == 1))
        elif self.stage == 3:
            level = lax.axis_index("row") // 2
            total = add(*self.state)
            self.state = [pick(total, 1, level)] + [
                swap(pick(total, 1, level ^ other), "row", 2 * other) for other in (1, 2, 3)
            ]
        else:
            total = self.state[0].astype(F32)
            for other in self.state[1:]:
                total = total + other.astype(F32)
            self.state = [total]

    def result(self):
        while custom_mesh() and self.stage < 4:
            self.advance()
        return self.state[0].astype(F32)


def tick(values, running):
    active = [r for r in running if r.stage < 4]
    if active and custom_mesh():
        values, states = lax.optimization_barrier((values, [r.state for r in active]))
        for reduction, state in zip(active, states):
            reduction.state = state
            reduction.advance()
    return values


def shards(
    latents,
    skip_input,
    condition,
    text_states,
    text_lengths,
    positions,
    out_grad,
    skip_weight,
    modulation,
    self_inputs,
    self_output,
    cross_query,
    cross_keyvalue,
    cross_output,
    expand_weight,
    reduce_weight,
    skip_gain,
    skip_bias,
    cross_gain,
    cross_bias,
    hidden_gain,
    hidden_bias,
    query_gain,
    key_gain,
    cross_query_gain,
    text_key_gain,
):
    cols = lax.axis_size("col")
    rows = lax.axis_size("row")
    mine = lax.axis_index("col")
    my_row = lax.axis_index("row")
    width, row_tokens = latents.shape
    depth = width * cols
    dim = query_gain.shape[0]
    heads = depth // dim
    sequences = row_tokens // L
    tokens = row_tokens // cols
    texts = text_states.shape[1]
    keys = -(-texts // KEYPAD) * KEYPAD
    pieces = pieces_of(cols, sequences)
    starts = [sum(p.count for p in pieces[:i]) for i in range(len(pieces))]
    core = (mine % 2).astype(jnp.int32)[None]
    place = jnp.stack([my_row // 2, my_row % 2]).astype(jnp.int32)
    base = (mine if custom_mesh() else jnp.zeros_like(mine)).astype(jnp.int32)[None]

    def cut(values, index):
        return values[..., starts[index] : starts[index] + pieces[index].count]

    weights_one = gather_weights(
        [skip_weight[0], skip_weight[1], self_inputs[:, 0], self_inputs[:, 1], self_inputs[:, 2]]
    )
    weights_two = gather_weights(
        [self_output.T, cross_query, cross_output.T, cross_keyvalue[:, 0], cross_keyvalue[:, 1]]
    )
    w_expand = gather_blocks(expand_weight, True, place)
    w_reduce = gather_blocks(reduce_weight.T, False, place)

    latent = to_tokens(latents, pieces, cols)
    skipped = to_tokens(skip_input, pieces, cols)
    grad_out = to_tokens(out_grad.astype(BF), pieces, cols)
    places = jnp.concatenate(
        [
            lax.dynamic_slice_in_dim(positions, p.start + mine * p.count, p.count, 1)
            for p in pieces
        ],
        1,
    )

    embed = jax.nn.silu(condition.astype(F32)).astype(BF)
    embed = shared(embed, "row").reshape(-1, width)
    embed = shared(embed, "col").transpose(1, 0, 2).reshape(-1, depth)
    block_rows = depth // rows
    embed_rows = lax.dynamic_slice_in_dim(embed, my_row * block_rows, block_rows, 1)
    modul = einsum("sd,dke->ske", embed_rows, modulation).reshape(rows, sequences, 2, width)
    modul = jnp.sum(lax.all_to_all(modul, "row", 0, 0, tiled=True), 0)
    gains = jnp.stack(
        [skip_gain, skip_bias, cross_gain, cross_bias, hidden_gain, hidden_bias], 0
    )
    table = jnp.concatenate([gains, modul.reshape(-1, width)], 0)
    table = shared(table, "col").transpose(1, 0, 2).reshape(-1, depth)
    modul = table[6:].reshape(sequences, 2, depth)
    chosen = [lax.dynamic_index_in_dim(modul, p.sequence, 0, False) for p in pieces]
    columns = lax.optimization_barrier(jnp.concatenate([table[:6], *chosen], 0)).T
    gain_skip, bias_skip, gain_cross, bias_cross, gain_hidden, bias_hidden = (
        columns[:, i : i + 1] for i in range(6)
    )
    token_index = lax.broadcasted_iota(jnp.int32, (1, tokens), 1)

    def per_token(which):
        result = columns[:, 6 + which : 7 + which]
        for index in range(1, len(pieces)):
            column = columns[:, 6 + 2 * index + which : 7 + 2 * index + which]
            result = jnp.where(token_index >= starts[index], column, result)
        return jnp.broadcast_to(result, (depth, tokens))

    shifting = per_token(0)
    scaling = 1.0 + per_token(1)

    joined = project(weights_one, [0, 1], [latent, skipped], [F32], True)[0]
    skip_normal, skip_inverse = normalize(joined)
    stream = skip_normal * gain_skip + bias_skip
    normal_one, inverse_one = normalize(stream)
    normed_one = (normal_one * scaling + shifting).astype(BF)
    raw = project(weights_one, [2, 3, 4], [normed_one], [F32, F32, BF])
    raw = [r.reshape(heads, dim, tokens) for r in raw]
    cosine, sine = rope_tables(places, dim)

    def self_piece(value, gain):
        normal = head_norm(value, gain)
        return normal * cosine[None] + rotate(normal) * sine[None]

    rot_query, query_pull = jax.vjp(self_piece, raw[0], query_gain)
    rot_key, key_pull = jax.vjp(self_piece, raw[1], key_gain)
    triple = [rot_query.astype(BF), rot_key.astype(BF), raw[2]]

    text = shared(jnp.pad(text_states, ((0, 0), (0, keys - texts), (0, 0))), "col")
    text = jnp.concatenate(
        [lax.dynamic_index_in_dim(text, p.sequence, 1, False) for p in pieces], 1
    )
    text = text.transpose(0, 2, 1).reshape(-1, len(pieces) * keys)
    text_rows = text.shape[0] // rows
    text_wide = jnp.pad(
        text.reshape(rows, text_rows, -1), ((0, 0), (0, block_rows - text_rows), (0, 0))
    ).reshape(depth, -1)

    def to_heads(parts, index):
        size = pieces[index].group
        split = [cut(p, index).reshape(size, heads // size, dim, -1) for p in parts]
        return exchange(jnp.stack(split, 1), size, cols)

    none = jnp.zeros((1,), jnp.int32)
    saved_self = []
    mixed_parts = []
    for index, piece in enumerate(pieces):
        whole = to_heads(triple, index)
        mixed, logs = attend(none, whole, whole, whole, (0, 1, 2), False, 2)
        saved_self.append((whole, mixed, logs))
        mixed_parts.append(exchange(mixed, piece.group, cols).reshape(depth, -1))
    mixed_one = jnp.concatenate(mixed_parts, 1)
    stream = stream + rebuild(weights_two, [0], [mixed_one], F32)
    normal_two, inverse_two = normalize(stream)
    normed_two = (normal_two * gain_cross + bias_cross).astype(BF)
    raw_cross = project(weights_two, [1], [normed_two], [F32])[0].reshape(heads, dim, tokens)
    norm_query, cross_pull = jax.vjp(head_norm, raw_cross, cross_query_gain)
    raw_text, value_two = project(weights_two, [3, 4], [text_wide], [F32, BF])
    norm_key, text_pull = jax.vjp(head_norm, raw_text.reshape(heads, dim, -1), text_key_gain)
    query_two = norm_query.astype(BF)
    key_two = norm_key.astype(BF)
    value_two = value_two.reshape(heads, dim, -1)
    saved_cross = []
    mixed_parts = []
    for index, piece in enumerate(pieces):
        length = lax.dynamic_index_in_dim(text_lengths, piece.sequence, 0, True)
        here = slice(index * keys, (index + 1) * keys)
        inputs = [cut(query_two, index), key_two[:, :, here], value_two[:, :, here]]
        inputs = [length] + [a[None, None] for a in inputs] + [(0, 0, 0)]
        mixed, logs = attend(*inputs, True, 4)
        saved_cross.append((inputs, mixed, logs))
        mixed_parts.append(mixed.reshape(depth, -1))
    mixed_two = jnp.concatenate(mixed_parts, 1)
    stream = stream + rebuild(weights_two, [2], [mixed_two], F32)
    normal_three, inverse_three = normalize(stream)
    normed_three = (normal_three * gain_hidden + bias_hidden).astype(BF)
    act, slopes = expand(w_expand, normed_three)
    output = contract(w_reduce, act, stream, BF)
    result = to_features(output, pieces, cols).astype(F32)

    g_inner = expand_back(w_reduce, grad_out, slopes)
    g_normed = contract(w_expand, g_inner, None, F32)
    g_hidden = hidden_outer(base, grad_out, act, normed_three, g_inner)
    g_hidden = lax.psum_scatter(
        g_hidden.reshape(2, -1, g_hidden.shape[3]), DEVICES, scatter_dimension=1, tiled=True
    ).astype(F32)
    g_hidden_gain = jnp.sum(g_normed * normal_three, 1)
    g_hidden_bias = jnp.sum(g_normed, 1)
    g_stream = grad_out.astype(F32) + norm_back(g_normed * gain_hidden, normal_three, inverse_three)

    running = []
    g_low = g_stream.astype(BF)
    g_mixed = project(weights_two, [2], [g_low], [BF])[0].reshape(heads, dim, tokens)
    r_cross = Reduction(core, g_low, [mixed_two], True)
    running.append(r_cross)
    g_queries = []
    g_keys = []
    g_values = []
    for index, piece in enumerate(pieces):
        inputs, mixed, logs = saved_cross[index]
        grads = attend_back(*inputs, mixed, cut(g_mixed, index)[None], logs, True, 4, False)
        g_queries.append(grads[0][0, 0])
        g_keys.append(grads[1][0, 0])
        g_values.append(grads[2][0, 0])
    g_queries, g_keys, g_values = tick((g_queries, g_keys, g_values), running)
    g_raw_cross, g_cq_gain = cross_pull(jnp.concatenate(g_queries, 2))
    g_raw_text, g_tk_gain = text_pull(jnp.concatenate(g_keys, 2))
    g_craw = g_raw_cross.astype(BF).reshape(depth, tokens)
    g_pair = [
        g_raw_text.astype(BF).reshape(depth, -1),
        jnp.concatenate(g_values, 2).astype(BF).reshape(depth, -1),
    ]
    g_normed = rebuild(weights_two, [1], [g_craw], F32)
    r_query = Reduction(core, normed_two, [g_craw], False)
    r_text = Reduction(core, text, g_pair, True)
    g_normed = tick(g_normed, running)
    running += [r_query, r_text]
    g_cross_gain = jnp.sum(g_normed * normal_two, 1)
    g_cross_bias = jnp.sum(g_normed, 1)
    g_stream = g_stream + norm_back(g_normed * gain_cross, normal_two, inverse_two)

    g_low = g_stream.astype(BF)
    g_mixed = project(weights_two, [0], [g_low], [BF])[0].reshape(heads, dim, tokens)
    g_mixed = tick(g_mixed, running)
    r_attn = Reduction(core, g_low, [mixed_one], False)
    g_parts = []
    for index, piece in enumerate(pieces):
        whole, mixed, logs = saved_self[index]
        grad = exchange(
            cut(g_mixed, index).reshape(piece.group, -1, dim, piece.count), piece.group, cols
        )
        part = attend_back(
            none, whole, whole, whole, (0, 1, 2), mixed, grad, logs, False, 2, True
        )
        part = tick(part, running)
        if index == 0:
            running.append(r_attn)
        g_parts.append(exchange(part, piece.group, cols))
    g_heads = [
        jnp.concatenate([p[:, i].reshape(heads, dim, -1) for p in g_parts], 2) for i in range(3)
    ]
    g_raw_q, g_q_gain = query_pull(g_heads[0].astype(F32))
    g_raw_k, g_k_gain = key_pull(g_heads[1].astype(F32))
    g_triple = [
        g.reshape(depth, tokens) for g in (g_raw_q.astype(BF), g_raw_k.astype(BF), g_heads[2])
    ]
    g_triple = tick(g_triple, running)
    g_normed = rebuild(weights_one, [2, 3, 4], g_triple, F32)
    g_normed = tick(g_normed, running)
    r_self = [
        Reduction(core, normed_one, g_triple[:2], True),
        Reduction(core, normed_one, g_triple[2:], False),
    ]
    crossed = g_normed * normal_one
    sums = jnp.stack(
        [
            jnp.stack([jnp.sum(cut(g_normed, i), 1), jnp.sum(cut(crossed, i), 1)], 0)
            for i in range(len(pieces))
        ],
        0,
    )
    which = jnp.stack(
        [jnp.where(jnp.arange(sequences) == p.sequence, 1.0, 0.0) for p in pieces], 0
    )
    g_modul = jnp.sum(which[:, :, None, None] * sums[:, None], 0)
    g_modul = g_modul.reshape(sequences, 2, cols, width).transpose(2, 0, 1, 3)
    g_modul = jnp.sum(lax.all_to_all(g_modul, "col", 0, 0, tiled=True), 0).astype(BF)
    g_modul = shared(g_modul, "row").reshape(-1, 2, width)
    g_modulation = einsum("sd,ske->dke", embed_rows, g_modul)
    g_stream = g_stream + norm_back(g_normed * scaling, normal_one, inverse_one)

    g_skip_gain = jnp.sum(g_stream * skip_normal, 1)
    g_skip_bias = jnp.sum(g_stream, 1)
    g_joined = norm_back(g_stream * gain_skip, skip_normal, skip_inverse).astype(BF)
    g_joined = tick(g_joined, running)
    r_skip = [
        Reduction(core, latent, [g_joined], True),
        Reduction(core, skipped, [g_joined], False),
    ]
    running += r_self
    g_latent = rebuild(weights_one, [0], [g_joined], BF)
    g_skipped = rebuild(weights_one, [1], [g_joined], BF)
    g_latent, g_skipped = tick((g_latent, g_skipped), running)
    g_latents = to_features(g_latent, pieces, cols).astype(F32)
    g_skip = to_features(g_skipped, pieces, cols).astype(F32)

    g_gains = jnp.stack(
        [g_skip_gain, g_skip_bias, g_cross_gain, g_cross_bias, g_hidden_gain, g_hidden_bias], 0
    )
    g_gains = g_gains.reshape(6, cols, width).transpose(1, 0, 2)
    g_head = jnp.stack([g_q_gain, g_k_gain, g_cq_gain, g_tk_gain], 0).reshape(1, -1, width)
    packed = jnp.concatenate([g_gains, jnp.broadcast_to(g_head, (cols, *g_head.shape[1:]))], 1)
    packed = jnp.sum(lax.all_to_all(packed, "col", 0, 0, tiled=True), 0)
    packed = jnp.sum(shared(packed, "row"), 0)
    g_gains = packed[:6]
    g_head = packed[6:].reshape(4, dim)
    return (
        result,
        g_latents,
        g_skip,
        jnp.concatenate([r.result() for r in r_skip], 0),
        g_modulation,
        jnp.concatenate([r.result() for r in r_self], 0).transpose(1, 0, 2),
        r_attn.result()[0].T,
        r_query.result()[0],
        r_text.result().transpose(1, 0, 2),
        r_cross.result()[0].T,
        g_hidden[0],
        g_hidden[1].T,
        *[g_gains[i] for i in range(6)],
        *[g_head[i] for i in range(4)],
    )


def solution(mesh):
    return jax.shard_map(
        shards,
        mesh=mesh,
        in_specs=(
            P("col", "row"),
            P("col", "row"),
            P("row", "col"),
            P("row", None, "col"),
            P("row"),
            P(None, "row"),
            P("col", "row"),
            P(None, "row", "col"),
            P("row", None, "col"),
            P("row", None, "col"),
            P("col", "row"),
            P("row", "col"),
            P("row", None, "col"),
            P("col", "row"),
            P("row", "col"),
            P("col", "row"),
            P("col"),
            P("col"),
            P("col"),
            P("col"),
            P("col"),
            P("col"),
            P(),
            P(),
            P(),
            P(),
        ),
        out_specs=(
            P("col", "row"),
            P("col", "row"),
            P("col", "row"),
            P(None, "row", "col"),
            P("row", None, "col"),
            P("row", None, "col"),
            P("col", "row"),
            P("row", "col"),
            P("row", None, "col"),
            P("col", "row"),
            P("row", "col"),
            P("col", "row"),
            P("col"),
            P("col"),
            P("col"),
            P("col"),
            P("col"),
            P("col"),
            P(),
            P(),
            P(),
            P(),
        ),
        check_vma=False,
    )
```

time: 1870 us -> 1630 us (0.87)
  matrix products: 335 us -> 1.28 us
  Pallas kernels: 167 us -> 479 us
  local copies, waits for them, and re-layouts: 445 us -> 167 us
  blocking collectives: 176 us -> 71.9 us
  waiting for transfers between devices: 336 us -> 412 us
  starting transfers between devices: 143 us -> 195 us
  other arithmetic: 223 us -> 273 us
    dot_general x48 -> x2, matrix products: 335 us -> 1.28 us  [einsum(): return jnp.einsum(spec, left, right, preferred_element_type=F32)]
    pallas_call x8 -> x44, Pallas kernels: 167 us -> 479 us  [the longest x16 95.7 us: outer(): pl.pallas_call(kernel, grid_spec=pltpu.PrefetchScalarGridSpec(num_scalar_...]
    all_to_all x0 -> x8, waiting for transfers between devices: none -> 157 us  [the longest x5 148 us: shared(): lax.all_to_all(jnp.broadcast_to(values[None], (size, *values.shape)), axi...]
    all_gather x5 -> x0, blocking collectives: 115 us -> none  [the longest x1 32.1 us: shards(): lax.all_gather(jax.nn.silu(condition.astype(F32)).astype(BF), 'row', axis...]
    all_gather x3 -> x2, waiting for transfers between devices: 89.8 us -> 0.02 us  [gather_weights(): whole = lax.all_gather(jnp.stack(padded, 0), DEVICES, axis=1, tiled=True)]
    another operation x25 -> x0, local copies, waits for them, and re-layouts: 86.8 us -> none  [the longest x6 52.4 us: gather_weights(): result.append(part.reshape(cols, -1, block.shape[1]))]
    slice x16 -> x7, local copies, waits for them, and re-layouts: 74.4 us -> 7.25 us  [the longest x2 6.47 us: shards(): p[:, i].reshape(heads, dim, -1)]
    all_to_all x0 -> x1, blocking collectives: none -> 66.2 us  [shared(): lax.all_to_all(jnp.broadcast_to(values[None], (size, *values.shape)), axi...]
  transfers between devices with their start and end apart: 89 -> 87, of which waited for: 27 -> 30; matrix products, arithmetic and copies ran while one was open for 40% -> 26% of each run, Pallas kernels for 5% -> 26%
where the time goes in v2:
time: 1630 us; the launch traced here: 1620 us
  Pallas kernels  479 us (29%)
  waiting for transfers between devices  412 us (25%)
  other arithmetic  273 us (17%)
  starting transfers between devices  195 us (12%)
  local copies, waits for them, and re-layouts  167 us (10%)
  blocking collectives  71.9 us (4%)
  between operations  16.9 us (1%)
    ppermute x63, waiting for transfers between devices, swap(): return lax.ppermute(values, axis, [(i, i ^ bit) for i in range(size)])  227 us
    all_to_all x5, waiting for transfers between devices, shared(): lax.all_to_all(jnp.broadcast_to(values[None], (size, *values.shape)), axi...  148 us
    pallas_call x16, Pallas kernels, outer(): pl.pallas_call(kernel, grid_spec=pltpu.PrefetchScalarGridSpec(num_scalar_...  95.7 us
    ppermute x63, starting transfers between devices, swap(): return lax.ppermute(values, axis, [(i, i ^ bit) for i in range(size)])  90.9 us
    all_to_all x1, blocking collectives, shared(): lax.all_to_all(jnp.broadcast_to(values[None], (size, *values.shape)), axi...  66.2 us
    pallas_call x4, Pallas kernels, attend_back(): pl.pallas_call(partial(attend_back_kernel, masked), grid=(heads // many,)...  64.5 us
    pallas_call x6, Pallas kernels, rebuild(): pl.pallas_call(kernel, grid=(4,), in_specs=[pl.BlockSpec((1, cols, tile,...  60.9 us
    pallas_call x6, Pallas kernels, project(): pl.pallas_call(kernel, grid=(cols,), in_specs=[pl.BlockSpec((1, 1, depth,...  60.3 us
  transfers between devices with their start and end apart: 87, of which 30 were waited for; matrix products, arithmetic and copies ran while one was open for 26% of the time, Pallas kernels for 26%

profile of v2, /device:TPU:0, one launch (start us, length us, event | category | flops | bytes accessed | tf_op | source)
XLA Modules:
  0.0 1616.3 jit_solution(15503398234162850662)
XLA Ops:
  18.5 32.5 %collective-permute-done.8 = bf16[176,1536]{1,0:T(8,128)(2,1)S(1)} collective-permute-done((bf16[176,1536]{1,0:T(8,128)(2,1)S(1)}, bf16[176,1536]{1,0:T(8,128)(2,1)S(1)}, u32[]{:S(2)}, u32[]{:S(2)}) %collective-permute-start.8) | collective-permute-done | bytes 540704 | tf_op jit(solution)/shard_map/ppermute | solution.py:534
  54.1 13.3 collective-permute-done.10
  70.7 66.2 %all_to_all.115 = bf16[8,3,352]{2,1,0:T(4,128)(2,1)S(1)} all-to-all(bf16[8,3,352]{2,1,0:T(4,128)(2,1)S(1)} %broadcast_in_dim.201), channel_id=1, replica_groups=mesh['row'=8,'col'=4] {'row'}, dimensions={0} | all-to-all | bytes 33792 | tf_op jit(solution)/shard_map/all_to_all | solution.py:527
  147.0 21.3 %all-to-all-start.4 = ((f32[8,3,2,352]{3,2,1,0:T(2,128)}), f32[8,3,2,352]{3,2,1,0:T(2,128)S(1)}, u32[]{:S(2)}, u32[]{:S(2)}) async-start(f32[8,3,2,352]{3,2,1,0:T(2,128)} %bitcast.26), calls=%async_computation.4 | async-start | bytes 147456 | tf_op jit(solution)/shard_map/all_to_all | solution.py:710
  188.8 26.8 %collective-permute-done = bf16[176,1536]{1,0:T(8,128)(2,1)} collective-permute-done((bf16[176,1536]{1,0:T(8,128)(2,1)}, bf16[176,1536]{1,0:T(8,128)(2,1)}, u32[]{:S(2)}, u32[]{:S(2)}) %collective-permute-start) | collective-permute-done | bytes 540704 | tf_op jit(solution)/shard_map/ppermute | solution.py:534
  218.4 15.7 collective-permute-done.2
  239.3 8.0 assemble.5
  259.7 42.5 %collective-permute-done.5.own_ref = bf16[4,176,1536]{2,1,0:T(8,128)(2,1)} collective-permute-done((bf16[4,176,1536]{2,1,0:T(8,128)(2,1)}, bf16[4,176,1536]{2,1,0:T(8,128)(2,1)}, u32[]{:S(2)}, u32[]{:S(2)}) %collective-permute-start.5) | collective-permute-done | bytes 2162720 | tf_op jit(solution)/shard_map/ppermute | solution.py:534
  318.5 138.7 %all-to-all-done.10 = bf16[4,3,384,256]{2,3,1,0:T(8,128)(2,1)} async-done(((bf16[4,3,384,256]{2,3,1,0:T(8,128)(2,1)}), bf16[4,3,384,256]{2,3,1,0:T(8,128)(2,1)}, u32[]{:S(2)}, u32[]{:S(2)}) %all-to-all-start.10) | async-done | bytes 2359328 | tf_op jit(solution)/shard_map/all_to_all | solution.py:527
  472.9 7.9 assemble.3
  480.8 7.9 assemble.4
  490.7 11.6 project.6
  516.3 15.0 project.7
  559.6 5.6 all-to-all-start.6
  573.4 10.6 project.9
  589.5 16.6 %attend.4 = (bf16[2,8,88,512]{3,2,1,0:T(8,128)(2,1)}, f32[8,1,1024]{2,1,0:T(1,128)}) custom-call(s32[1]{0:T(128)} %constant.400.clone.1.length_ref, bf16[2,3,8,88,512]{4,3,2,1,0:T(8,128)(2,1)} %all-to-all-done.6.q_ref.k_ref.v_ref, bf16[2,3,8,88,512]{4,3,2,1,0:T(8,128)(2,1)} %all-to-all-done.6.q_ref.k_ref.v_ref, ...), custom_call_target="tpu_custom_call" | custom-call | flops 8589934592 | bytes 5767168 | tf_op jit(solution)/shard_map/attend/pallas_call | solution.py:137
  611.1 9.6 attend.5
  629.5 5.8 all-to-all-done.9
  641.9 8.5 rebuild.6
  658.5 7.9 project.8
  675.6 7.3 attend.7
  682.9 11.5 attend.6
  697.3 8.5 rebuild.7
  712.8 27.7 %expand.1 = (bf16[4,1536,768]{2,1,0:T(8,128)(2,1)}, bf16[4,1536,768]{2,1,0:T(8,128)(2,1)}) custom-call(bf16[1408,1536]{1,0:T(8,128)(2,1)} %bitcast.620, bf16[1408,1536]{1,0:T(8,128)(2,1)} %collective-permute-done.12.refs_1_, bf16[1408,1536]{1,0:T(8,128)(2,1)} %collective-permute-done.13.refs_2_, bf16[1408,1536]{1,0:T(8,128)(2,1)} %collective-permute-done.14.refs_3_, ...), custom_call_target="tpu_custom_call" | custom-call | flops 13287555072 | bytes 25952256 | tf_op jit(solution)/shard_map/expand/pallas_call | solution.py:304
  741.9 20.6 %expand_back.1.refs_4_.inner_ref = bf16[4,1536,768]{2,1,0:T(8,128)(2,1)} custom-call(bf16[1408,1536]{1,0:T(8,128)(2,1)} %bitcast.623, bf16[1408,1536]{1,0:T(8,128)(2,1)} %collective-permute-done.4.refs_1_, bf16[1408,1536]{1,0:T(8,128)(2,1)} %bitcast.626, bf16[1408,1536]{1,0:T(8,128)(2,1)} %collective-permute-done.7.refs_3_, bf16[1408,768]{1,0:T(8,128)(2,1)} %bitcast.552, ...), custom_call_target="tpu_custom_call" | custom-call | flops 13287555072 | bytes 25952256 | tf_op jit(solution)/shard_map/expand_back/pallas_call | solution.py:328
  762.4 36.3 %hidden_outer.1 = bf16[2,4,1408,1536]{3,2,1,0:T(8,128)(2,1)} custom-call(s32[1]{0:T(128)} %bitcast.213.base_ref, bf16[1408,768]{1,0:T(8,128)(2,1)} %bitcast.553, bf16[4,1536,768]{2,1,0:T(8,128)(2,1)} %get-tuple-element.113.refs_4_.act_ref, bf16[1408,768]{1,0:T(8,128)(2,1)} %add_convert_fusion.4.refs_4_.normed_ref, ...), custom_call_target="tpu_custom_call" | custom-call | flops 26575110144 | bytes 43253760 | tf_op jit(solution)/shard_map/hidden_outer/pallas_call | solution.py:388
  798.8 21.1 %contract.3 = f32[1408,768]{1,0:T(8,128)} custom-call(bf16[1408,1536]{1,0:T(8,128)(2,1)} %bitcast.621, bf16[1408,1536]{1,0:T(8,128)(2,1)} %collective-permute-done.12.refs_1_, bf16[1408,1536]{1,0:T(8,128)(2,1)} %collective-permute-done.13.refs_2_, bf16[1408,1536]{1,0:T(8,128)(2,1)} %collective-permute-done.14.refs_3_, ...), custom_call_target="tpu_custom_call" | custom-call | flops 13287555072 | bytes 25952256 | tf_op jit(solution)/shard_map/contract/pallas_call | solution.py:357
  819.9 6.6 multiply_reduce_fusion.2
  832.3 5.9 outer.17
  842.6 23.1 %contract.2 = bf16[1408,768]{1,0:T(8,128)(2,1)} custom-call(bf16[1408,1536]{1,0:T(8,128)(2,1)} %bitcast.624, bf16[1408,1536]{1,0:T(8,128)(2,1)} %collective-permute-done.4.refs_1_, bf16[1408,1536]{1,0:T(8,128)(2,1)} %bitcast.627, bf16[1408,1536]{1,0:T(8,128)(2,1)} %collective-permute-done.7.refs_3_, ...), custom_call_target="tpu_custom_call" | custom-call | flops 13287555072 | bytes 25952256 | tf_op jit(solution)/shard_map/contract/pallas_call | solution.py:357
  870.7 7.5 project.10
  887.0 9.5 attend_back.5
  897.7 15.2 attend_back.4
  937.4 6.7 outer.21
  974.6 6.6 outer.20
  981.2 8.8 rebuild.8
  1000.5 7.2 fusion.94
  1024.2 7.6 project.11
  1035.8 7.8 reshape.1687
  1061.0 12.6 collective-permute-start.20
  1073.7 5.7 all_to_all.116.g_ref
  1084.0 25.8 %attend_back.6 = bf16[2,3,8,88,512]{4,3,2,1,0:T(8,128)(2,1)} custom-call(s32[1]{0:T(128)} %constant.400.clone.1.length_ref, bf16[2,3,8,88,512]{4,3,2,1,0:T(8,128)(2,1)} %all-to-all-done.6.q_ref.k_ref.v_ref, bf16[2,3,8,88,512]{4,3,2,1,0:T(8,128)(2,1)} %all-to-all-done.6.q_ref.k_ref.v_ref, bf16[2,3,8,88,512]{4,3,2,1,0:T(8,128)(2,1)} %all-to-all-done.6.q_ref.k_ref.v_ref, ...), custom_call_target="tpu_custom_call" | custom-call | flops 21474836480 | bytes 14417920 | tf_op jit(solution)/shard_map/attend_back/pallas_call | solution.py:167
  1125.7 14.1 attend_back.7
  1139.8 5.7 all-to-all-start.14
  1172.8 8.9 all-to-all-done.16
  1192.2 8.1 multiply_reduce_fusion.7
  1237.9 8.2 outer.25
  1246.1 6.4 copy.388
  1254.2 19.0 %rebuild.9 = f32[1408,768]{1,0:T(8,128)} custom-call(bf16[5,4,1408,352]{3,2,1,0:T(8,128)(2,1)} %bitcast.476, bf16[5,4,1408,352]{3,2,1,0:T(8,128)(2,1)} %bitcast.477, bf16[5,4,1408,352]{3,2,1,0:T(8,128)(2,1)} %bitcast.478, bf16[1408,768]{1,0:T(8,128)(2,1)} %bitcast.598, bf16[1408,768]{1,0:T(8,128)(2,1)} %bitcast.595, ...), custom_call_target="tpu_custom_call" | custom-call | flops 9135194112 | bytes 8650752 | tf_op jit(solution)/shard_map/rebuild/pallas_call | solution.py:236
  1275.1 8.2 outer.24
  1283.3 5.9 fusion.18
  1289.3 10.9 multiply_reduce_fusion.4
  1300.6 7.3 collective-permute-start.36
  1390.3 8.1 rebuild.11
  1398.4 8.1 rebuild.10
  1431.5 6.5 collective-permute-done.42
  1440.2 7.3 collective-permute-done.48
  1449.6 6.4 copy.389
  1480.4 6.2 collective-permute-done.58
  1495.7 8.0 all-to-all-done.18
  1509.6 23.0 %collective-permute-done.59 = bf16[1,4,176,352]{3,2,1,0:T(8,128)(2,1)} collective-permute-done((bf16[1,4,176,352]{3,2,1,0:T(8,128)(2,1)}, bf16[1,4,176,352]{3,2,1,0:T(8,128)(2,1)}, u32[]{:S(2)}, u32[]{:S(2)}) %collective-permute-start.59) | collective-permute-done | bytes 495648 | tf_op jit(solution)/shard_map/ppermute | solution.py:534
  1541.0 8.1 collective-permute-done.61
  1562.6 16.2 %collective-permute-done.54 = bf16[2,4,176,352]{3,2,1,0:T(8,128)(2,1)} collective-permute-done((bf16[2,4,176,352]{3,2,1,0:T(8,128)(2,1)}, bf16[2,4,176,352]{3,2,1,0:T(8,128)(2,1)}, u32[]{:S(2)}, u32[]{:S(2)}) %collective-permute-start.54) | collective-permute-done | bytes 991264 | tf_op jit(solution)/shard_map/ppermute | solution.py:534
  1592.2 13.2 collective-permute-done.56
  (826 shorter events, 624.2 us)
Async XLA Ops:
  7.2 482.0 %all-gather.3.cloned.1.call-start = ((), (), s32[]{:S(2)}) async-start(), calls=%async_computation.24 | async-start | bytes 22302720 | tf_op jit(solution)/shard_map/all_gather | solution.py:545
  10.5 563.0 %all-gather.5.cloned.1.call-start = ((), (), s32[]{:S(2)}) async-start(), calls=%async_computation.25 | async-start | bytes 22302720 | tf_op jit(solution)/shard_map/all_gather | solution.py:545
  12.8 38.2 %collective-permute-start.8 = (bf16[176,1536]{1,0:T(8,128)(2,1)S(1)}, bf16[176,1536]{1,0:T(8,128)(2,1)S(1)}, u32[]{:S(2)}, u32[]{:S(2)}) collective-permute-start(bf16[176,1536]{1,0:T(8,128)(2,1)S(1)} %copy-done.90), channel_id=1, source_target_pairs={{0,8},{4,12},{8,0},{12,4},{16,24},{20,28},{24,16},{28,20},{1,9},{5... | collective-permute-start | bytes 1622024 | tf_op jit(solution)/shard_map/ppermute | solution.py:534
  15.9 38.2 %collective-permute-start.9 = (bf16[176,1536]{1,0:T(8,128)(2,1)S(1)}, bf16[176,1536]{1,0:T(8,128)(2,1)S(1)}, u32[]{:S(2)}, u32[]{:S(2)}) collective-permute-start(bf16[176,1536]{1,0:T(8,128)(2,1)S(1)} %copy-done.90), channel_id=1, source_target_pairs={{0,16},{4,20},{8,24},{12,28},{16,0},{20,4},{24,8},{28,12},{1,17},{... | collective-permute-start | bytes 1622024 | tf_op jit(solution)/shard_map/ppermute | solution.py:534
  18.5 48.9 %collective-permute-start.10 = (bf16[176,1536]{1,0:T(8,128)(2,1)S(1)}, bf16[176,1536]{1,0:T(8,128)(2,1)S(1)}, u32[]{:S(2)}, u32[]{:S(2)}) collective-permute-start(bf16[176,1536]{1,0:T(8,128)(2,1)S(1)} %copy-done.90), channel_id=1, source_target_pairs={{0,24},{4,28},{8,16},{12,20},{16,8},{20,12},{24,0},{28,4},{1,25},{... | collective-permute-start | bytes 1622024 | tf_op jit(solution)/shard_map/ppermute | solution.py:534
  69.1 170.2 %collective-permute-start.11 = (bf16[4,176,1536]{2,1,0:T(8,128)(2,1)}, bf16[4,176,1536]{2,1,0:T(8,128)(2,1)}, u32[]{:S(2)}, u32[]{:S(2)}) collective-permute-start(bf16[4,176,1536]{2,1,0:T(8,128)(2,1)} %pad_maximum_fusion.4.own_ref), channel_id=1, source_target_pairs={{0,4},{4,0},{8,12},{12,8},{16,20},{20,16},{24,28},{28,24},{1,5},{5... | collective-permute-start | bytes 6488072 | tf_op jit(solution)/shard_map/ppermute | solution.py:534
  147.0 29.7 %all-to-all-start.4 = ((f32[8,3,2,352]{3,2,1,0:T(2,128)}), f32[8,3,2,352]{3,2,1,0:T(2,128)S(1)}, u32[]{:S(2)}, u32[]{:S(2)}) async-start(f32[8,3,2,352]{3,2,1,0:T(2,128)} %bitcast.26), calls=%async_computation.4 | async-start | bytes 147456 | tf_op jit(solution)/shard_map/all_to_all | solution.py:710
  168.3 47.2 %collective-permute-start = (bf16[176,1536]{1,0:T(8,128)(2,1)}, bf16[176,1536]{1,0:T(8,128)(2,1)}, u32[]{:S(2)}, u32[]{:S(2)}) collective-permute-start(bf16[176,1536]{1,0:T(8,128)(2,1)} %bitcast.2), channel_id=1, source_target_pairs={{0,8},{4,12},{8,0},{12,4},{16,24},{20,28},{24,16},{28,20},{1,9},{5... | collective-permute-start | bytes 1622024 | tf_op jit(solution)/shard_map/ppermute | solution.py:534
  170.3 48.0 %collective-permute-start.1 = (bf16[176,1536]{1,0:T(8,128)(2,1)}, bf16[176,1536]{1,0:T(8,128)(2,1)}, u32[]{:S(2)}, u32[]{:S(2)}) collective-permute-start(bf16[176,1536]{1,0:T(8,128)(2,1)} %bitcast.2), channel_id=1, source_target_pairs={{0,16},{4,20},{8,24},{12,28},{16,0},{20,4},{24,8},{28,12},{1,17},{... | collective-permute-start | bytes 1622024 | tf_op jit(solution)/shard_map/ppermute | solution.py:534
  172.7 61.4 %collective-permute-start.2 = (bf16[176,1536]{1,0:T(8,128)(2,1)}, bf16[176,1536]{1,0:T(8,128)(2,1)}, u32[]{:S(2)}, u32[]{:S(2)}) collective-permute-start(bf16[176,1536]{1,0:T(8,128)(2,1)} %bitcast.2), channel_id=1, source_target_pairs={{0,24},{4,28},{8,16},{12,20},{16,8},{20,12},{24,0},{28,4},{1,25},{... | collective-permute-start | bytes 1622024 | tf_op jit(solution)/shard_map/ppermute | solution.py:534
  185.1 64.2 %all-to-all-start = ((bf16[4,352,768]{2,1,0:T(8,128)(2,1)}), bf16[4,352,768]{2,1,0:T(8,128)(2,1)S(1)}, u32[]{:S(2)}, u32[]{:S(2)}) async-start(bf16[4,352,768]{2,1,0:T(8,128)(2,1)} %pad_maximum_fusion.5), calls=%async_computation | async-start | bytes 4325376 | tf_op jit(solution)/shard_map/all_to_all | solution.py:497
  237.4 64.8 %collective-permute-start.5 = (bf16[4,176,1536]{2,1,0:T(8,128)(2,1)}, bf16[4,176,1536]{2,1,0:T(8,128)(2,1)}, u32[]{:S(2)}, u32[]{:S(2)}) collective-permute-start(bf16[4,176,1536]{2,1,0:T(8,128)(2,1)} %pad_maximum_fusion.3.own_ref), channel_id=1, source_target_pairs={{0,2},{1,3},{2,0},{3,1},{4,6},{5,7},{6,4},{7,5},{8,10},{9,11},{10,... | collective-permute-start | bytes 6488072 | tf_op jit(solution)/shard_map/ppermute | solution.py:534
  247.3 241.9 %collective-permute-start.13 = (bf16[1408,1536]{1,0:T(8,128)(2,1)}, bf16[1408,1536]{1,0:T(8,128)(2,1)}, u32[]{:S(2)}, u32[]{:S(2)}) collective-permute-start(bf16[1408,1536]{1,0:T(8,128)(2,1)} %bitcast.618), channel_id=1, source_target_pairs={{0,2},{1,3},{2,0},{3,1},{4,6},{5,7},{6,4},{7,5},{8,10},{9,11},{10,... | collective-permute-start | bytes 12976136 | tf_op jit(solution)/shard_map/ppermute | solution.py:534
  252.4 204.7 %all-to-all-start.10 = ((bf16[4,3,384,256]{2,3,1,0:T(8,128)(2,1)}), bf16[4,3,384,256]{2,3,1,0:T(8,128)(2,1)}, u32[]{:S(2)}, u32[]{:S(2)}) async-start(bf16[4,3,384,256]{2,3,1,0:T(8,128)(2,1)} %broadcast_in_dim.215), calls=%async_computation.10 | async-start | bytes 4718592 | tf_op jit(solution)/shard_map/all_to_all | solution.py:527
  258.4 214.5 %collective-permute-start.3 = (bf16[4,176,1536]{2,1,0:T(8,128)(2,1)}, bf16[4,176,1536]{2,1,0:T(8,128)(2,1)}, u32[]{:S(2)}, u32[]{:S(2)}) collective-permute-start(bf16[4,176,1536]{2,1,0:T(8,128)(2,1)} %pad_maximum_fusion.3.own_ref), channel_id=1, source_target_pairs={{0,4},{4,0},{8,12},{12,8},{16,20},{20,16},{24,28},{28,24},{1,5},{5... | collective-permute-start | bytes 6488072 | tf_op jit(solution)/shard_map/ppermute | solution.py:534
  302.2 178.6 %collective-permute-start.6 = (bf16[4,176,1536]{2,1,0:T(8,128)(2,1)}, bf16[4,176,1536]{2,1,0:T(8,128)(2,1)}, u32[]{:S(2)}, u32[]{:S(2)}) collective-permute-start(bf16[4,176,1536]{2,1,0:T(8,128)(2,1)} %collective-permute-done.5.own_ref), channel_id=1, source_target_pairs={{0,4},{4,0},{8,12},{12,8},{16,20},{20,16},{24,28},{28,24},{1,5},{5... | collective-permute-start | bytes 6488072 | tf_op jit(solution)/shard_map/ppermute | solution.py:534
  457.2 32.1 %all-to-all-start.1 = ((bf16[4,352,768]{2,1,0:T(8,128)(2,1)}), bf16[4,352,768]{2,1,0:T(8,128)(2,1)S(1)}, u32[]{:S(2)}, u32[]{:S(2)}) async-start(bf16[4,352,768]{2,1,0:T(8,128)(2,1)} %pad_maximum_fusion.6), calls=%async_computation.1 | async-start | bytes 4325376 | tf_op jit(solution)/shard_map/all_to_all | solution.py:497
  472.4 240.4 %collective-permute-start.12 = (bf16[1408,1536]{1,0:T(8,128)(2,1)}, bf16[1408,1536]{1,0:T(8,128)(2,1)}, u32[]{:S(2)}, u32[]{:S(2)}) collective-permute-start(bf16[1408,1536]{1,0:T(8,128)(2,1)} %bitcast.619), channel_id=1, source_target_pairs={{0,1},{1,0},{2,3},{3,2},{4,5},{5,4},{6,7},{7,6},{8,9},{9,8},{10,11... | collective-permute-start | bytes 12976136 | tf_op jit(solution)/shard_map/ppermute | solution.py:534
  480.8 259.7 %collective-permute-start.4 = (bf16[1408,1536]{1,0:T(8,128)(2,1)}, bf16[1408,1536]{1,0:T(8,128)(2,1)}, u32[]{:S(2)}, u32[]{:S(2)}) collective-permute-start(bf16[1408,1536]{1,0:T(8,128)(2,1)} %bitcast.622), channel_id=1, source_target_pairs={{0,1},{1,0},{2,3},{3,2},{4,5},{5,4},{6,7},{7,6},{8,9},{9,8},{10,11... | collective-permute-start | bytes 12976136 | tf_op jit(solution)/shard_map/ppermute | solution.py:534
  488.7 251.8 %collective-permute-start.7 = (bf16[1408,1536]{1,0:T(8,128)(2,1)}, bf16[1408,1536]{1,0:T(8,128)(2,1)}, u32[]{:S(2)}, u32[]{:S(2)}) collective-permute-start(bf16[1408,1536]{1,0:T(8,128)(2,1)} %bitcast.625), channel_id=1, source_target_pairs={{0,1},{1,0},{2,3},{3,2},{4,5},{5,4},{6,7},{7,6},{8,9},{9,8},{10,11... | collective-permute-start | bytes 12976136 | tf_op jit(solution)/shard_map/ppermute | solution.py:534
  489.2 223.6 %collective-permute-start.14 = (bf16[1408,1536]{1,0:T(8,128)(2,1)}, bf16[1408,1536]{1,0:T(8,128)(2,1)}, u32[]{:S(2)}, u32[]{:S(2)}) collective-permute-start(bf16[1408,1536]{1,0:T(8,128)(2,1)} %collective-permute-done.13.refs_2_), channel_id=1, source_target_pairs={{0,1},{1,0},{2,3},{3,2},{4,5},{5,4},{6,7},{7,6},{8,9},{9,8},{10,11... | collective-permute-start | bytes 12976136 | tf_op jit(solution)/shard_map/ppermute | solution.py:534
  569.8 36.3 %all-to-all-start.8 = ((bf16[4,3,4,88,256]{4,3,2,1,0:T(8,128)(2,1)}), bf16[4,3,4,88,256]{4,3,2,1,0:T(8,128)(2,1)S(1)}, u32[]{:S(2)}, u32[]{:S(2)}) async-start(bf16[4,3,4,88,256]{4,3,2,1,0:T(8,128)(2,1)} %pad_maximum_fusion.7), calls=%async_computation.8 | async-start | bytes 4325376 | tf_op jit(solution)/shard_map/all_to_all | solution.py:497
  635.4 105.1 %all-to-all-start.12 = ((bf16[4,352,768]{2,1,0:T(8,128)(2,1)}), bf16[4,352,768]{2,1,0:T(8,128)(2,1)S(1)}, u32[]{:S(2)}, u32[]{:S(2)}) async-start(bf16[4,352,768]{2,1,0:T(8,128)(2,1)} %pad_maximum_fusion.10), calls=%async_computation.12 | async-start | bytes 4325376 | tf_op jit(solution)/shard_map/all_to_all | solution.py:497
  639.0 967.5 %reduce-scatter.2.cloned.1.call-start = ((), (), s32[]{:S(2)}) async-start(), calls=%async_computation.26 | async-start | bytes 35684352 | tf_op jit(solution)/shard_map/reduce_scatter | solution.py:806
  842.5 76.0 %collective-permute-start.15 = (bf16[1,2,1408,352]{2,3,1,0:T(8,128)(2,1)}, bf16[1,2,1408,352]{2,3,1,0:T(8,128)(2,1)}, u32[]{:S(2)}, u32[]{:S(2)}) collective-permute-start(bf16[1,2,1408,352]{2,3,1,0:T(8,128)(2,1)} %copy.367), channel_id=1, source_target_pairs={{0,1},{1,0},{2,3},{3,2},{4,5},{5,4},{6,7},{7,6},{8,9},{9,8},{10,11... | collective-permute-start | bytes 5947400 | tf_op jit(solution)/shard_map/ppermute | solution.py:534
  865.8 47.1 %all-to-all-start.11 = ((bf16[4,352,768]{2,1,0:T(8,128)(2,1)}), bf16[4,352,768]{2,1,0:T(8,128)(2,1)}, u32[]{:S(2)}, u32[]{:S(2)}) async-start(bf16[4,352,768]{2,1,0:T(8,128)(2,1)} %bitcast.646), calls=%async_computation.11 | async-start | bytes 4325376 | tf_op jit(solution)/shard_map/all_to_all | solution.py:497
  925.3 66.5 %collective-permute-start.16 = (bf16[1,2,4,176,352]{4,3,2,1,0:T(8,128)(2,1)}, bf16[1,2,4,176,352]{4,3,2,1,0:T(8,128)(2,1)}, u32[]{:S(2)}, u32[]{:S(2)}) collective-permute-start(bf16[1,2,4,176,352]{4,3,2,1,0:T(8,128)(2,1)} %fusion.26), channel_id=1, source_target_pairs={{0,4},{4,0},{8,12},{12,8},{16,20},{20,16},{24,28},{28,24},{1,5},{5... | collective-permute-start | bytes 2973704 | tf_op jit(solution)/shard_map/ppermute | solution.py:534
  948.9 86.9 %collective-permute-start.19 = (bf16[2,2,1024,352]{2,3,1,0:T(8,128)(2,1)}, bf16[2,2,1024,352]{2,3,1,0:T(8,128)(2,1)}, u32[]{:S(2)}, u32[]{:S(2)}) collective-permute-start(bf16[2,2,1024,352]{2,3,1,0:T(8,128)(2,1)} %copy.373), channel_id=1, source_target_pairs={{0,1},{1,0},{2,3},{3,2},{4,5},{5,4},{6,7},{7,6},{8,9},{9,8},{10,11... | collective-permute-start | bytes 8650760 | tf_op jit(solution)/shard_map/ppermute | solution.py:534
  968.5 63.3 %collective-permute-start.18 = (bf16[1,2,1408,352]{2,3,1,0:T(8,128)(2,1)}, bf16[1,2,1408,352]{2,3,1,0:T(8,128)(2,1)}, u32[]{:S(2)}, u32[]{:S(2)}) collective-permute-start(bf16[1,2,1408,352]{2,3,1,0:T(8,128)(2,1)} %copy.371), channel_id=1, source_target_pairs={{0,1},{1,0},{2,3},{3,2},{4,5},{5,4},{6,7},{7,6},{8,9},{9,8},{10,11... | collective-permute-start | bytes 5947400 | tf_op jit(solution)/shard_map/ppermute | solution.py:534
  994.5 49.2 %collective-permute-start.17 = (bf16[1,4,176,352]{3,2,1,0:T(8,128)(2,1)}, bf16[1,4,176,352]{3,2,1,0:T(8,128)(2,1)}, u32[]{:S(2)}, u32[]{:S(2)}) collective-permute-start(bf16[1,4,176,352]{3,2,1,0:T(8,128)(2,1)} %get-tuple-element.404), channel_id=1, source_target_pairs={{0,2},{1,3},{2,0},{3,1},{4,6},{5,7},{6,4},{7,5},{8,10},{9,11},{10,... | collective-permute-start | bytes 1486856 | tf_op jit(solution)/shard_map/ppermute | solution.py:534
  1017.3 92.5 %collective-permute-start.27 = (bf16[1,2,1408,352]{2,3,1,0:T(8,128)(2,1)}, bf16[1,2,1408,352]{2,3,1,0:T(8,128)(2,1)}, u32[]{:S(2)}, u32[]{:S(2)}) collective-permute-start(bf16[1,2,1408,352]{2,3,1,0:T(8,128)(2,1)} %copy.382), channel_id=1, source_target_pairs={{0,1},{1,0},{2,3},{3,2},{4,5},{5,4},{6,7},{7,6},{8,9},{9,8},{10,11... | collective-permute-start | bytes 5947400 | tf_op jit(solution)/shard_map/ppermute | solution.py:534
  1056.3 61.7 %collective-permute-start.24 = (bf16[2,2,4,128,352]{3,4,2,1,0:T(8,128)(2,1)}, bf16[2,2,4,128,352]{3,4,2,1,0:T(8,128)(2,1)}, u32[]{:S(2)}, u32[]{:S(2)}) collective-permute-start(bf16[2,2,4,128,352]{3,4,2,1,0:T(8,128)(2,1)} %get-tuple-element.368), channel_id=1, source_target_pairs={{0,4},{4,0},{8,12},{12,8},{16,20},{20,16},{24,28},{28,24},{1,5},{5... | collective-permute-start | bytes 4325384 | tf_op jit(solution)/shard_map/ppermute | solution.py:534
  1058.6 59.5 %collective-permute-start.23 = (bf16[1,4,2,176,352]{4,3,2,1,0:T(8,128)(2,1)}, bf16[1,4,2,176,352]{4,3,2,1,0:T(8,128)(2,1)}, u32[]{:S(2)}, u32[]{:S(2)}) collective-permute-start(bf16[1,4,2,176,352]{4,3,2,1,0:T(8,128)(2,1)} %fusion.28), channel_id=1, source_target_pairs={{0,2},{1,3},{2,0},{3,1},{4,6},{5,7},{6,4},{7,5},{8,10},{9,11},{10,... | collective-permute-start | bytes 2973704 | tf_op jit(solution)/shard_map/ppermute | solution.py:534
  1061.0 56.8 %collective-permute-start.20 = (bf16[1,176,352]{2,1,0:T(8,128)(2,1)}, bf16[1,176,352]{2,1,0:T(8,128)(2,1)S(1)}, u32[]{:S(2)}, u32[]{:S(2)}) collective-permute-start(bf16[1,176,352]{2,1,0:T(8,128)(2,1)} %get-tuple-element.436), channel_id=1, source_target_pairs={{0,8},{4,12},{8,0},{12,4},{16,24},{20,28},{24,16},{28,20},{1,9},{5... | collective-permute-start | bytes 371720 | tf_op jit(solution)/shard_map/ppermute | solution.py:534
  1073.7 44.2 %collective-permute-start.21 = (bf16[1,176,352]{2,1,0:T(8,128)(2,1)}, bf16[1,176,352]{2,1,0:T(8,128)(2,1)}, u32[]{:S(2)}, u32[]{:S(2)}) collective-permute-start(bf16[1,176,352]{2,1,0:T(8,128)(2,1)} %get-tuple-element.435), channel_id=1, source_target_pairs={{0,16},{4,20},{8,24},{12,28},{16,0},{20,4},{24,8},{28,12},{1,17},{... | collective-permute-start | bytes 371720 | tf_op jit(solution)/shard_map/ppermute | solution.py:534
  1079.4 46.4 %all-to-all-start.15 = ((bf16[4,4,88,256]{3,2,1,0:T(8,128)(2,1)}), bf16[4,4,88,256]{3,2,1,0:T(8,128)(2,1)}, u32[]{:S(2)}, u32[]{:S(2)}) async-start(bf16[4,4,88,256]{3,2,1,0:T(8,128)(2,1)} %bitcast.119), calls=%async_computation.15 | async-start | bytes 1441792 | tf_op jit(solution)/shard_map/all_to_all | solution.py:497
  1121.1 26.4 %collective-permute-start.26 = (bf16[2,4,128,352]{2,3,1,0:T(8,128)(2,1)S(1)}, bf16[2,4,128,352]{2,3,1,0:T(8,128)(2,1)S(1)}, u32[]{:S(2)}, u32[]{:S(2)}) collective-permute-start(bf16[2,4,128,352]{2,3,1,0:T(8,128)(2,1)S(1)} %get-tuple-element.391), channel_id=1, source_target_pairs={{0,2},{1,3},{2,0},{3,1},{4,6},{5,7},{6,4},{7,5},{8,10},{9,11},{10,... | collective-permute-start | bytes 2162696 | tf_op jit(solution)/shard_map/ppermute | solution.py:534
  1124.9 22.6 %collective-permute-start.25 = (bf16[1,4,176,352]{3,2,1,0:T(8,128)(2,1)}, bf16[1,4,176,352]{3,2,1,0:T(8,128)(2,1)S(1)}, u32[]{:S(2)}, u32[]{:S(2)}) collective-permute-start(bf16[1,4,176,352]{3,2,1,0:T(8,128)(2,1)} %fusion.53), channel_id=1, source_target_pairs={{0,4},{4,0},{8,12},{12,8},{16,20},{20,16},{24,28},{28,24},{1,5},{5... | collective-permute-start | bytes 1486856 | tf_op jit(solution)/shard_map/ppermute | solution.py:534
  1150.1 31.6 %all-to-all-start.16 = ((bf16[4,3,4,88,256]{4,3,2,1,0:T(8,128)(2,1)}), bf16[4,3,4,88,256]{4,3,2,1,0:T(8,128)(2,1)}, u32[]{:S(2)}, u32[]{:S(2)}) async-start(bf16[4,3,4,88,256]{4,3,2,1,0:T(8,128)(2,1)} %attend_back.7), calls=%async_computation.16 | async-start | bytes 4325376 | tf_op jit(solution)/shard_map/all_to_all | solution.py:497
  1161.7 63.9 %collective-permute-start.34 = (bf16[1,4,2,176,352]{4,3,2,1,0:T(8,128)(2,1)}, bf16[1,4,2,176,352]{4,3,2,1,0:T(8,128)(2,1)}, u32[]{:S(2)}, u32[]{:S(2)}) collective-permute-start(bf16[1,4,2,176,352]{4,3,2,1,0:T(8,128)(2,1)} %fusion.30), channel_id=1, source_target_pairs={{0,2},{1,3},{2,0},{3,1},{4,6},{5,7},{6,4},{7,5},{8,10},{9,11},{10,... | collective-permute-start | bytes 2973704 | tf_op jit(solution)/shard_map/ppermute | solution.py:534
  1164.7 60.9 %collective-permute-start.31 = (bf16[2,128,352]{1,2,0:T(8,128)(2,1)}, bf16[2,128,352]{1,2,0:T(8,128)(2,1)}, u32[]{:S(2)}, u32[]{:S(2)}) collective-permute-start(bf16[2,128,352]{1,2,0:T(8,128)(2,1)} %get-tuple-element.415), channel_id=1, source_target_pairs={{0,8},{4,12},{8,0},{12,4},{16,24},{20,28},{24,16},{28,20},{1,9},{5... | collective-permute-start | bytes 540680 | tf_op jit(solution)/shard_map/ppermute | solution.py:534
  1167.3 58.3 %collective-permute-start.32 = (bf16[2,128,352]{1,2,0:T(8,128)(2,1)}, bf16[2,128,352]{1,2,0:T(8,128)(2,1)}, u32[]{:S(2)}, u32[]{:S(2)}) collective-permute-start(bf16[2,128,352]{1,2,0:T(8,128)(2,1)} %get-tuple-element.414), channel_id=1, source_target_pairs={{0,16},{4,20},{8,24},{12,28},{16,0},{20,4},{24,8},{28,12},{1,17},{... | collective-permute-start | bytes 540680 | tf_op jit(solution)/shard_map/ppermute | solution.py:534
  1169.5 45.7 %collective-permute-start.28 = (bf16[1,176,352]{2,1,0:T(8,128)(2,1)}, bf16[1,176,352]{2,1,0:T(8,128)(2,1)}, u32[]{:S(2)}, u32[]{:S(2)}) collective-permute-start(bf16[1,176,352]{2,1,0:T(8,128)(2,1)} %get-tuple-element.432), channel_id=1, source_target_pairs={{0,8},{4,12},{8,0},{12,4},{16,24},{20,28},{24,16},{28,20},{1,9},{5... | collective-permute-start | bytes 371720 | tf_op jit(solution)/shard_map/ppermute | solution.py:534
  1171.5 45.9 %collective-permute-start.29 = (bf16[1,176,352]{2,1,0:T(8,128)(2,1)}, bf16[1,176,352]{2,1,0:T(8,128)(2,1)}, u32[]{:S(2)}, u32[]{:S(2)}) collective-permute-start(bf16[1,176,352]{2,1,0:T(8,128)(2,1)} %get-tuple-element.431), channel_id=1, source_target_pairs={{0,16},{4,20},{8,24},{12,28},{16,0},{20,4},{24,8},{28,12},{1,17},{... | collective-permute-start | bytes 371720 | tf_op jit(solution)/shard_map/ppermute | solution.py:534
  1226.9 56.4 %collective-permute-start.35 = (bf16[1,4,176,352]{3,2,1,0:T(8,128)(2,1)S(1)}, bf16[1,4,176,352]{3,2,1,0:T(8,128)(2,1)S(1)}, u32[]{:S(2)}, u32[]{:S(2)}) collective-permute-start(bf16[1,4,176,352]{3,2,1,0:T(8,128)(2,1)S(1)} %fusion.54), channel_id=1, source_target_pairs={{0,4},{4,0},{8,12},{12,8},{16,20},{20,16},{24,28},{28,24},{1,5},{5... | collective-permute-start | bytes 1486856 | tf_op jit(solution)/shard_map/ppermute | solution.py:534
  1237.9 185.8 %collective-permute-start.40 = (bf16[1,2,1408,352]{2,3,1,0:T(8,128)(2,1)}, bf16[1,2,1408,352]{2,3,1,0:T(8,128)(2,1)}, u32[]{:S(2)}, u32[]{:S(2)}) collective-permute-start(bf16[1,2,1408,352]{2,3,1,0:T(8,128)(2,1)} %copy.390), channel_id=1, source_target_pairs={{0,1},{1,0},{2,3},{3,2},{4,5},{5,4},{6,7},{7,6},{8,9},{9,8},{10,11... | collective-permute-start | bytes 5947400 | tf_op jit(solution)/shard_map/ppermute | solution.py:534
  1252.5 197.1 %collective-permute-start.39 = (bf16[2,2,1408,352]{2,3,1,0:T(8,128)(2,1)}, bf16[2,2,1408,352]{2,3,1,0:T(8,128)(2,1)}, u32[]{:S(2)}, u32[]{:S(2)}) collective-permute-start(bf16[2,2,1408,352]{2,3,1,0:T(8,128)(2,1)} %copy.388), channel_id=1, source_target_pairs={{0,1},{1,0},{2,3},{3,2},{4,5},{5,4},{6,7},{7,6},{8,9},{9,8},{10,11... | collective-permute-start | bytes 11894792 | tf_op jit(solution)/shard_map/ppermute | solution.py:534
  1300.6 22.2 %collective-permute-start.36 = (bf16[1,176,352]{2,1,0:T(8,128)(2,1)S(1)}, bf16[1,176,352]{2,1,0:T(8,128)(2,1)}, u32[]{:S(2)}, u32[]{:S(2)}) collective-permute-start(bf16[1,176,352]{2,1,0:T(8,128)(2,1)S(1)} %get-tuple-element.428), channel_id=1, source_target_pairs={{0,8},{4,12},{8,0},{12,4},{16,24},{20,28},{24,16},{28,20},{1,9},{5... | collective-permute-start | bytes 371720 | tf_op jit(solution)/shard_map/ppermute | solution.py:534
  1332.3 74.1 %collective-permute-start.41 = (bf16[1,2,1408,352]{2,3,1,0:T(8,128)(2,1)}, bf16[1,2,1408,352]{2,3,1,0:T(8,128)(2,1)}, u32[]{:S(2)}, u32[]{:S(2)}) collective-permute-start(bf16[1,2,1408,352]{2,3,1,0:T(8,128)(2,1)} %copy.397), channel_id=1, source_target_pairs={{0,1},{1,0},{2,3},{3,2},{4,5},{5,4},{6,7},{7,6},{8,9},{9,8},{10,11... | collective-permute-start | bytes 5947400 | tf_op jit(solution)/shard_map/ppermute | solution.py:534
  1342.0 73.1 %collective-permute-start.47 = (bf16[1,2,1408,352]{2,3,1,0:T(8,128)(2,1)}, bf16[1,2,1408,352]{2,3,1,0:T(8,128)(2,1)}, u32[]{:S(2)}, u32[]{:S(2)}) collective-permute-start(bf16[1,2,1408,352]{2,3,1,0:T(8,128)(2,1)} %copy.401), channel_id=1, source_target_pairs={{0,1},{1,0},{2,3},{3,2},{4,5},{5,4},{6,7},{7,6},{8,9},{9,8},{10,11... | collective-permute-start | bytes 5947400 | tf_op jit(solution)/shard_map/ppermute | solution.py:534
  1369.7 52.8 %all-to-all-start.22 = ((f32[8,7,352]{2,1,0:T(8,128)}), f32[8,7,352]{2,1,0:T(8,128)S(1)}, u32[]{:S(2)}, u32[]{:S(2)}) async-start(f32[8,7,352]{2,1,0:T(8,128)} %broadcast_in_dim.242), calls=%async_computation.23 | async-start | bytes 196608 | tf_op jit(solution)/shard_map/all_to_all | solution.py:527
  1413.1 24.9 %collective-permute-start.42 = (bf16[1,2,4,176,352]{4,3,2,1,0:T(8,128)(2,1)}, bf16[1,2,4,176,352]{4,3,2,1,0:T(8,128)(2,1)}, u32[]{:S(2)}, u32[]{:S(2)}) collective-permute-start(bf16[1,2,4,176,352]{4,3,2,1,0:T(8,128)(2,1)} %fusion.31), channel_id=1, source_target_pairs={{0,4},{4,0},{8,12},{12,8},{16,20},{20,16},{24,28},{28,24},{1,5},{5... | collective-permute-start | bytes 2973704 | tf_op jit(solution)/shard_map/ppermute | solution.py:534
  1420.4 27.1 %collective-permute-start.48 = (bf16[1,4,2,176,352]{4,3,1,2,0:T(8,128)(2,1)}, bf16[1,4,2,176,352]{4,3,1,2,0:T(8,128)(2,1)}, u32[]{:S(2)}, u32[]{:S(2)}) collective-permute-start(bf16[1,4,2,176,352]{4,3,1,2,0:T(8,128)(2,1)} %fusion.32), channel_id=1, source_target_pairs={{0,2},{1,3},{2,0},{3,1},{4,6},{5,7},{6,4},{7,5},{8,10},{9,11},{10,... | collective-permute-start | bytes 2973704 | tf_op jit(solution)/shard_map/ppermute | solution.py:534
  1440.0 33.0 %collective-permute-start.43 = (bf16[1,4,176,352]{3,2,1,0:T(8,128)(2,1)}, bf16[1,4,176,352]{3,2,1,0:T(8,128)(2,1)}, u32[]{:S(2)}, u32[]{:S(2)}) collective-permute-start(bf16[1,4,176,352]{3,2,1,0:T(8,128)(2,1)} %fusion.56), channel_id=1, source_target_pairs={{0,2},{1,3},{2,0},{3,1},{4,6},{5,7},{6,4},{7,5},{8,10},{9,11},{10,... | collective-permute-start | bytes 1486856 | tf_op jit(solution)/shard_map/ppermute | solution.py:534
  1449.6 28.8 %collective-permute-start.49 = (bf16[1,4,176,352]{3,2,1,0:T(8,128)(2,1)}, bf16[1,4,176,352]{3,2,1,0:T(8,128)(2,1)}, u32[]{:S(2)}, u32[]{:S(2)}) collective-permute-start(bf16[1,4,176,352]{3,2,1,0:T(8,128)(2,1)} %fusion.58), channel_id=1, source_target_pairs={{0,4},{4,0},{8,12},{12,8},{16,20},{20,16},{24,28},{28,24},{1,5},{5... | collective-permute-start | bytes 1486856 | tf_op jit(solution)/shard_map/ppermute | solution.py:534
  1459.5 27.1 %collective-permute-start.58 = (bf16[1,4,2,176,352]{4,3,1,2,0:T(8,128)(2,1)}, bf16[1,4,2,176,352]{4,3,1,2,0:T(8,128)(2,1)}, u32[]{:S(2)}, u32[]{:S(2)}) collective-permute-start(bf16[1,4,2,176,352]{4,3,1,2,0:T(8,128)(2,1)} %get-tuple-element.371), channel_id=1, source_target_pairs={{0,2},{1,3},{2,0},{3,1},{4,6},{5,7},{6,4},{7,5},{8,10},{9,11},{10,... | collective-permute-start | bytes 2973704 | tf_op jit(solution)/shard_map/ppermute | solution.py:534
  1459.6 44.1 %all-to-all-start.18 = ((bf16[4,352,768]{2,1,0:T(8,128)(2,1)}), bf16[4,352,768]{2,1,0:T(8,128)(2,1)}, u32[]{:S(2)}, u32[]{:S(2)}) async-start(bf16[4,352,768]{2,1,0:T(8,128)(2,1)} %bitcast.158), calls=%async_computation.18 | async-start | bytes 4325376 | tf_op jit(solution)/shard_map/all_to_all | solution.py:497
  1471.2 81.9 %collective-permute-start.53 = (bf16[2,2,4,176,352]{4,3,2,1,0:T(8,128)(2,1)}, bf16[2,2,4,176,352]{4,3,2,1,0:T(8,128)(2,1)}, u32[]{:S(2)}, u32[]{:S(2)}) collective-permute-start(bf16[2,2,4,176,352]{4,3,2,1,0:T(8,128)(2,1)} %fusion.19), channel_id=1, source_target_pairs={{0,4},{4,0},{8,12},{12,8},{16,20},{20,16},{24,28},{28,24},{1,5},{5... | collective-permute-start | bytes 5947400 | tf_op jit(solution)/shard_map/ppermute | solution.py:534
  1488.6 43.9 %collective-permute-start.59 = (bf16[1,4,176,352]{3,2,1,0:T(8,128)(2,1)}, bf16[1,4,176,352]{3,2,1,0:T(8,128)(2,1)}, u32[]{:S(2)}, u32[]{:S(2)}) collective-permute-start(bf16[1,4,176,352]{3,2,1,0:T(8,128)(2,1)} %fusion.60), channel_id=1, source_target_pairs={{0,4},{4,0},{8,12},{12,8},{16,20},{20,16},{24,28},{28,24},{1,5},{5... | collective-permute-start | bytes 1486856 | tf_op jit(solution)/shard_map/ppermute | solution.py:534
  1491.2 17.1 %collective-permute-start.50 = (bf16[1,176,352]{2,1,0:T(8,128)(2,1)}, bf16[1,176,352]{2,1,0:T(8,128)(2,1)}, u32[]{:S(2)}, u32[]{:S(2)}) collective-permute-start(bf16[1,176,352]{2,1,0:T(8,128)(2,1)} %get-tuple-element.423), channel_id=1, source_target_pairs={{0,8},{4,12},{8,0},{12,4},{16,24},{20,28},{24,16},{28,20},{1,9},{5... | collective-permute-start | bytes 371720 | tf_op jit(solution)/shard_map/ppermute | solution.py:534
  1503.7 53.3 %all-to-all-start.17 = ((bf16[4,352,768]{2,1,0:T(8,128)(2,1)}), bf16[4,352,768]{2,1,0:T(8,128)(2,1)}, u32[]{:S(2)}, u32[]{:S(2)}) async-start(bf16[4,352,768]{2,1,0:T(8,128)(2,1)} %bitcast.155), calls=%async_computation.17 | async-start | bytes 4325376 | tf_op jit(solution)/shard_map/all_to_all | solution.py:497
  1555.7 23.1 %collective-permute-start.54 = (bf16[2,4,176,352]{3,2,1,0:T(8,128)(2,1)}, bf16[2,4,176,352]{3,2,1,0:T(8,128)(2,1)}, u32[]{:S(2)}, u32[]{:S(2)}) collective-permute-start(bf16[2,4,176,352]{3,2,1,0:T(8,128)(2,1)} %fusion.35), channel_id=1, source_target_pairs={{0,2},{1,3},{2,0},{3,1},{4,6},{5,7},{6,4},{7,5},{8,10},{9,11},{10,... | collective-permute-start | bytes 2973704 | tf_op jit(solution)/shard_map/ppermute | solution.py:534
  1584.4 21.0 %collective-permute-start.56 = (bf16[2,176,352]{2,1,0:T(8,128)(2,1)S(1)}, bf16[2,176,352]{2,1,0:T(8,128)(2,1)S(1)}, u32[]{:S(2)}, u32[]{:S(2)}) collective-permute-start(bf16[2,176,352]{2,1,0:T(8,128)(2,1)S(1)} %get-tuple-element.412), channel_id=1, source_target_pairs={{0,16},{4,20},{8,24},{12,28},{16,0},{20,4},{24,8},{28,12},{1,17},{... | collective-permute-start | bytes 743432 | tf_op jit(solution)/shard_map/ppermute | solution.py:534
  1585.8 19.6 %collective-permute-start.57 = (bf16[2,176,352]{2,1,0:T(8,128)(2,1)S(1)}, bf16[2,176,352]{2,1,0:T(8,128)(2,1)S(1)}, u32[]{:S(2)}, u32[]{:S(2)}) collective-permute-start(bf16[2,176,352]{2,1,0:T(8,128)(2,1)S(1)} %get-tuple-element.411), channel_id=1, source_target_pairs={{0,24},{4,28},{8,16},{12,20},{16,8},{20,12},{24,0},{28,4},{1,25},{... | collective-permute-start | bytes 743432 | tf_op jit(solution)/shard_map/ppermute | solution.py:534
  (203 other events, 3559.6 us)
Sparse Core Ops, SparseCore 0:
  11.7 230.0 all-gather.2
  245.5 198.0 all-gather.4
  798.9 363.1 reduce-scatter.1

commit v3 on v2

--- a/solution.py
+++ b/solution.py
@@ -43,7 +43,7 @@
     return lax.broadcasted_iota(jnp.int32, (keys, step), 0) < length_ref[0]
 
 
-def attend_kernel(masked, length_ref, q_ref, k_ref, v_ref, o_ref, l_ref):
+def attend_kernel(masked, length_ref, q_ref, k_ref, v_ref, o_ref, r_ref, l_ref):
     groups, _, heads, dim, count = q_ref.shape
     step = step_of(count)
     factor = dim ** (-0.5) * LOG2E
@@ -60,12 +60,15 @@
                 expo = jnp.where(valid_keys(length_ref, keys, step), expo, 0.0)
             both = dot(value, expo.astype(BF), ((1,), (0,)))
             total = both[dim : dim + 1]
-            o_ref[group, head, :, first : first + step] = (both[:dim] * (1.0 / total)).astype(BF)
+            mixed = both[:dim] * (1.0 / total)
+            high = mixed.astype(BF)
+            o_ref[group, head, :, first : first + step] = high
+            r_ref[group, head, :, first : first + step] = (mixed - high.astype(F32)).astype(BF)
             l_ref[head, :, place : place + step] = jnp.log2(total)
 
 
 def attend_back_kernel(
-    masked, length_ref, q_ref, k_ref, v_ref, m_ref, g_ref, l_ref, *outs
+    masked, length_ref, q_ref, k_ref, v_ref, m_ref, r_ref, g_ref, l_ref, *outs
 ):
     groups, _, heads, dim, count = q_ref.shape
     step = step_of(count)
@@ -81,9 +84,9 @@
             here = slice(first, first + step)
             query = q_ref[group, 0, head, :, here]
             grad = g_ref[group, head, :, here]
-            delta = -jnp.sum(
-                grad.astype(F32) * m_ref[group, head, :, here].astype(F32), 0, keepdims=True
-            )
+            mixed = m_ref[group, head, :, here].astype(F32)
+            mixed = mixed + r_ref[group, head, :, here].astype(F32)
+            delta = -jnp.sum(grad.astype(F32) * mixed, 0, keepdims=True)
             high = delta.astype(BF)
             rest = (delta - high.astype(F32)).astype(BF)
             more = jnp.concatenate([grad, high, rest, jnp.zeros((6, step), BF)], 0)
@@ -141,9 +144,11 @@
         + [head_block(a.shape, many, kind) for a, kind in zip((query, key, value), kinds)],
         out_specs=[
             mix_block(query.shape, many),
+            mix_block(query.shape, many),
             pl.BlockSpec((many, 1, total), lambda h: (h, 0, 0)),
         ],
         out_shape=[
+            jax.ShapeDtypeStruct((groups, heads, dim, count), BF),
             jax.ShapeDtypeStruct((groups, heads, dim, count), BF),
             jax.ShapeDtypeStruct((heads, 1, total), F32),
         ],
@@ -153,7 +158,8 @@
     )(length, query, key, value)
 
 
-def attend_back(length, query, key, value, kinds, mixed, grad, logs, masked, most, stacked):
+def attend_back(length, query, key, value, kinds, kept, grad, masked, most, stacked):
+    mixed, rest, logs = kept
     groups, _, heads, dim, count = query.shape
     many = math.gcd(heads, most)
     total = groups * count
@@ -169,18 +175,22 @@
         grid=(heads // many,),
         in_specs=[pl.BlockSpec(memory_space=pltpu.SMEM)]
         + [head_block(a.shape, many, kind) for a, kind in zip((query, key, value), kinds)]
-        + [mix_block(query.shape, many)] * 2
+        + [mix_block(query.shape, many)] * 3
         + [pl.BlockSpec((many, 1, total), lambda h: (h, 0, 0))],
         out_specs=out_specs,
         out_shape=out_shape,
         cost_estimate=costs(heads, total, keys, dim, 5),
         compiler_params=params(),
         name="attend_back",
-    )(length, query, key, value, mixed, grad, logs)
+    )(length, query, key, value, mixed, rest, grad, logs)
 
 
 def work(rows, depth, tokens, moved):
     return pl.CostEstimate(flops=2 * rows * depth * tokens, transcendentals=0, bytes_accessed=moved)
+
+
+def lanes(width):
+    return -(-width // 128) * 128
 
 
 def full(shape):
@@ -249,14 +259,82 @@
     )(*([weight] * len(kinds)), *values)
 
 
+def project_blocks(base, blocks, width, values):
+    many = len(blocks)
+    depth, broad = blocks[0].shape
+    tokens = values.shape[1]
+    tile = depth // 4
+
+    def kernel(base_ref, *refs):
+        values_ref, out_ref = refs[many:]
+
+        @pl.when(pl.program_id(0) == 0)
+        def _():
+            out_ref[...] = jnp.zeros_like(out_ref)
+
+        for index in range(many):
+            here = pl.ds(pl.multiple_of((index ^ base_ref[0]) * width, width), width)
+            out_ref[here, :] += dot(refs[index][...], values_ref[...], ((0,), (0,)))[:width]
+
+    return pl.pallas_call(
+        kernel,
+        grid_spec=pltpu.PrefetchScalarGridSpec(
+            num_scalar_prefetch=1,
+            grid=(4,),
+            in_specs=[pl.BlockSpec((tile, broad), lambda j, b: (j, 0))] * many
+            + [pl.BlockSpec((tile, tokens), lambda j, b: (j, 0))],
+            out_specs=pl.BlockSpec((many * width, tokens), lambda j, b: (0, 0)),
+        ),
+        out_shape=jax.ShapeDtypeStruct((many * width, tokens), F32),
+        cost_estimate=work(many * width, depth, tokens, 4 * depth * tokens),
+        compiler_params=params(),
+        name="project_blocks",
+    )(base, *blocks, values)
+
+
+def rebuild_blocks(base, blocks, width, values):
+    many = len(blocks)
+    depth, broad = blocks[0].shape
+    tokens = values.shape[1]
+    tile = depth // 4
+
+    def kernel(base_ref, *refs):
+        values_ref, out_ref = refs[many:]
+        total = None
+        for index in range(many):
+            here = pl.ds(pl.multiple_of((index ^ base_ref[0]) * width, width), width)
+            part = dot(refs[index][:, :width], values_ref[here, :], ((1,), (0,)))
+            total = part if total is None else total + part
+        out_ref[...] = total.astype(BF)
+
+    return pl.pallas_call(
+        kernel,
+        grid_spec=pltpu.PrefetchScalarGridSpec(
+            num_scalar_prefetch=1,
+            grid=(4,),
+            in_specs=[pl.BlockSpec((tile, broad), lambda j, b: (j, 0))] * many
+            + [pl.BlockSpec(values.shape, lambda j, b: (0, 0))],
+            out_specs=pl.BlockSpec((tile, tokens), lambda j, b: (j, 0)),
+        ),
+        out_shape=jax.ShapeDtypeStruct((depth, tokens), BF),
+        cost_estimate=work(many * width, depth, tokens, 4 * depth * tokens),
+        compiler_params=params(),
+        name="rebuild_blocks",
+    )(base, *blocks, values)
+
+
 def outer(core, left, rights, flip):
     rows, tokens = left.shape
     cols = lax.axis_size("col")
     width = rights[0].shape[0] // cols
+    broad = lanes(width)
 
     def kernel(core_ref, left_ref, *refs):
         for index in range(len(rights)):
-            part = dot(left_ref[...], refs[index][...], ((1,), (1,)))
+            right = refs[index][...]
+            if broad > width:
+                right = jnp.concatenate([right, jnp.zeros((broad - width, tokens), BF)], 0)
+            part = dot(left_ref[...], right, ((1,), (1,)))
             refs[-1][index, 0] = part.astype(BF)
 
     return pl.pallas_call(
@@ -270,10 +348,10 @@
                 for _ in rights
             ],
             out_specs=pl.BlockSpec(
-                (len(rights), 1, rows, width), lambda y, core: (0, y, 0, 0)
+                (len(rights), 1, rows, broad), lambda y, core: (0, y, 0, 0)
             ),
         ),
-        out_shape=jax.ShapeDtypeStruct((len(rights), cols // 2, rows, width), BF),
+        out_shape=jax.ShapeDtypeStruct((len(rights), cols // 2, rows, broad), BF),
         cost_estimate=work(
             rows, tokens, len(rights) * cols // 2 * width, 3 * rows * cols * width * len(rights)
         ),
@@ -546,20 +624,44 @@
     return whole.reshape(len(blocks), cols, -1, blocks[0].shape[1])
 
 
-def gather_blocks(block, across, place):
-    if not custom_mesh():
-        cols = lax.axis_size("col")
-        whole = lax.all_gather(block, DEVICES, axis=0, tiled=True).reshape(cols, -1, block.shape[1])
-        return [whole[i] for i in range(cols)]
-    stack = jnp.stack([block] + [swap(block, "row", 2 * level) for level in (1, 2, 3)], 0)
-    if across:
-        mine = assemble(place, stack, swap(stack, "row", 1))
-        other = swap(mine, "col", 2)
-    else:
-        up = swap(stack, "col", 2)
-        mine = assemble(place, stack, swap(stack, "row", 1))
-        other = assemble(place, up, swap(up, "row", 1))
-    return [mine, swap(mine, "col", 1), other, swap(other, "col", 1)]
+class Gathering:
+    last = 4
+
+    def __init__(self, block, across, place):
+        self.across = across
+        self.place = place
+        self.stage = 0
+        self.state = [block]
+        if not custom_mesh():
+            cols = lax.axis_size("col")
+            whole = lax.all_gather(block, DEVICES, axis=0, tiled=True)
+            self.state = list(whole.reshape(cols, -1, block.shape[1]))
+            self.stage = self.last
+
+    def advance(self):
+        state = self.state
+        self.stage += 1
+        if self.stage == 1:
+            self.state = state + [swap(state[0], "row", 2 * level) for level in (1, 2, 3)]
+        elif self.stage == 2:
+            stack = jnp.stack(state, 0)
+            self.state = [stack, swap(stack, "row", 1) if self.across else swap(stack, "col", 2)]
+        elif self.stage == 3 and self.across:
+            mine = assemble(self.place, *state)
+            self.state = [mine, swap(mine, "col", 1), swap(mine, "col", 2)]
+        elif self.stage == 3:
+            self.state = state + [swap(a, "row", 1) for a in state]
+        elif self.across:
+            self.state = state + [swap(state[2], "col", 1)]
+        else:
+            mine = assemble(self.place, state[0], state[2])
+            other = assemble(self.place, state[1], state[3])
+            self.state = [mine, swap(mine, "col", 1), other, swap(other, "col", 1)]
+
+    def result(self):
+        while self.stage < self.last:
+            self.advance()
+        return self.state
 
 
 def pick(values, axis, index):
@@ -571,10 +673,12 @@
 
 
 class Reduction:
+    last = 4
+
     def __init__(self, core, left, rights, across):
         self.across = across
         self.many = len(rights)
-        self.stage = 0
+        self.stage = 0 if custom_mesh() else self.last
         if not custom_mesh():
             cols = lax.axis_size("col")
             whole = jnp.stack(
@@ -583,7 +687,8 @@
             flat = whole.reshape(self.many, -1, whole.shape[3]).astype(BF)
             self.state = [lax.psum_scatter(flat, DEVICES, scatter_dimension=1, tiled=True)]
             return
-        shape = (self.many, 2, 4, 2, left.shape[0] // 8, rights[0].shape[0] // 4)
+        self.width = rights[0].shape[0] // 4
+        shape = (self.many, 2, 4, 2, left.shape[0] // 8, lanes(self.width))
         send = outer(core, left, rights, 1)
         got = swap(send, "col", 1)
         keep = outer(core, left, rights, 0)
@@ -599,8 +704,6 @@
         self.state = [here, swap(away, name, bit)]
 
     def advance(self):
-        if not custom_mesh() or self.stage == 4:
-            return
         self.stage += 1
         if self.stage <= 2:
             self.half(self.across == (self.stage == 1))
@@ -614,22 +717,26 @@
             total = self.state[0].astype(F32)
             for other in self.state[1:]:
                 total = total + other.astype(F32)
-            self.state = [total]
+            self.state = [total[..., : self.width]]
 
     def result(self):
-        while custom_mesh() and self.stage < 4:
+        while self.stage < self.last:
             self.advance()
         return self.state[0].astype(F32)
 
 
 def tick(values, running):
-    active = [r for r in running if r.stage < 4]
-    if active and custom_mesh():
+    active = [r for r in running if r.stage < r.last]
+    if active:
         values, states = lax.optimization_barrier((values, [r.state for r in active]))
-        for reduction, state in zip(active, states):
-            reduction.state = state
-            reduction.advance()
+        for beside, state in zip(active, states):
+            beside.state = state
+            beside.advance()
     return values
+
+
+def after(values, done):
+    return lax.optimization_barrier((values, done))[0]
 
 
 def shards(
@@ -681,18 +788,19 @@
     def cut(values, index):
         return values[..., starts[index] : starts[index] + pieces[index].count]
 
-    weights_one = gather_weights(
-        [skip_weight[0], skip_weight[1], self_inputs[:, 0], self_inputs[:, 1], self_inputs[:, 2]]
-    )
-    weights_two = gather_weights(
-        [self_output.T, cross_query, cross_output.T, cross_keyvalue[:, 0], cross_keyvalue[:, 1]]
-    )
-    w_expand = gather_blocks(expand_weight, True, place)
-    w_reduce = gather_blocks(reduce_weight.T, False, place)
-
-    latent = to_tokens(latents, pieces, cols)
-    skipped = to_tokens(skip_input, pieces, cols)
-    grad_out = to_tokens(out_grad.astype(BF), pieces, cols)
+    block_rows = depth // rows
+    split = (width // block_rows, block_rows, row_tokens)
+    both = jnp.stack([latents.reshape(split), skip_input.reshape(split)], 1)
+    both = to_tokens(both.reshape(2 * width, row_tokens), pieces, cols)
+
+    weights_one = gather_weights([self_inputs[:, i] for i in range(3)])
+    skip_block = jnp.concatenate([skip_weight[0], skip_weight[1]], 0)
+    skip_block = jnp.pad(skip_block, ((0, 0), (0, lanes(width) - width)))
+    w_skip = Gathering(skip_block, True, place).result()
+    expanding = Gathering(expand_weight, True, place)
+    reducing = Gathering(reduce_weight.T, False, place)
+    gathers = [expanding, reducing]
+
     places = jnp.concatenate(
         [
             lax.dynamic_slice_in_dim(positions, p.start + mine * p.count, p.count, 1)
@@ -704,7 +812,6 @@
     embed = jax.nn.silu(condition.astype(F32)).astype(BF)
     embed = shared(embed, "row").reshape(-1, width)
     embed = shared(embed, "col").transpose(1, 0, 2).reshape(-1, depth)
-    block_rows = depth // rows
     embed_rows = lax.dynamic_slice_in_dim(embed, my_row * block_rows, block_rows, 1)
     modul = einsum("sd,dke->ske", embed_rows, modulation).reshape(rows, sequences, 2, width)
     modul = jnp.sum(lax.all_to_all(modul, "row", 0, 0, tiled=True), 0)
@@ -731,12 +838,17 @@
     shifting = per_token(0)
     scaling = 1.0 + per_token(1)
 
-    joined = project(weights_one, [0, 1], [latent, skipped], [F32], True)[0]
+    joined = project_blocks(base, w_skip, width, both)
+    joined = tick(joined, gathers)
+    weights_two = gather_weights(
+        [self_output.T, cross_query, cross_output.T, cross_keyvalue[:, 0], cross_keyvalue[:, 1]]
+    )
     skip_normal, skip_inverse = normalize(joined)
     stream = skip_normal * gain_skip + bias_skip
     normal_one, inverse_one = normalize(stream)
     normed_one = (normal_one * scaling + shifting).astype(BF)
-    raw = project(weights_one, [2, 3, 4], [normed_one], [F32, F32, BF])
+    raw = project(weights_one, [0, 1, 2], [normed_one], [F32, F32, BF])
+    raw = tick(raw, gathers)
     raw = [r.reshape(heads, dim, tokens) for r in raw]
     cosine, sine = rope_tables(places, dim)
 
@@ -748,7 +860,7 @@
     rot_key, key_pull = jax.vjp(self_piece, raw[1], key_gain)
     triple = [rot_query.astype(BF), rot_key.astype(BF), raw[2]]
 
-    text = shared(jnp.pad(text_states, ((0, 0), (0, keys - texts), (0, 0))), "col")
+    text = shared(jnp.pad(after(text_states, joined), ((0, 0), (0, keys - texts), (0, 0))), "col")
     text = jnp.concatenate(
         [lax.dynamic_index_in_dim(text, p.sequence, 1, False) for p in pieces], 1
     )
@@ -768,8 +880,9 @@
     mixed_parts = []
     for index, piece in enumerate(pieces):
         whole = to_heads(triple, index)
-        mixed, logs = attend(none, whole, whole, whole, (0, 1, 2), False, 2)
-        saved_self.append((whole, mixed, logs))
+        kept = attend(none, whole, whole, whole, (0, 1, 2), False, 2)
+        saved_self.append((whole, kept))
+        mixed = tick(kept[0], gathers)
         mixed_parts.append(exchange(mixed, piece.group, cols).reshape(depth, -1))
     mixed_one = jnp.concatenate(mixed_parts, 1)
     stream = stream + rebuild(weights_two, [0], [mixed_one], F32)
@@ -789,13 +902,16 @@
         here = slice(index * keys, (index + 1) * keys)
         inputs = [cut(query_two, index), key_two[:, :, here], value_two[:, :, here]]
         inputs = [length] + [a[None, None] for a in inputs] + [(0, 0, 0)]
-        mixed, logs = attend(*inputs, True, 4)
-        saved_cross.append((inputs, mixed, logs))
-        mixed_parts.append(mixed.reshape(depth, -1))
+        kept = attend(*inputs, True, 4)
+        saved_cross.append((inputs, kept))
+        mixed_parts.append(kept[0].reshape(depth, -1))
     mixed_two = jnp.concatenate(mixed_parts, 1)
     stream = stream + rebuild(weights_two, [2], [mixed_two], F32)
     normal_three, inverse_three = normalize(stream)
     normed_three = (normal_three * gain_hidden + bias_hidden).astype(BF)
+    w_expand = expanding.result()
+    w_reduce = reducing.result()
+    grad_out = to_tokens(after(out_grad, joined).astype(BF), pieces, cols)
     act, slopes = expand(w_expand, normed_three)
     output = contract(w_reduce, act, stream, BF)
     result = to_features(output, pieces, cols).astype(F32)
@@ -819,8 +935,8 @@
     g_keys = []
     g_values = []
     for index, piece in enumerate(pieces):
-        inputs, mixed, logs = saved_cross[index]
-        grads = attend_back(*inputs, mixed, cut(g_mixed, index)[None], logs, True, 4, False)
+        inputs, kept = saved_cross[index]
+        grads = attend_back(*inputs, kept, cut(g_mixed, index)[None], True, 4, False)
         g_queries.append(grads[0][0, 0])
         g_keys.append(grads[1][0, 0])
         g_values.append(grads[2][0, 0])
@@ -847,12 +963,12 @@
     r_attn = Reduction(core, g_low, [mixed_one], False)
     g_parts = []
     for index, piece in enumerate(pieces):
-        whole, mixed, logs = saved_self[index]
+        whole, kept = saved_self[index]
         grad = exchange(
             cut(g_mixed, index).reshape(piece.group, -1, dim, piece.count), piece.group, cols
         )
         part = attend_back(
-            none, whole, whole, whole, (0, 1, 2), mixed, grad, logs, False, 2, True
+            none, whole, whole, whole, (0, 1, 2), kept, grad, False, 2, True
         )
         part = tick(part, running)
         if index == 0:
@@ -867,12 +983,13 @@
         g.reshape(depth, tokens) for g in (g_raw_q.astype(BF), g_raw_k.astype(BF), g_heads[2])
     ]
     g_triple = tick(g_triple, running)
-    g_normed = rebuild(weights_one, [2, 3, 4], g_triple, F32)
-    g_normed = tick(g_normed, running)
     r_self = [
         Reduction(core, normed_one, g_triple[:2], True),
         Reduction(core, normed_one, g_triple[2:], False),
     ]
+    g_normed = rebuild(weights_one, [0, 1, 2], g_triple, F32)
+    g_normed = tick(g_normed, running)
+    running += r_self
     crossed = g_normed * normal_one
     sums = jnp.stack(
         [
@@ -895,16 +1012,10 @@
     g_skip_bias = jnp.sum(g_stream, 1)
     g_joined = norm_back(g_stream * gain_skip, skip_normal, skip_inverse).astype(BF)
     g_joined = tick(g_joined, running)
-    r_skip = [
-        Reduction(core, latent, [g_joined], True),
-        Reduction(core, skipped, [g_joined], False),
-    ]
-    running += r_self
-    g_latent = rebuild(weights_one, [0], [g_joined], BF)
-    g_skipped = rebuild(weights_one, [1], [g_joined], BF)
-    g_latent, g_skipped = tick((g_latent, g_skipped), running)
-    g_latents = to_features(g_latent, pieces, cols).astype(F32)
-    g_skip = to_features(g_skipped, pieces, cols).astype(F32)
+    r_skip = Reduction(core, both, [g_joined], True)
+    g_both = rebuild_blocks(base, w_skip, width, g_joined)
+    g_both = to_features(g_both, pieces, cols).reshape(split[0], 2, block_rows, row_tokens)
+    g_latents, g_skip = (g_both[:, i].reshape(width, row_tokens).astype(F32) for i in range(2))
 
     g_gains = jnp.stack(
         [g_skip_gain, g_skip_bias, g_cross_gain, g_cross_bias, g_hidden_gain, g_hidden_bias], 0
@@ -920,7 +1031,7 @@
         result,
         g_latents,
         g_skip,
-        jnp.concatenate([r.result() for r in r_skip], 0),
+        r_skip.result().reshape(2, block_rows, width),
         g_modulation,
         jnp.concatenate([r.result() for r in r_self], 0).transpose(1, 0, 2),
         r_attn.result()[0].T,

time: 1630 us -> 1600 us (0.982)
  waiting for transfers between devices: 412 us -> 481 us
  local copies, waits for them, and re-layouts: 167 us -> 115 us
  blocking collectives: 71.9 us -> 21.5 us
    all_to_all x10 -> x8, waiting for transfers between devices: 22.7 us -> 172 us  [exchange(): return lax.all_to_all(values, 'col', 0, 0, tiled=True)]
    all_to_all x1 -> x0, blocking collectives: 66.2 us -> none  [shared(): lax.all_to_all(jnp.broadcast_to(values[None], (size, *values.shape)), axi...]
    all_to_all x5 -> x6, waiting for transfers between devices: 148 us -> 89.1 us  [shared(): lax.all_to_all(jnp.broadcast_to(values[None], (size, *values.shape)), axi...]
    pallas_call x8 -> x0, local copies, waits for them, and re-layouts: 36.1 us -> none  [outer(): pl.pallas_call(kernel, grid_spec=pltpu.PrefetchScalarGridSpec(num_scalar_...]
    ppermute x7 -> x0, local copies, waits for them, and re-layouts: 29.6 us -> none  [swap(): return lax.ppermute(values, axis, [(i, i ^ bit) for i in range(size)])]
    pallas_call x0 -> x2, Pallas kernels: none -> 27.3 us  [the longest x1 13.9 us: project_blocks(): pl.pallas_call(kernel, grid_spec=pltpu.PrefetchScalarGridSpec(num_scalar_...]
    pallas_call x6 -> x4, Pallas kernels: 60.9 us -> 44.9 us  [rebuild(): pl.pallas_call(kernel, grid=(4,), in_specs=[pl.BlockSpec((1, cols, tile,...]
    pallas_call x6 -> x5, Pallas kernels: 60.3 us -> 49.2 us  [project(): pl.pallas_call(kernel, grid=(cols,), in_specs=[pl.BlockSpec((1, 1, depth,...]
  transfers between devices with their start and end apart: 87 -> 85, of which waited for: 30 -> 25; matrix products, arithmetic and copies ran while one was open for 26% -> 24% of each run, Pallas kernels for 26% -> 27%
where the time goes in v3:
time: 1600 us; the launch traced here: 1590 us
  waiting for transfers between devices  481 us (30%)
  Pallas kernels  481 us (30%)
  other arithmetic  279 us (17%)
  starting transfers between devices  192 us (12%)
  local copies, waits for them, and re-layouts  115 us (7%)
  blocking collectives  21.5 us (1%)
  between operations  17 us (1%)
    ppermute x64, waiting for transfers between devices, swap(): return lax.ppermute(values, axis, [(i, i ^ bit) for i in range(size)])  216 us
    all_to_all x8, waiting for transfers between devices, exchange(): return lax.all_to_all(values, 'col', 0, 0, tiled=True)  172 us
    ppermute x64, starting transfers between devices, swap(): return lax.ppermute(values, axis, [(i, i ^ bit) for i in range(size)])  99.5 us
    pallas_call x14, Pallas kernels, outer(): pl.pallas_call(kernel, grid_spec=pltpu.PrefetchScalarGridSpec(num_scalar_...  91.6 us
    all_to_all x6, waiting for transfers between devices, shared(): lax.all_to_all(jnp.broadcast_to(values[None], (size, *values.shape)), axi...  89.1 us
    convert_element_type x30, other arithmetic, add(): return (left.astype(F32) + right.astype(F32)).astype(BF)  66.4 us
    pallas_call x4, Pallas kernels, attend_back(): pl.pallas_call(partial(attend_back_kernel, masked), grid=(heads // many,)...  65.2 us
    pallas_call x5, Pallas kernels, project(): pl.pallas_call(kernel, grid=(cols,), in_specs=[pl.BlockSpec((1, 1, depth,...  49.2 us
  transfers between devices with their start and end apart: 85, of which 25 were waited for; matrix products, arithmetic and copies ran while one was open for 24% of the time, Pallas kernels for 27%

profile of v3, /device:TPU:0, one launch (start us, length us, event | category | flops | bytes accessed | tf_op | source)
XLA Modules:
  0.0 1588.9 jit_solution(9237835768343757130)
XLA Ops:
  20.1 11.0 collective-permute-done
  31.1 12.5 collective-permute-done.1
  45.9 11.7 all-to-all-start.1
  57.7 21.7 %all-to-all-done.1 = bf16[8,3,352]{2,1,0:T(4,128)(2,1)S(1)} async-done(((bf16[8,3,352]{2,1,0:T(4,128)(2,1)}), bf16[8,3,352]{2,1,0:T(4,128)(2,1)S(1)}, u32[]{:S(2)}, u32[]{:S(2)}) %all-to-all-start.1) | async-done | bytes 16928 | tf_op jit(solution)/shard_map/all_to_all | solution.py:605
  92.7 6.6 assemble.4
  101.1 14.0 all-to-all-start.3
  120.2 6.1 reshape.1470
  140.5 27.4 %all-to-all-done.4 = f32[4,12,352]{2,1,0:T(8,128)S(1)} async-done(((f32[4,12,352]{2,1,0:T(8,128)}), f32[4,12,352]{2,1,0:T(8,128)S(1)}, u32[]{:S(2)}, u32[]{:S(2)}) %all-to-all-start.4) | async-done | bytes 67616 | tf_op jit(solution)/shard_map/all_to_all | solution.py:605
  177.4 55.2 %all-to-all-done = bf16[4,704,768]{2,1,0:T(8,128)(2,1)} async-done(((bf16[4,704,768]{2,1,0:T(8,128)(2,1)}), bf16[4,704,768]{2,1,0:T(8,128)(2,1)}, u32[]{:S(2)}, u32[]{:S(2)}) %all-to-all-start) | async-done | bytes 4325408 | tf_op jit(solution)/shard_map/all_to_all | solution.py:575
  232.6 13.9 project_blocks.1
  268.5 28.3 %collective-permute-done.10 = bf16[176,1536]{1,0:T(8,128)(2,1)S(1)} collective-permute-done((bf16[176,1536]{1,0:T(8,128)(2,1)S(1)}, bf16[176,1536]{1,0:T(8,128)(2,1)S(1)}, u32[]{:S(2)}, u32[]{:S(2)}) %collective-permute-start.10) | collective-permute-done | bytes 540704 | tf_op jit(solution)/shard_map/ppermute | solution.py:612
  298.7 15.2 project.5
  314.0 8.0 collective-permute-done.12
  322.0 18.1 %collective-permute-done.7 = bf16[176,1536]{1,0:T(8,128)(2,1)S(1)} collective-permute-done((bf16[176,1536]{1,0:T(8,128)(2,1)S(1)}, bf16[176,1536]{1,0:T(8,128)(2,1)S(1)}, u32[]{:S(2)}, u32[]{:S(2)}) %collective-permute-start.7) | collective-permute-done | bytes 540704 | tf_op jit(solution)/shard_map/ppermute | solution.py:612
  340.1 36.5 %collective-permute-done.8 = bf16[176,1536]{1,0:T(8,128)(2,1)} collective-permute-done((bf16[176,1536]{1,0:T(8,128)(2,1)S(1)}, bf16[176,1536]{1,0:T(8,128)(2,1)}, u32[]{:S(2)}, u32[]{:S(2)}) %collective-permute-start.8) | collective-permute-done | bytes 540704 | tf_op jit(solution)/shard_map/ppermute | solution.py:612
  411.7 8.3 all_to_all.105.q_ref.k_ref.v_ref
  420.0 16.7 %attend.5 = (bf16[2,8,88,512]{3,2,1,0:T(8,128)(2,1)}, bf16[2,8,88,512]{3,2,1,0:T(8,128)(2,1)}, f32[8,1,1024]{2,1,0:T(1,128)}) custom-call(s32[1]{0:T(128)} %constant.365.clone.1.length_ref, bf16[2,3,8,88,512]{4,3,2,1,0:T(8,128)(2,1)} %all_to_all.105.q_ref.k_ref.v_ref, bf16[2,3,8,88,512]{4,3,2,1,0:T(8,128)(2,1)} %all_to_all.105.q_ref.k_ref.v_ref, ...), custom_call_target="tpu_custom_call" | custom-call | flops 8589934592 | bytes 5767168 | tf_op jit(solution)/shard_map/attend/pallas_call | solution.py:140
  436.8 7.9 assemble.5
  456.6 107.4 %all-to-all-done.5.q_ref.k_ref.v_ref = bf16[4,3,4,88,256]{4,3,2,1,0:T(8,128)(2,1)} async-done(((bf16[4,3,4,88,256]{4,3,2,1,0:T(8,128)(2,1)}), bf16[4,3,4,88,256]{4,3,2,1,0:T(8,128)(2,1)}, u32[]{:S(2)}, u32[]{:S(2)}) %all-to-all-start.5) | async-done | bytes 2162720 | tf_op jit(solution)/shard_map/all_to_all | solution.py:575
  576.7 9.4 attend.4
  586.1 11.7 all-to-all-done.9
  597.7 7.5 all_to_all.106
  615.3 7.9 assemble.7
  623.2 7.9 assemble.6
  638.1 10.8 project.7
  654.2 8.5 rebuild.4
  670.9 7.9 project.6
  691.3 7.4 attend.7
  698.7 11.7 attend.6
  713.3 8.7 rebuild.5
  729.0 27.5 %expand.1 = (bf16[4,1536,768]{2,1,0:T(8,128)(2,1)}, bf16[4,1536,768]{2,1,0:T(8,128)(2,1)}) custom-call(bf16[1408,1536]{1,0:T(8,128)(2,1)} %bitcast.542, bf16[1408,1536]{1,0:T(8,128)(2,1)} %collective-permute-done.15.refs_1_, bf16[1408,1536]{1,0:T(8,128)(2,1)} %collective-permute-done.16.refs_2_, bf16[1408,1536]{1,0:T(8,128)(2,1)} %collective-permute-done.21.refs_3_, ...), custom_call_target="tpu_custom_call" | custom-call | flops 13287555072 | bytes 25952256 | tf_op jit(solution)/shard_map/expand/pallas_call | solution.py:382
  757.8 20.5 %expand_back.1.refs_4_.inner_ref = bf16[4,1536,768]{2,1,0:T(8,128)(2,1)} custom-call(bf16[1408,1536]{1,0:T(8,128)(2,1)} %bitcast.549, bf16[1408,1536]{1,0:T(8,128)(2,1)} %collective-permute-done.19.refs_1_, bf16[1408,1536]{1,0:T(8,128)(2,1)} %bitcast.546, bf16[1408,1536]{1,0:T(8,128)(2,1)} %collective-permute-done.20.refs_3_, bf16[1408,768]{1,0:T(8,128)(2,1)} %bitcast.488, ...), custom_call_target="tpu_custom_call" | custom-call | flops 13287555072 | bytes 25952256 | tf_op jit(solution)/shard_map/expand_back/pallas_call | solution.py:406
  778.3 36.5 %hidden_outer.1 = bf16[2,4,1408,1536]{3,2,1,0:T(8,128)(2,1)} custom-call(s32[1]{0:T(128)} %bitcast.6.base_ref, bf16[1408,768]{1,0:T(8,128)(2,1)} %bitcast.489, bf16[4,1536,768]{2,1,0:T(8,128)(2,1)} %get-tuple-element.172.refs_4_.act_ref, bf16[1408,768]{1,0:T(8,128)(2,1)} %add_convert_fusion.6.refs_4_.normed_ref, ...), custom_call_target="tpu_custom_call" | custom-call | flops 26575110144 | bytes 43253760 | tf_op jit(solution)/shard_map/hidden_outer/pallas_call | solution.py:466
  814.8 20.8 %contract.3 = f32[1408,768]{1,0:T(8,128)} custom-call(bf16[1408,1536]{1,0:T(8,128)(2,1)} %bitcast.543, bf16[1408,1536]{1,0:T(8,128)(2,1)} %collective-permute-done.15.refs_1_, bf16[1408,1536]{1,0:T(8,128)(2,1)} %collective-permute-done.16.refs_2_, bf16[1408,1536]{1,0:T(8,128)(2,1)} %collective-permute-done.21.refs_3_, ...), custom_call_target="tpu_custom_call" | custom-call | flops 13287555072 | bytes 25952256 | tf_op jit(solution)/shard_map/contract/pallas_call | solution.py:435
  835.6 6.5 multiply_reduce_fusion.2
  854.5 22.5 %contract.2 = bf16[1408,768]{1,0:T(8,128)(2,1)} custom-call(bf16[1408,1536]{1,0:T(8,128)(2,1)} %bitcast.550, bf16[1408,1536]{1,0:T(8,128)(2,1)} %collective-permute-done.19.refs_1_, bf16[1408,1536]{1,0:T(8,128)(2,1)} %bitcast.547, bf16[1408,1536]{1,0:T(8,128)(2,1)} %collective-permute-done.20.refs_3_, ...), custom_call_target="tpu_custom_call" | custom-call | flops 13287555072 | bytes 25952256 | tf_op jit(solution)/shard_map/contract/pallas_call | solution.py:435
  880.8 7.7 project.8
  900.0 9.4 attend_back.5
  909.4 15.3 attend_back.4
  940.1 7.1 outer.19
  970.5 6.5 outer.18
  977.0 8.7 rebuild.6
  998.1 6.5 fusion.91
  1017.0 7.6 project.9
  1038.1 12.4 collective-permute-start.27
  1060.4 25.9 %attend_back.6 = bf16[2,3,8,88,512]{4,3,2,1,0:T(8,128)(2,1)} custom-call(s32[1]{0:T(128)} %constant.365.clone.1.length_ref, bf16[2,3,8,88,512]{4,3,2,1,0:T(8,128)(2,1)} %all_to_all.105.q_ref.k_ref.v_ref, bf16[2,3,8,88,512]{4,3,2,1,0:T(8,128)(2,1)} %all_to_all.105.q_ref.k_ref.v_ref, bf16[2,3,8,88,512]{4,3,2,1,0:T(8,128)(2,1)} %all_to_all.105.q_ref.k_ref.v_ref, ...), custom_call_target="tpu_custom_call" | custom-call | flops 21474836480 | bytes 14417920 | tf_op jit(solution)/shard_map/attend_back/pallas_call | solution.py:173
  1093.6 14.5 attend_back.7
  1116.4 6.1 all-to-all-start.13
  1128.7 6.9 collective-permute-done.33
  1167.4 9.7 all-to-all-done.15
  1187.7 7.5 multiply_reduce_fusion.7
  1237.9 8.1 outer.23
  1246.1 19.1 %rebuild.7 = f32[1408,768]{1,0:T(8,128)} custom-call(bf16[3,4,1408,352]{3,2,1,0:T(8,128)(2,1)} %bitcast.426, bf16[3,4,1408,352]{3,2,1,0:T(8,128)(2,1)} %bitcast.427, bf16[3,4,1408,352]{3,2,1,0:T(8,128)(2,1)} %bitcast.428, bf16[1408,768]{1,0:T(8,128)(2,1)} %bitcast.512, bf16[1408,768]{1,0:T(8,128)(2,1)} %bitcast.509, ...), custom_call_target="tpu_custom_call" | custom-call | flops 9135194112 | bytes 8650752 | tf_op jit(solution)/shard_map/rebuild/pallas_call | solution.py:246
  1267.9 8.2 outer.22
  1281.9 10.9 multiply_reduce_fusion.4
  1331.0 8.7 outer.27
  1357.0 13.4 rebuild_blocks.1
  1370.4 24.6 %all-to-all-done.20 = f32[8,7,352]{2,1,0:T(8,128)S(1)} async-done(((f32[8,7,352]{2,1,0:T(8,128)}), f32[8,7,352]{2,1,0:T(8,128)S(1)}, u32[]{:S(2)}, u32[]{:S(2)}) %all-to-all-start.20) | async-done | bytes 78880 | tf_op jit(solution)/shard_map/all_to_all | solution.py:605
  1417.0 8.6 outer.26
  1434.1 7.7 collective-permute-done.62
  1441.9 30.9 %collective-permute-done.55 = bf16[2,4,176,384]{3,2,0,1:T(8,128)(2,1)} collective-permute-done((bf16[2,4,176,384]{3,2,0,1:T(8,128)(2,1)}, bf16[2,4,176,384]{3,2,0,1:T(8,128)(2,1)}, u32[]{:S(2)}, u32[]{:S(2)}) %collective-permute-start.55) | collective-permute-done | bytes 1081376 | tf_op jit(solution)/shard_map/ppermute | solution.py:612
  1510.2 17.0 %collective-permute-done.49 = bf16[1,2,4,352,384]{4,3,2,1,0:T(8,128)(2,1)} collective-permute-done((bf16[1,2,4,352,384]{4,3,2,1,0:T(8,128)(2,1)}, bf16[1,2,4,352,384]{4,3,2,1,0:T(8,128)(2,1)}, u32[]{:S(2)}, u32[]{:S(2)}) %collective-permute-start.49) | collective-permute-done | bytes 2162720 | tf_op jit(solution)/shard_map/ppermute | solution.py:612
  1534.8 18.5 %collective-permute-done.50 = bf16[1,4,352,384]{3,2,1,0:T(8,128)(2,1)S(1)} collective-permute-done((bf16[1,4,352,384]{3,2,1,0:T(8,128)(2,1)S(1)}, bf16[1,4,352,384]{3,2,1,0:T(8,128)(2,1)S(1)}, u32[]{:S(2)}, u32[]{:S(2)}) %collective-permute-start.50) | collective-permute-done | bytes 1081376 | tf_op jit(solution)/shard_map/ppermute | solution.py:612
  1565.2 13.1 collective-permute-done.52
  (787 shorter events, 571.2 us)
Async XLA Ops:
  7.2 291.5 %all-gather.3.cloned.1.call-start = ((), (), s32[]{:S(2)}) async-start(), calls=%async_computation.22 | async-start | bytes 13381632 | tf_op jit(solution)/shard_map/all_gather | solution.py:623
  9.3 628.8 %all-gather.5.cloned.1.call-start = ((), (), s32[]{:S(2)}) async-start(), calls=%async_computation.23 | async-start | bytes 22302720 | tf_op jit(solution)/shard_map/all_gather | solution.py:623
  43.7 49.0 %collective-permute-start.3 = (bf16[4,352,384]{2,1,0:T(8,128)(2,1)S(1)}, bf16[4,352,384]{2,1,0:T(8,128)(2,1)}, u32[]{:S(2)}, u32[]{:S(2)}) collective-permute-start(bf16[4,352,384]{2,1,0:T(8,128)(2,1)S(1)} %pad_maximum_fusion.16.own_ref), channel_id=1, source_target_pairs={{0,4},{4,0},{8,12},{12,8},{16,20},{20,16},{24,28},{28,24},{1,5},{5... | collective-permute-start | bytes 3244040 | tf_op jit(solution)/shard_map/ppermute | solution.py:612
  45.9 33.4 %all-to-all-start.1 = ((bf16[8,3,352]{2,1,0:T(4,128)(2,1)}), bf16[8,3,352]{2,1,0:T(4,128)(2,1)S(1)}, u32[]{:S(2)}, u32[]{:S(2)}) async-start(bf16[8,3,352]{2,1,0:T(4,128)(2,1)} %broadcast_in_dim.202), calls=%async_computation.1 | async-start | bytes 49152 | tf_op jit(solution)/shard_map/all_to_all | solution.py:605
  99.3 74.3 %collective-permute-start.5 = (bf16[2816,384]{1,0:T(8,128)(2,1)}, bf16[2816,384]{1,0:T(8,128)(2,1)}, u32[]{:S(2)}, u32[]{:S(2)}) collective-permute-start(bf16[2816,384]{1,0:T(8,128)(2,1)} %bitcast.566), channel_id=1, source_target_pairs={{0,2},{1,3},{2,0},{3,1},{4,6},{5,7},{6,4},{7,5},{8,10},{9,11},{10,... | collective-permute-start | bytes 6488072 | tf_op jit(solution)/shard_map/ppermute | solution.py:612
  101.1 29.3 %all-to-all-start.3 = ((f32[8,3,2,352]{3,2,1,0:T(2,128)}), f32[8,3,2,352]{3,2,1,0:T(2,128)S(1)}, u32[]{:S(2)}, u32[]{:S(2)}) async-start(f32[8,3,2,352]{3,2,1,0:T(2,128)} %bitcast.23), calls=%async_computation.3 | async-start | bytes 147456 | tf_op jit(solution)/shard_map/all_to_all | solution.py:817
  131.2 36.7 %all-to-all-start.4 = ((f32[4,12,352]{2,1,0:T(8,128)}), f32[4,12,352]{2,1,0:T(8,128)S(1)}, u32[]{:S(2)}, u32[]{:S(2)}) async-start(f32[4,12,352]{2,1,0:T(8,128)} %broadcast_in_dim.205), calls=%async_computation.4 | async-start | bytes 196608 | tf_op jit(solution)/shard_map/all_to_all | solution.py:605
  167.9 64.7 %all-to-all-start = ((bf16[4,704,768]{2,1,0:T(8,128)(2,1)}), bf16[4,704,768]{2,1,0:T(8,128)(2,1)}, u32[]{:S(2)}, u32[]{:S(2)}) async-start(bf16[4,704,768]{2,1,0:T(8,128)(2,1)} %copy.266), calls=%async_computation | async-start | bytes 8650752 | tf_op jit(solution)/shard_map/all_to_all | solution.py:575
  173.0 59.6 %collective-permute-start.4 = (bf16[2816,384]{1,0:T(8,128)(2,1)S(1)}, bf16[2816,384]{1,0:T(8,128)(2,1)}, u32[]{:S(2)}, u32[]{:S(2)}) collective-permute-start(bf16[2816,384]{1,0:T(8,128)(2,1)S(1)} %bitcast.569), channel_id=1, source_target_pairs={{0,1},{1,0},{2,3},{3,2},{4,5},{5,4},{6,7},{7,6},{8,9},{9,8},{10,11... | collective-permute-start | bytes 6488072 | tf_op jit(solution)/shard_map/ppermute | solution.py:612
  173.6 59.0 %collective-permute-start.6 = (bf16[2816,384]{1,0:T(8,128)(2,1)}, bf16[2816,384]{1,0:T(8,128)(2,1)}, u32[]{:S(2)}, u32[]{:S(2)}) collective-permute-start(bf16[2816,384]{1,0:T(8,128)(2,1)} %collective-permute-done.5.refs_2_), channel_id=1, source_target_pairs={{0,1},{1,0},{2,3},{3,2},{4,5},{5,4},{6,7},{7,6},{8,9},{9,8},{10,11... | collective-permute-start | bytes 6488072 | tf_op jit(solution)/shard_map/ppermute | solution.py:612
  246.6 50.2 %collective-permute-start.10 = (bf16[176,1536]{1,0:T(8,128)(2,1)S(1)}, bf16[176,1536]{1,0:T(8,128)(2,1)S(1)}, u32[]{:S(2)}, u32[]{:S(2)}) collective-permute-start(bf16[176,1536]{1,0:T(8,128)(2,1)S(1)} %bitcast.577), channel_id=1, source_target_pairs={{0,8},{4,12},{8,0},{12,4},{16,24},{20,28},{24,16},{28,20},{1,9},{5... | collective-permute-start | bytes 1622024 | tf_op jit(solution)/shard_map/ppermute | solution.py:612
  248.3 65.7 %collective-permute-start.11 = (bf16[176,1536]{1,0:T(8,128)(2,1)S(1)}, bf16[176,1536]{1,0:T(8,128)(2,1)S(1)}, u32[]{:S(2)}, u32[]{:S(2)}) collective-permute-start(bf16[176,1536]{1,0:T(8,128)(2,1)S(1)} %bitcast.578), channel_id=1, source_target_pairs={{0,16},{4,20},{8,24},{12,28},{16,0},{20,4},{24,8},{28,12},{1,17},{... | collective-permute-start | bytes 1622024 | tf_op jit(solution)/shard_map/ppermute | solution.py:612
  250.1 71.9 %collective-permute-start.12 = (bf16[176,1536]{1,0:T(8,128)(2,1)S(1)}, bf16[176,1536]{1,0:T(8,128)(2,1)}, u32[]{:S(2)}, u32[]{:S(2)}) collective-permute-start(bf16[176,1536]{1,0:T(8,128)(2,1)S(1)} %bitcast.579), channel_id=1, source_target_pairs={{0,24},{4,28},{8,16},{12,20},{16,8},{20,12},{24,0},{28,4},{1,25},{... | collective-permute-start | bytes 1622024 | tf_op jit(solution)/shard_map/ppermute | solution.py:612
  251.0 89.1 %collective-permute-start.7 = (bf16[176,1536]{1,0:T(8,128)(2,1)S(1)}, bf16[176,1536]{1,0:T(8,128)(2,1)S(1)}, u32[]{:S(2)}, u32[]{:S(2)}) collective-permute-start(bf16[176,1536]{1,0:T(8,128)(2,1)S(1)} %copy-done.77), channel_id=1, source_target_pairs={{0,8},{4,12},{8,0},{12,4},{16,24},{20,28},{24,16},{28,20},{1,9},{5... | collective-permute-start | bytes 1622024 | tf_op jit(solution)/shard_map/ppermute | solution.py:612
  251.8 124.8 %collective-permute-start.8 = (bf16[176,1536]{1,0:T(8,128)(2,1)S(1)}, bf16[176,1536]{1,0:T(8,128)(2,1)}, u32[]{:S(2)}, u32[]{:S(2)}) collective-permute-start(bf16[176,1536]{1,0:T(8,128)(2,1)S(1)} %copy-done.77), channel_id=1, source_target_pairs={{0,16},{4,20},{8,24},{12,28},{16,0},{20,4},{24,8},{28,12},{1,17},{... | collective-permute-start | bytes 1622024 | tf_op jit(solution)/shard_map/ppermute | solution.py:612
  296.8 79.8 %collective-permute-start.9 = (bf16[176,1536]{1,0:T(8,128)(2,1)S(1)}, bf16[176,1536]{1,0:T(8,128)(2,1)}, u32[]{:S(2)}, u32[]{:S(2)}) collective-permute-start(bf16[176,1536]{1,0:T(8,128)(2,1)S(1)} %copy-done.77), channel_id=1, source_target_pairs={{0,24},{4,28},{8,16},{12,20},{16,8},{20,12},{24,0},{28,4},{1,25},{... | collective-permute-start | bytes 1622024 | tf_op jit(solution)/shard_map/ppermute | solution.py:612
  379.3 57.4 %collective-permute-start.14 = (bf16[4,176,1536]{2,1,0:T(8,128)(2,1)}, bf16[4,176,1536]{2,1,0:T(8,128)(2,1)}, u32[]{:S(2)}, u32[]{:S(2)}) collective-permute-start(bf16[4,176,1536]{2,1,0:T(8,128)(2,1)} %pad_maximum_fusion.7.own_ref), channel_id=1, source_target_pairs={{0,2},{1,3},{2,0},{3,1},{4,6},{5,7},{6,4},{7,5},{8,10},{9,11},{10,... | collective-permute-start | bytes 6488072 | tf_op jit(solution)/shard_map/ppermute | solution.py:612
  383.4 53.4 %collective-permute-start.13 = (bf16[4,176,1536]{2,1,0:T(8,128)(2,1)}, bf16[4,176,1536]{2,1,0:T(8,128)(2,1)}, u32[]{:S(2)}, u32[]{:S(2)}) collective-permute-start(bf16[4,176,1536]{2,1,0:T(8,128)(2,1)} %pad_maximum_fusion.6.own_ref), channel_id=1, source_target_pairs={{0,4},{4,0},{8,12},{12,8},{16,20},{20,16},{24,28},{28,24},{1,5},{5... | collective-permute-start | bytes 6488072 | tf_op jit(solution)/shard_map/ppermute | solution.py:612
  444.7 141.4 %collective-permute-start.15 = (bf16[1408,1536]{1,0:T(8,128)(2,1)}, bf16[1408,1536]{1,0:T(8,128)(2,1)}, u32[]{:S(2)}, u32[]{:S(2)}) collective-permute-start(bf16[1408,1536]{1,0:T(8,128)(2,1)} %bitcast.540), channel_id=1, source_target_pairs={{0,1},{1,0},{2,3},{3,2},{4,5},{5,4},{6,7},{7,6},{8,9},{9,8},{10,11... | collective-permute-start | bytes 12976136 | tf_op jit(solution)/shard_map/ppermute | solution.py:612
  444.8 141.3 %collective-permute-start.16 = (bf16[1408,1536]{1,0:T(8,128)(2,1)}, bf16[1408,1536]{1,0:T(8,128)(2,1)}, u32[]{:S(2)}, u32[]{:S(2)}) collective-permute-start(bf16[1408,1536]{1,0:T(8,128)(2,1)} %bitcast.541), channel_id=1, source_target_pairs={{0,2},{1,3},{2,0},{3,1},{4,6},{5,7},{6,4},{7,5},{8,10},{9,11},{10,... | collective-permute-start | bytes 12976136 | tf_op jit(solution)/shard_map/ppermute | solution.py:612
  449.6 114.4 %all-to-all-start.5 = ((bf16[4,3,4,88,256]{4,3,2,1,0:T(8,128)(2,1)}), bf16[4,3,4,88,256]{4,3,2,1,0:T(8,128)(2,1)}, u32[]{:S(2)}, u32[]{:S(2)}) async-start(bf16[4,3,4,88,256]{4,3,2,1,0:T(8,128)(2,1)} %pad_maximum_fusion.5), calls=%async_computation.5 | async-start | bytes 4325376 | tf_op jit(solution)/shard_map/all_to_all | solution.py:575
  454.0 132.0 %collective-permute-start.17 = (bf16[4,176,1536]{2,1,0:T(8,128)(2,1)}, bf16[4,176,1536]{2,1,0:T(8,128)(2,1)}, u32[]{:S(2)}, u32[]{:S(2)}) collective-permute-start(bf16[4,176,1536]{2,1,0:T(8,128)(2,1)} %pad_maximum_fusion.7.own_ref), channel_id=1, source_target_pairs={{0,4},{4,0},{8,12},{12,8},{16,20},{20,16},{24,28},{28,24},{1,5},{5... | collective-permute-start | bytes 6488072 | tf_op jit(solution)/shard_map/ppermute | solution.py:612
  454.7 131.4 %collective-permute-start.18 = (bf16[4,176,1536]{2,1,0:T(8,128)(2,1)}, bf16[4,176,1536]{2,1,0:T(8,128)(2,1)}, u32[]{:S(2)}, u32[]{:S(2)}) collective-permute-start(bf16[4,176,1536]{2,1,0:T(8,128)(2,1)} %collective-permute-done.14.own_ref), channel_id=1, source_target_pairs={{0,4},{4,0},{8,12},{12,8},{16,20},{20,16},{24,28},{28,24},{1,5},{5... | collective-permute-start | bytes 6488072 | tf_op jit(solution)/shard_map/ppermute | solution.py:612
  565.6 32.1 %all-to-all-start.9 = ((bf16[4,3,384,256]{2,3,1,0:T(8,128)(2,1)}), bf16[4,3,384,256]{2,3,1,0:T(8,128)(2,1)S(1)}, u32[]{:S(2)}, u32[]{:S(2)}) async-start(bf16[4,3,384,256]{2,3,1,0:T(8,128)(2,1)} %broadcast_in_dim.216), calls=%async_computation.9 | async-start | bytes 4718592 | tf_op jit(solution)/shard_map/all_to_all | solution.py:605
  605.2 26.4 %all-to-all-start.8 = ((bf16[4,4,88,256]{3,2,1,0:T(8,128)(2,1)}), bf16[4,4,88,256]{3,2,1,0:T(8,128)(2,1)S(1)}, u32[]{:S(2)}, u32[]{:S(2)}) async-start(bf16[4,4,88,256]{3,2,1,0:T(8,128)(2,1)} %get-tuple-element.166.m_ref), calls=%async_computation.8 | async-start | bytes 1441792 | tf_op jit(solution)/shard_map/all_to_all | solution.py:575
  614.8 114.1 %collective-permute-start.21 = (bf16[1408,1536]{1,0:T(8,128)(2,1)}, bf16[1408,1536]{1,0:T(8,128)(2,1)}, u32[]{:S(2)}, u32[]{:S(2)}) collective-permute-start(bf16[1408,1536]{1,0:T(8,128)(2,1)} %collective-permute-done.16.refs_2_), channel_id=1, source_target_pairs={{0,1},{1,0},{2,3},{3,2},{4,5},{5,4},{6,7},{7,6},{8,9},{9,8},{10,11... | collective-permute-start | bytes 12976136 | tf_op jit(solution)/shard_map/ppermute | solution.py:612
  623.2 133.3 %collective-permute-start.20 = (bf16[1408,1536]{1,0:T(8,128)(2,1)}, bf16[1408,1536]{1,0:T(8,128)(2,1)}, u32[]{:S(2)}, u32[]{:S(2)}) collective-permute-start(bf16[1408,1536]{1,0:T(8,128)(2,1)} %bitcast.545), channel_id=1, source_target_pairs={{0,1},{1,0},{2,3},{3,2},{4,5},{5,4},{6,7},{7,6},{8,9},{9,8},{10,11... | collective-permute-start | bytes 12976136 | tf_op jit(solution)/shard_map/ppermute | solution.py:612
  631.1 125.4 %collective-permute-start.19 = (bf16[1408,1536]{1,0:T(8,128)(2,1)}, bf16[1408,1536]{1,0:T(8,128)(2,1)}, u32[]{:S(2)}, u32[]{:S(2)}) collective-permute-start(bf16[1408,1536]{1,0:T(8,128)(2,1)} %bitcast.548), channel_id=1, source_target_pairs={{0,1},{1,0},{2,3},{3,2},{4,5},{5,4},{6,7},{7,6},{8,9},{9,8},{10,11... | collective-permute-start | bytes 12976136 | tf_op jit(solution)/shard_map/ppermute | solution.py:612
  631.6 124.9 %all-to-all-start.11 = ((bf16[4,352,768]{2,1,0:T(8,128)(2,1)}), bf16[4,352,768]{2,1,0:T(8,128)(2,1)S(1)}, u32[]{:S(2)}, u32[]{:S(2)}) async-start(bf16[4,352,768]{2,1,0:T(8,128)(2,1)} %pad_maximum_fusion.10), calls=%async_computation.11 | async-start | bytes 4325376 | tf_op jit(solution)/shard_map/all_to_all | solution.py:575
  635.2 943.9 %reduce-scatter.2.cloned.1.call-start = ((), (), s32[]{:S(2)}) async-start(), calls=%async_computation.24 | async-start | bytes 35684352 | tf_op jit(solution)/shard_map/reduce_scatter | solution.py:922
  853.9 74.0 %collective-permute-start.22 = (bf16[1,2,1408,384]{3,2,1,0:T(8,128)(2,1)}, bf16[1,2,1408,384]{3,2,1,0:T(8,128)(2,1)}, u32[]{:S(2)}, u32[]{:S(2)}) collective-permute-start(bf16[1,2,1408,384]{3,2,1,0:T(8,128)(2,1)} %outer.15), channel_id=1, source_target_pairs={{0,1},{1,0},{2,3},{3,2},{4,5},{5,4},{6,7},{7,6},{8,9},{9,8},{10,11... | collective-permute-start | bytes 6488072 | tf_op jit(solution)/shard_map/ppermute | solution.py:612
  876.9 47.8 %all-to-all-start.10 = ((bf16[4,352,768]{2,1,0:T(8,128)(2,1)}), bf16[4,352,768]{2,1,0:T(8,128)(2,1)S(1)}, u32[]{:S(2)}, u32[]{:S(2)}) async-start(bf16[4,352,768]{2,1,0:T(8,128)(2,1)} %bitcast.570), calls=%async_computation.10 | async-start | bytes 4325376 | tf_op jit(solution)/shard_map/all_to_all | solution.py:575
  931.3 56.1 %collective-permute-start.23 = (bf16[1,2,4,176,384]{4,3,2,1,0:T(8,128)(2,1)}, bf16[1,2,4,176,384]{4,3,2,1,0:T(8,128)(2,1)}, u32[]{:S(2)}, u32[]{:S(2)}) collective-permute-start(bf16[1,2,4,176,384]{4,3,2,1,0:T(8,128)(2,1)} %fusion.31), channel_id=1, source_target_pairs={{0,4},{4,0},{8,12},{12,8},{16,20},{20,16},{24,28},{28,24},{1,5},{5... | collective-permute-start | bytes 3244040 | tf_op jit(solution)/shard_map/ppermute | solution.py:612
  947.3 77.3 %collective-permute-start.26 = (bf16[2,2,1024,384]{3,2,1,0:T(8,128)(2,1)}, bf16[2,2,1024,384]{3,2,1,0:T(8,128)(2,1)}, u32[]{:S(2)}, u32[]{:S(2)}) collective-permute-start(bf16[2,2,1024,384]{3,2,1,0:T(8,128)(2,1)} %outer.19), channel_id=1, source_target_pairs={{0,1},{1,0},{2,3},{3,2},{4,5},{5,4},{6,7},{7,6},{8,9},{9,8},{10,11... | collective-permute-start | bytes 9437192 | tf_op jit(solution)/shard_map/ppermute | solution.py:612
  964.3 60.3 %collective-permute-start.25 = (bf16[1,2,1408,384]{3,2,1,0:T(8,128)(2,1)}, bf16[1,2,1408,384]{3,2,1,0:T(8,128)(2,1)}, u32[]{:S(2)}, u32[]{:S(2)}) collective-permute-start(bf16[1,2,1408,384]{3,2,1,0:T(8,128)(2,1)} %outer.17), channel_id=1, source_target_pairs={{0,1},{1,0},{2,3},{3,2},{4,5},{5,4},{6,7},{7,6},{8,9},{9,8},{10,11... | collective-permute-start | bytes 6488072 | tf_op jit(solution)/shard_map/ppermute | solution.py:612
  996.0 28.6 %collective-permute-start.24 = (bf16[1,4,176,384]{3,2,1,0:T(8,128)(2,1)}, bf16[1,4,176,384]{3,2,1,0:T(8,128)(2,1)}, u32[]{:S(2)}, u32[]{:S(2)}) collective-permute-start(bf16[1,4,176,384]{3,2,1,0:T(8,128)(2,1)} %get-tuple-element.460), channel_id=1, source_target_pairs={{0,2},{1,3},{2,0},{3,1},{4,6},{5,7},{6,4},{7,5},{8,10},{9,11},{10,... | collective-permute-start | bytes 1622024 | tf_op jit(solution)/shard_map/ppermute | solution.py:612
  1010.2 118.4 %collective-permute-start.34 = (bf16[1,2,1408,384]{3,2,1,0:T(8,128)(2,1)}, bf16[1,2,1408,384]{3,2,1,0:T(8,128)(2,1)}, u32[]{:S(2)}, u32[]{:S(2)}) collective-permute-start(bf16[1,2,1408,384]{3,2,1,0:T(8,128)(2,1)} %outer.21), channel_id=1, source_target_pairs={{0,1},{1,0},{2,3},{3,2},{4,5},{5,4},{6,7},{7,6},{8,9},{9,8},{10,11... | collective-permute-start | bytes 6488072 | tf_op jit(solution)/shard_map/ppermute | solution.py:612
  1032.1 76.1 %collective-permute-start.31 = (bf16[2,2,4,128,384]{4,3,2,1,0:T(8,128)(2,1)}, bf16[2,2,4,128,384]{4,3,2,1,0:T(8,128)(2,1)}, u32[]{:S(2)}, u32[]{:S(2)}) collective-permute-start(bf16[2,2,4,128,384]{4,3,2,1,0:T(8,128)(2,1)} %fusion.28), channel_id=1, source_target_pairs={{0,4},{4,0},{8,12},{12,8},{16,20},{20,16},{24,28},{28,24},{1,5},{5... | collective-permute-start | bytes 4718600 | tf_op jit(solution)/shard_map/ppermute | solution.py:612
  1035.7 72.4 %collective-permute-start.30 = (bf16[1,4,2,176,384]{4,3,2,1,0:T(8,128)(2,1)}, bf16[1,4,2,176,384]{4,3,2,1,0:T(8,128)(2,1)}, u32[]{:S(2)}, u32[]{:S(2)}) collective-permute-start(bf16[1,4,2,176,384]{4,3,2,1,0:T(8,128)(2,1)} %fusion.33), channel_id=1, source_target_pairs={{0,2},{1,3},{2,0},{3,1},{4,6},{5,7},{6,4},{7,5},{8,10},{9,11},{10,... | collective-permute-start | bytes 3244040 | tf_op jit(solution)/shard_map/ppermute | solution.py:612
  1038.1 53.0 %collective-permute-start.27 = (bf16[1,176,384]{2,1,0:T(8,128)(2,1)}, bf16[1,176,384]{2,1,0:T(8,128)(2,1)S(1)}, u32[]{:S(2)}, u32[]{:S(2)}) collective-permute-start(bf16[1,176,384]{2,1,0:T(8,128)(2,1)} %get-tuple-element.492), channel_id=1, source_target_pairs={{0,8},{4,12},{8,0},{12,4},{16,24},{20,28},{24,16},{28,20},{1,9},{5... | collective-permute-start | bytes 405512 | tf_op jit(solution)/shard_map/ppermute | solution.py:612
  1050.5 57.6 %collective-permute-start.28 = (bf16[1,176,384]{2,1,0:T(8,128)(2,1)}, bf16[1,176,384]{2,1,0:T(8,128)(2,1)S(1)}, u32[]{:S(2)}, u32[]{:S(2)}) collective-permute-start(bf16[1,176,384]{2,1,0:T(8,128)(2,1)} %get-tuple-element.491), channel_id=1, source_target_pairs={{0,16},{4,20},{8,24},{12,28},{16,0},{20,4},{24,8},{28,12},{1,17},{... | collective-permute-start | bytes 405512 | tf_op jit(solution)/shard_map/ppermute | solution.py:612
  1056.2 37.4 %all-to-all-start.14 = ((bf16[4,4,88,256]{3,2,1,0:T(8,128)(2,1)}), bf16[4,4,88,256]{3,2,1,0:T(8,128)(2,1)}, u32[]{:S(2)}, u32[]{:S(2)}) async-start(bf16[4,4,88,256]{3,2,1,0:T(8,128)(2,1)} %bitcast.554), calls=%async_computation.14 | async-start | bytes 1441792 | tf_op jit(solution)/shard_map/all_to_all | solution.py:575
  1135.6 41.5 %all-to-all-start.15 = ((bf16[4,3,4,88,256]{4,3,2,1,0:T(8,128)(2,1)}), bf16[4,3,4,88,256]{4,3,2,1,0:T(8,128)(2,1)}, u32[]{:S(2)}, u32[]{:S(2)}) async-start(bf16[4,3,4,88,256]{4,3,2,1,0:T(8,128)(2,1)} %attend_back.7), calls=%async_computation.15 | async-start | bytes 4325376 | tf_op jit(solution)/shard_map/all_to_all | solution.py:575
  1146.6 72.8 %collective-permute-start.41 = (bf16[1,4,2,176,384]{4,3,2,1,0:T(8,128)(2,1)}, bf16[1,4,2,176,384]{4,3,2,1,0:T(8,128)(2,1)}, u32[]{:S(2)}, u32[]{:S(2)}) collective-permute-start(bf16[1,4,2,176,384]{4,3,2,1,0:T(8,128)(2,1)} %fusion.35), channel_id=1, source_target_pairs={{0,2},{1,3},{2,0},{3,1},{4,6},{5,7},{6,4},{7,5},{8,10},{9,11},{10,... | collective-permute-start | bytes 3244040 | tf_op jit(solution)/shard_map/ppermute | solution.py:612
  1152.9 66.4 %collective-permute-start.38 = (bf16[2,128,384]{1,2,0:T(8,128)(2,1)}, bf16[2,128,384]{1,2,0:T(8,128)(2,1)}, u32[]{:S(2)}, u32[]{:S(2)}) collective-permute-start(bf16[2,128,384]{1,2,0:T(8,128)(2,1)} %bitcast.594), channel_id=1, source_target_pairs={{0,8},{4,12},{8,0},{12,4},{16,24},{20,28},{24,16},{28,20},{1,9},{5... | collective-permute-start | bytes 589832 | tf_op jit(solution)/shard_map/ppermute | solution.py:612
  1158.5 60.9 %collective-permute-start.39 = (bf16[2,128,384]{1,2,0:T(8,128)(2,1)}, bf16[2,128,384]{1,2,0:T(8,128)(2,1)}, u32[]{:S(2)}, u32[]{:S(2)}) collective-permute-start(bf16[2,128,384]{1,2,0:T(8,128)(2,1)} %bitcast.595), channel_id=1, source_target_pairs={{0,16},{4,20},{8,24},{12,28},{16,0},{20,4},{24,8},{28,12},{1,17},{... | collective-permute-start | bytes 589832 | tf_op jit(solution)/shard_map/ppermute | solution.py:612
  1161.6 48.7 %collective-permute-start.35 = (bf16[1,176,384]{2,1,0:T(8,128)(2,1)}, bf16[1,176,384]{2,1,0:T(8,128)(2,1)}, u32[]{:S(2)}, u32[]{:S(2)}) collective-permute-start(bf16[1,176,384]{2,1,0:T(8,128)(2,1)} %get-tuple-element.488), channel_id=1, source_target_pairs={{0,8},{4,12},{8,0},{12,4},{16,24},{20,28},{24,16},{28,20},{1,9},{5... | collective-permute-start | bytes 405512 | tf_op jit(solution)/shard_map/ppermute | solution.py:612
  1163.5 47.1 %collective-permute-start.36 = (bf16[1,176,384]{2,1,0:T(8,128)(2,1)}, bf16[1,176,384]{2,1,0:T(8,128)(2,1)}, u32[]{:S(2)}, u32[]{:S(2)}) collective-permute-start(bf16[1,176,384]{2,1,0:T(8,128)(2,1)} %get-tuple-element.487), channel_id=1, source_target_pairs={{0,16},{4,20},{8,24},{12,28},{16,0},{20,4},{24,8},{28,12},{1,17},{... | collective-permute-start | bytes 405512 | tf_op jit(solution)/shard_map/ppermute | solution.py:612
  1221.5 54.6 %collective-permute-start.42 = (bf16[1,4,176,384]{3,2,1,0:T(8,128)(2,1)}, bf16[1,4,176,384]{3,2,1,0:T(8,128)(2,1)}, u32[]{:S(2)}, u32[]{:S(2)}) collective-permute-start(bf16[1,4,176,384]{3,2,1,0:T(8,128)(2,1)} %fusion.53), channel_id=1, source_target_pairs={{0,4},{4,0},{8,12},{12,8},{16,20},{20,16},{24,28},{28,24},{1,5},{5... | collective-permute-start | bytes 1622024 | tf_op jit(solution)/shard_map/ppermute | solution.py:612
  1265.3 65.7 %collective-permute-start.47 = (bf16[1,2,1408,384]{3,2,1,0:T(8,128)(2,1)S(1)}, bf16[1,2,1408,384]{3,2,1,0:T(8,128)(2,1)}, u32[]{:S(2)}, u32[]{:S(2)}) collective-permute-start(bf16[1,2,1408,384]{3,2,1,0:T(8,128)(2,1)S(1)} %copy-done.47), channel_id=1, source_target_pairs={{0,1},{1,0},{2,3},{3,2},{4,5},{5,4},{6,7},{7,6},{8,9},{9,8},{10,11... | collective-permute-start | bytes 6488072 | tf_op jit(solution)/shard_map/ppermute | solution.py:612
  1265.3 65.7 %collective-permute-start.46 = (bf16[2,2,1408,384]{3,2,1,0:T(8,128)(2,1)}, bf16[2,2,1408,384]{3,2,1,0:T(8,128)(2,1)}, u32[]{:S(2)}, u32[]{:S(2)}) collective-permute-start(bf16[2,2,1408,384]{3,2,1,0:T(8,128)(2,1)} %outer.23), channel_id=1, source_target_pairs={{0,1},{1,0},{2,3},{3,2},{4,5},{5,4},{6,7},{7,6},{8,9},{9,8},{10,11... | collective-permute-start | bytes 12976136 | tf_op jit(solution)/shard_map/ppermute | solution.py:612
  1294.9 36.0 %collective-permute-start.43 = (bf16[1,176,384]{2,1,0:T(8,128)(2,1)}, bf16[1,176,384]{2,1,0:T(8,128)(2,1)S(1)}, u32[]{:S(2)}, u32[]{:S(2)}) collective-permute-start(bf16[1,176,384]{2,1,0:T(8,128)(2,1)} %get-tuple-element.484), channel_id=1, source_target_pairs={{0,8},{4,12},{8,0},{12,4},{16,24},{20,28},{24,16},{28,20},{1,9},{5... | collective-permute-start | bytes 405512 | tf_op jit(solution)/shard_map/ppermute | solution.py:612
  1299.0 32.0 %collective-permute-start.44 = (bf16[1,176,384]{2,1,0:T(8,128)(2,1)}, bf16[1,176,384]{2,1,0:T(8,128)(2,1)S(1)}, u32[]{:S(2)}, u32[]{:S(2)}) collective-permute-start(bf16[1,176,384]{2,1,0:T(8,128)(2,1)} %get-tuple-element.483), channel_id=1, source_target_pairs={{0,16},{4,20},{8,24},{12,28},{16,0},{20,4},{24,8},{28,12},{1,17},{... | collective-permute-start | bytes 405512 | tf_op jit(solution)/shard_map/ppermute | solution.py:612
  1300.2 30.8 %collective-permute-start.45 = (bf16[1,176,384]{2,1,0:T(8,128)(2,1)S(1)}, bf16[1,176,384]{2,1,0:T(8,128)(2,1)S(1)}, u32[]{:S(2)}, u32[]{:S(2)}) collective-permute-start(bf16[1,176,384]{2,1,0:T(8,128)(2,1)S(1)} %get-tuple-element.482), channel_id=1, source_target_pairs={{0,24},{4,28},{8,16},{12,20},{16,8},{20,12},{24,0},{28,4},{1,25},{... | collective-permute-start | bytes 405512 | tf_op jit(solution)/shard_map/ppermute | solution.py:612
  1339.8 135.0 %collective-permute-start.48 = (bf16[1,2,2816,384]{3,2,1,0:T(8,128)(2,1)}, bf16[1,2,2816,384]{3,2,1,0:T(8,128)(2,1)}, u32[]{:S(2)}, u32[]{:S(2)}) collective-permute-start(bf16[1,2,2816,384]{3,2,1,0:T(8,128)(2,1)} %outer.27), channel_id=1, source_target_pairs={{0,1},{1,0},{2,3},{3,2},{4,5},{5,4},{6,7},{7,6},{8,9},{9,8},{10,11... | collective-permute-start | bytes 12976136 | tf_op jit(solution)/shard_map/ppermute | solution.py:612
  1344.3 68.2 %collective-permute-start.54 = (bf16[2,2,4,176,384]{4,3,0,2,1:T(8,128)(2,1)}, bf16[2,2,4,176,384]{4,3,0,2,1:T(8,128)(2,1)}, u32[]{:S(2)}, u32[]{:S(2)}) collective-permute-start(bf16[2,2,4,176,384]{4,3,0,2,1:T(8,128)(2,1)} %fusion.20), channel_id=1, source_target_pairs={{0,4},{4,0},{8,12},{12,8},{16,20},{20,16},{24,28},{28,24},{1,5},{5... | collective-permute-start | bytes 6488072 | tf_op jit(solution)/shard_map/ppermute | solution.py:612
  1349.4 57.6 %collective-permute-start.59 = (bf16[1,4,2,176,384]{4,3,1,2,0:T(8,128)(2,1)}, bf16[1,4,2,176,384]{4,3,1,2,0:T(8,128)(2,1)S(1)}, u32[]{:S(2)}, u32[]{:S(2)}) collective-permute-start(bf16[1,4,2,176,384]{4,3,1,2,0:T(8,128)(2,1)} %get-tuple-element.431), channel_id=1, source_target_pairs={{0,2},{1,3},{2,0},{3,1},{4,6},{5,7},{6,4},{7,5},{8,10},{9,11},{10,... | collective-permute-start | bytes 3244040 | tf_op jit(solution)/shard_map/ppermute | solution.py:612
  1352.0 43.0 %all-to-all-start.20 = ((f32[8,7,352]{2,1,0:T(8,128)}), f32[8,7,352]{2,1,0:T(8,128)S(1)}, u32[]{:S(2)}, u32[]{:S(2)}) async-start(f32[8,7,352]{2,1,0:T(8,128)} %broadcast_in_dim.242), calls=%async_computation.21 | async-start | bytes 196608 | tf_op jit(solution)/shard_map/all_to_all | solution.py:605
  1395.0 90.4 %all-to-all-start.16 = ((bf16[4,704,768]{2,1,0:T(8,128)(2,1)}), bf16[4,704,768]{2,1,0:T(8,128)(2,1)}, u32[]{:S(2)}, u32[]{:S(2)}) async-start(bf16[4,704,768]{2,1,0:T(8,128)(2,1)} %bitcast.544), calls=%async_computation.16 | async-start | bytes 8650752 | tf_op jit(solution)/shard_map/all_to_all | solution.py:575
  1415.0 57.8 %collective-permute-start.55 = (bf16[2,4,176,384]{3,2,0,1:T(8,128)(2,1)}, bf16[2,4,176,384]{3,2,0,1:T(8,128)(2,1)}, u32[]{:S(2)}, u32[]{:S(2)}) collective-permute-start(bf16[2,4,176,384]{3,2,0,1:T(8,128)(2,1)} %fusion.40), channel_id=1, source_target_pairs={{0,2},{1,3},{2,0},{3,1},{4,6},{5,7},{6,4},{7,5},{8,10},{9,11},{10,... | collective-permute-start | bytes 3244040 | tf_op jit(solution)/shard_map/ppermute | solution.py:612
  1478.3 48.9 %collective-permute-start.49 = (bf16[1,2,4,352,384]{4,3,2,1,0:T(8,128)(2,1)}, bf16[1,2,4,352,384]{4,3,2,1,0:T(8,128)(2,1)}, u32[]{:S(2)}, u32[]{:S(2)}) collective-permute-start(bf16[1,2,4,352,384]{4,3,2,1,0:T(8,128)(2,1)} %fusion.19), channel_id=1, source_target_pairs={{0,4},{4,0},{8,12},{12,8},{16,20},{20,16},{24,28},{28,24},{1,5},{5... | collective-permute-start | bytes 6488072 | tf_op jit(solution)/shard_map/ppermute | solution.py:612
  1481.0 78.3 %collective-permute-start.56 = (bf16[2,176,384]{2,1,0:T(8,128)(2,1)}, bf16[2,176,384]{2,1,0:T(8,128)(2,1)}, u32[]{:S(2)}, u32[]{:S(2)}) collective-permute-start(bf16[2,176,384]{2,1,0:T(8,128)(2,1)} %get-tuple-element.466), channel_id=1, source_target_pairs={{0,8},{4,12},{8,0},{12,4},{16,24},{20,28},{24,16},{28,20},{1,9},{5... | collective-permute-start | bytes 811016 | tf_op jit(solution)/shard_map/ppermute | solution.py:612
  1482.4 77.1 %collective-permute-start.57 = (bf16[2,176,384]{2,1,0:T(8,128)(2,1)}, bf16[2,176,384]{2,1,0:T(8,128)(2,1)}, u32[]{:S(2)}, u32[]{:S(2)}) collective-permute-start(bf16[2,176,384]{2,1,0:T(8,128)(2,1)} %get-tuple-element.468), channel_id=1, source_target_pairs={{0,16},{4,20},{8,24},{12,28},{16,0},{20,4},{24,8},{28,12},{1,17},{... | collective-permute-start | bytes 811016 | tf_op jit(solution)/shard_map/ppermute | solution.py:612
  1484.8 74.8 %collective-permute-start.58 = (bf16[2,176,384]{2,1,0:T(8,128)(2,1)}, bf16[2,176,384]{2,1,0:T(8,128)(2,1)}, u32[]{:S(2)}, u32[]{:S(2)}) collective-permute-start(bf16[2,176,384]{2,1,0:T(8,128)(2,1)} %get-tuple-element.467), channel_id=1, source_target_pairs={{0,24},{4,28},{8,16},{12,20},{16,8},{20,12},{24,0},{28,4},{1,25},{... | collective-permute-start | bytes 811016 | tf_op jit(solution)/shard_map/ppermute | solution.py:612
  (191 other events, 5147.2 us)
Sparse Core Ops, SparseCore 0:
  11.7 139.1 all-gather.2
  154.6 188.0 all-gather.4
  815.0 388.0 reduce-scatter.1

commit v4 on v3

--- a/solution.py
+++ b/solution.py
@@ -186,7 +186,11 @@
 
 
 def work(rows, depth, tokens, moved):
-    return pl.CostEstimate(flops=2 * rows * depth * tokens, transcendentals=0, bytes_accessed=moved)
+    return pl.CostEstimate(
+        flops=2 * rows * depth * tokens,
+        transcendentals=0,
+        bytes_accessed=moved,
+    )
 
 
 def lanes(width):
@@ -360,18 +364,16 @@
     )(core, left, *rights)
 
 
-def expand(blocks, values):
-    many = len(blocks)
-    depth, hidden = blocks[0].shape
+def expand(weight, kind, values):
+    _, many, depth, hidden = weight.shape
     tokens = values.shape[1]
     tile = 384 if hidden % 384 == 0 else hidden
     slope = 0.79788456
     cubic = 0.044715
 
-    def kernel(*refs):
-        values_ref, act_ref, slope_ref = refs[many:]
+    def kernel(weight_ref, values_ref, act_ref, slope_ref):
         for index in range(many):
-            inner = dot(refs[index][...], values_ref[...], ((0,), (0,)))
+            inner = dot(weight_ref[0, index], values_ref[...], ((0,), (0,)))
             square = inner * inner
             bent = jnp.tanh(inner * (slope + slope * cubic * square))
             half = 0.5 + 0.5 * bent
@@ -382,52 +384,54 @@
     return pl.pallas_call(
         kernel,
         grid=(hidden // tile,),
-        in_specs=[pl.BlockSpec((depth, tile), lambda j: (0, j))] * many + [full(values.shape)],
+        in_specs=[
+            pl.BlockSpec((1, many, depth, tile), lambda j: (kind, 0, 0, j)),
+            full(values.shape),
+        ],
         out_specs=[pl.BlockSpec((many, tile, tokens), lambda j: (0, j, 0))] * 2,
         out_shape=[jax.ShapeDtypeStruct((many, hidden, tokens), BF)] * 2,
         cost_estimate=work(many * hidden, depth, tokens, 3 * many * hidden * depth),
         compiler_params=params(),
         name="expand",
-    )(*blocks, values)
-
-
-def expand_back(blocks, values, slopes):
-    many = len(blocks)
-    depth, hidden = blocks[0].shape
+    )(weight, values)
+
+
+def expand_back(weight, kind, values, slopes):
+    _, many, depth, hidden = weight.shape
     tokens = values.shape[1]
     tile = 384 if hidden % 384 == 0 else hidden
 
-    def kernel(*refs):
-        values_ref, slope_ref, out_ref = refs[many:]
+    def kernel(weight_ref, values_ref, slope_ref, out_ref):
         for index in range(many):
-            part = dot(refs[index][...], values_ref[...], ((0,), (0,)))
+            part = dot(weight_ref[0, index], values_ref[...], ((0,), (0,)))
             out_ref[index] = (part * slope_ref[index].astype(F32)).astype(BF)
 
     return pl.pallas_call(
         kernel,
         grid=(hidden // tile,),
-        in_specs=[pl.BlockSpec((depth, tile), lambda j: (0, j))] * many
-        + [full(values.shape), pl.BlockSpec((many, tile, tokens), lambda j: (0, j, 0))],
+        in_specs=[
+            pl.BlockSpec((1, many, depth, tile), lambda j: (kind, 0, 0, j)),
+            full(values.shape),
+            pl.BlockSpec((many, tile, tokens), lambda j: (0, j, 0)),
+        ],
         out_specs=pl.BlockSpec((many, tile, tokens), lambda j: (0, j, 0)),
         out_shape=jax.ShapeDtypeStruct((many, hidden, tokens), BF),
         cost_estimate=work(many * hidden, depth, tokens, 3 * many * hidden * depth),
         compiler_params=params(),
         name="expand_back",
-    )(*blocks, values, slopes)
-
-
-def contract(blocks, values, added, dtype):
-    many = len(blocks)
-    depth, hidden = blocks[0].shape
+    )(weight, values, slopes)
+
+
+def contract(weight, kind, values, added, dtype):
+    _, many, depth, hidden = weight.shape
     tokens = values.shape[2]
     tile = depth // 4
     extra = [] if added is None else [added]
 
-    def kernel(*refs):
-        values_ref = refs[many]
-        total = refs[many + 1][...] if extra else None
+    def kernel(weight_ref, values_ref, *refs):
+        total = refs[0][...] if extra else None
         for index in range(many):
-            part = dot(refs[index][...], values_ref[index], ((1,), (0,)))
+            part = dot(weight_ref[0, index], values_ref[index], ((1,), (0,)))
             total = part if total is None else total + part
         refs[-1][...] = total.astype(dtype)
 
@@ -435,24 +439,26 @@
     return pl.pallas_call(
         kernel,
         grid=(4,),
-        in_specs=[pl.BlockSpec((tile, hidden), lambda j: (j, 0))] * many
-        + [full(values.shape)]
+        in_specs=[
+            pl.BlockSpec((1, many, tile, hidden), lambda j: (kind, 0, j, 0)),
+            full(values.shape),
+        ]
         + [line] * len(extra),
         out_specs=line,
         out_shape=jax.ShapeDtypeStruct((depth, tokens), dtype),
         cost_estimate=work(depth, many * hidden, tokens, 3 * many * hidden * depth),
         compiler_params=params(),
         name="contract",
-    )(*blocks, values, *extra)
-
-
-def hidden_outer(base, grad_out, act, normed, grad_inner):
+    )(weight, values, *extra)
+
+
+def hidden_outer(grad_out, act, normed, grad_inner):
     many, hidden, tokens = act.shape
     depth = grad_out.shape[0]
     parts = 2 if hidden % 256 == 0 else 1
     tile = hidden // parts
 
-    def kernel(base_ref, out_ref, act_ref, normed_ref, inner_ref, grad_ref):
+    def kernel(out_ref, act_ref, normed_ref, inner_ref, grad_ref):
         kind = pl.program_id(0)
 
         @pl.when(kind == 0)
@@ -462,53 +468,59 @@
         @pl.when(kind == 1)
         def _():
             grad_ref[0, 0] = dot(out_ref[...], act_ref[0], ((1,), (1,))).astype(BF)
+
+    return pl.pallas_call(
+        kernel,
+        grid=(2, many, parts),
+        in_specs=[
+            pl.BlockSpec((depth, tokens), lambda s, p, j: (0, 0)),
+            pl.BlockSpec((1, tile, tokens), lambda s, p, j: (s * p, s * j, 0)),
+            pl.BlockSpec((depth, tokens), lambda s, p, j: (0, 0)),
+            pl.BlockSpec(
+                (1, tile, tokens),
+                lambda s, p, j: (p + s * (many - 1 - p), j + s * (parts - 1 - j), 0),
+            ),
+        ],
+        out_specs=pl.BlockSpec((1, 1, depth, tile), lambda s, p, j: (s, p, 0, j)),
+        out_shape=jax.ShapeDtypeStruct((2, many, depth, hidden), BF),
+        cost_estimate=work(2 * depth, tokens, many * hidden, 5 * many * depth * hidden),
+        compiler_params=params(),
+        name="hidden_outer",
+    )(grad_out, act, normed, grad_inner)
+
+
+def assemble(place, own, got, middle=None):
+    rows, width = own.shape[-2:]
+
+    def kernel(place_ref, own_ref, got_ref, out_ref):
+        @pl.when(pl.program_id(0) == place_ref[1])
+        def _():
+            out_ref[0, 0] = own_ref[...].reshape(rows, width)
+
+        @pl.when(pl.program_id(0) != place_ref[1])
+        def _():
+            out_ref[0, 0] = got_ref[...].reshape(rows, width)
+
+    def spec(ours):
+        def index(x, z, place):
+            phase = place[1] if ours else 1 - place[1]
+            inside = (x == phase).astype(jnp.int32)
+            level = (inside * z + (1 - inside) * 3 * (1 - phase)) ^ place[0]
+            return (level, 0, 0) if middle is None else (level, middle, 0, 0)
+
+        shape = (1, rows, width) if middle is None else (1, 1, rows, width)
+        return pl.BlockSpec(shape, index)
 
     return pl.pallas_call(
         kernel,
         grid_spec=pltpu.PrefetchScalarGridSpec(
             num_scalar_prefetch=1,
-            grid=(2, many, parts),
-            in_specs=[
-                pl.BlockSpec((depth, tokens), lambda s, p, j, b: (0, 0)),
-                pl.BlockSpec((1, tile, tokens), lambda s, p, j, b: (s * p, s * j, 0)),
-                pl.BlockSpec((depth, tokens), lambda s, p, j, b: (0, 0)),
-                pl.BlockSpec(
-                    (1, tile, tokens),
-                    lambda s, p, j, b: (p + s * (many - 1 - p), j + s * (parts - 1 - j), 0),
-                ),
-            ],
-            out_specs=pl.BlockSpec((1, 1, depth, tile), lambda s, p, j, b: (s, p ^ b[0], 0, j)),
-        ),
-        out_shape=jax.ShapeDtypeStruct((2, many, depth, hidden), BF),
-        cost_estimate=work(2 * depth, tokens, many * hidden, 5 * many * depth * hidden),
-        compiler_params=params(),
-        name="hidden_outer",
-    )(base, grad_out, act, normed, grad_inner)
-
-
-def assemble(place, own, got):
-    _, rows, width = own.shape
-
-    def kernel(place_ref, own_ref, got_ref, out_ref):
-        @pl.when(pl.program_id(1) == place_ref[1])
-        def _():
-            out_ref[0, 0] = own_ref[0]
-
-        @pl.when(pl.program_id(1) != place_ref[1])
-        def _():
-            out_ref[0, 0] = got_ref[0]
-
-    spec = pl.BlockSpec((1, rows, width), lambda z, x, place: (z ^ place[0], 0, 0))
-    return pl.pallas_call(
-        kernel,
-        grid_spec=pltpu.PrefetchScalarGridSpec(
-            num_scalar_prefetch=1,
-            grid=(4, 2),
-            in_specs=[spec, spec],
-            out_specs=pl.BlockSpec((1, 1, rows, width), lambda z, x, place: (z, x, 0, 0)),
+            grid=(2, 4),
+            in_specs=[spec(True), spec(False)],
+            out_specs=pl.BlockSpec((1, 1, rows, width), lambda x, z, place: (z, x, 0, 0)),
         ),
         out_shape=jax.ShapeDtypeStruct((4, 2, rows, width), BF),
-        cost_estimate=work(1, 1, 1, 48 * rows * width),
+        cost_estimate=work(1, 1, 1, 32 * rows * width),
         name="assemble",
     )(place, own, got).reshape(8 * rows, width)
 
@@ -579,23 +591,22 @@
 
 
 def to_tokens(values, pieces, cols):
-    width = values.shape[0]
-    parts = []
-    for piece in pieces:
-        region = values[:, piece.start : piece.start + cols * piece.count]
-        parts.append(region.reshape(width, cols, piece.count).transpose(1, 0, 2))
-    stacked = jnp.concatenate(parts, 2)
-    return exchange(stacked, cols, cols).reshape(cols * width, -1)
+    parts = [
+        jnp.concatenate(
+            [values[:, p.start + j * p.count : p.start + (j + 1) * p.count] for p in pieces], 1
+        )
+        for j in range(cols)
+    ]
+    got = exchange(jnp.stack(parts, 0), cols, cols)
+    return got.reshape(-1, got.shape[2])
 
 
 def to_features(values, pieces, cols):
-    width = values.shape[0] // cols
-    got = exchange(values.reshape(cols, width, -1), cols, cols)
+    got = exchange(values.reshape(cols, -1, values.shape[1]), cols, cols)
     parts = []
     at = 0
     for piece in pieces:
-        part = got[:, :, at : at + piece.count]
-        parts.append(part.transpose(1, 0, 2).reshape(width, cols * piece.count))
+        parts += [got[j, :, at : at + piece.count] for j in range(cols)]
         at += piece.count
     return jnp.concatenate(parts, 1)
 
@@ -627,8 +638,8 @@
 class Gathering:
     last = 4
 
-    def __init__(self, block, across, place):
-        self.across = across
+    def __init__(self, block, up, place):
+        self.up = up
         self.place = place
         self.stage = 0
         self.state = [block]
@@ -638,24 +649,28 @@
             self.state = list(whole.reshape(cols, -1, block.shape[1]))
             self.stage = self.last
 
+    def levels(self, block):
+        return [block] + [swap(block, "row", 2 * level) for level in (1, 2, 3)]
+
     def advance(self):
         state = self.state
         self.stage += 1
         if self.stage == 1:
-            self.state = state + [swap(state[0], "row", 2 * level) for level in (1, 2, 3)]
+            self.state = [state[0], swap(state[0], "col", 2)] if self.up else self.levels(state[0])
         elif self.stage == 2:
             stack = jnp.stack(state, 0)
-            self.state = [stack, swap(stack, "row", 1) if self.across else swap(stack, "col", 2)]
-        elif self.stage == 3 and self.across:
-            mine = assemble(self.place, *state)
-            self.state = [mine, swap(mine, "col", 1), swap(mine, "col", 2)]
+            self.state = self.levels(stack) if self.up else [stack, swap(stack, "col", 2)]
+        elif self.stage == 3 and self.up:
+            stack = jnp.stack(state, 0)
+            self.state = [stack, swap(stack, "row", 1)]
         elif self.stage == 3:
             self.state = state + [swap(a, "row", 1) for a in state]
-        elif self.across:
-            self.state = state + [swap(state[2], "col", 1)]
         else:
-            mine = assemble(self.place, state[0], state[2])
-            other = assemble(self.place, state[1], state[3])
+            if self.up:
+                mine, other = (assemble(self.place, *state, k) for k in (0, 1))
+            else:
+                mine = assemble(self.place, state[0], state[2])
+                other = assemble(self.place, state[1], state[3])
             self.state = [mine, swap(mine, "col", 1), other, swap(other, "col", 1)]
 
     def result(self):
@@ -793,13 +808,14 @@
     both = jnp.stack([latents.reshape(split), skip_input.reshape(split)], 1)
     both = to_tokens(both.reshape(2 * width, row_tokens), pieces, cols)
 
-    weights_one = gather_weights([self_inputs[:, i] for i in range(3)])
+    weights_one = gather_weights([*(self_inputs[:, i] for i in range(3)), self_output.T])
+    weights_two = gather_weights(
+        [cross_query, cross_output.T, cross_keyvalue[:, 0], cross_keyvalue[:, 1]]
+    )
     skip_block = jnp.concatenate([skip_weight[0], skip_weight[1]], 0)
     skip_block = jnp.pad(skip_block, ((0, 0), (0, lanes(width) - width)))
-    w_skip = Gathering(skip_block, True, place).result()
-    expanding = Gathering(expand_weight, True, place)
-    reducing = Gathering(reduce_weight.T, False, place)
-    gathers = [expanding, reducing]
+    w_skip = Gathering(skip_block, False, place).result()
+    weights_hidden = gather_weights([expand_weight, reduce_weight.T])
 
     places = jnp.concatenate(
         [
@@ -809,7 +825,7 @@
         1,
     )
 
-    embed = jax.nn.silu(condition.astype(F32)).astype(BF)
+    embed = jax.nn.silu(after(condition, both).astype(F32)).astype(BF)
     embed = shared(embed, "row").reshape(-1, width)
     embed = shared(embed, "col").transpose(1, 0, 2).reshape(-1, depth)
     embed_rows = lax.dynamic_slice_in_dim(embed, my_row * block_rows, block_rows, 1)
@@ -839,16 +855,11 @@
     scaling = 1.0 + per_token(1)
 
     joined = project_blocks(base, w_skip, width, both)
-    joined = tick(joined, gathers)
-    weights_two = gather_weights(
-        [self_output.T, cross_query, cross_output.T, cross_keyvalue[:, 0], cross_keyvalue[:, 1]]
-    )
     skip_normal, skip_inverse = normalize(joined)
     stream = skip_normal * gain_skip + bias_skip
     normal_one, inverse_one = normalize(stream)
     normed_one = (normal_one * scaling + shifting).astype(BF)
     raw = project(weights_one, [0, 1, 2], [normed_one], [F32, F32, BF])
-    raw = tick(raw, gathers)
     raw = [r.reshape(heads, dim, tokens) for r in raw]
     cosine, sine = rope_tables(places, dim)
 
@@ -860,15 +871,7 @@
     rot_key, key_pull = jax.vjp(self_piece, raw[1], key_gain)
     triple = [rot_query.astype(BF), rot_key.astype(BF), raw[2]]
 
-    text = shared(jnp.pad(after(text_states, joined), ((0, 0), (0, keys - texts), (0, 0))), "col")
-    text = jnp.concatenate(
-        [lax.dynamic_index_in_dim(text, p.sequence, 1, False) for p in pieces], 1
-    )
-    text = text.transpose(0, 2, 1).reshape(-1, len(pieces) * keys)
-    text_rows = text.shape[0] // rows
-    text_wide = jnp.pad(
-        text.reshape(rows, text_rows, -1), ((0, 0), (0, block_rows - text_rows), (0, 0))
-    ).reshape(depth, -1)
+    text = shared(jnp.pad(after(text_states, raw), ((0, 0), (0, keys - texts), (0, 0))), "col")
 
     def to_heads(parts, index):
         size = pieces[index].group
@@ -882,15 +885,23 @@
         whole = to_heads(triple, index)
         kept = attend(none, whole, whole, whole, (0, 1, 2), False, 2)
         saved_self.append((whole, kept))
-        mixed = tick(kept[0], gathers)
-        mixed_parts.append(exchange(mixed, piece.group, cols).reshape(depth, -1))
+        mixed_parts.append(exchange(kept[0], piece.group, cols).reshape(depth, -1))
     mixed_one = jnp.concatenate(mixed_parts, 1)
-    stream = stream + rebuild(weights_two, [0], [mixed_one], F32)
+    mixed_one, text = lax.optimization_barrier((mixed_one, text))
+    stream = stream + rebuild(weights_one, [3], [mixed_one], F32)
     normal_two, inverse_two = normalize(stream)
     normed_two = (normal_two * gain_cross + bias_cross).astype(BF)
-    raw_cross = project(weights_two, [1], [normed_two], [F32])[0].reshape(heads, dim, tokens)
+    raw_cross = project(weights_two, [0], [normed_two], [F32])[0].reshape(heads, dim, tokens)
     norm_query, cross_pull = jax.vjp(head_norm, raw_cross, cross_query_gain)
-    raw_text, value_two = project(weights_two, [3, 4], [text_wide], [F32, BF])
+    text = jnp.concatenate(
+        [lax.dynamic_index_in_dim(text, p.sequence, 1, False) for p in pieces], 1
+    )
+    text = text.transpose(0, 2, 1).reshape(-1, len(pieces) * keys)
+    text_rows = text.shape[0] // rows
+    text_wide = jnp.pad(
+        text.reshape(rows, text_rows, -1), ((0, 0), (0, block_rows - text_rows), (0, 0))
+    ).reshape(depth, -1)
+    raw_text, value_two = project(weights_two, [2, 3], [text_wide], [F32, BF])
     norm_key, text_pull = jax.vjp(head_norm, raw_text.reshape(heads, dim, -1), text_key_gain)
     query_two = norm_query.astype(BF)
     key_two = norm_key.astype(BF)
@@ -906,19 +917,17 @@
         saved_cross.append((inputs, kept))
         mixed_parts.append(kept[0].reshape(depth, -1))
     mixed_two = jnp.concatenate(mixed_parts, 1)
-    stream = stream + rebuild(weights_two, [2], [mixed_two], F32)
+    stream = stream + rebuild(weights_two, [1], [mixed_two], F32)
     normal_three, inverse_three = normalize(stream)
     normed_three = (normal_three * gain_hidden + bias_hidden).astype(BF)
-    w_expand = expanding.result()
-    w_reduce = reducing.result()
     grad_out = to_tokens(after(out_grad, joined).astype(BF), pieces, cols)
-    act, slopes = expand(w_expand, normed_three)
-    output = contract(w_reduce, act, stream, BF)
+    act, slopes = expand(weights_hidden, 0, normed_three)
+    output = contract(weights_hidden, 1, act, stream, BF)
     result = to_features(output, pieces, cols).astype(F32)
 
-    g_inner = expand_back(w_reduce, grad_out, slopes)
-    g_normed = contract(w_expand, g_inner, None, F32)
-    g_hidden = hidden_outer(base, grad_out, act, normed_three, g_inner)
+    g_inner = expand_back(weights_hidden, 1, grad_out, slopes)
+    g_normed = contract(weights_hidden, 0, g_inner, None, F32)
+    g_hidden = hidden_outer(grad_out, act, normed_three, g_inner)
     g_hidden = lax.psum_scatter(
         g_hidden.reshape(2, -1, g_hidden.shape[3]), DEVICES, scatter_dimension=1, tiled=True
     ).astype(F32)
@@ -928,7 +937,7 @@
 
     running = []
     g_low = g_stream.astype(BF)
-    g_mixed = project(weights_two, [2], [g_low], [BF])[0].reshape(heads, dim, tokens)
+    g_mixed = project(weights_two, [1], [g_low], [BF])[0].reshape(heads, dim, tokens)
     r_cross = Reduction(core, g_low, [mixed_two], True)
     running.append(r_cross)
     g_queries = []
@@ -948,7 +957,7 @@
         g_raw_text.astype(BF).reshape(depth, -1),
         jnp.concatenate(g_values, 2).astype(BF).reshape(depth, -1),
     ]
-    g_normed = rebuild(weights_two, [1], [g_craw], F32)
+    g_normed = rebuild(weights_two, [0], [g_craw], F32)
     r_query = Reduction(core, normed_two, [g_craw], False)
     r_text = Reduction(core, text, g_pair, True)
     g_normed = tick(g_normed, running)
@@ -958,7 +967,7 @@
     g_stream = g_stream + norm_back(g_normed * gain_cross, normal_two, inverse_two)
 
     g_low = g_stream.astype(BF)
-    g_mixed = project(weights_two, [0], [g_low], [BF])[0].reshape(heads, dim, tokens)
+    g_mixed = project(weights_one, [3], [g_low], [BF])[0].reshape(heads, dim, tokens)
     g_mixed = tick(g_mixed, running)
     r_attn = Reduction(core, g_low, [mixed_one], False)
     g_parts = []
@@ -988,8 +997,8 @@
         Reduction(core, normed_one, g_triple[2:], False),
     ]
     g_normed = rebuild(weights_one, [0, 1, 2], g_triple, F32)
+    running += r_self
     g_normed = tick(g_normed, running)
-    running += r_self
     crossed = g_normed * normal_one
     sums = jnp.stack(
         [
@@ -1014,14 +1023,16 @@
     g_joined = tick(g_joined, running)
     r_skip = Reduction(core, both, [g_joined], True)
     g_both = rebuild_blocks(base, w_skip, width, g_joined)
-    g_both = to_features(g_both, pieces, cols).reshape(split[0], 2, block_rows, row_tokens)
-    g_latents, g_skip = (g_both[:, i].reshape(width, row_tokens).astype(F32) for i in range(2))
+    g_both = tick(g_both, [r_skip])
+    g_inputs = to_features(g_both, pieces, cols).reshape(split[0], 2, block_rows, row_tokens)
+    g_latents, g_skip = (g_inputs[:, i].reshape(width, row_tokens).astype(F32) for i in range(2))
 
     g_gains = jnp.stack(
         [g_skip_gain, g_skip_bias, g_cross_gain, g_cross_bias, g_hidden_gain, g_hidden_bias], 0
     )
     g_gains = g_gains.reshape(6, cols, width).transpose(1, 0, 2)
     g_head = jnp.stack([g_q_gain, g_k_gain, g_cq_gain, g_tk_gain], 0).reshape(1, -1, width)
+    g_gains = after(g_gains, g_both)
     packed = jnp.concatenate([g_gains, jnp.broadcast_to(g_head, (cols, *g_head.shape[1:]))], 1)
     packed = jnp.sum(lax.all_to_all(packed, "col", 0, 0, tiled=True), 0)
     packed = jnp.sum(shared(packed, "row"), 0)

time: 1600 us -> 1410 us (0.88)
  waiting for transfers between devices: 481 us -> 377 us
  starting transfers between devices: 192 us -> 167 us
  blocking collectives: 21.5 us -> 0 us
  Pallas kernels: 481 us -> 462 us
    all_to_all x8, waiting for transfers between devices: 172 us -> 47.5 us  [exchange(): return lax.all_to_all(values, 'col', 0, 0, tiled=True)]
    ppermute x64 -> x50, starting transfers between devices: 99.5 us -> 66.9 us  [swap(): return lax.ppermute(values, axis, [(i, i ^ bit) for i in range(size)])]
    all_to_all x3 -> x0, blocking collectives: 21.5 us -> none  [exchange(): lax.all_to_all(values, 'col', 0, 0, tiled=True, axis_index_groups=groups_...]
    all_gather x2 -> x3, waiting for transfers between devices: 0.01 us -> 17.2 us  [gather_weights(): whole = lax.all_gather(jnp.stack(padded, 0), DEVICES, axis=1, tiled=True)]
    pallas_call x4 -> x2, Pallas kernels: 30.3 us -> 13.3 us  [assemble(): pl.pallas_call(kernel, grid_spec=pltpu.PrefetchScalarGridSpec(num_scalar_...]
    unnamed x351 -> x376, local copies, waits for them, and re-layouts: 22 us -> 36.5 us
    ppermute x64 -> x50, waiting for transfers between devices: 216 us -> 211 us  [swap(): return lax.ppermute(values, axis, [(i, i ^ bit) for i in range(size)])]
    convert_element_type x30 -> x29, other arithmetic: 66.4 us -> 67.6 us  [add(): return (left.astype(F32) + right.astype(F32)).astype(BF)]
  transfers between devices with their start and end apart: 85 -> 75, of which waited for: 25 -> 31; matrix products, arithmetic and copies ran while one was open for 24% -> 25% of each run, Pallas kernels for 27% -> 30%
where the time goes in v4:
time: 1410 us; the launch traced here: 1400 us
  Pallas kernels  462 us (33%)
  waiting for transfers between devices  377 us (27%)
  other arithmetic  276 us (20%)
  starting transfers between devices  167 us (12%)
  local copies, waits for them, and re-layouts  104 us (7%)
  between operations  16.9 us (1%)
    ppermute x50, waiting for transfers between devices, swap(): return lax.ppermute(values, axis, [(i, i ^ bit) for i in range(size)])  211 us
    pallas_call x14, Pallas kernels, outer(): pl.pallas_call(kernel, grid_spec=pltpu.PrefetchScalarGridSpec(num_scalar_...  91.4 us
    all_to_all x6, waiting for transfers between devices, shared(): lax.all_to_all(jnp.broadcast_to(values[None], (size, *values.shape)), axi...  88.6 us
    convert_element_type x29, other arithmetic, add(): return (left.astype(F32) + right.astype(F32)).astype(BF)  67.6 us
    ppermute x50, starting transfers between devices, swap(): return lax.ppermute(values, axis, [(i, i ^ bit) for i in range(size)])  66.9 us
    pallas_call x4, Pallas kernels, attend_back(): pl.pallas_call(partial(attend_back_kernel, masked), grid=(heads // many,)...  66.1 us
    pallas_call x5, Pallas kernels, project(): pl.pallas_call(kernel, grid=(cols,), in_specs=[pl.BlockSpec((1, 1, depth,...  50.1 us
    all_to_all x8, waiting for transfers between devices, exchange(): return lax.all_to_all(values, 'col', 0, 0, tiled=True)  47.5 us
  transfers between devices with their start and end apart: 75, of which 31 were waited for; matrix products, arithmetic and copies ran while one was open for 25% of the time, Pallas kernels for 30%

profile of v4, /device:TPU:0, one launch (start us, length us, event | category | flops | bytes accessed | tf_op | source)
XLA Modules:
  0.0 1404.1 jit_solution(8794629854528207169)
XLA Ops:
  35.6 14.5 %collective-permute-done = bf16[352,384]{1,0:T(8,128)(2,1)S(1)} collective-permute-done((bf16[352,384]{1,0:T(8,128)(2,1)S(1)}, bf16[352,384]{1,0:T(8,128)(2,1)S(1)}, u32[]{:S(2)}, u32[]{:S(2)}) %collective-permute-start) | collective-permute-done | bytes 270368 | tf_op jit(solution)/shard_map/ppermute | solution.py:623
  50.1 9.7 collective-permute-done.2
  63.1 66.7 %collective-permute-done.5.own_ref = bf16[4,352,384]{2,1,0:T(8,128)(2,1)S(1)} collective-permute-done((bf16[4,352,384]{2,1,0:T(8,128)(2,1)S(1)}, bf16[4,352,384]{2,1,0:T(8,128)(2,1)S(1)}, u32[]{:S(2)}, u32[]{:S(2)}) %collective-permute-start.5) | collective-permute-done | bytes 1081376 | tf_op jit(solution)/shard_map/ppermute | solution.py:623
  133.2 6.7 assemble.2
  139.9 15.4 %collective-permute-done.6.got_ref = bf16[4,352,384]{2,1,0:T(8,128)(2,1)S(1)} collective-permute-done((bf16[4,352,384]{2,1,0:T(8,128)(2,1)S(1)}, bf16[4,352,384]{2,1,0:T(8,128)(2,1)S(1)}, u32[]{:S(2)}, u32[]{:S(2)}) %collective-permute-start.6) | collective-permute-done | bytes 1081376 | tf_op jit(solution)/shard_map/ppermute | solution.py:623
  156.4 6.6 assemble.3
  165.0 6.5 all-to-all-start.1
  171.5 6.6 all-to-all-done.1
  191.7 5.8 all-to-all-done.3
  209.8 13.0 project_blocks.1
  231.2 5.6 add_convert_fusion.8.refs_3_.left_ref
  236.7 15.4 %project.5 = (f32[1408,768]{1,0:T(8,128)}, f32[1408,768]{1,0:T(8,128)}, bf16[1408,768]{1,0:T(8,128)(2,1)}) custom-call(bf16[4,4,1408,352]{3,2,1,0:T(8,128)(2,1)} %bitcast.426, bf16[4,4,1408,352]{3,2,1,0:T(8,128)(2,1)} %bitcast.427, bf16[4,4,1408,352]{3,2,1,0:T(8,128)(2,1)} %bitcast.428, bf16[1408,768]{1,0:T(8,128)(2,1)} %add_convert_fusion.8.refs_3_.left_ref), custom_call_target="tpu_custom_call" | custom-call | flops 9135194112 | bytes 8650752 | tf_op jit(solution)/shard_map/project/pallas_call | solution.py:221
  274.0 6.1 fusion.13
  284.0 5.8 all-to-all-start.5
  298.1 16.7 %attend.4 = (bf16[2,8,88,512]{3,2,1,0:T(8,128)(2,1)}, bf16[2,8,88,512]{3,2,1,0:T(8,128)(2,1)}, f32[8,1,1024]{2,1,0:T(1,128)}) custom-call(s32[1]{0:T(128)} %constant.370.clone.1.length_ref, bf16[2,3,8,88,512]{4,3,2,1,0:T(8,128)(2,1)} %all-to-all-done.5.q_ref.k_ref.v_ref, bf16[2,3,8,88,512]{4,3,2,1,0:T(8,128)(2,1)} %all-to-all-done.5.q_ref.k_ref.v_ref, ...), custom_call_target="tpu_custom_call" | custom-call | flops 8589934592 | bytes 5767168 | tf_op jit(solution)/shard_map/attend/pallas_call | solution.py:140
  314.9 14.0 all-to-all-done.7.q_ref.k_ref.v_ref
  333.9 9.6 attend.5
  349.2 8.7 all-to-all-done.8
  372.4 24.3 %all-to-all-done.9 = bf16[4,3,384,256]{2,3,1,0:T(8,128)(2,1)S(1)} async-done(((bf16[4,3,384,256]{2,3,1,0:T(8,128)(2,1)}), bf16[4,3,384,256]{2,3,1,0:T(8,128)(2,1)S(1)}, u32[]{:S(2)}, u32[]{:S(2)}) %all-to-all-start.9) | async-done | bytes 2359328 | tf_op jit(solution)/shard_map/all_to_all | solution.py:616
  406.1 8.5 rebuild.4
  422.8 7.9 project.6
  433.3 10.7 project.7
  457.2 7.4 attend.7
  467.1 11.7 attend.6
  482.1 8.9 rebuild.5
  499.3 17.2 %all-gather.4.cloned.1.call-done = bf16[2,5632,1536]{2,1,0:T(8,128)(2,1)} async-done(((bf16[2,176,1536]{2,1,0:T(8,128)(2,1)}), bf16[2,5632,1536]{2,1,0:T(8,128)(2,1)}) %all-gather.4.cloned.1.call-update) | async-done | bytes 34603024 | tf_op jit(solution)/shard_map/all_gather | solution.py:634
  516.5 27.1 %expand.1 = (bf16[4,1536,768]{2,1,0:T(8,128)(2,1)}, bf16[4,1536,768]{2,1,0:T(8,128)(2,1)}) custom-call(bf16[2,4,1408,1536]{3,2,1,0:T(8,128)(2,1)} %bitcast.484, bf16[1408,768]{1,0:T(8,128)(2,1)} %add_convert_fusion.6.values_ref.normed_ref), custom_call_target="tpu_custom_call" | custom-call | flops 13287555072 | bytes 25952256 | tf_op jit(solution)/shard_map/expand/pallas_call | solution.py:384
  545.0 20.5 %expand_back.1.values_ref.inner_ref = bf16[4,1536,768]{2,1,0:T(8,128)(2,1)} custom-call(bf16[2,4,1408,1536]{3,2,1,0:T(8,128)(2,1)} %bitcast.485, bf16[1408,768]{1,0:T(8,128)(2,1)} %bitcast.499, bf16[4,1536,768]{2,1,0:T(8,128)(2,1)} %get-tuple-element.134.slope_ref), custom_call_target="tpu_custom_call" | custom-call | flops 13287555072 | bytes 25952256 | tf_op jit(solution)/shard_map/expand_back/pallas_call | solution.py:409
  565.5 20.3 %contract.3 = f32[1408,768]{1,0:T(8,128)} custom-call(bf16[2,4,1408,1536]{3,2,1,0:T(8,128)(2,1)} %bitcast.486, bf16[4,1536,768]{2,1,0:T(8,128)(2,1)} %expand_back.1.values_ref.inner_ref), custom_call_target="tpu_custom_call" | custom-call | flops 13287555072 | bytes 25952256 | tf_op jit(solution)/shard_map/contract/pallas_call | solution.py:439
  585.8 5.8 multiply_reduce_fusion.2
  601.7 36.1 %hidden_outer.1 = bf16[2,4,1408,1536]{3,2,1,0:T(8,128)(2,1)} custom-call(bf16[1408,768]{1,0:T(8,128)(2,1)} %bitcast.500, bf16[4,1536,768]{2,1,0:T(8,128)(2,1)} %get-tuple-element.132.values_ref.act_ref, bf16[1408,768]{1,0:T(8,128)(2,1)} %add_convert_fusion.6.values_ref.normed_ref, bf16[4,1536,768]{2,1,0:T(8,128)(2,1)} %expand_back.1.values_ref.inner_ref), custom_call_target="tpu_custom_call" | custom-call | flops 26575110144 | bytes 43253760 | tf_op jit(solution)/shard_map/hidden_outer/pallas_call | solution.py:472
  643.3 8.4 project.8
  656.6 9.8 attend_back.5
  666.5 16.1 %attend_back.4 = (f32[1,1,16,88,512]{4,3,2,1,0:T(8,128)}, f32[1,1,16,88,384]{4,3,2,1,0:T(8,128)}, f32[1,1,16,88,384]{4,3,2,1,0:T(8,128)}) custom-call(s32[1]{0:T(128)} %get-tuple-element.509.length_ref, bf16[1,1,16,88,512]{4,3,2,1,0:T(8,128)(2,1)} %slice_bitcast_fusion.1.q_ref, bf16[1,1,16,88,384]{4,3,2,1,0:T(8,128)(2,1)} %get-tuple-element.458.k_ref, ...), custom_call_target="tpu_custom_call" | custom-call | flops 8053063680 | bytes 12615680 | tf_op jit(solution)/shard_map/attend_back/pallas_call | solution.py:173
  716.4 7.0 outer.19
  728.9 6.5 outer.18
  735.4 8.8 rebuild.6
  746.0 6.6 multiply_reduce_fusion.3
  754.4 6.4 fusion.97
  772.0 7.7 project.9
  809.7 26.1 %attend_back.6 = bf16[2,3,8,88,512]{4,3,2,1,0:T(8,128)(2,1)} custom-call(s32[1]{0:T(128)} %constant.370.clone.1.length_ref, bf16[2,3,8,88,512]{4,3,2,1,0:T(8,128)(2,1)} %all-to-all-done.5.q_ref.k_ref.v_ref, bf16[2,3,8,88,512]{4,3,2,1,0:T(8,128)(2,1)} %all-to-all-done.5.q_ref.k_ref.v_ref, bf16[2,3,8,88,512]{4,3,2,1,0:T(8,128)(2,1)} %all-to-all-done.5.q_ref.k_ref.v_ref, ...), custom_call_target="tpu_custom_call" | custom-call | flops 21474836480 | bytes 14417920 | tf_op jit(solution)/shard_map/attend_back/pallas_call | solution.py:173
  842.8 10.8 collective-permute-done.17
  859.3 14.2 %attend_back.7 = bf16[4,3,4,88,256]{4,3,2,1,0:T(8,128)(2,1)} custom-call(s32[1]{0:T(128)} %constant.370.clone.1.length_ref, bf16[4,3,4,88,256]{4,3,2,1,0:T(8,128)(2,1)} %copy-done.58, bf16[4,3,4,88,256]{4,3,2,1,0:T(8,128)(2,1)} %copy-done.58, bf16[4,3,4,88,256]{4,3,2,1,0:T(8,128)(2,1)} %copy-done.58, bf16[4,4,88,256]{3,2,1,0:T(8,128)(2,1)} %get-tuple-element.124.m_ref, ...), custom_call_target="tpu_custom_call" | custom-call | flops 10737418240 | bytes 7208960 | tf_op jit(solution)/shard_map/attend_back/pallas_call | solution.py:173
  873.5 5.8 all-to-all-start.13
  920.8 6.5 all-to-all-done.15
  938.2 7.5 multiply_reduce_fusion.7
  968.9 7.9 collective-permute-done.25
  977.6 8.3 outer.23
  985.9 20.3 %contract.2 = bf16[1408,768]{1,0:T(8,128)(2,1)} custom-call(bf16[2,4,1408,1536]{3,2,1,0:T(8,128)(2,1)} %bitcast.487, bf16[4,1536,768]{2,1,0:T(8,128)(2,1)} %get-tuple-element.132.values_ref.act_ref, f32[1408,768]{1,0:T(8,128)} %copy-done.3), custom_call_target="tpu_custom_call" | custom-call | flops 13287555072 | bytes 25952256 | tf_op jit(solution)/shard_map/contract/pallas_call | solution.py:439
  1017.8 18.4 %all-to-all-done.10 = bf16[4,352,768]{2,1,0:T(8,128)(2,1)S(1)} async-done(((bf16[4,352,768]{2,1,0:T(8,128)(2,1)}), bf16[4,352,768]{2,1,0:T(8,128)(2,1)S(1)}, u32[]{:S(2)}, u32[]{:S(2)}) %all-to-all-start.10) | async-done | bytes 2162720 | tf_op jit(solution)/shard_map/all_to_all | solution.py:587
  1039.2 18.9 %rebuild.7 = f32[1408,768]{1,0:T(8,128)} custom-call(bf16[4,4,1408,352]{3,2,1,0:T(8,128)(2,1)} %bitcast.431, bf16[4,4,1408,352]{3,2,1,0:T(8,128)(2,1)} %bitcast.432, bf16[4,4,1408,352]{3,2,1,0:T(8,128)(2,1)} %bitcast.433, bf16[1408,768]{1,0:T(8,128)(2,1)} %bitcast.529, bf16[1408,768]{1,0:T(8,128)(2,1)} %bitcast.532, ...), custom_call_target="tpu_custom_call" | custom-call | flops 9135194112 | bytes 8650752 | tf_op jit(solution)/shard_map/rebuild/pallas_call | solution.py:250
  1065.6 8.3 outer.22
  1088.0 10.8 multiply_reduce_fusion.4
  1116.5 15.1 %collective-permute-done.34 = bf16[2,2,4,176,384]{4,3,0,2,1:T(8,128)(2,1)} collective-permute-done((bf16[2,2,4,176,384]{4,3,0,2,1:T(8,128)(2,1)}, bf16[2,2,4,176,384]{4,3,0,2,1:T(8,128)(2,1)}, u32[]{:S(2)}, u32[]{:S(2)}) %collective-permute-start.34) | collective-permute-done | bytes 2162720 | tf_op jit(solution)/shard_map/ppermute | solution.py:623
  1131.6 8.7 outer.27
  1177.8 8.7 outer.26
  1186.4 13.4 rebuild_blocks.1
  1212.6 9.3 all-to-all-start.18
  1226.3 43.2 %all-to-all-done.18 = bf16[8,3,2,352]{3,2,1,0:T(2,128)(2,1)S(1)} async-done(((bf16[8,3,2,352]{3,2,1,0:T(2,128)(2,1)}), bf16[8,3,2,352]{3,2,1,0:T(2,128)(2,1)S(1)}, u32[]{:S(2)}, u32[]{:S(2)}) %all-to-all-start.18) | async-done | bytes 33824 | tf_op jit(solution)/shard_map/all_to_all | solution.py:616
  1270.2 9.3 all-to-all-start.20
  1315.4 5.8 collective-permute-done.45
  1321.2 15.3 %collective-permute-done.44 = bf16[2,176,384]{2,1,0:T(8,128)(2,1)S(1)} collective-permute-done((bf16[2,176,384]{2,1,0:T(8,128)(2,1)S(1)}, bf16[2,176,384]{2,1,0:T(8,128)(2,1)S(1)}, u32[]{:S(2)}, u32[]{:S(2)}) %collective-permute-start.44) | collective-permute-done | bytes 270368 | tf_op jit(solution)/shard_map/ppermute | solution.py:623
  1339.7 25.0 %collective-permute-done.38 = bf16[1,4,352,384]{3,2,1,0:T(8,128)(2,1)} collective-permute-done((bf16[1,4,352,384]{3,2,1,0:T(8,128)(2,1)S(1)}, bf16[1,4,352,384]{3,2,1,0:T(8,128)(2,1)}, u32[]{:S(2)}, u32[]{:S(2)}) %collective-permute-start.38) | collective-permute-done | bytes 1081376 | tf_op jit(solution)/shard_map/ppermute | solution.py:623
  1382.0 11.4 collective-permute-done.40
  (788 shorter events, 541.4 us)
Async XLA Ops:
  7.2 229.5 %all-gather.6.cloned.1.call-start = ((), (), s32[]{:S(2)}) async-start(), calls=%async_computation.23 | async-start | bytes 17842176 | tf_op jit(solution)/shard_map/all_gather | solution.py:634
  10.4 412.4 %all-gather.8.cloned.1.call-start = ((), (), s32[]{:S(2)}) async-start(), calls=%async_computation.24 | async-start | bytes 17842176 | tf_op jit(solution)/shard_map/all_gather | solution.py:634
  18.2 498.3 %all-gather.4.cloned.1.call-start = ((), (), s32[]{:S(2)}) async-start(), calls=%async_computation.22 | async-start | bytes 35684352 | tf_op jit(solution)/shard_map/all_gather | solution.py:634
  24.7 139.6 %all-to-all-start = ((bf16[4,704,768]{2,1,0:T(8,128)(2,1)}), bf16[4,704,768]{2,1,0:T(8,128)(2,1)}, u32[]{:S(2)}, u32[]{:S(2)}) async-start(bf16[4,704,768]{2,1,0:T(8,128)(2,1)} %pad_maximum_fusion.1), calls=%async_computation | async-start | bytes 8650752 | tf_op jit(solution)/shard_map/all_to_all | solution.py:587
  29.9 20.3 %collective-permute-start = (bf16[352,384]{1,0:T(8,128)(2,1)S(1)}, bf16[352,384]{1,0:T(8,128)(2,1)S(1)}, u32[]{:S(2)}, u32[]{:S(2)}) collective-permute-start(bf16[352,384]{1,0:T(8,128)(2,1)S(1)} %get-tuple-element.496), channel_id=1, source_target_pairs={{0,8},{4,12},{8,0},{12,4},{16,24},{20,28},{24,16},{28,20},{1,9},{5... | collective-permute-start | bytes 811016 | tf_op jit(solution)/shard_map/ppermute | solution.py:623
  33.0 17.1 %collective-permute-start.1 = (bf16[352,384]{1,0:T(8,128)(2,1)S(1)}, bf16[352,384]{1,0:T(8,128)(2,1)S(1)}, u32[]{:S(2)}, u32[]{:S(2)}) collective-permute-start(bf16[352,384]{1,0:T(8,128)(2,1)S(1)} %get-tuple-element.496), channel_id=1, source_target_pairs={{0,16},{4,20},{8,24},{12,28},{16,0},{20,4},{24,8},{28,12},{1,17},{... | collective-permute-start | bytes 811016 | tf_op jit(solution)/shard_map/ppermute | solution.py:623
  35.6 24.2 %collective-permute-start.2 = (bf16[352,384]{1,0:T(8,128)(2,1)S(1)}, bf16[352,384]{1,0:T(8,128)(2,1)S(1)}, u32[]{:S(2)}, u32[]{:S(2)}) collective-permute-start(bf16[352,384]{1,0:T(8,128)(2,1)S(1)} %get-tuple-element.496), channel_id=1, source_target_pairs={{0,24},{4,28},{8,16},{12,20},{16,8},{20,12},{24,0},{28,4},{1,25},{... | collective-permute-start | bytes 811016 | tf_op jit(solution)/shard_map/ppermute | solution.py:623
  60.0 69.8 %collective-permute-start.5 = (bf16[4,352,384]{2,1,0:T(8,128)(2,1)S(1)}, bf16[4,352,384]{2,1,0:T(8,128)(2,1)S(1)}, u32[]{:S(2)}, u32[]{:S(2)}) collective-permute-start(bf16[4,352,384]{2,1,0:T(8,128)(2,1)S(1)} %pad_maximum_fusion.15.own_ref), channel_id=1, source_target_pairs={{0,2},{1,3},{2,0},{3,1},{4,6},{5,7},{6,4},{7,5},{8,10},{9,11},{10,... | collective-permute-start | bytes 3244040 | tf_op jit(solution)/shard_map/ppermute | solution.py:623
  61.6 71.6 %collective-permute-start.3 = (bf16[4,352,384]{2,1,0:T(8,128)(2,1)S(1)}, bf16[4,352,384]{2,1,0:T(8,128)(2,1)}, u32[]{:S(2)}, u32[]{:S(2)}) collective-permute-start(bf16[4,352,384]{2,1,0:T(8,128)(2,1)S(1)} %pad_maximum_fusion.15.own_ref), channel_id=1, source_target_pairs={{0,4},{4,0},{8,12},{12,8},{16,20},{20,16},{24,28},{28,24},{1,5},{5... | collective-permute-start | bytes 3244040 | tf_op jit(solution)/shard_map/ppermute | solution.py:623
  129.8 25.6 %collective-permute-start.6 = (bf16[4,352,384]{2,1,0:T(8,128)(2,1)S(1)}, bf16[4,352,384]{2,1,0:T(8,128)(2,1)S(1)}, u32[]{:S(2)}, u32[]{:S(2)}) collective-permute-start(bf16[4,352,384]{2,1,0:T(8,128)(2,1)S(1)} %collective-permute-done.5.own_ref), channel_id=1, source_target_pairs={{0,4},{4,0},{8,12},{12,8},{16,20},{20,16},{24,28},{28,24},{1,5},{5... | collective-permute-start | bytes 3244040 | tf_op jit(solution)/shard_map/ppermute | solution.py:623
  139.9 68.5 %collective-permute-start.4 = (bf16[2816,384]{1,0:T(8,128)(2,1)}, bf16[2816,384]{1,0:T(8,128)(2,1)}, u32[]{:S(2)}, u32[]{:S(2)}) collective-permute-start(bf16[2816,384]{1,0:T(8,128)(2,1)} %bitcast.573), channel_id=1, source_target_pairs={{0,1},{1,0},{2,3},{3,2},{4,5},{5,4},{6,7},{7,6},{8,9},{9,8},{10,11... | collective-permute-start | bytes 6488072 | tf_op jit(solution)/shard_map/ppermute | solution.py:623
  163.0 45.5 %collective-permute-start.7 = (bf16[2816,384]{1,0:T(8,128)(2,1)}, bf16[2816,384]{1,0:T(8,128)(2,1)S(1)}, u32[]{:S(2)}, u32[]{:S(2)}) collective-permute-start(bf16[2816,384]{1,0:T(8,128)(2,1)} %bitcast.576), channel_id=1, source_target_pairs={{0,1},{1,0},{2,3},{3,2},{4,5},{5,4},{6,7},{7,6},{8,9},{9,8},{10,11... | collective-permute-start | bytes 6488072 | tf_op jit(solution)/shard_map/ppermute | solution.py:623
  165.0 13.1 all-to-all-start.1
  294.4 34.4 %all-to-all-start.7 = ((bf16[4,3,4,88,256]{4,3,2,1,0:T(8,128)(2,1)}), bf16[4,3,4,88,256]{4,3,2,1,0:T(8,128)(2,1)S(1)}, u32[]{:S(2)}, u32[]{:S(2)}) async-start(bf16[4,3,4,88,256]{4,3,2,1,0:T(8,128)(2,1)} %pad_maximum_fusion.5), calls=%async_computation.7 | async-start | bytes 4325376 | tf_op jit(solution)/shard_map/all_to_all | solution.py:587
  330.2 13.2 all-to-all-start.6
  343.4 14.4 %all-to-all-start.8 = ((bf16[4,4,88,256]{3,2,1,0:T(8,128)(2,1)}), bf16[4,4,88,256]{3,2,1,0:T(8,128)(2,1)S(1)}, u32[]{:S(2)}, u32[]{:S(2)}) async-start(bf16[4,4,88,256]{3,2,1,0:T(8,128)(2,1)} %get-tuple-element.124.m_ref), calls=%async_computation.8 | async-start | bytes 1441792 | tf_op jit(solution)/shard_map/all_to_all | solution.py:587
  360.6 36.1 %all-to-all-start.9 = ((bf16[4,3,384,256]{2,3,1,0:T(8,128)(2,1)}), bf16[4,3,384,256]{2,3,1,0:T(8,128)(2,1)S(1)}, u32[]{:S(2)}, u32[]{:S(2)}) async-start(bf16[4,3,384,256]{2,3,1,0:T(8,128)(2,1)} %broadcast_in_dim.215), calls=%async_computation.9 | async-start | bytes 4718592 | tf_op jit(solution)/shard_map/all_to_all | solution.py:616
  398.1 145.5 %all-to-all-start.11 = ((bf16[4,352,768]{2,1,0:T(8,128)(2,1)}), bf16[4,352,768]{2,1,0:T(8,128)(2,1)S(1)}, u32[]{:S(2)}, u32[]{:S(2)}) async-start(bf16[4,352,768]{2,1,0:T(8,128)(2,1)} %pad_maximum_fusion.8), calls=%async_computation.11 | async-start | bytes 4325376 | tf_op jit(solution)/shard_map/all_to_all | solution.py:587
  401.7 992.7 %reduce-scatter.2.cloned.1.call-start = ((), (), s32[]{:S(2)}) async-start(), calls=%async_computation.25 | async-start | bytes 35684352 | tf_op jit(solution)/shard_map/reduce_scatter | solution.py:931
  601.5 81.1 %collective-permute-start.8 = (bf16[1,2,1408,384]{3,2,1,0:T(8,128)(2,1)}, bf16[1,2,1408,384]{3,2,1,0:T(8,128)(2,1)}, u32[]{:S(2)}, u32[]{:S(2)}) collective-permute-start(bf16[1,2,1408,384]{3,2,1,0:T(8,128)(2,1)} %outer.15), channel_id=1, source_target_pairs={{0,1},{1,0},{2,3},{3,2},{4,5},{5,4},{6,7},{7,6},{8,9},{9,8},{10,11... | collective-permute-start | bytes 6488072 | tf_op jit(solution)/shard_map/ppermute | solution.py:623
  689.5 56.5 %collective-permute-start.9 = (bf16[1,2,4,176,384]{4,3,2,1,0:T(8,128)(2,1)}, bf16[1,2,4,176,384]{4,3,2,1,0:T(8,128)(2,1)}, u32[]{:S(2)}, u32[]{:S(2)}) collective-permute-start(bf16[1,2,4,176,384]{4,3,2,1,0:T(8,128)(2,1)} %fusion.30), channel_id=1, source_target_pairs={{0,4},{4,0},{8,12},{12,8},{16,20},{20,16},{24,28},{28,24},{1,5},{5... | collective-permute-start | bytes 3244040 | tf_op jit(solution)/shard_map/ppermute | solution.py:623
  704.7 75.0 %collective-permute-start.11 = (bf16[1,2,1408,384]{3,2,1,0:T(8,128)(2,1)}, bf16[1,2,1408,384]{3,2,1,0:T(8,128)(2,1)}, u32[]{:S(2)}, u32[]{:S(2)}) collective-permute-start(bf16[1,2,1408,384]{3,2,1,0:T(8,128)(2,1)} %outer.17), channel_id=1, source_target_pairs={{0,1},{1,0},{2,3},{3,2},{4,5},{5,4},{6,7},{7,6},{8,9},{9,8},{10,11... | collective-permute-start | bytes 6488072 | tf_op jit(solution)/shard_map/ppermute | solution.py:623
  723.3 56.4 %collective-permute-start.12 = (bf16[2,2,1024,384]{3,2,1,0:T(8,128)(2,1)}, bf16[2,2,1024,384]{3,2,1,0:T(8,128)(2,1)}, u32[]{:S(2)}, u32[]{:S(2)}) collective-permute-start(bf16[2,2,1024,384]{3,2,1,0:T(8,128)(2,1)} %outer.19), channel_id=1, source_target_pairs={{0,1},{1,0},{2,3},{3,2},{4,5},{5,4},{6,7},{7,6},{8,9},{9,8},{10,11... | collective-permute-start | bytes 9437192 | tf_op jit(solution)/shard_map/ppermute | solution.py:623
  754.1 25.6 %collective-permute-start.10 = (bf16[1,4,176,384]{3,2,1,0:T(8,128)(2,1)S(1)}, bf16[1,4,176,384]{3,2,1,0:T(8,128)(2,1)S(1)}, u32[]{:S(2)}, u32[]{:S(2)}) collective-permute-start(bf16[1,4,176,384]{3,2,1,0:T(8,128)(2,1)S(1)} %get-tuple-element.446), channel_id=1, source_target_pairs={{0,2},{1,3},{2,0},{3,1},{4,6},{5,7},{6,4},{7,5},{8,10},{9,11},{10,... | collective-permute-start | bytes 1622024 | tf_op jit(solution)/shard_map/ppermute | solution.py:623
  766.3 117.3 %collective-permute-start.20 = (bf16[1,2,1408,384]{3,2,1,0:T(8,128)(2,1)}, bf16[1,2,1408,384]{3,2,1,0:T(8,128)(2,1)}, u32[]{:S(2)}, u32[]{:S(2)}) collective-permute-start(bf16[1,2,1408,384]{3,2,1,0:T(8,128)(2,1)} %outer.21), channel_id=1, source_target_pairs={{0,1},{1,0},{2,3},{3,2},{4,5},{5,4},{6,7},{7,6},{8,9},{9,8},{10,11... | collective-permute-start | bytes 6488072 | tf_op jit(solution)/shard_map/ppermute | solution.py:623
  786.7 49.1 %collective-permute-start.15 = (bf16[1,176,384]{2,1,0:T(8,128)(2,1)}, bf16[1,176,384]{2,1,0:T(8,128)(2,1)S(1)}, u32[]{:S(2)}, u32[]{:S(2)}) collective-permute-start(bf16[1,176,384]{2,1,0:T(8,128)(2,1)} %get-tuple-element.484), channel_id=1, source_target_pairs={{0,24},{4,28},{8,16},{12,20},{16,8},{20,12},{24,0},{28,4},{1,25},{... | collective-permute-start | bytes 405512 | tf_op jit(solution)/shard_map/ppermute | solution.py:623
  788.9 51.1 %collective-permute-start.14 = (bf16[1,176,384]{2,1,0:T(8,128)(2,1)}, bf16[1,176,384]{2,1,0:T(8,128)(2,1)S(1)}, u32[]{:S(2)}, u32[]{:S(2)}) collective-permute-start(bf16[1,176,384]{2,1,0:T(8,128)(2,1)} %get-tuple-element.485), channel_id=1, source_target_pairs={{0,16},{4,20},{8,24},{12,28},{16,0},{20,4},{24,8},{28,12},{1,17},{... | collective-permute-start | bytes 405512 | tf_op jit(solution)/shard_map/ppermute | solution.py:623
  789.5 16.1 %all-to-all-start.12 = ((bf16[2,8,88,512]{3,2,1,0:T(8,128)(2,1)}), bf16[2,8,88,512]{3,2,1,0:T(8,128)(2,1)}, u32[]{:S(2)}, u32[]{:S(2)}) async-start(bf16[2,8,88,512]{3,2,1,0:T(8,128)(2,1)} %bitcast.548), calls=%async_computation.12 | async-start | bytes 2883584 | tf_op jit(solution)/shard_map/all_to_all | solution.py:588
  797.0 45.8 %collective-permute-start.16 = (bf16[1,4,2,176,384]{4,3,2,1,0:T(8,128)(2,1)}, bf16[1,4,2,176,384]{4,3,2,1,0:T(8,128)(2,1)}, u32[]{:S(2)}, u32[]{:S(2)}) collective-permute-start(bf16[1,4,2,176,384]{4,3,2,1,0:T(8,128)(2,1)} %fusion.32), channel_id=1, source_target_pairs={{0,2},{1,3},{2,0},{3,1},{4,6},{5,7},{6,4},{7,5},{8,10},{9,11},{10,... | collective-permute-start | bytes 3244040 | tf_op jit(solution)/shard_map/ppermute | solution.py:623
  801.4 52.2 %collective-permute-start.17 = (bf16[2,2,4,128,384]{4,3,2,1,0:T(8,128)(2,1)}, bf16[2,2,4,128,384]{4,3,2,1,0:T(8,128)(2,1)}, u32[]{:S(2)}, u32[]{:S(2)}) collective-permute-start(bf16[2,2,4,128,384]{4,3,2,1,0:T(8,128)(2,1)} %fusion.27), channel_id=1, source_target_pairs={{0,4},{4,0},{8,12},{12,8},{16,20},{20,16},{24,28},{28,24},{1,5},{5... | collective-permute-start | bytes 4718600 | tf_op jit(solution)/shard_map/ppermute | solution.py:623
  805.6 53.8 %all-to-all-start.14 = ((bf16[4,4,88,256]{3,2,1,0:T(8,128)(2,1)}), bf16[4,4,88,256]{3,2,1,0:T(8,128)(2,1)}, u32[]{:S(2)}, u32[]{:S(2)}) async-start(bf16[4,4,88,256]{3,2,1,0:T(8,128)(2,1)} %bitcast.559), calls=%async_computation.14 | async-start | bytes 1441792 | tf_op jit(solution)/shard_map/all_to_all | solution.py:587
  855.6 28.0 %collective-permute-start.18 = (bf16[1,4,176,384]{3,2,1,0:T(8,128)(2,1)}, bf16[1,4,176,384]{3,2,1,0:T(8,128)(2,1)}, u32[]{:S(2)}, u32[]{:S(2)}) collective-permute-start(bf16[1,4,176,384]{3,2,1,0:T(8,128)(2,1)} %fusion.52), channel_id=1, source_target_pairs={{0,4},{4,0},{8,12},{12,8},{16,20},{20,16},{24,28},{28,24},{1,5},{5... | collective-permute-start | bytes 1622024 | tf_op jit(solution)/shard_map/ppermute | solution.py:623
  859.0 28.7 %collective-permute-start.19 = (bf16[2,4,128,384]{3,2,1,0:T(8,128)(2,1)}, bf16[2,4,128,384]{3,2,1,0:T(8,128)(2,1)}, u32[]{:S(2)}, u32[]{:S(2)}) collective-permute-start(bf16[2,4,128,384]{3,2,1,0:T(8,128)(2,1)} %fusion.45), channel_id=1, source_target_pairs={{0,2},{1,3},{2,0},{3,1},{4,6},{5,7},{6,4},{7,5},{8,10},{9,11},{10,... | collective-permute-start | bytes 2359304 | tf_op jit(solution)/shard_map/ppermute | solution.py:623
  873.5 14.2 %all-to-all-start.13 = ((bf16[2,3,8,88,512]{4,3,2,1,0:T(8,128)(2,1)}), bf16[2,3,8,88,512]{4,3,2,1,0:T(8,128)(2,1)}, u32[]{:S(2)}, u32[]{:S(2)}) async-start(bf16[2,3,8,88,512]{4,3,2,1,0:T(8,128)(2,1)} %attend_back.6), calls=%async_computation.13 | async-start | bytes 8650752 | tf_op jit(solution)/shard_map/all_to_all | solution.py:588
  887.7 39.6 %all-to-all-start.15 = ((bf16[4,3,4,88,256]{4,3,2,1,0:T(8,128)(2,1)}), bf16[4,3,4,88,256]{4,3,2,1,0:T(8,128)(2,1)}, u32[]{:S(2)}, u32[]{:S(2)}) async-start(bf16[4,3,4,88,256]{4,3,2,1,0:T(8,128)(2,1)} %attend_back.7), calls=%async_computation.15 | async-start | bytes 4325376 | tf_op jit(solution)/shard_map/all_to_all | solution.py:587
  898.7 62.3 %collective-permute-start.23 = (bf16[1,176,384]{2,1,0:T(8,128)(2,1)}, bf16[1,176,384]{2,1,0:T(8,128)(2,1)}, u32[]{:S(2)}, u32[]{:S(2)}) collective-permute-start(bf16[1,176,384]{2,1,0:T(8,128)(2,1)} %get-tuple-element.480), channel_id=1, source_target_pairs={{0,24},{4,28},{8,16},{12,20},{16,8},{20,12},{24,0},{28,4},{1,25},{... | collective-permute-start | bytes 405512 | tf_op jit(solution)/shard_map/ppermute | solution.py:623
  901.8 61.8 %collective-permute-start.22 = (bf16[1,176,384]{2,1,0:T(8,128)(2,1)}, bf16[1,176,384]{2,1,0:T(8,128)(2,1)}, u32[]{:S(2)}, u32[]{:S(2)}) collective-permute-start(bf16[1,176,384]{2,1,0:T(8,128)(2,1)} %get-tuple-element.481), channel_id=1, source_target_pairs={{0,16},{4,20},{8,24},{12,28},{16,0},{20,4},{24,8},{28,12},{1,17},{... | collective-permute-start | bytes 405512 | tf_op jit(solution)/shard_map/ppermute | solution.py:623
  905.5 63.4 %collective-permute-start.21 = (bf16[1,176,384]{2,1,0:T(8,128)(2,1)}, bf16[1,176,384]{2,1,0:T(8,128)(2,1)}, u32[]{:S(2)}, u32[]{:S(2)}) collective-permute-start(bf16[1,176,384]{2,1,0:T(8,128)(2,1)} %get-tuple-element.482), channel_id=1, source_target_pairs={{0,8},{4,12},{8,0},{12,4},{16,24},{20,28},{24,16},{28,20},{1,9},{5... | collective-permute-start | bytes 405512 | tf_op jit(solution)/shard_map/ppermute | solution.py:623
  911.2 57.7 %collective-permute-start.24 = (bf16[2,128,384]{1,2,0:T(8,128)(2,1)S(1)}, bf16[2,128,384]{1,2,0:T(8,128)(2,1)}, u32[]{:S(2)}, u32[]{:S(2)}) collective-permute-start(bf16[2,128,384]{1,2,0:T(8,128)(2,1)S(1)} %bitcast.603), channel_id=1, source_target_pairs={{0,8},{4,12},{8,0},{12,4},{16,24},{20,28},{24,16},{28,20},{1,9},{5... | collective-permute-start | bytes 589832 | tf_op jit(solution)/shard_map/ppermute | solution.py:623
  916.0 61.5 %collective-permute-start.27 = (bf16[1,4,2,176,384]{4,3,2,1,0:T(8,128)(2,1)}, bf16[1,4,2,176,384]{4,3,2,1,0:T(8,128)(2,1)}, u32[]{:S(2)}, u32[]{:S(2)}) collective-permute-start(bf16[1,4,2,176,384]{4,3,2,1,0:T(8,128)(2,1)} %fusion.34), channel_id=1, source_target_pairs={{0,2},{1,3},{2,0},{3,1},{4,6},{5,7},{6,4},{7,5},{8,10},{9,11},{10,... | collective-permute-start | bytes 3244040 | tf_op jit(solution)/shard_map/ppermute | solution.py:623
  961.0 15.9 %collective-permute-start.25 = (bf16[2,128,384]{1,2,0:T(8,128)(2,1)S(1)}, bf16[2,128,384]{1,2,0:T(8,128)(2,1)S(1)}, u32[]{:S(2)}, u32[]{:S(2)}) collective-permute-start(bf16[2,128,384]{1,2,0:T(8,128)(2,1)S(1)} %bitcast.602), channel_id=1, source_target_pairs={{0,16},{4,20},{8,24},{12,28},{16,0},{20,4},{24,8},{28,12},{1,17},{... | collective-permute-start | bytes 589832 | tf_op jit(solution)/shard_map/ppermute | solution.py:623
  963.6 13.3 collective-permute-start.26
  985.9 88.0 %collective-permute-start.29 = (bf16[2,2,1408,384]{3,2,1,0:T(8,128)(2,1)}, bf16[2,2,1408,384]{3,2,1,0:T(8,128)(2,1)}, u32[]{:S(2)}, u32[]{:S(2)}) collective-permute-start(bf16[2,2,1408,384]{3,2,1,0:T(8,128)(2,1)} %outer.23), channel_id=1, source_target_pairs={{0,1},{1,0},{2,3},{3,2},{4,5},{5,4},{6,7},{7,6},{8,9},{9,8},{10,11... | collective-permute-start | bytes 12976136 | tf_op jit(solution)/shard_map/ppermute | solution.py:623
  1006.2 30.0 %all-to-all-start.10 = ((bf16[4,352,768]{2,1,0:T(8,128)(2,1)}), bf16[4,352,768]{2,1,0:T(8,128)(2,1)S(1)}, u32[]{:S(2)}, u32[]{:S(2)}) async-start(bf16[4,352,768]{2,1,0:T(8,128)(2,1)} %bitcast.534), calls=%async_computation.10 | async-start | bytes 4325376 | tf_op jit(solution)/shard_map/all_to_all | solution.py:587
  1015.4 58.5 %collective-permute-start.30 = (bf16[1,2,1408,384]{3,2,1,0:T(8,128)(2,1)}, bf16[1,2,1408,384]{3,2,1,0:T(8,128)(2,1)}, u32[]{:S(2)}, u32[]{:S(2)}) collective-permute-start(bf16[1,2,1408,384]{3,2,1,0:T(8,128)(2,1)} %outer.25), channel_id=1, source_target_pairs={{0,1},{1,0},{2,3},{3,2},{4,5},{5,4},{6,7},{7,6},{8,9},{9,8},{10,11... | collective-permute-start | bytes 6488072 | tf_op jit(solution)/shard_map/ppermute | solution.py:623
  1039.0 34.9 %collective-permute-start.28 = (bf16[1,4,176,384]{3,2,1,0:T(8,128)(2,1)}, bf16[1,4,176,384]{3,2,1,0:T(8,128)(2,1)}, u32[]{:S(2)}, u32[]{:S(2)}) collective-permute-start(bf16[1,4,176,384]{3,2,1,0:T(8,128)(2,1)} %fusion.53), channel_id=1, source_target_pairs={{0,4},{4,0},{8,12},{12,8},{16,20},{20,16},{24,28},{28,24},{1,5},{5... | collective-permute-start | bytes 1622024 | tf_op jit(solution)/shard_map/ppermute | solution.py:623
  1077.4 39.1 %collective-permute-start.35 = (bf16[1,4,2,176,384]{4,3,1,2,0:T(8,128)(2,1)}, bf16[1,4,2,176,384]{4,3,1,2,0:T(8,128)(2,1)}, u32[]{:S(2)}, u32[]{:S(2)}) collective-permute-start(bf16[1,4,2,176,384]{4,3,1,2,0:T(8,128)(2,1)} %get-tuple-element.410), channel_id=1, source_target_pairs={{0,2},{1,3},{2,0},{3,1},{4,6},{5,7},{6,4},{7,5},{8,10},{9,11},{10,... | collective-permute-start | bytes 3244040 | tf_op jit(solution)/shard_map/ppermute | solution.py:623
  1082.8 48.8 %collective-permute-start.34 = (bf16[2,2,4,176,384]{4,3,0,2,1:T(8,128)(2,1)}, bf16[2,2,4,176,384]{4,3,0,2,1:T(8,128)(2,1)}, u32[]{:S(2)}, u32[]{:S(2)}) collective-permute-start(bf16[2,2,4,176,384]{4,3,0,2,1:T(8,128)(2,1)} %get-tuple-element.398), channel_id=1, source_target_pairs={{0,4},{4,0},{8,12},{12,8},{16,20},{20,16},{24,28},{28,24},{1,5},{5... | collective-permute-start | bytes 6488072 | tf_op jit(solution)/shard_map/ppermute | solution.py:623
  1140.2 59.6 %collective-permute-start.36 = (bf16[1,2,2816,384]{3,2,1,0:T(8,128)(2,1)}, bf16[1,2,2816,384]{3,2,1,0:T(8,128)(2,1)}, u32[]{:S(2)}, u32[]{:S(2)}) collective-permute-start(bf16[1,2,2816,384]{3,2,1,0:T(8,128)(2,1)} %outer.27), channel_id=1, source_target_pairs={{0,1},{1,0},{2,3},{3,2},{4,5},{5,4},{6,7},{7,6},{8,9},{9,8},{10,11... | collective-permute-start | bytes 12976136 | tf_op jit(solution)/shard_map/ppermute | solution.py:623
  1207.9 99.0 %collective-permute-start.37 = (bf16[1,2,4,352,384]{4,3,2,1,0:T(8,128)(2,1)}, bf16[1,2,4,352,384]{4,3,2,1,0:T(8,128)(2,1)}, u32[]{:S(2)}, u32[]{:S(2)}) collective-permute-start(bf16[1,2,4,352,384]{4,3,2,1,0:T(8,128)(2,1)} %fusion.21), channel_id=1, source_target_pairs={{0,4},{4,0},{8,12},{12,8},{16,20},{20,16},{24,28},{28,24},{1,5},{5... | collective-permute-start | bytes 6488072 | tf_op jit(solution)/shard_map/ppermute | solution.py:623
  1211.6 84.2 %collective-permute-start.46 = (bf16[1,4,176,384]{3,2,1,0:T(8,128)(2,1)}, bf16[1,4,176,384]{3,2,1,0:T(8,128)(2,1)}, u32[]{:S(2)}, u32[]{:S(2)}) collective-permute-start(bf16[1,4,176,384]{3,2,1,0:T(8,128)(2,1)} %fusion.51), channel_id=1, source_target_pairs={{0,4},{4,0},{8,12},{12,8},{16,20},{20,16},{24,28},{28,24},{1,5},{5... | collective-permute-start | bytes 1622024 | tf_op jit(solution)/shard_map/ppermute | solution.py:623
  1212.6 57.0 %all-to-all-start.18 = ((bf16[8,3,2,352]{3,2,1,0:T(2,128)(2,1)}), bf16[8,3,2,352]{3,2,1,0:T(2,128)(2,1)S(1)}, u32[]{:S(2)}, u32[]{:S(2)}) async-start(bf16[8,3,2,352]{3,2,1,0:T(2,128)(2,1)} %broadcast_in_dim.239), calls=%async_computation.18 | async-start | bytes 73728 | tf_op jit(solution)/shard_map/all_to_all | solution.py:616
  1224.3 76.6 %collective-permute-start.42 = (bf16[2,4,176,384]{3,2,0,1:T(8,128)(2,1)}, bf16[2,4,176,384]{3,2,0,1:T(8,128)(2,1)}, u32[]{:S(2)}, u32[]{:S(2)}) collective-permute-start(bf16[2,4,176,384]{3,2,0,1:T(8,128)(2,1)} %fusion.38), channel_id=1, source_target_pairs={{0,2},{1,3},{2,0},{3,1},{4,6},{5,7},{6,4},{7,5},{8,10},{9,11},{10,... | collective-permute-start | bytes 3244040 | tf_op jit(solution)/shard_map/ppermute | solution.py:623
  1270.2 16.5 %all-to-all-start.20 = ((f32[8,7,352]{2,1,0:T(8,128)}), f32[8,7,352]{2,1,0:T(8,128)}, u32[]{:S(2)}, u32[]{:S(2)}) async-start(f32[8,7,352]{2,1,0:T(8,128)} %broadcast_in_dim.242), calls=%async_computation.21 | async-start | bytes 196608 | tf_op jit(solution)/shard_map/all_to_all | solution.py:616
  1286.7 83.6 %all-to-all-start.16 = ((bf16[4,704,768]{2,1,0:T(8,128)(2,1)}), bf16[4,704,768]{2,1,0:T(8,128)(2,1)}, u32[]{:S(2)}, u32[]{:S(2)}) async-start(bf16[4,704,768]{2,1,0:T(8,128)(2,1)} %bitcast.556), calls=%async_computation.16 | async-start | bytes 8650752 | tf_op jit(solution)/shard_map/all_to_all | solution.py:587
  1297.4 13.0 collective-permute-start.47
  1297.4 13.6 collective-permute-start.49
  1299.3 14.7 %collective-permute-start.48 = (bf16[1,176,384]{2,1,0:T(8,128)(2,1)S(1)}, bf16[1,176,384]{2,1,0:T(8,128)(2,1)S(1)}, u32[]{:S(2)}, u32[]{:S(2)}) collective-permute-start(bf16[1,176,384]{2,1,0:T(8,128)(2,1)S(1)} %get-tuple-element.474), channel_id=1, source_target_pairs={{0,16},{4,20},{8,24},{12,28},{16,0},{20,4},{24,8},{28,12},{1,17},{... | collective-permute-start | bytes 405512 | tf_op jit(solution)/shard_map/ppermute | solution.py:623
  1306.9 14.3 %collective-permute-start.45 = (bf16[2,176,384]{2,1,0:T(8,128)(2,1)S(1)}, bf16[2,176,384]{2,1,0:T(8,128)(2,1)S(1)}, u32[]{:S(2)}, u32[]{:S(2)}) collective-permute-start(bf16[2,176,384]{2,1,0:T(8,128)(2,1)S(1)} %get-tuple-element.461), channel_id=1, source_target_pairs={{0,24},{4,28},{8,16},{12,20},{16,8},{20,12},{24,0},{28,4},{1,25},{... | collective-permute-start | bytes 811016 | tf_op jit(solution)/shard_map/ppermute | solution.py:623
  1310.3 26.2 %collective-permute-start.44 = (bf16[2,176,384]{2,1,0:T(8,128)(2,1)S(1)}, bf16[2,176,384]{2,1,0:T(8,128)(2,1)S(1)}, u32[]{:S(2)}, u32[]{:S(2)}) collective-permute-start(bf16[2,176,384]{2,1,0:T(8,128)(2,1)S(1)} %get-tuple-element.462), channel_id=1, source_target_pairs={{0,16},{4,20},{8,24},{12,28},{16,0},{20,4},{24,8},{28,12},{1,17},{... | collective-permute-start | bytes 811016 | tf_op jit(solution)/shard_map/ppermute | solution.py:623
  1311.1 53.6 %collective-permute-start.38 = (bf16[1,4,352,384]{3,2,1,0:T(8,128)(2,1)S(1)}, bf16[1,4,352,384]{3,2,1,0:T(8,128)(2,1)}, u32[]{:S(2)}, u32[]{:S(2)}) collective-permute-start(bf16[1,4,352,384]{3,2,1,0:T(8,128)(2,1)S(1)} %fusion.40), channel_id=1, source_target_pairs={{0,2},{1,3},{2,0},{3,1},{4,6},{5,7},{6,4},{7,5},{8,10},{9,11},{10,... | collective-permute-start | bytes 3244040 | tf_op jit(solution)/shard_map/ppermute | solution.py:623
  1366.8 13.3 collective-permute-start.39
  1366.9 15.1 %collective-permute-start.41 = (bf16[1,352,384]{2,1,0:T(8,128)(2,1)S(1)}, bf16[1,352,384]{2,1,0:T(8,128)(2,1)S(1)}, u32[]{:S(2)}, u32[]{:S(2)}) collective-permute-start(bf16[1,352,384]{2,1,0:T(8,128)(2,1)S(1)} %get-tuple-element.465), channel_id=1, source_target_pairs={{0,24},{4,28},{8,16},{12,20},{16,8},{20,12},{24,0},{28,4},{1,25},{... | collective-permute-start | bytes 811016 | tf_op jit(solution)/shard_map/ppermute | solution.py:623
  1368.7 24.7 %collective-permute-start.40 = (bf16[1,352,384]{2,1,0:T(8,128)(2,1)S(1)}, bf16[1,352,384]{2,1,0:T(8,128)(2,1)S(1)}, u32[]{:S(2)}, u32[]{:S(2)}) collective-permute-start(bf16[1,352,384]{2,1,0:T(8,128)(2,1)S(1)} %get-tuple-element.466), channel_id=1, source_target_pairs={{0,16},{4,20},{8,24},{12,28},{16,0},{20,4},{24,8},{28,12},{1,17},{... | collective-permute-start | bytes 811016 | tf_op jit(solution)/shard_map/ppermute | solution.py:623
  (190 other events, 2399.3 us)
Sparse Core Ops, SparseCore 0:
  11.7 154.0 all-gather.5
  169.4 114.7 all-gather.7
  287.9 228.5 all-gather.3
  638.0 380.3 reduce-scatter.1

commit v5 on v4

--- a/solution.py
+++ b/solution.py
@@ -327,41 +327,90 @@
     )(base, *blocks, values)
 
 
-def outer(core, left, rights, flip):
-    rows, tokens = left.shape
+def outer(place, pairs, across, got=None):
     cols = lax.axis_size("col")
+    lefts = []
+    for left, _ in pairs:
+        if not any(left is other for other in lefts):
+            lefts.append(left)
+    which = [next(i for i, l in enumerate(lefts) if l is left) for left, _ in pairs]
+    rights = [right for _, right in pairs]
+    many = len(pairs)
+    rows, tokens = lefts[0].shape
     width = rights[0].shape[0] // cols
     broad = lanes(width)
-
-    def kernel(core_ref, left_ref, *refs):
-        for index in range(len(rights)):
-            right = refs[index][...]
+    tile = rows // 4
+    chunk = tile // 2
+    flip = 1 if got is None else 0
+
+    def kernel(place_ref, *refs):
+        left_refs = refs[: len(lefts)]
+        right_refs = refs[len(lefts) : len(lefts) + many]
+        rest = refs[len(lefts) + many :]
+        for index in range(many):
+            right = right_refs[index][...]
             if broad > width:
                 right = jnp.concatenate([right, jnp.zeros((broad - width, tokens), BF)], 0)
-            part = dot(left_ref[...], right, ((1,), (1,)))
-            refs[-1][index, 0] = part.astype(BF)
-
+            part = dot(left_refs[which[index]][...], right, ((1,), (1,)))
+            if got is None:
+                rest[0][index, 0] = part.astype(BF)
+            elif not across:
+                part = (part + rest[0][index, 0].astype(F32)).astype(BF)
+
+                @pl.when(pl.program_id(0) == place_ref[2])
+                def _():
+                    rest[1][index, 0] = part.reshape(2, chunk, broad)
+
+                @pl.when(pl.program_id(0) != place_ref[2])
+                def _():
+                    rest[2][index, 0] = part.reshape(2, chunk, broad)
+            else:
+                part = part + rest[0][index, 0].astype(F32)
+                first, second = part[:chunk].astype(BF), part[chunk:].astype(BF)
+                lower = place_ref[1] == 0
+                rest[1][index, 0, 0] = jnp.where(lower, first, second)
+                rest[2][index, 0, 0] = jnp.where(lower, second, first)
+
+    whole = pl.BlockSpec((many, 1, tile, broad), lambda y, z, place: (0, y, z, 0))
+    piece = pl.BlockSpec((many, 1, 1, chunk, broad), lambda y, z, place: (0, y, z, 0, 0))
+
+    def phase(ours):
+        def index(y, z, place):
+            phase = place[2] if ours else 1 - place[2]
+            inside = (y == phase).astype(jnp.int32)
+            return (0, inside * z + (1 - inside) * 3 * (1 - phase), 0, 0, 0)
+
+        return pl.BlockSpec((many, 1, 2, chunk, broad), index)
+
+    if got is None:
+        given, out_specs = [], whole
+        out_shape = jax.ShapeDtypeStruct((many, cols // 2, rows, broad), BF)
+    else:
+        given, out_specs = [got], [piece, piece] if across else [phase(True), phase(False)]
+        shape = (many, cols // 2, 4, chunk, broad) if across else (many, 4, 2, chunk, broad)
+        out_shape = [jax.ShapeDtypeStruct(shape, BF)] * 2
     return pl.pallas_call(
         kernel,
         grid_spec=pltpu.PrefetchScalarGridSpec(
             num_scalar_prefetch=1,
-            grid=(cols // 2,),
-            in_specs=[pl.BlockSpec((rows, tokens), lambda y, core: (0, 0))]
+            grid=(cols // 2, 4),
+            in_specs=[pl.BlockSpec((tile, tokens), lambda y, z, place: (z, 0)) for _ in lefts]
             + [
-                pl.BlockSpec((width, tokens), lambda y, core: (2 * y + (core[0] ^ flip), 0))
+                pl.BlockSpec(
+                    (width, tokens), lambda y, z, place: (2 * y + (place[0] ^ flip), 0)
+                )
                 for _ in rights
-            ],
-            out_specs=pl.BlockSpec(
-                (len(rights), 1, rows, broad), lambda y, core: (0, y, 0, 0)
-            ),
+            ]
+            + [whole] * len(given),
+            out_specs=out_specs,
         ),
-        out_shape=jax.ShapeDtypeStruct((len(rights), cols // 2, rows, broad), BF),
+        out_shape=out_shape,
         cost_estimate=work(
-            rows, tokens, len(rights) * cols // 2 * width, 3 * rows * cols * width * len(rights)
+            rows, tokens, many * cols // 2 * broad, 2 * rows * cols * broad * many
         ),
         compiler_params=params(),
         name="outer",
-    )(core, left, *rights)
+    )(place, *lefts, *rights, *given)
 
 
 def expand(weight, kind, values):
@@ -590,25 +639,104 @@
     )
 
 
-def to_tokens(values, pieces, cols):
-    parts = [
-        jnp.concatenate(
-            [values[:, p.start + j * p.count : p.start + (j + 1) * p.count] for p in pieces], 1
-        )
-        for j in range(cols)
-    ]
-    got = exchange(jnp.stack(parts, 0), cols, cols)
-    return got.reshape(-1, got.shape[2])
-
-
-def to_features(values, pieces, cols):
-    got = exchange(values.reshape(cols, -1, values.shape[1]), cols, cols)
-    parts = []
+def cut_size(pieces):
+    return math.gcd(*(p.count for p in pieces), *(p.start for p in pieces))
+
+
+def locate(pieces, unit, block):
+    device = inside = None
     at = 0
     for piece in pieces:
-        parts += [got[j, :, at : at + piece.count] for j in range(cols)]
-        at += piece.count
-    return jnp.concatenate(parts, 1)
+        each = piece.count // unit
+        rest = block - piece.start // unit
+        there = (rest // each, at + rest % each)
+        if device is None:
+            device, inside = there
+        else:
+            later = (rest >= 0).astype(jnp.int32)
+            device = later * there[0] + (1 - later) * device
+            inside = later * there[1] + (1 - later) * inside
+        at += each
+    return device, inside
+
+
+def to_tokens(arrays, pieces, cols, rows):
+    width, tokens = arrays[0].shape
+    kinds = len(arrays)
+    unit = cut_size(pieces)
+    total = sum(p.count for p in pieces)
+    if unit % 128:
+        values = jnp.stack([a.reshape(-1, rows, tokens) for a in arrays], 1).astype(BF)
+        values = values.reshape(kinds * width, tokens)
+        parts = [
+            jnp.concatenate(
+                [values[:, p.start + j * p.count : p.start + (j + 1) * p.count] for p in pieces], 1
+            )
+            for j in range(cols)
+        ]
+        dealt = jnp.stack(parts, 0)
+    else:
+
+        def kernel(*refs):
+            for kind in range(kinds):
+                for at in range(0, width, rows):
+                    to = at * kinds + kind * rows
+                    refs[-1][0, to : to + rows] = refs[kind][at : at + rows].astype(BF)
+
+        def index(block):
+            device, inside = locate(pieces, unit, block)
+            return (device, 0, inside)
+
+        dealt = pl.pallas_call(
+            kernel,
+            grid=(tokens // unit,),
+            in_specs=[pl.BlockSpec((width, unit), lambda b: (0, b))] * kinds,
+            out_specs=pl.BlockSpec((1, kinds * width, unit), index),
+            out_shape=jax.ShapeDtypeStruct((cols, kinds * width, total), BF),
+            cost_estimate=pl.CostEstimate(
+                flops=0, transcendentals=0, bytes_accessed=4 * kinds * width * tokens
+            ),
+            name="deal",
+        )(*arrays)
+    got = exchange(dealt, cols, cols)
+    return got.reshape(-1, total)
+
+
+def to_features(values, pieces, cols, kinds, rows):
+    got = exchange(values.reshape(cols, -1, values.shape[1]), cols, cols)
+    unit = cut_size(pieces)
+    width = got.shape[1] // kinds
+    tokens = cols * got.shape[2]
+    if unit % 128:
+        parts = []
+        at = 0
+        for piece in pieces:
+            parts += [got[j, :, at : at + piece.count] for j in range(cols)]
+            at += piece.count
+        whole = jnp.concatenate(parts, 1).astype(F32).reshape(-1, kinds, rows, tokens)
+        return [whole[:, kind].reshape(width, tokens) for kind in range(kinds)]
+
+    def kernel(got_ref, *refs):
+        for kind in range(kinds):
+            for at in range(0, width, rows):
+                start = at * kinds + kind * rows
+                refs[kind][at : at + rows] = got_ref[0, start : start + rows].astype(F32)
+
+    def index(block):
+        device, inside = locate(pieces, unit, block)
+        return (device, 0, inside)
+
+    return pl.pallas_call(
+        kernel,
+        grid=(tokens // unit,),
+        in_specs=[pl.BlockSpec((1, kinds * width, unit), index)],
+        out_specs=[pl.BlockSpec((width, unit), lambda b: (0, b))] * kinds,
+        out_shape=[jax.ShapeDtypeStruct((width, tokens), F32)] * kinds,
+        cost_estimate=pl.CostEstimate(
+            flops=0, transcendentals=0, bytes_accessed=6 * kinds * width * tokens
+        ),
+        name="undeal",
+    )(got)
 
 
 def shared(values, axis):
@@ -690,47 +818,43 @@
 class Reduction:
     last = 4
 
-    def __init__(self, core, left, rights, across):
+    def __init__(self, place, pairs, across):
+        self.place = place
         self.across = across
-        self.many = len(rights)
-        self.stage = 0 if custom_mesh() else self.last
-        if not custom_mesh():
-            cols = lax.axis_size("col")
-            whole = jnp.stack(
-                [einsum("kt,cnt->ckn", left, r.reshape(cols, -1, r.shape[1])) for r in rights], 0
-            )
-            flat = whole.reshape(self.many, -1, whole.shape[3]).astype(BF)
-            self.state = [lax.psum_scatter(flat, DEVICES, scatter_dimension=1, tiled=True)]
+        self.pairs = pairs
+        self.width = pairs[0][1].shape[0] // lax.axis_size("col")
+        self.stage = 0
+        if custom_mesh():
+            self.state = [swap(outer(place, pairs, across), "col", 1)]
             return
-        self.width = rights[0].shape[0] // 4
-        shape = (self.many, 2, 4, 2, left.shape[0] // 8, lanes(self.width))
-        send = outer(core, left, rights, 1)
-        got = swap(send, "col", 1)
-        keep = outer(core, left, rights, 0)
-        self.state = [keep.reshape(shape), got.reshape(shape)]
-
-    def half(self, side):
-        kept, got = self.state
-        axis = (3 if kept.ndim == 6 else 2) if side else 1
-        name, bit = ("row", 1) if side else ("col", 2)
-        index = lax.axis_index("row") % 2 if side else lax.axis_index("col") // 2
-        away = add(pick(kept, axis, 1 - index), pick(got, axis, 1 - index))
-        here = add(pick(kept, axis, index), pick(got, axis, index))
-        self.state = [here, swap(away, name, bit)]
+        self.stage = self.last
+        cols = lax.axis_size("col")
+        whole = jnp.stack(
+            [einsum("kt,cnt->ckn", a, b.reshape(cols, -1, b.shape[1])) for a, b in pairs], 0
+        )
+        flat = whole.reshape(len(pairs), -1, whole.shape[3]).astype(BF)
+        self.state = [lax.psum_scatter(flat, DEVICES, scatter_dimension=1, tiled=True)]
 
     def advance(self):
+        state = self.state
         self.stage += 1
-        if self.stage <= 2:
-            self.half(self.across == (self.stage == 1))
+        if self.stage == 1:
+            here, away = outer(self.place, self.pairs, self.across, state[0])
+            self.state = [here, swap(away, "row", 1) if self.across else swap(away, "col", 2)]
+        elif self.stage == 2:
+            axis, index = (1, self.place[2]) if self.across else (2, self.place[1])
+            away = add(*(pick(a, axis, 1 - index) for a in state))
+            here = add(*(pick(a, axis, index) for a in state))
+            self.state = [here, swap(away, "col", 2) if self.across else swap(away, "row", 1)]
         elif self.stage == 3:
             level = lax.axis_index("row") // 2
-            total = add(*self.state)
+            total = add(*state)
             self.state = [pick(total, 1, level)] + [
                 swap(pick(total, 1, level ^ other), "row", 2 * other) for other in (1, 2, 3)
             ]
         else:
-            total = self.state[0].astype(F32)
-            for other in self.state[1:]:
+            total = state[0].astype(F32)
+            for other in state[1:]:
                 total = total + other.astype(F32)
             self.state = [total[..., : self.width]]
 
@@ -796,17 +920,15 @@
     keys = -(-texts // KEYPAD) * KEYPAD
     pieces = pieces_of(cols, sequences)
     starts = [sum(p.count for p in pieces[:i]) for i in range(len(pieces))]
-    core = (mine % 2).astype(jnp.int32)[None]
     place = jnp.stack([my_row // 2, my_row % 2]).astype(jnp.int32)
+    corner = jnp.stack([mine % 2, my_row % 2, mine // 2]).astype(jnp.int32)
     base = (mine if custom_mesh() else jnp.zeros_like(mine)).astype(jnp.int32)[None]
 
     def cut(values, index):
         return values[..., starts[index] : starts[index] + pieces[index].count]
 
     block_rows = depth // rows
-    split = (width // block_rows, block_rows, row_tokens)
-    both = jnp.stack([latents.reshape(split), skip_input.reshape(split)], 1)
-    both = to_tokens(both.reshape(2 * width, row_tokens), pieces, cols)
+    both = to_tokens([latents, skip_input], pieces, cols, block_rows)
 
     weights_one = gather_weights([*(self_inputs[:, i] for i in range(3)), self_output.T])
     weights_two = gather_weights(
@@ -814,7 +936,7 @@
     )
     skip_block = jnp.concatenate([skip_weight[0], skip_weight[1]], 0)
     skip_block = jnp.pad(skip_block, ((0, 0), (0, lanes(width) - width)))
-    w_skip = Gathering(skip_block, False, place).result()
+    w_skip = Gathering(skip_block, True, place).result()
     weights_hidden = gather_weights([expand_weight, reduce_weight.T])
 
     places = jnp.concatenate(
@@ -854,7 +976,9 @@
     shifting = per_token(0)
     scaling = 1.0 + per_token(1)
 
+    text = shared(jnp.pad(after(text_states, both), ((0, 0), (0, keys - texts), (0, 0))), "col")
     joined = project_blocks(base, w_skip, width, both)
+    joined, text = lax.optimization_barrier((joined, text))
     skip_normal, skip_inverse = normalize(joined)
     stream = skip_normal * gain_skip + bias_skip
     normal_one, inverse_one = normalize(stream)
@@ -870,8 +994,6 @@
     rot_query, query_pull = jax.vjp(self_piece, raw[0], query_gain)
     rot_key, key_pull = jax.vjp(self_piece, raw[1], key_gain)
     triple = [rot_query.astype(BF), rot_key.astype(BF), raw[2]]
-
-    text = shared(jnp.pad(after(text_states, raw), ((0, 0), (0, keys - texts), (0, 0))), "col")
 
     def to_heads(parts, index):
         size = pieces[index].group
@@ -887,7 +1009,7 @@
         saved_self.append((whole, kept))
         mixed_parts.append(exchange(kept[0], piece.group, cols).reshape(depth, -1))
     mixed_one = jnp.concatenate(mixed_parts, 1)
-    mixed_one, text = lax.optimization_barrier((mixed_one, text))
+    text = after(text, mixed_one)
     stream = stream + rebuild(weights_one, [3], [mixed_one], F32)
     normal_two, inverse_two = normalize(stream)
     normed_two = (normal_two * gain_cross + bias_cross).astype(BF)
@@ -920,10 +1042,8 @@
     stream = stream + rebuild(weights_two, [1], [mixed_two], F32)
     normal_three, inverse_three = normalize(stream)
     normed_three = (normal_three * gain_hidden + bias_hidden).astype(BF)
-    grad_out = to_tokens(after(out_grad, joined).astype(BF), pieces, cols)
+    grad_out = to_tokens([after(out_grad, joined)], pieces, cols, width)
     act, slopes = expand(weights_hidden, 0, normed_three)
-    output = contract(weights_hidden, 1, act, stream, BF)
-    result = to_features(output, pieces, cols).astype(F32)
 
     g_inner = expand_back(weights_hidden, 1, grad_out, slopes)
     g_normed = contract(weights_hidden, 0, g_inner, None, F32)
@@ -935,11 +1055,10 @@
     g_hidden_bias = jnp.sum(g_normed, 1)
     g_stream = grad_out.astype(F32) + norm_back(g_normed * gain_hidden, normal_three, inverse_three)
 
-    running = []
     g_low = g_stream.astype(BF)
     g_mixed = project(weights_two, [1], [g_low], [BF])[0].reshape(heads, dim, tokens)
-    r_cross = Reduction(core, g_low, [mixed_two], True)
-    running.append(r_cross)
+    r_cross = Reduction(corner, [(g_low, mixed_two)], True)
+    running = [r_cross]
     g_queries = []
     g_keys = []
     g_values = []
@@ -958,8 +1077,8 @@
         jnp.concatenate(g_values, 2).astype(BF).reshape(depth, -1),
     ]
     g_normed = rebuild(weights_two, [0], [g_craw], F32)
-    r_query = Reduction(core, normed_two, [g_craw], False)
-    r_text = Reduction(core, text, g_pair, True)
+    r_query = Reduction(corner, [(normed_two, g_craw)], False)
+    r_text = Reduction(corner, [(text, g) for g in g_pair], True)
     g_normed = tick(g_normed, running)
     running += [r_query, r_text]
     g_cross_gain = jnp.sum(g_normed * normal_two, 1)
@@ -969,7 +1088,7 @@
     g_low = g_stream.astype(BF)
     g_mixed = project(weights_one, [3], [g_low], [BF])[0].reshape(heads, dim, tokens)
     g_mixed = tick(g_mixed, running)
-    r_attn = Reduction(core, g_low, [mixed_one], False)
+    r_attn = Reduction(corner, [(g_low, mixed_one)], False)
     g_parts = []
     for index, piece in enumerate(pieces):
         whole, kept = saved_self[index]
@@ -993,8 +1112,8 @@
     ]
     g_triple = tick(g_triple, running)
     r_self = [
-        Reduction(core, normed_one, g_triple[:2], True),
-        Reduction(core, normed_one, g_triple[2:], False),
+        Reduction(corner, [(normed_one, g) for g in g_triple[:2]], True),
+        Reduction(corner, [(normed_one, g_triple[2])], False),
     ]
     g_normed = rebuild(weights_one, [0, 1, 2], g_triple, F32)
     running += r_self
@@ -1013,26 +1132,37 @@
     g_modul = jnp.sum(which[:, :, None, None] * sums[:, None], 0)
     g_modul = g_modul.reshape(sequences, 2, cols, width).transpose(2, 0, 1, 3)
     g_modul = jnp.sum(lax.all_to_all(g_modul, "col", 0, 0, tiled=True), 0).astype(BF)
-    g_modul = shared(g_modul, "row").reshape(-1, 2, width)
-    g_modulation = einsum("sd,ske->dke", embed_rows, g_modul)
     g_stream = g_stream + norm_back(g_normed * scaling, normal_one, inverse_one)
 
     g_skip_gain = jnp.sum(g_stream * skip_normal, 1)
     g_skip_bias = jnp.sum(g_stream, 1)
     g_joined = norm_back(g_stream * gain_skip, skip_normal, skip_inverse).astype(BF)
-    g_joined = tick(g_joined, running)
-    r_skip = Reduction(core, both, [g_joined], True)
+    g_joined, g_modul = lax.optimization_barrier((g_joined, g_modul))
+    r_skip = Reduction(corner, [(both, g_joined)], True)
     g_both = rebuild_blocks(base, w_skip, width, g_joined)
-    g_both = tick(g_both, [r_skip])
-    g_inputs = to_features(g_both, pieces, cols).reshape(split[0], 2, block_rows, row_tokens)
-    g_latents, g_skip = (g_inputs[:, i].reshape(width, row_tokens).astype(F32) for i in range(2))
+    late = act
+    if custom_mesh():
+        g_both, got = lax.optimization_barrier((g_both, r_skip.state[0]))
+        here, away = outer(corner, r_skip.pairs, True, got)
+        states = [r.state for r in r_self]
+        g_both, away, late, states = lax.optimization_barrier((g_both, away, late, states))
+        r_skip.stage, r_skip.state = 1, [here, swap(away, "row", 1)]
+        for beside, state in zip(r_self, states):
+            beside.state = state
+            beside.advance()
+        late = tick(late, [r_skip])
+    g_latents, g_skip = to_features(g_both, pieces, cols, 2, block_rows)
+    output = contract(weights_hidden, 1, late, stream, BF)
+    result = to_features(output, pieces, cols, 1, width)[0]
+    g_modul = shared(after(g_modul, g_skip), "row").reshape(-1, 2, width)
+    g_modulation = einsum("sd,ske->dke", embed_rows, g_modul)
 
     g_gains = jnp.stack(
         [g_skip_gain, g_skip_bias, g_cross_gain, g_cross_bias, g_hidden_gain, g_hidden_bias], 0
     )
     g_gains = g_gains.reshape(6, cols, width).transpose(1, 0, 2)
     g_head = jnp.stack([g_q_gain, g_k_gain, g_cq_gain, g_tk_gain], 0).reshape(1, -1, width)
-    g_gains = after(g_gains, g_both)
+    g_gains = after(g_gains, g_skip)
     packed = jnp.concatenate([g_gains, jnp.broadcast_to(g_head, (cols, *g_head.shape[1:]))], 1)
     packed = jnp.sum(lax.all_to_all(packed, "col", 0, 0, tiled=True), 0)
     packed = jnp.sum(shared(packed, "row"), 0)

time: 1410 us -> 1410 us (level)
  Pallas kernels: 462 us -> 543 us
  other arithmetic: 276 us -> 236 us
  local copies, waits for them, and re-layouts: 104 us -> 66.9 us
  starting transfers between devices: 167 us -> 147 us
    ppermute x50 -> x49, waiting for transfers between devices: 211 us -> 273 us  [swap(): return lax.ppermute(values, axis, [(i, i ^ bit) for i in range(size)])]
    pallas_call x14, Pallas kernels: 91.4 us -> 139 us  [outer(): pl.pallas_call(kernel, grid_spec=pltpu.PrefetchScalarGridSpec(num_scalar_...]
    all_to_all x6 -> x5, waiting for transfers between devices: 88.6 us -> 42.4 us  [shared(): lax.all_to_all(jnp.broadcast_to(values[None], (size, *values.shape)), axi...]
    convert_element_type x29 -> x17, other arithmetic: 67.6 us -> 32.2 us  [add(): return (left.astype(F32) + right.astype(F32)).astype(BF)]
    pallas_call x0 -> x4, Pallas kernels: none -> 33.9 us  [the longest x2 17.2 us: to_features(): pl.pallas_call(kernel, grid=(tokens // unit,), in_specs=[pl.BlockSpec((1,...]
    unnamed x376 -> x297, local copies, waits for them, and re-layouts: 36.5 us -> 17.7 us
    all_to_all x6 -> x5, starting transfers between devices: 35.6 us -> 18.2 us  [shared(): lax.all_to_all(jnp.broadcast_to(values[None], (size, *values.shape)), axi...]
    ppermute x50 -> x49, starting transfers between devices: 66.9 us -> 65 us  [swap(): return lax.ppermute(values, axis, [(i, i ^ bit) for i in range(size)])]
  transfers between devices with their start and end apart: 75 -> 73, of which waited for: 31 -> 23; matrix products, arithmetic and copies ran while one was open for 25% -> 20% of each run, Pallas kernels for 30% -> 35%
where the time goes in v5:
time: 1410 us; the launch traced here: 1400 us
  Pallas kernels  543 us (39%)
  waiting for transfers between devices  376 us (27%)
  other arithmetic  236 us (17%)
  starting transfers between devices  147 us (10%)
  local copies, waits for them, and re-layouts  66.9 us (5%)
  between operations  17.1 us (1%)
    ppermute x49, waiting for transfers between devices, swap(): return lax.ppermute(values, axis, [(i, i ^ bit) for i in range(size)])  273 us
    pallas_call x14, Pallas kernels, outer(): pl.pallas_call(kernel, grid_spec=pltpu.PrefetchScalarGridSpec(num_scalar_...  139 us
    pallas_call x4, Pallas kernels, attend_back(): pl.pallas_call(partial(attend_back_kernel, masked), grid=(heads // many,)...  65.5 us
    ppermute x49, starting transfers between devices, swap(): return lax.ppermute(values, axis, [(i, i ^ bit) for i in range(size)])  65 us
    pallas_call x5, Pallas kernels, project(): pl.pallas_call(kernel, grid=(cols,), in_specs=[pl.BlockSpec((1, 1, depth,...  49.6 us
    pallas_call x4, Pallas kernels, rebuild(): pl.pallas_call(kernel, grid=(4,), in_specs=[pl.BlockSpec((1, cols, tile,...  45.9 us
    pallas_call x4, Pallas kernels, attend(): pl.pallas_call(partial(attend_kernel, masked), grid=(heads // many,), in_...  45.3 us
    all_to_all x5, waiting for transfers between devices, shared(): lax.all_to_all(jnp.broadcast_to(values[None], (size, *values.shape)), axi...  42.4 us
  transfers between devices with their start and end apart: 73, of which 23 were waited for; matrix products, arithmetic and copies ran while one was open for 20% of the time, Pallas kernels for 35%

profile of v5, /device:TPU:0, one launch (start us, length us, event | category | flops | bytes accessed | tf_op | source)
XLA Modules:
  0.0 1398.4 jit_solution(5334878847814013349)
XLA Ops:
  17.9 8.7 deal.2
  36.0 15.3 %collective-permute-done.3 = bf16[2,352,384]{2,1,0:T(8,128)(2,1)S(1)} collective-permute-done((bf16[2,352,384]{2,1,0:T(8,128)(2,1)S(1)}, bf16[2,352,384]{2,1,0:T(8,128)(2,1)S(1)}, u32[]{:S(2)}, u32[]{:S(2)}) %collective-permute-start.3) | collective-permute-done | bytes 540704 | tf_op jit(solution)/shard_map/ppermute | solution.py:751
  51.3 57.4 %collective-permute-done.2 = bf16[2,352,384]{2,1,0:T(8,128)(2,1)S(1)} collective-permute-done((bf16[2,352,384]{2,1,0:T(8,128)(2,1)S(1)}, bf16[2,352,384]{2,1,0:T(8,128)(2,1)S(1)}, u32[]{:S(2)}, u32[]{:S(2)}) %collective-permute-start.2) | collective-permute-done | bytes 540704 | tf_op jit(solution)/shard_map/ppermute | solution.py:751
  111.2 78.0 %collective-permute-done.4.got_ref = bf16[4,2,352,384]{3,2,1,0:T(8,128)(2,1)} collective-permute-done((bf16[4,2,352,384]{3,2,1,0:T(8,128)(2,1)S(1)}, bf16[4,2,352,384]{3,2,1,0:T(8,128)(2,1)}, u32[]{:S(2)}, u32[]{:S(2)}) %collective-permute-start.4) | collective-permute-done | bytes 2162720 | tf_op jit(solution)/shard_map/ppermute | solution.py:751
  189.2 6.6 assemble.2
  195.9 6.8 assemble.3
  203.0 9.7 all_to_all.105
  249.3 13.0 project_blocks.1
  262.3 20.8 %all-to-all-done.1 = bf16[4,3,384,256]{2,3,1,0:T(8,128)(2,1)S(1)} async-done(((bf16[4,3,384,256]{2,3,1,0:T(8,128)(2,1)}), bf16[4,3,384,256]{2,3,1,0:T(8,128)(2,1)S(1)}, u32[]{:S(2)}, u32[]{:S(2)}) %all-to-all-start.1) | async-done | bytes 2359328 | tf_op jit(solution)/shard_map/all_to_all | solution.py:744
  298.0 15.3 %project.5 = (f32[1408,768]{1,0:T(8,128)}, f32[1408,768]{1,0:T(8,128)}, bf16[1408,768]{1,0:T(8,128)(2,1)}) custom-call(bf16[4,4,1408,352]{3,2,1,0:T(8,128)(2,1)} %bitcast.311, bf16[4,4,1408,352]{3,2,1,0:T(8,128)(2,1)} %bitcast.312, bf16[4,4,1408,352]{3,2,1,0:T(8,128)(2,1)} %bitcast.313, bf16[1408,768]{1,0:T(8,128)(2,1)} %add_convert_fusion.4.refs_3_.refs_0_), custom_call_target="tpu_custom_call" | custom-call | flops 9135194112 | bytes 8650752 | tf_op jit(solution)/shard_map/project/pallas_call | solution.py:221
  358.7 16.8 %attend.4 = (bf16[2,8,88,512]{3,2,1,0:T(8,128)(2,1)}, bf16[2,8,88,512]{3,2,1,0:T(8,128)(2,1)}, f32[8,1,1024]{2,1,0:T(1,128)}) custom-call(s32[1]{0:T(128)} %constant.278.clone.1.length_ref, bf16[2,3,8,88,512]{4,3,2,1,0:T(8,128)(2,1)} %all-to-all-done.7.q_ref.k_ref.v_ref, bf16[2,3,8,88,512]{4,3,2,1,0:T(8,128)(2,1)} %all-to-all-done.7.q_ref.k_ref.v_ref, ...), custom_call_target="tpu_custom_call" | custom-call | flops 8589934592 | bytes 5767168 | tf_op jit(solution)/shard_map/attend/pallas_call | solution.py:140
  375.5 22.7 %all-to-all-done.9.q_ref.k_ref.v_ref = bf16[4,3,4,88,256]{4,3,2,1,0:T(8,128)(2,1)S(1)} async-done(((bf16[4,3,4,88,256]{4,3,2,1,0:T(8,128)(2,1)}), bf16[4,3,4,88,256]{4,3,2,1,0:T(8,128)(2,1)S(1)}, u32[]{:S(2)}, u32[]{:S(2)}) %all-to-all-start.9) | async-done | bytes 2162720 | tf_op jit(solution)/shard_map/all_to_all | solution.py:636
  403.2 9.4 attend.5
  417.3 8.0 deal.3
  433.7 8.7 rebuild.4
  450.6 7.9 project.6
  465.5 10.6 project.7
  489.3 7.4 attend.7
  499.3 11.7 attend.6
  513.8 9.5 rebuild.5
  531.7 17.7 %all-gather.4.cloned.1.call-done = bf16[2,5632,1536]{2,1,0:T(8,128)(2,1)} async-done(((bf16[2,176,1536]{2,1,0:T(8,128)(2,1)}), bf16[2,5632,1536]{2,1,0:T(8,128)(2,1)}) %all-gather.4.cloned.1.call-update) | async-done | bytes 34603024 | tf_op jit(solution)/shard_map/all_gather | solution.py:762
  549.4 27.0 %expand.1 = (bf16[4,1536,768]{2,1,0:T(8,128)(2,1)}, bf16[4,1536,768]{2,1,0:T(8,128)(2,1)}) custom-call(bf16[2,4,1408,1536]{3,2,1,0:T(8,128)(2,1)} %bitcast.365, bf16[1408,768]{1,0:T(8,128)(2,1)} %add_convert_fusion.2.values_ref.normed_ref), custom_call_target="tpu_custom_call" | custom-call | flops 13287555072 | bytes 25952256 | tf_op jit(solution)/shard_map/expand/pallas_call | solution.py:433
  577.7 20.5 %expand_back.1.values_ref.inner_ref = bf16[4,1536,768]{2,1,0:T(8,128)(2,1)} custom-call(bf16[2,4,1408,1536]{3,2,1,0:T(8,128)(2,1)} %bitcast.366, bf16[1408,768]{1,0:T(8,128)(2,1)} %bitcast.378, bf16[4,1536,768]{2,1,0:T(8,128)(2,1)} %get-tuple-element.148.slope_ref), custom_call_target="tpu_custom_call" | custom-call | flops 13287555072 | bytes 25952256 | tf_op jit(solution)/shard_map/expand_back/pallas_call | solution.py:458
  598.2 36.4 %hidden_outer.1 = bf16[2,4,1408,1536]{3,2,1,0:T(8,128)(2,1)} custom-call(bf16[1408,768]{1,0:T(8,128)(2,1)} %bitcast.379, bf16[4,1536,768]{2,1,0:T(8,128)(2,1)} %get-tuple-element.217.values_ref.act_ref, bf16[1408,768]{1,0:T(8,128)(2,1)} %add_convert_fusion.2.values_ref.normed_ref, bf16[4,1536,768]{2,1,0:T(8,128)(2,1)} %expand_back.1.values_ref.inner_ref), custom_call_target="tpu_custom_call" | custom-call | flops 26575110144 | bytes 43253760 | tf_op jit(solution)/shard_map/hidden_outer/pallas_call | solution.py:521
  634.6 20.8 %contract.2 = f32[1408,768]{1,0:T(8,128)} custom-call(bf16[2,4,1408,1536]{3,2,1,0:T(8,128)(2,1)} %bitcast.367, bf16[4,1536,768]{2,1,0:T(8,128)(2,1)} %expand_back.1.values_ref.inner_ref), custom_call_target="tpu_custom_call" | custom-call | flops 13287555072 | bytes 25952256 | tf_op jit(solution)/shard_map/contract/pallas_call | solution.py:488
  655.5 7.1 multiply_reduce_fusion.2
  668.0 9.3 outer.14
  677.7 8.1 project.8
  690.7 9.5 attend_back.5
  700.2 15.8 %attend_back.4 = (f32[1,1,16,88,512]{4,3,2,1,0:T(8,128)}, f32[1,1,16,88,384]{4,3,2,1,0:T(8,128)}, f32[1,1,16,88,384]{4,3,2,1,0:T(8,128)}) custom-call(s32[1]{0:T(128)} %get-tuple-element.510.length_ref, bf16[1,1,16,88,512]{4,3,2,1,0:T(8,128)(2,1)} %slice_bitcast_fusion.1.q_ref, bf16[1,1,16,88,384]{4,3,2,1,0:T(8,128)(2,1)} %get-tuple-element.457.k_ref, ...), custom_call_target="tpu_custom_call" | custom-call | flops 8053063680 | bytes 12615680 | tf_op jit(solution)/shard_map/attend_back/pallas_call | solution.py:173
  716.0 9.3 outer.15
  739.8 9.5 outer.17
  762.6 8.5 rebuild.6
  771.1 9.4 outer.16
  790.4 7.2 fusion.75
  797.6 8.8 outer.20
  807.0 7.6 project.9
  829.8 9.3 outer.18
  840.8 10.1 outer.19
  856.3 25.9 %attend_back.6 = bf16[2,3,8,88,512]{4,3,2,1,0:T(8,128)(2,1)} custom-call(s32[1]{0:T(128)} %constant.278.clone.1.length_ref, bf16[2,3,8,88,512]{4,3,2,1,0:T(8,128)(2,1)} %all-to-all-done.7.q_ref.k_ref.v_ref, bf16[2,3,8,88,512]{4,3,2,1,0:T(8,128)(2,1)} %all-to-all-done.7.q_ref.k_ref.v_ref, bf16[2,3,8,88,512]{4,3,2,1,0:T(8,128)(2,1)} %all-to-all-done.7.q_ref.k_ref.v_ref, ...), custom_call_target="tpu_custom_call" | custom-call | flops 21474836480 | bytes 14417920 | tf_op jit(solution)/shard_map/attend_back/pallas_call | solution.py:173
  882.3 25.0 %collective-permute-done.16 = bf16[2,2,4,128,384]{4,3,2,1,0:T(8,128)(2,1)} collective-permute-done((bf16[2,2,4,128,384]{4,3,2,1,0:T(8,128)(2,1)}, bf16[2,2,4,128,384]{4,3,2,1,0:T(8,128)(2,1)}, u32[]{:S(2)}, u32[]{:S(2)}) %collective-permute-start.16) | collective-permute-done | bytes 1572896 | tf_op jit(solution)/shard_map/ppermute | solution.py:751
  911.7 14.3 %attend_back.7 = bf16[4,3,4,88,256]{4,3,2,1,0:T(8,128)(2,1)} custom-call(s32[1]{0:T(128)} %constant.278.clone.1.length_ref, bf16[4,3,4,88,256]{4,3,2,1,0:T(8,128)(2,1)} %copy-done.40, bf16[4,3,4,88,256]{4,3,2,1,0:T(8,128)(2,1)} %copy-done.40, bf16[4,3,4,88,256]{4,3,2,1,0:T(8,128)(2,1)} %copy-done.40, bf16[4,4,88,256]{3,2,1,0:T(8,128)(2,1)} %get-tuple-element.141.m_ref, ...), custom_call_target="tpu_custom_call" | custom-call | flops 10737418240 | bytes 7208960 | tf_op jit(solution)/shard_map/attend_back/pallas_call | solution.py:173
  958.8 9.3 outer.21
  970.1 9.9 all-to-all-done.14
  990.6 7.5 multiply_reduce_fusion.7
  1017.8 11.0 collective-permute-done.24
  1028.9 10.7 outer.22
  1039.6 8.9 outer.23
  1052.1 19.2 %rebuild.7 = f32[1408,768]{1,0:T(8,128)} custom-call(bf16[4,4,1408,352]{3,2,1,0:T(8,128)(2,1)} %bitcast.316, bf16[4,4,1408,352]{3,2,1,0:T(8,128)(2,1)} %bitcast.317, bf16[4,4,1408,352]{3,2,1,0:T(8,128)(2,1)} %bitcast.318, bf16[1408,768]{1,0:T(8,128)(2,1)} %bitcast.404, bf16[1408,768]{1,0:T(8,128)(2,1)} %bitcast.407, ...), custom_call_target="tpu_custom_call" | custom-call | flops 9135194112 | bytes 8650752 | tf_op jit(solution)/shard_map/rebuild/pallas_call | solution.py:250
  1072.9 6.3 fusion.18
  1079.2 10.8 multiply_reduce_fusion.4
  1102.1 6.0 multiply_convert_fusion.refs_4_.refs_1_
  1108.1 11.2 outer.24
  1119.8 11.5 outer.26
  1132.2 9.3 outer.27
  1143.1 13.4 rebuild_blocks.1
  1156.5 11.9 outer.25
  1168.5 12.1 collective-permute-done.31
  1208.1 44.3 %collective-permute-done.42 = bf16[1,4,176,384]{3,2,1,0:T(8,128)(2,1)} collective-permute-done((bf16[1,4,176,384]{3,2,1,0:T(8,128)(2,1)}, bf16[1,4,176,384]{3,2,1,0:T(8,128)(2,1)}, u32[]{:S(2)}, u32[]{:S(2)}) %collective-permute-start.42) | collective-permute-done | bytes 540704 | tf_op jit(solution)/shard_map/ppermute | solution.py:751
  1273.9 9.2 undeal.3
  1302.3 12.3 all-to-all-done.18
  1319.6 20.3 %contract.3 = bf16[1408,768]{1,0:T(8,128)(2,1)} custom-call(bf16[2,4,1408,1536]{3,2,1,0:T(8,128)(2,1)} %bitcast.368, bf16[4,1536,768]{2,1,0:T(8,128)(2,1)} %get-tuple-element.217.values_ref.act_ref, f32[1408,768]{1,0:T(8,128)} %copy-done.3), custom_call_target="tpu_custom_call" | custom-call | flops 13287555072 | bytes 25952256 | tf_op jit(solution)/shard_map/contract/pallas_call | solution.py:488
  1360.6 16.5 %collective-permute-done.36 = bf16[1,352,384]{2,1,0:T(8,128)(2,1)} collective-permute-done((bf16[1,352,384]{2,1,0:T(8,128)(2,1)S(1)}, bf16[1,352,384]{2,1,0:T(8,128)(2,1)}, u32[]{:S(2)}, u32[]{:S(2)}) %collective-permute-start.36) | collective-permute-done | bytes 270368 | tf_op jit(solution)/shard_map/ppermute | solution.py:751
  1380.3 8.0 undeal.2
  (670 shorter events, 440.4 us)
Async XLA Ops:
  7.2 290.8 %all-gather.6.cloned.1.call-start = ((), (), s32[]{:S(2)}) async-start(), calls=%async_computation.23 | async-start | bytes 17842176 | tf_op jit(solution)/shard_map/all_gather | solution.py:762
  10.3 440.3 %all-gather.8.cloned.1.call-start = ((), (), s32[]{:S(2)}) async-start(), calls=%async_computation.24 | async-start | bytes 17842176 | tf_op jit(solution)/shard_map/all_gather | solution.py:762
  13.6 535.8 %all-gather.4.cloned.1.call-start = ((), (), s32[]{:S(2)}) async-start(), calls=%async_computation.22 | async-start | bytes 35684352 | tf_op jit(solution)/shard_map/all_gather | solution.py:762
  14.8 16.6 %collective-permute-start = (bf16[352,384]{1,0:T(8,128)(2,1)S(1)}, bf16[352,384]{1,0:T(8,128)(2,1)S(1)}, u32[]{:S(2)}, u32[]{:S(2)}) collective-permute-start(bf16[352,384]{1,0:T(8,128)(2,1)S(1)} %get-tuple-element.496), channel_id=1, source_target_pairs={{0,2},{1,3},{2,0},{3,1},{4,6},{5,7},{6,4},{7,5},{8,10},{9,11},{10,... | collective-permute-start | bytes 811016 | tf_op jit(solution)/shard_map/ppermute | solution.py:751
  26.5 176.4 %all-to-all-start = ((bf16[4,704,768]{2,1,0:T(8,128)(2,1)}), bf16[4,704,768]{2,1,0:T(8,128)(2,1)}, u32[]{:S(2)}, u32[]{:S(2)}) async-start(bf16[4,704,768]{2,1,0:T(8,128)(2,1)} %deal.2), calls=%async_computation | async-start | bytes 8650752 | tf_op jit(solution)/shard_map/all_to_all | solution.py:636
  31.6 19.8 %collective-permute-start.3 = (bf16[2,352,384]{2,1,0:T(8,128)(2,1)S(1)}, bf16[2,352,384]{2,1,0:T(8,128)(2,1)S(1)}, u32[]{:S(2)}, u32[]{:S(2)}) collective-permute-start(bf16[2,352,384]{2,1,0:T(8,128)(2,1)S(1)} %get-tuple-element.489), channel_id=1, source_target_pairs={{0,24},{4,28},{8,16},{12,20},{16,8},{20,12},{24,0},{28,4},{1,25},{... | collective-permute-start | bytes 1622024 | tf_op jit(solution)/shard_map/ppermute | solution.py:751
  35.2 73.5 %collective-permute-start.2 = (bf16[2,352,384]{2,1,0:T(8,128)(2,1)S(1)}, bf16[2,352,384]{2,1,0:T(8,128)(2,1)S(1)}, u32[]{:S(2)}, u32[]{:S(2)}) collective-permute-start(bf16[2,352,384]{2,1,0:T(8,128)(2,1)S(1)} %get-tuple-element.489), channel_id=1, source_target_pairs={{0,16},{4,20},{8,24},{12,28},{16,0},{20,4},{24,8},{28,12},{1,17},{... | collective-permute-start | bytes 1622024 | tf_op jit(solution)/shard_map/ppermute | solution.py:751
  35.2 73.5 %collective-permute-start.1 = (bf16[2,352,384]{2,1,0:T(8,128)(2,1)S(1)}, bf16[2,352,384]{2,1,0:T(8,128)(2,1)S(1)}, u32[]{:S(2)}, u32[]{:S(2)}) collective-permute-start(bf16[2,352,384]{2,1,0:T(8,128)(2,1)S(1)} %get-tuple-element.489), channel_id=1, source_target_pairs={{0,8},{4,12},{8,0},{12,4},{16,24},{20,28},{24,16},{28,20},{1,9},{5... | collective-permute-start | bytes 1622024 | tf_op jit(solution)/shard_map/ppermute | solution.py:751
  109.1 80.1 %collective-permute-start.4 = (bf16[4,2,352,384]{3,2,1,0:T(8,128)(2,1)S(1)}, bf16[4,2,352,384]{3,2,1,0:T(8,128)(2,1)}, u32[]{:S(2)}, u32[]{:S(2)}) collective-permute-start(bf16[4,2,352,384]{3,2,1,0:T(8,128)(2,1)S(1)} %pad_maximum_fusion.3.own_ref), channel_id=1, source_target_pairs={{0,4},{4,0},{8,12},{12,8},{16,20},{20,16},{24,28},{28,24},{1,5},{5... | collective-permute-start | bytes 6488072 | tf_op jit(solution)/shard_map/ppermute | solution.py:751
  195.8 53.4 %collective-permute-start.5 = (bf16[2816,384]{1,0:T(8,128)(2,1)}, bf16[2816,384]{1,0:T(8,128)(2,1)}, u32[]{:S(2)}, u32[]{:S(2)}) collective-permute-start(bf16[2816,384]{1,0:T(8,128)(2,1)} %bitcast.428), channel_id=1, source_target_pairs={{0,1},{1,0},{2,3},{3,2},{4,5},{5,4},{6,7},{7,6},{8,9},{9,8},{10,11... | collective-permute-start | bytes 6488072 | tf_op jit(solution)/shard_map/ppermute | solution.py:751
  202.8 46.5 %collective-permute-start.6 = (bf16[2816,384]{1,0:T(8,128)(2,1)}, bf16[2816,384]{1,0:T(8,128)(2,1)}, u32[]{:S(2)}, u32[]{:S(2)}) collective-permute-start(bf16[2816,384]{1,0:T(8,128)(2,1)} %bitcast.431), channel_id=1, source_target_pairs={{0,1},{1,0},{2,3},{3,2},{4,5},{5,4},{6,7},{7,6},{8,9},{9,8},{10,11... | collective-permute-start | bytes 6488072 | tf_op jit(solution)/shard_map/ppermute | solution.py:751
  243.6 39.5 %all-to-all-start.1 = ((bf16[4,3,384,256]{2,3,1,0:T(8,128)(2,1)}), bf16[4,3,384,256]{2,3,1,0:T(8,128)(2,1)S(1)}, u32[]{:S(2)}, u32[]{:S(2)}) async-start(bf16[4,3,384,256]{2,3,1,0:T(8,128)(2,1)} %broadcast_in_dim.199), calls=%async_computation.1 | async-start | bytes 4718592 | tf_op jit(solution)/shard_map/all_to_all | solution.py:744
  355.1 43.1 %all-to-all-start.9 = ((bf16[4,3,4,88,256]{4,3,2,1,0:T(8,128)(2,1)}), bf16[4,3,4,88,256]{4,3,2,1,0:T(8,128)(2,1)S(1)}, u32[]{:S(2)}, u32[]{:S(2)}) async-start(bf16[4,3,4,88,256]{4,3,2,1,0:T(8,128)(2,1)} %pad_maximum_fusion.4), calls=%async_computation.9 | async-start | bytes 4325376 | tf_op jit(solution)/shard_map/all_to_all | solution.py:636
  399.5 13.1 all-to-all-start.8
  412.6 14.4 %all-to-all-start.10 = ((bf16[4,4,88,256]{3,2,1,0:T(8,128)(2,1)}), bf16[4,4,88,256]{3,2,1,0:T(8,128)(2,1)S(1)}, u32[]{:S(2)}, u32[]{:S(2)}) async-start(bf16[4,4,88,256]{3,2,1,0:T(8,128)(2,1)} %get-tuple-element.141.m_ref), calls=%async_computation.10 | async-start | bytes 1441792 | tf_op jit(solution)/shard_map/all_to_all | solution.py:636
  427.1 149.3 %all-to-all-start.2 = ((bf16[4,352,768]{2,1,0:T(8,128)(2,1)}), bf16[4,352,768]{2,1,0:T(8,128)(2,1)S(1)}, u32[]{:S(2)}, u32[]{:S(2)}) async-start(bf16[4,352,768]{2,1,0:T(8,128)(2,1)} %deal.3), calls=%async_computation.2 | async-start | bytes 4325376 | tf_op jit(solution)/shard_map/all_to_all | solution.py:636
  430.8 957.5 %reduce-scatter.2.cloned.1.call-start = ((), (), s32[]{:S(2)}) async-start(), calls=%async_computation.25 | async-start | bytes 35684352 | tf_op jit(solution)/shard_map/reduce_scatter | solution.py:1051
  677.3 38.7 %collective-permute-start.7 = (bf16[1,2,1408,384]{3,2,1,0:T(8,128)(2,1)}, bf16[1,2,1408,384]{3,2,1,0:T(8,128)(2,1)}, u32[]{:S(2)}, u32[]{:S(2)}) collective-permute-start(bf16[1,2,1408,384]{3,2,1,0:T(8,128)(2,1)} %outer.14), channel_id=1, source_target_pairs={{0,1},{1,0},{2,3},{3,2},{4,5},{5,4},{6,7},{7,6},{8,9},{9,8},{10,11... | collective-permute-start | bytes 6488072 | tf_op jit(solution)/shard_map/ppermute | solution.py:751
  725.3 55.4 %collective-permute-start.8 = (bf16[1,2,4,176,384]{4,3,2,1,0:T(8,128)(2,1)}, bf16[1,2,4,176,384]{4,3,2,1,0:T(8,128)(2,1)S(1)}, u32[]{:S(2)}, u32[]{:S(2)}) collective-permute-start(bf16[1,2,4,176,384]{4,3,2,1,0:T(8,128)(2,1)} %get-tuple-element.163), channel_id=1, source_target_pairs={{0,4},{4,0},{8,12},{12,8},{16,20},{20,16},{24,28},{28,24},{1,5},{5... | collective-permute-start | bytes 3244040 | tf_op jit(solution)/shard_map/ppermute | solution.py:751
  749.4 65.3 %collective-permute-start.11 = (bf16[2,2,1024,384]{3,2,1,0:T(8,128)(2,1)}, bf16[2,2,1024,384]{3,2,1,0:T(8,128)(2,1)}, u32[]{:S(2)}, u32[]{:S(2)}) collective-permute-start(bf16[2,2,1024,384]{3,2,1,0:T(8,128)(2,1)} %outer.17), channel_id=1, source_target_pairs={{0,1},{1,0},{2,3},{3,2},{4,5},{5,4},{6,7},{7,6},{8,9},{9,8},{10,11... | collective-permute-start | bytes 9437192 | tf_op jit(solution)/shard_map/ppermute | solution.py:751
  780.6 34.1 %collective-permute-start.10 = (bf16[1,2,1408,384]{3,2,1,0:T(8,128)(2,1)}, bf16[1,2,1408,384]{3,2,1,0:T(8,128)(2,1)}, u32[]{:S(2)}, u32[]{:S(2)}) collective-permute-start(bf16[1,2,1408,384]{3,2,1,0:T(8,128)(2,1)} %outer.16), channel_id=1, source_target_pairs={{0,1},{1,0},{2,3},{3,2},{4,5},{5,4},{6,7},{7,6},{8,9},{9,8},{10,11... | collective-permute-start | bytes 6488072 | tf_op jit(solution)/shard_map/ppermute | solution.py:751
  784.4 30.2 %collective-permute-start.9 = (bf16[1,4,176,384]{3,2,1,0:T(8,128)(2,1)}, bf16[1,4,176,384]{3,2,1,0:T(8,128)(2,1)S(1)}, u32[]{:S(2)}, u32[]{:S(2)}) collective-permute-start(bf16[1,4,176,384]{3,2,1,0:T(8,128)(2,1)} %get-tuple-element.452), channel_id=1, source_target_pairs={{0,2},{1,3},{2,0},{3,1},{4,6},{5,7},{6,4},{7,5},{8,10},{9,11},{10,... | collective-permute-start | bytes 1622024 | tf_op jit(solution)/shard_map/ppermute | solution.py:751
  806.4 132.6 %collective-permute-start.19 = (bf16[1,2,1408,384]{3,2,1,0:T(8,128)(2,1)}, bf16[1,2,1408,384]{3,2,1,0:T(8,128)(2,1)S(1)}, u32[]{:S(2)}, u32[]{:S(2)}) collective-permute-start(bf16[1,2,1408,384]{3,2,1,0:T(8,128)(2,1)} %outer.20), channel_id=1, source_target_pairs={{0,1},{1,0},{2,3},{3,2},{4,5},{5,4},{6,7},{7,6},{8,9},{9,8},{10,11... | collective-permute-start | bytes 6488072 | tf_op jit(solution)/shard_map/ppermute | solution.py:751
  819.3 31.6 %all-to-all-start.11 = ((bf16[2,8,88,512]{3,2,1,0:T(8,128)(2,1)}), bf16[2,8,88,512]{3,2,1,0:T(8,128)(2,1)}, u32[]{:S(2)}, u32[]{:S(2)}) async-start(bf16[2,8,88,512]{3,2,1,0:T(8,128)(2,1)} %bitcast.95), calls=%async_computation.11 | async-start | bytes 2883584 | tf_op jit(solution)/shard_map/all_to_all | solution.py:637
  824.9 30.2 %collective-permute-start.12 = (bf16[1,176,384]{2,1,0:T(8,128)(2,1)}, bf16[1,176,384]{2,1,0:T(8,128)(2,1)S(1)}, u32[]{:S(2)}, u32[]{:S(2)}) collective-permute-start(bf16[1,176,384]{2,1,0:T(8,128)(2,1)} %get-tuple-element.484), channel_id=1, source_target_pairs={{0,8},{4,12},{8,0},{12,4},{16,24},{20,28},{24,16},{28,20},{1,9},{5... | collective-permute-start | bytes 405512 | tf_op jit(solution)/shard_map/ppermute | solution.py:751
  827.4 54.8 %collective-permute-start.13 = (bf16[1,176,384]{2,1,0:T(8,128)(2,1)}, bf16[1,176,384]{2,1,0:T(8,128)(2,1)S(1)}, u32[]{:S(2)}, u32[]{:S(2)}) collective-permute-start(bf16[1,176,384]{2,1,0:T(8,128)(2,1)} %get-tuple-element.483), channel_id=1, source_target_pairs={{0,16},{4,20},{8,24},{12,28},{16,0},{20,4},{24,8},{28,12},{1,17},{... | collective-permute-start | bytes 405512 | tf_op jit(solution)/shard_map/ppermute | solution.py:751
  827.4 54.8 %collective-permute-start.14 = (bf16[1,176,384]{2,1,0:T(8,128)(2,1)}, bf16[1,176,384]{2,1,0:T(8,128)(2,1)}, u32[]{:S(2)}, u32[]{:S(2)}) collective-permute-start(bf16[1,176,384]{2,1,0:T(8,128)(2,1)} %get-tuple-element.482), channel_id=1, source_target_pairs={{0,24},{4,28},{8,16},{12,20},{16,8},{20,12},{24,0},{28,4},{1,25},{... | collective-permute-start | bytes 405512 | tf_op jit(solution)/shard_map/ppermute | solution.py:751
  839.1 43.2 %collective-permute-start.15 = (bf16[1,4,2,176,384]{4,3,2,1,0:T(8,128)(2,1)}, bf16[1,4,2,176,384]{4,3,2,1,0:T(8,128)(2,1)S(1)}, u32[]{:S(2)}, u32[]{:S(2)}) collective-permute-start(bf16[1,4,2,176,384]{4,3,2,1,0:T(8,128)(2,1)} %get-tuple-element.178), channel_id=1, source_target_pairs={{0,2},{1,3},{2,0},{3,1},{4,6},{5,7},{6,4},{7,5},{8,10},{9,11},{10,... | collective-permute-start | bytes 3244040 | tf_op jit(solution)/shard_map/ppermute | solution.py:751
  850.9 60.8 %all-to-all-start.13 = ((bf16[4,4,88,256]{3,2,1,0:T(8,128)(2,1)}), bf16[4,4,88,256]{3,2,1,0:T(8,128)(2,1)}, u32[]{:S(2)}, u32[]{:S(2)}) async-start(bf16[4,4,88,256]{3,2,1,0:T(8,128)(2,1)} %bitcast.102), calls=%async_computation.13 | async-start | bytes 1441792 | tf_op jit(solution)/shard_map/all_to_all | solution.py:636
  855.1 52.1 %collective-permute-start.16 = (bf16[2,2,4,128,384]{4,3,2,1,0:T(8,128)(2,1)}, bf16[2,2,4,128,384]{4,3,2,1,0:T(8,128)(2,1)}, u32[]{:S(2)}, u32[]{:S(2)}) collective-permute-start(bf16[2,2,4,128,384]{4,3,2,1,0:T(8,128)(2,1)} %get-tuple-element.181), channel_id=1, source_target_pairs={{0,4},{4,0},{8,12},{12,8},{16,20},{20,16},{24,28},{28,24},{1,5},{5... | collective-permute-start | bytes 4718600 | tf_op jit(solution)/shard_map/ppermute | solution.py:751
  909.7 31.0 %collective-permute-start.18 = (bf16[2,4,128,384]{3,2,1,0:T(8,128)(2,1)}, bf16[2,4,128,384]{3,2,1,0:T(8,128)(2,1)}, u32[]{:S(2)}, u32[]{:S(2)}) collective-permute-start(bf16[2,4,128,384]{3,2,1,0:T(8,128)(2,1)} %fusion.27), channel_id=1, source_target_pairs={{0,2},{1,3},{2,0},{3,1},{4,6},{5,7},{6,4},{7,5},{8,10},{9,11},{10,... | collective-permute-start | bytes 2359304 | tf_op jit(solution)/shard_map/ppermute | solution.py:751
  928.0 12.6 collective-permute-start.17
  928.9 11.7 all-to-all-start.12
  940.6 39.3 %all-to-all-start.14 = ((bf16[4,3,4,88,256]{4,3,2,1,0:T(8,128)(2,1)}), bf16[4,3,4,88,256]{4,3,2,1,0:T(8,128)(2,1)}, u32[]{:S(2)}, u32[]{:S(2)}) async-start(bf16[4,3,4,88,256]{4,3,2,1,0:T(8,128)(2,1)} %attend_back.7), calls=%async_computation.14 | async-start | bytes 4325376 | tf_op jit(solution)/shard_map/all_to_all | solution.py:636
  951.3 61.2 %collective-permute-start.20 = (bf16[1,176,384]{2,1,0:T(8,128)(2,1)}, bf16[1,176,384]{2,1,0:T(8,128)(2,1)}, u32[]{:S(2)}, u32[]{:S(2)}) collective-permute-start(bf16[1,176,384]{2,1,0:T(8,128)(2,1)} %get-tuple-element.480), channel_id=1, source_target_pairs={{0,8},{4,12},{8,0},{12,4},{16,24},{20,28},{24,16},{28,20},{1,9},{5... | collective-permute-start | bytes 405512 | tf_op jit(solution)/shard_map/ppermute | solution.py:751
  952.9 59.6 %collective-permute-start.21 = (bf16[1,176,384]{2,1,0:T(8,128)(2,1)}, bf16[1,176,384]{2,1,0:T(8,128)(2,1)}, u32[]{:S(2)}, u32[]{:S(2)}) collective-permute-start(bf16[1,176,384]{2,1,0:T(8,128)(2,1)} %get-tuple-element.479), channel_id=1, source_target_pairs={{0,16},{4,20},{8,24},{12,28},{16,0},{20,4},{24,8},{28,12},{1,17},{... | collective-permute-start | bytes 405512 | tf_op jit(solution)/shard_map/ppermute | solution.py:751
  952.9 64.9 %collective-permute-start.22 = (bf16[1,176,384]{2,1,0:T(8,128)(2,1)}, bf16[1,176,384]{2,1,0:T(8,128)(2,1)}, u32[]{:S(2)}, u32[]{:S(2)}) collective-permute-start(bf16[1,176,384]{2,1,0:T(8,128)(2,1)} %get-tuple-element.478), channel_id=1, source_target_pairs={{0,24},{4,28},{8,16},{12,20},{16,8},{20,12},{24,0},{28,4},{1,25},{... | collective-permute-start | bytes 405512 | tf_op jit(solution)/shard_map/ppermute | solution.py:751
  958.0 59.8 %collective-permute-start.23 = (bf16[2,128,384]{2,1,0:T(8,128)(2,1)}, bf16[2,128,384]{2,1,0:T(8,128)(2,1)S(1)}, u32[]{:S(2)}, u32[]{:S(2)}) collective-permute-start(bf16[2,128,384]{2,1,0:T(8,128)(2,1)} %get-tuple-element.468), channel_id=1, source_target_pairs={{0,8},{4,12},{8,0},{12,4},{16,24},{20,28},{24,16},{28,20},{1,9},{5... | collective-permute-start | bytes 589832 | tf_op jit(solution)/shard_map/ppermute | solution.py:751
  968.1 60.7 %collective-permute-start.26 = (bf16[1,4,2,176,384]{4,3,2,1,0:T(8,128)(2,1)}, bf16[1,4,2,176,384]{4,3,2,1,0:T(8,128)(2,1)}, u32[]{:S(2)}, u32[]{:S(2)}) collective-permute-start(bf16[1,4,2,176,384]{4,3,2,1,0:T(8,128)(2,1)} %get-tuple-element.196), channel_id=1, source_target_pairs={{0,2},{1,3},{2,0},{3,1},{4,6},{5,7},{6,4},{7,5},{8,10},{9,11},{10,... | collective-permute-start | bytes 3244040 | tf_op jit(solution)/shard_map/ppermute | solution.py:751
  1012.5 16.4 %collective-permute-start.24 = (bf16[2,128,384]{2,1,0:T(8,128)(2,1)S(1)}, bf16[2,128,384]{2,1,0:T(8,128)(2,1)S(1)}, u32[]{:S(2)}, u32[]{:S(2)}) collective-permute-start(bf16[2,128,384]{2,1,0:T(8,128)(2,1)S(1)} %copy-done.85), channel_id=1, source_target_pairs={{0,16},{4,20},{8,24},{12,28},{16,0},{20,4},{24,8},{28,12},{1,17},{... | collective-permute-start | bytes 589832 | tf_op jit(solution)/shard_map/ppermute | solution.py:751
  1012.5 16.4 %collective-permute-start.25 = (bf16[2,128,384]{2,1,0:T(8,128)(2,1)S(1)}, bf16[2,128,384]{2,1,0:T(8,128)(2,1)}, u32[]{:S(2)}, u32[]{:S(2)}) collective-permute-start(bf16[2,128,384]{2,1,0:T(8,128)(2,1)S(1)} %copy-done.84), channel_id=1, source_target_pairs={{0,24},{4,28},{8,16},{12,20},{16,8},{20,12},{24,0},{28,4},{1,25},{... | collective-permute-start | bytes 589832 | tf_op jit(solution)/shard_map/ppermute | solution.py:751
  1039.6 33.2 %collective-permute-start.28 = (bf16[2,2,1408,384]{3,2,1,0:T(8,128)(2,1)}, bf16[2,2,1408,384]{3,2,1,0:T(8,128)(2,1)}, u32[]{:S(2)}, u32[]{:S(2)}) collective-permute-start(bf16[2,2,1408,384]{3,2,1,0:T(8,128)(2,1)} %outer.22), channel_id=1, source_target_pairs={{0,1},{1,0},{2,3},{3,2},{4,5},{5,4},{6,7},{7,6},{8,9},{9,8},{10,11... | collective-permute-start | bytes 12976136 | tf_op jit(solution)/shard_map/ppermute | solution.py:751
  1048.5 24.3 %collective-permute-start.29 = (bf16[1,2,1408,384]{3,2,1,0:T(8,128)(2,1)}, bf16[1,2,1408,384]{3,2,1,0:T(8,128)(2,1)S(1)}, u32[]{:S(2)}, u32[]{:S(2)}) collective-permute-start(bf16[1,2,1408,384]{3,2,1,0:T(8,128)(2,1)} %outer.23), channel_id=1, source_target_pairs={{0,1},{1,0},{2,3},{3,2},{4,5},{5,4},{6,7},{7,6},{8,9},{9,8},{10,11... | collective-permute-start | bytes 6488072 | tf_op jit(solution)/shard_map/ppermute | solution.py:751
  1050.9 21.8 %collective-permute-start.27 = (bf16[1,4,176,384]{3,2,1,0:T(8,128)(2,1)}, bf16[1,4,176,384]{3,2,1,0:T(8,128)(2,1)S(1)}, u32[]{:S(2)}, u32[]{:S(2)}) collective-permute-start(bf16[1,4,176,384]{3,2,1,0:T(8,128)(2,1)} %fusion.33), channel_id=1, source_target_pairs={{0,4},{4,0},{8,12},{12,8},{16,20},{20,16},{24,28},{28,24},{1,5},{5... | collective-permute-start | bytes 1622024 | tf_op jit(solution)/shard_map/ppermute | solution.py:751
  1119.3 37.2 %collective-permute-start.30 = (bf16[1,2,2816,384]{3,2,1,0:T(8,128)(2,1)}, bf16[1,2,2816,384]{3,2,1,0:T(8,128)(2,1)}, u32[]{:S(2)}, u32[]{:S(2)}) collective-permute-start(bf16[1,2,2816,384]{3,2,1,0:T(8,128)(2,1)} %outer.24), channel_id=1, source_target_pairs={{0,1},{1,0},{2,3},{3,2},{4,5},{5,4},{6,7},{7,6},{8,9},{9,8},{10,11... | collective-permute-start | bytes 12976136 | tf_op jit(solution)/shard_map/ppermute | solution.py:751
  1131.2 49.3 %collective-permute-start.31 = (bf16[2,2,4,176,384]{4,3,2,1,0:T(8,128)(2,1)}, bf16[2,2,4,176,384]{4,3,2,1,0:T(8,128)(2,1)}, u32[]{:S(2)}, u32[]{:S(2)}) collective-permute-start(bf16[2,2,4,176,384]{4,3,2,1,0:T(8,128)(2,1)} %get-tuple-element.210), channel_id=1, source_target_pairs={{0,4},{4,0},{8,12},{12,8},{16,20},{20,16},{24,28},{28,24},{1,5},{5... | collective-permute-start | bytes 6488072 | tf_op jit(solution)/shard_map/ppermute | solution.py:751
  1141.5 27.0 %collective-permute-start.32 = (bf16[1,4,2,176,384]{4,3,2,1,0:T(8,128)(2,1)}, bf16[1,4,2,176,384]{4,3,2,1,0:T(8,128)(2,1)}, u32[]{:S(2)}, u32[]{:S(2)}) collective-permute-start(bf16[1,4,2,176,384]{4,3,2,1,0:T(8,128)(2,1)} %get-tuple-element.213), channel_id=1, source_target_pairs={{0,2},{1,3},{2,0},{3,1},{4,6},{5,7},{6,4},{7,5},{8,10},{9,11},{10,... | collective-permute-start | bytes 3244040 | tf_op jit(solution)/shard_map/ppermute | solution.py:751
  1180.6 93.3 %all-to-all-start.17 = ((bf16[4,704,768]{2,1,0:T(8,128)(2,1)}), bf16[4,704,768]{2,1,0:T(8,128)(2,1)}, u32[]{:S(2)}, u32[]{:S(2)}) async-start(bf16[4,704,768]{2,1,0:T(8,128)(2,1)} %bitcast.420), calls=%async_computation.17 | async-start | bytes 8650752 | tf_op jit(solution)/shard_map/all_to_all | solution.py:636
  1191.0 102.0 %collective-permute-start.33 = (bf16[1,2,4,352,384]{4,3,2,1,0:T(8,128)(2,1)}, bf16[1,2,4,352,384]{4,3,2,1,0:T(8,128)(2,1)}, u32[]{:S(2)}, u32[]{:S(2)}) collective-permute-start(bf16[1,2,4,352,384]{4,3,2,1,0:T(8,128)(2,1)} %get-tuple-element.216), channel_id=1, source_target_pairs={{0,4},{4,0},{8,12},{12,8},{16,20},{20,16},{24,28},{28,24},{1,5},{5... | collective-permute-start | bytes 6488072 | tf_op jit(solution)/shard_map/ppermute | solution.py:751
  1194.2 58.2 %collective-permute-start.42 = (bf16[1,4,176,384]{3,2,1,0:T(8,128)(2,1)}, bf16[1,4,176,384]{3,2,1,0:T(8,128)(2,1)}, u32[]{:S(2)}, u32[]{:S(2)}) collective-permute-start(bf16[1,4,176,384]{3,2,1,0:T(8,128)(2,1)} %fusion.35), channel_id=1, source_target_pairs={{0,4},{4,0},{8,12},{12,8},{16,20},{20,16},{24,28},{28,24},{1,5},{5... | collective-permute-start | bytes 1622024 | tf_op jit(solution)/shard_map/ppermute | solution.py:751
  1198.8 73.0 %collective-permute-start.38 = (bf16[2,4,176,384]{3,2,1,0:T(8,128)(2,1)}, bf16[2,4,176,384]{3,2,1,0:T(8,128)(2,1)S(1)}, u32[]{:S(2)}, u32[]{:S(2)}) collective-permute-start(bf16[2,4,176,384]{3,2,1,0:T(8,128)(2,1)} %fusion.24), channel_id=1, source_target_pairs={{0,2},{1,3},{2,0},{3,1},{4,6},{5,7},{6,4},{7,5},{8,10},{9,11},{10,... | collective-permute-start | bytes 3244040 | tf_op jit(solution)/shard_map/ppermute | solution.py:751
  1202.1 55.6 %collective-permute-start.48 = (bf16[1,176,384]{2,1,0:T(8,128)(2,1)S(1)}, bf16[1,176,384]{2,1,0:T(8,128)(2,1)S(1)}, u32[]{:S(2)}, u32[]{:S(2)}) collective-permute-start(bf16[1,176,384]{2,1,0:T(8,128)(2,1)S(1)} %get-tuple-element.471), channel_id=1, source_target_pairs={{0,24},{4,28},{8,16},{12,20},{16,8},{20,12},{24,0},{28,4},{1,25},{... | collective-permute-start | bytes 405512 | tf_op jit(solution)/shard_map/ppermute | solution.py:751
  1202.2 56.8 %collective-permute-start.47 = (bf16[1,176,384]{2,1,0:T(8,128)(2,1)S(1)}, bf16[1,176,384]{2,1,0:T(8,128)(2,1)S(1)}, u32[]{:S(2)}, u32[]{:S(2)}) collective-permute-start(bf16[1,176,384]{2,1,0:T(8,128)(2,1)S(1)} %get-tuple-element.472), channel_id=1, source_target_pairs={{0,16},{4,20},{8,24},{12,28},{16,0},{20,4},{24,8},{28,12},{1,17},{... | collective-permute-start | bytes 405512 | tf_op jit(solution)/shard_map/ppermute | solution.py:751
  1258.9 12.1 collective-permute-start.44
  1259.4 11.6 collective-permute-start.43
  1288.6 55.1 %collective-permute-start.41 = (bf16[2,176,384]{2,1,0:T(8,128)(2,1)}, bf16[2,176,384]{2,1,0:T(8,128)(2,1)}, u32[]{:S(2)}, u32[]{:S(2)}) collective-permute-start(bf16[2,176,384]{2,1,0:T(8,128)(2,1)} %get-tuple-element.459), channel_id=1, source_target_pairs={{0,24},{4,28},{8,16},{12,20},{16,8},{20,12},{24,0},{28,4},{1,25},{... | collective-permute-start | bytes 811016 | tf_op jit(solution)/shard_map/ppermute | solution.py:751
  1289.8 53.9 %collective-permute-start.40 = (bf16[2,176,384]{2,1,0:T(8,128)(2,1)}, bf16[2,176,384]{2,1,0:T(8,128)(2,1)}, u32[]{:S(2)}, u32[]{:S(2)}) collective-permute-start(bf16[2,176,384]{2,1,0:T(8,128)(2,1)} %get-tuple-element.460), channel_id=1, source_target_pairs={{0,16},{4,20},{8,24},{12,28},{16,0},{20,4},{24,8},{28,12},{1,17},{... | collective-permute-start | bytes 811016 | tf_op jit(solution)/shard_map/ppermute | solution.py:751
  1289.8 53.9 %collective-permute-start.39 = (bf16[2,176,384]{2,1,0:T(8,128)(2,1)}, bf16[2,176,384]{2,1,0:T(8,128)(2,1)}, u32[]{:S(2)}, u32[]{:S(2)}) collective-permute-start(bf16[2,176,384]{2,1,0:T(8,128)(2,1)} %get-tuple-element.458), channel_id=1, source_target_pairs={{0,8},{4,12},{8,0},{12,4},{16,24},{20,28},{24,16},{28,20},{1,9},{5... | collective-permute-start | bytes 811016 | tf_op jit(solution)/shard_map/ppermute | solution.py:751
  1293.7 20.9 %all-to-all-start.18 = ((bf16[8,3,2,352]{3,2,1,0:T(2,128)(2,1)}), bf16[8,3,2,352]{3,2,1,0:T(2,128)(2,1)S(1)}, u32[]{:S(2)}, u32[]{:S(2)}) async-start(bf16[8,3,2,352]{3,2,1,0:T(2,128)(2,1)} %broadcast_in_dim.235), calls=%async_computation.18 | async-start | bytes 73728 | tf_op jit(solution)/shard_map/all_to_all | solution.py:744
  1299.5 46.4 %collective-permute-start.34 = (bf16[1,4,352,384]{3,2,1,0:T(8,128)(2,1)}, bf16[1,4,352,384]{3,2,1,0:T(8,128)(2,1)}, u32[]{:S(2)}, u32[]{:S(2)}) collective-permute-start(bf16[1,4,352,384]{3,2,1,0:T(8,128)(2,1)} %fusion.22), channel_id=1, source_target_pairs={{0,2},{1,3},{2,0},{3,1},{4,6},{5,7},{6,4},{7,5},{8,10},{9,11},{10,... | collective-permute-start | bytes 3244040 | tf_op jit(solution)/shard_map/ppermute | solution.py:751
  1315.2 24.7 %all-to-all-start.20 = ((f32[8,7,352]{2,1,0:T(8,128)}), f32[8,7,352]{2,1,0:T(8,128)S(1)}, u32[]{:S(2)}, u32[]{:S(2)}) async-start(f32[8,7,352]{2,1,0:T(8,128)} %broadcast_in_dim.238), calls=%async_computation.21 | async-start | bytes 196608 | tf_op jit(solution)/shard_map/all_to_all | solution.py:744
  1339.9 39.1 %all-to-all-start.16 = ((bf16[4,352,768]{2,1,0:T(8,128)(2,1)}), bf16[4,352,768]{2,1,0:T(8,128)(2,1)S(1)}, u32[]{:S(2)}, u32[]{:S(2)}) async-start(bf16[4,352,768]{2,1,0:T(8,128)(2,1)} %bitcast.409), calls=%async_computation.16 | async-start | bytes 4325376 | tf_op jit(solution)/shard_map/all_to_all | solution.py:636
  1352.9 24.2 %collective-permute-start.36 = (bf16[1,352,384]{2,1,0:T(8,128)(2,1)S(1)}, bf16[1,352,384]{2,1,0:T(8,128)(2,1)}, u32[]{:S(2)}, u32[]{:S(2)}) collective-permute-start(bf16[1,352,384]{2,1,0:T(8,128)(2,1)S(1)} %get-tuple-element.464), channel_id=1, source_target_pairs={{0,16},{4,20},{8,24},{12,28},{16,0},{20,4},{24,8},{28,12},{1,17},{... | collective-permute-start | bytes 811016 | tf_op jit(solution)/shard_map/ppermute | solution.py:751
  1352.9 24.2 %collective-permute-start.35 = (bf16[1,352,384]{2,1,0:T(8,128)(2,1)S(1)}, bf16[1,352,384]{2,1,0:T(8,128)(2,1)}, u32[]{:S(2)}, u32[]{:S(2)}) collective-permute-start(bf16[1,352,384]{2,1,0:T(8,128)(2,1)S(1)} %get-tuple-element.462), channel_id=1, source_target_pairs={{0,8},{4,12},{8,0},{12,4},{16,24},{20,28},{24,16},{28,20},{1,9},{5... | collective-permute-start | bytes 811016 | tf_op jit(solution)/shard_map/ppermute | solution.py:751
  (155 other events, 2866.5 us)
Sparse Core Ops, SparseCore 0:
  11.7 189.4 all-gather.5
  204.9 121.6 all-gather.7
  330.3 219.0 all-gather.3
  634.8 358.0 reduce-scatter.1

commit v6 on v5

--- a/solution.py
+++ b/solution.py
@@ -339,8 +339,7 @@
     rows, tokens = lefts[0].shape
     width = rights[0].shape[0] // cols
     broad = lanes(width)
-    tile = rows // 4
-    chunk = tile // 2
+    chunk = rows // 8
     flip = 1 if got is None else 0
 
     def kernel(place_ref, *refs):
@@ -359,46 +358,43 @@
 
                 @pl.when(pl.program_id(0) == place_ref[2])
                 def _():
-                    rest[1][index, 0] = part.reshape(2, chunk, broad)
+                    rest[1][index] = part.reshape(4, 2, chunk, broad)
 
                 @pl.when(pl.program_id(0) != place_ref[2])
                 def _():
-                    rest[2][index, 0] = part.reshape(2, chunk, broad)
+                    rest[2][index] = part.reshape(4, 2, chunk, broad)
             else:
-                part = part + rest[0][index, 0].astype(F32)
-                first, second = part[:chunk].astype(BF), part[chunk:].astype(BF)
-                lower = place_ref[1] == 0
-                rest[1][index, 0, 0] = jnp.where(lower, first, second)
-                rest[2][index, 0, 0] = jnp.where(lower, second, first)
-
-    whole = pl.BlockSpec((many, 1, tile, broad), lambda y, z, place: (0, y, z, 0))
-    piece = pl.BlockSpec((many, 1, 1, chunk, broad), lambda y, z, place: (0, y, z, 0, 0))
-
-    def phase(ours):
-        def index(y, z, place):
-            phase = place[2] if ours else 1 - place[2]
-            inside = (y == phase).astype(jnp.int32)
-            return (0, inside * z + (1 - inside) * 3 * (1 - phase), 0, 0, 0)
-
-        return pl.BlockSpec((many, 1, 2, chunk, broad), index)
-
+                part = (part + rest[0][index, 0].astype(F32)).astype(BF)
+                part = part.reshape(4, 2, chunk, broad)
+
+                @pl.when(place_ref[1] == 0)
+                def _():
+                    rest[1][index, 0] = part[:, 0]
+                    rest[2][index, 0] = part[:, 1]
+
+                @pl.when(place_ref[1] != 0)
+                def _():
+                    rest[1][index, 0] = part[:, 1]
+                    rest[2][index, 0] = part[:, 0]
+
+    whole = pl.BlockSpec((many, 1, rows, broad), lambda y, place: (0, y, 0, 0))
+    piece = pl.BlockSpec((many, 1, 4, chunk, broad), lambda y, place: (0, y, 0, 0, 0))
+    all_rows = pl.BlockSpec((many, 4, 2, chunk, broad), lambda y, place: (0, 0, 0, 0, 0))
     if got is None:
         given, out_specs = [], whole
         out_shape = jax.ShapeDtypeStruct((many, cols // 2, rows, broad), BF)
     else:
-        given, out_specs = [got], [piece, piece] if across else [phase(True), phase(False)]
+        given, out_specs = [got], [piece, piece] if across else [all_rows, all_rows]
         shape = (many, cols // 2, 4, chunk, broad) if across else (many, 4, 2, chunk, broad)
         out_shape = [jax.ShapeDtypeStruct(shape, BF)] * 2
     return pl.pallas_call(
         kernel,
         grid_spec=pltpu.PrefetchScalarGridSpec(
             num_scalar_prefetch=1,
-            grid=(cols // 2, 4),
-            in_specs=[pl.BlockSpec((tile, tokens), lambda y, z, place: (z, 0)) for _ in lefts]
+            grid=(cols // 2,),
+            in_specs=[pl.BlockSpec((rows, tokens), lambda y, place: (0, 0)) for _ in lefts]
             + [
-                pl.BlockSpec(
-                    (width, tokens), lambda y, z, place: (2 * y + (place[0] ^ flip), 0)
-                )
+                pl.BlockSpec((width, tokens), lambda y, place: (2 * y + (place[0] ^ flip), 0))
                 for _ in rights
             ]
             + [whole] * len(given),
@@ -930,13 +926,18 @@
     block_rows = depth // rows
     both = to_tokens([latents, skip_input], pieces, cols, block_rows)
 
-    weights_one = gather_weights([*(self_inputs[:, i] for i in range(3)), self_output.T])
-    weights_two = gather_weights(
-        [cross_query, cross_output.T, cross_keyvalue[:, 0], cross_keyvalue[:, 1]]
+    weights = gather_weights(
+        [
+            *(self_inputs[:, i] for i in range(3)),
+            self_output.T,
+            cross_query,
+            cross_output.T,
+            *(cross_keyvalue[:, i] for i in range(2)),
+        ]
     )
     skip_block = jnp.concatenate([skip_weight[0], skip_weight[1]], 0)
     skip_block = jnp.pad(skip_block, ((0, 0), (0, lanes(width) - width)))
-    w_skip = Gathering(skip_block, True, place).result()
+    w_skip = Gathering(skip_block, False, place).result()
     weights_hidden = gather_weights([expand_weight, reduce_weight.T])
 
     places = jnp.concatenate(
@@ -977,13 +978,13 @@
     scaling = 1.0 + per_token(1)
 
     text = shared(jnp.pad(after(text_states, both), ((0, 0), (0, keys - texts), (0, 0))), "col")
+    both, text = lax.optimization_barrier((both, text))
     joined = project_blocks(base, w_skip, width, both)
-    joined, text = lax.optimization_barrier((joined, text))
     skip_normal, skip_inverse = normalize(joined)
     stream = skip_normal * gain_skip + bias_skip
     normal_one, inverse_one = normalize(stream)
     normed_one = (normal_one * scaling + shifting).astype(BF)
-    raw = project(weights_one, [0, 1, 2], [normed_one], [F32, F32, BF])
+    raw = project(weights, [0, 1, 2], [normed_one], [F32, F32, BF])
     raw = [r.reshape(heads, dim, tokens) for r in raw]
     cosine, sine = rope_tables(places, dim)
 
@@ -1010,10 +1011,10 @@
         mixed_parts.append(exchange(kept[0], piece.group, cols).reshape(depth, -1))
     mixed_one = jnp.concatenate(mixed_parts, 1)
     text = after(text, mixed_one)
-    stream = stream + rebuild(weights_one, [3], [mixed_one], F32)
+    stream = stream + rebuild(weights, [3], [mixed_one], F32)
     normal_two, inverse_two = normalize(stream)
     normed_two = (normal_two * gain_cross + bias_cross).astype(BF)
-    raw_cross = project(weights_two, [0], [normed_two], [F32])[0].reshape(heads, dim, tokens)
+    raw_cross = project(weights, [4], [normed_two], [F32])[0].reshape(heads, dim, tokens)
     norm_query, cross_pull = jax.vjp(head_norm, raw_cross, cross_query_gain)
     text = jnp.concatenate(
         [lax.dynamic_index_in_dim(text, p.sequence, 1, False) for p in pieces], 1
@@ -1023,7 +1024,7 @@
     text_wide = jnp.pad(
         text.reshape(rows, text_rows, -1), ((0, 0), (0, block_rows - text_rows), (0, 0))
     ).reshape(depth, -1)
-    raw_text, value_two = project(weights_two, [2, 3], [text_wide], [F32, BF])
+    raw_text, value_two = project(weights, [6, 7], [text_wide], [F32, BF])
     norm_key, text_pull = jax.vjp(head_norm, raw_text.reshape(heads, dim, -1), text_key_gain)
     query_two = norm_query.astype(BF)
     key_two = norm_key.astype(BF)
@@ -1039,7 +1040,7 @@
         saved_cross.append((inputs, kept))
         mixed_parts.append(kept[0].reshape(depth, -1))
     mixed_two = jnp.concatenate(mixed_parts, 1)
-    stream = stream + rebuild(weights_two, [1], [mixed_two], F32)
+    stream = stream + rebuild(weights, [5], [mixed_two], F32)
     normal_three, inverse_three = normalize(stream)
     normed_three = (normal_three * gain_hidden + bias_hidden).astype(BF)
     grad_out = to_tokens([after(out_grad, joined)], pieces, cols, width)
@@ -1056,7 +1057,7 @@
     g_stream = grad_out.astype(F32) + norm_back(g_normed * gain_hidden, normal_three, inverse_three)
 
     g_low = g_stream.astype(BF)
-    g_mixed = project(weights_two, [1], [g_low], [BF])[0].reshape(heads, dim, tokens)
+    g_mixed = project(weights, [5], [g_low], [BF])[0].reshape(heads, dim, tokens)
     r_cross = Reduction(corner, [(g_low, mixed_two)], True)
     running = [r_cross]
     g_queries = []
@@ -1076,7 +1077,7 @@
         g_raw_text.astype(BF).reshape(depth, -1),
         jnp.concatenate(g_values, 2).astype(BF).reshape(depth, -1),
     ]
-    g_normed = rebuild(weights_two, [0], [g_craw], F32)
+    g_normed = rebuild(weights, [4], [g_craw], F32)
     r_query = Reduction(corner, [(normed_two, g_craw)], False)
     r_text = Reduction(corner, [(text, g) for g in g_pair], True)
     g_normed = tick(g_normed, running)
@@ -1086,7 +1087,7 @@
     g_stream = g_stream + norm_back(g_normed * gain_cross, normal_two, inverse_two)
 
     g_low = g_stream.astype(BF)
-    g_mixed = project(weights_one, [3], [g_low], [BF])[0].reshape(heads, dim, tokens)
+    g_mixed = project(weights, [3], [g_low], [BF])[0].reshape(heads, dim, tokens)
     g_mixed = tick(g_mixed, running)
     r_attn = Reduction(corner, [(g_low, mixed_one)], False)
     g_parts = []
@@ -1098,7 +1099,7 @@
         part = attend_back(
             none, whole, whole, whole, (0, 1, 2), kept, grad, False, 2, True
         )
-        part = tick(part, running)
+        part = tick(part, [r_cross, r_query] if index == 0 else running)
         if index == 0:
             running.append(r_attn)
         g_parts.append(exchange(part, piece.group, cols))
@@ -1115,7 +1116,7 @@
         Reduction(corner, [(normed_one, g) for g in g_triple[:2]], True),
         Reduction(corner, [(normed_one, g_triple[2])], False),
     ]
-    g_normed = rebuild(weights_one, [0, 1, 2], g_triple, F32)
+    g_normed = rebuild(weights, [0, 1, 2], g_triple, F32)
     running += r_self
     g_normed = tick(g_normed, running)
     crossed = g_normed * normal_one
@@ -1140,21 +1141,29 @@
     g_joined, g_modul = lax.optimization_barrier((g_joined, g_modul))
     r_skip = Reduction(corner, [(both, g_joined)], True)
     g_both = rebuild_blocks(base, w_skip, width, g_joined)
-    late = act
     if custom_mesh():
-        g_both, got = lax.optimization_barrier((g_both, r_skip.state[0]))
+        states = [r.state for r in r_self]
+        g_both, got, states = lax.optimization_barrier((g_both, r_skip.state[0], states))
         here, away = outer(corner, r_skip.pairs, True, got)
-        states = [r.state for r in r_self]
-        g_both, away, late, states = lax.optimization_barrier((g_both, away, late, states))
+        g_both, away, act, states = lax.optimization_barrier((g_both, away, act, states))
         r_skip.stage, r_skip.state = 1, [here, swap(away, "row", 1)]
         for beside, state in zip(r_self, states):
             beside.state = state
             beside.advance()
-        late = tick(late, [r_skip])
-    g_latents, g_skip = to_features(g_both, pieces, cols, 2, block_rows)
-    output = contract(weights_hidden, 1, late, stream, BF)
+        g_latents, g_skip = to_features(g_both, pieces, cols, 2, block_rows)
+        output = contract(weights_hidden, 1, act, stream, BF)
+        output = tick(output, [r_skip])
+        states = [r.state for r in r_self]
+        states, here = lax.optimization_barrier((states, r_skip.state[0]))
+        r_skip.state[0] = here
+        for beside, state in zip(r_self, states):
+            beside.state = state
+            beside.advance()
+    else:
+        g_latents, g_skip = to_features(g_both, pieces, cols, 2, block_rows)
+        output = contract(weights_hidden, 1, act, stream, BF)
     result = to_features(output, pieces, cols, 1, width)[0]
-    g_modul = shared(after(g_modul, g_skip), "row").reshape(-1, 2, width)
+    g_modul = shared(after(g_modul, result), "row").reshape(-1, 2, width)
     g_modulation = einsum("sd,ske->dke", embed_rows, g_modul)
 
     g_gains = jnp.stack(
@@ -1162,7 +1171,7 @@
     )
     g_gains = g_gains.reshape(6, cols, width).transpose(1, 0, 2)
     g_head = jnp.stack([g_q_gain, g_k_gain, g_cq_gain, g_tk_gain], 0).reshape(1, -1, width)
-    g_gains = after(g_gains, g_skip)
+    g_gains = after(g_gains, result)
     packed = jnp.concatenate([g_gains, jnp.broadcast_to(g_head, (cols, *g_head.shape[1:]))], 1)
     packed = jnp.sum(lax.all_to_all(packed, "col", 0, 0, tiled=True), 0)
     packed = jnp.sum(shared(packed, "row"), 0)

time: 1410 us -> 1430 us (1.014)
  waiting for transfers between devices: 376 us -> 429 us
  Pallas kernels: 543 us -> 513 us
  other arithmetic: 236 us -> 220 us
    all_to_all x5 -> x6, waiting for transfers between devices: 42.4 us -> 86.9 us  [shared(): lax.all_to_all(jnp.broadcast_to(values[None], (size, *values.shape)), axi...]
    pallas_call x14, Pallas kernels: 139 us -> 109 us  [outer(): pl.pallas_call(kernel, grid_spec=pltpu.PrefetchScalarGridSpec(num_scalar_...]
    all_to_all x8, waiting for transfers between devices: 34.3 us -> 50.4 us  [exchange(): return lax.all_to_all(values, 'col', 0, 0, tiled=True)]
    ppermute x49 -> x50, starting transfers between devices: 65 us -> 71.7 us  [swap(): return lax.ppermute(values, axis, [(i, i ^ bit) for i in range(size)])]
    convert_element_type x17 -> x19, other arithmetic: 32.2 us -> 26.7 us  [add(): return (left.astype(F32) + right.astype(F32)).astype(BF)]
    ppermute x49 -> x50, waiting for transfers between devices: 273 us -> 270 us  [swap(): return lax.ppermute(values, axis, [(i, i ^ bit) for i in range(size)])]
  transfers between devices with their start and end apart: 73 -> 74, of which waited for: 23 -> 27; matrix products, arithmetic and copies ran while one was open for 20% -> 19% of each run, Pallas kernels for 35% -> 31%
where the time goes in v6:
time: 1430 us; the launch traced here: 1420 us
  Pallas kernels  513 us (36%)
  waiting for transfers between devices  429 us (30%)
  other arithmetic  220 us (15%)
  starting transfers between devices  158 us (11%)
  local copies, waits for them, and re-layouts  79 us (6%)
  between operations  16.7 us (1%)
    ppermute x50, waiting for transfers between devices, swap(): return lax.ppermute(values, axis, [(i, i ^ bit) for i in range(size)])  270 us
    pallas_call x14, Pallas kernels, outer(): pl.pallas_call(kernel, grid_spec=pltpu.PrefetchScalarGridSpec(num_scalar_...  109 us
    all_to_all x6, waiting for transfers between devices, shared(): lax.all_to_all(jnp.broadcast_to(values[None], (size, *values.shape)), axi...  86.9 us
    ppermute x50, starting transfers between devices, swap(): return lax.ppermute(values, axis, [(i, i ^ bit) for i in range(size)])  71.7 us
    pallas_call x4, Pallas kernels, attend_back(): pl.pallas_call(partial(attend_back_kernel, masked), grid=(heads // many,)...  66 us
    all_to_all x8, waiting for transfers between devices, exchange(): return lax.all_to_all(values, 'col', 0, 0, tiled=True)  50.4 us
    pallas_call x5, Pallas kernels, project(): pl.pallas_call(kernel, grid=(cols,), in_specs=[pl.BlockSpec((1, 1, depth,...  49.4 us
    pallas_call x4, Pallas kernels, attend(): pl.pallas_call(partial(attend_kernel, masked), grid=(heads // many,), in_...  45.2 us
  transfers between devices with their start and end apart: 74, of which 27 were waited for; matrix products, arithmetic and copies ran while one was open for 19% of the time, Pallas kernels for 31%

profile of v6, /device:TPU:0, one launch (start us, length us, event | category | flops | bytes accessed | tf_op | source)
XLA Modules:
  0.0 1418.0 jit_solution(15203128265382049760)
XLA Ops:
  17.5 8.6 deal.2
  37.2 12.4 collective-permute-done.2
  49.6 28.2 %collective-permute-done.1 = bf16[352,384]{1,0:T(8,128)(2,1)S(1)} collective-permute-done((bf16[352,384]{1,0:T(8,128)(2,1)S(1)}, bf16[352,384]{1,0:T(8,128)(2,1)S(1)}, u32[]{:S(2)}, u32[]{:S(2)}) %collective-permute-start.1) | collective-permute-done | bytes 270368 | tf_op jit(solution)/shard_map/ppermute | solution.py:747
  81.0 41.6 %collective-permute-done.5.own_ref = bf16[4,352,384]{2,1,0:T(8,128)(2,1)S(1)} collective-permute-done((bf16[4,352,384]{2,1,0:T(8,128)(2,1)S(1)}, bf16[4,352,384]{2,1,0:T(8,128)(2,1)S(1)}, u32[]{:S(2)}, u32[]{:S(2)}) %collective-permute-start.5) | collective-permute-done | bytes 1081376 | tf_op jit(solution)/shard_map/ppermute | solution.py:747
  129.3 29.4 %all-to-all-done.3 = bf16[8,3,352]{2,1,0:T(4,128)(2,1)S(1)} async-done(((bf16[8,3,352]{2,1,0:T(4,128)(2,1)}), bf16[8,3,352]{2,1,0:T(4,128)(2,1)S(1)}, u32[]{:S(2)}, u32[]{:S(2)}) %all-to-all-start.3) | async-done | bytes 16928 | tf_op jit(solution)/shard_map/all_to_all | solution.py:740
  165.3 7.0 assemble.2
  186.1 8.3 all-to-all-done.5
  213.8 42.7 %all-to-all-done.1 = bf16[4,3,384,256]{2,3,1,0:T(8,128)(2,1)S(1)} async-done(((bf16[4,3,384,256]{2,3,1,0:T(8,128)(2,1)}), bf16[4,3,384,256]{2,3,1,0:T(8,128)(2,1)S(1)}, u32[]{:S(2)}, u32[]{:S(2)}) %all-to-all-start.1) | async-done | bytes 2359328 | tf_op jit(solution)/shard_map/all_to_all | solution.py:740
  256.5 13.8 project_blocks.1
  286.7 15.0 %project.5 = (f32[1408,768]{1,0:T(8,128)}, f32[1408,768]{1,0:T(8,128)}, bf16[1408,768]{1,0:T(8,128)(2,1)}) custom-call(bf16[8,4,1408,352]{3,2,1,0:T(8,128)(2,1)} %bitcast.301, bf16[8,4,1408,352]{3,2,1,0:T(8,128)(2,1)} %bitcast.302, bf16[8,4,1408,352]{3,2,1,0:T(8,128)(2,1)} %bitcast.303, bf16[1408,768]{1,0:T(8,128)(2,1)} %add_convert_fusion.4.refs_3_.refs_0_), custom_call_target="tpu_custom_call" | custom-call | flops 9135194112 | bytes 8650752 | tf_op jit(solution)/shard_map/project/pallas_call | solution.py:221
  345.9 16.8 %attend.4 = (bf16[2,8,88,512]{3,2,1,0:T(8,128)(2,1)}, bf16[2,8,88,512]{3,2,1,0:T(8,128)(2,1)}, f32[8,1,1024]{2,1,0:T(1,128)}) custom-call(s32[1]{0:T(128)} %constant.278.clone.1.length_ref, bf16[2,3,8,88,512]{4,3,2,1,0:T(8,128)(2,1)} %all-to-all-done.7.q_ref.k_ref.v_ref, bf16[2,3,8,88,512]{4,3,2,1,0:T(8,128)(2,1)} %all-to-all-done.7.q_ref.k_ref.v_ref, ...), custom_call_target="tpu_custom_call" | custom-call | flops 8589934592 | bytes 5767168 | tf_op jit(solution)/shard_map/attend/pallas_call | solution.py:140
  362.7 10.7 all-to-all-done.9.q_ref.k_ref.v_ref
  378.4 9.4 attend.5
  392.6 8.1 deal.3
  400.6 9.7 all-to-all-done.10
  416.8 8.7 rebuild.4
  433.8 7.9 project.6
  448.7 10.6 project.7
  472.7 7.4 attend.7
  482.7 11.7 attend.6
  497.1 8.9 rebuild.5
  514.4 7.8 all-gather.3.cloned.1.call-done
  522.2 27.1 %expand.1 = (bf16[4,1536,768]{2,1,0:T(8,128)(2,1)}, bf16[4,1536,768]{2,1,0:T(8,128)(2,1)}) custom-call(bf16[2,4,1408,1536]{3,2,1,0:T(8,128)(2,1)} %bitcast.353, bf16[1408,768]{1,0:T(8,128)(2,1)} %add_convert_fusion.2.values_ref.normed_ref), custom_call_target="tpu_custom_call" | custom-call | flops 13287555072 | bytes 25952256 | tf_op jit(solution)/shard_map/expand/pallas_call | solution.py:429
  550.6 20.5 %expand_back.1.values_ref.inner_ref = bf16[4,1536,768]{2,1,0:T(8,128)(2,1)} custom-call(bf16[2,4,1408,1536]{3,2,1,0:T(8,128)(2,1)} %bitcast.354, bf16[1408,768]{1,0:T(8,128)(2,1)} %bitcast.368, bf16[4,1536,768]{2,1,0:T(8,128)(2,1)} %get-tuple-element.157.slope_ref), custom_call_target="tpu_custom_call" | custom-call | flops 13287555072 | bytes 25952256 | tf_op jit(solution)/shard_map/expand_back/pallas_call | solution.py:454
  571.1 20.3 %contract.2 = f32[1408,768]{1,0:T(8,128)} custom-call(bf16[2,4,1408,1536]{3,2,1,0:T(8,128)(2,1)} %bitcast.355, bf16[4,1536,768]{2,1,0:T(8,128)(2,1)} %expand_back.1.values_ref.inner_ref), custom_call_target="tpu_custom_call" | custom-call | flops 13287555072 | bytes 25952256 | tf_op jit(solution)/shard_map/contract/pallas_call | solution.py:484
  597.1 36.0 %hidden_outer.1 = bf16[2,4,1408,1536]{3,2,1,0:T(8,128)(2,1)} custom-call(bf16[1408,768]{1,0:T(8,128)(2,1)} %bitcast.369, bf16[4,1536,768]{2,1,0:T(8,128)(2,1)} %get-tuple-element.227.values_ref.act_ref, bf16[1408,768]{1,0:T(8,128)(2,1)} %add_convert_fusion.2.values_ref.normed_ref, bf16[4,1536,768]{2,1,0:T(8,128)(2,1)} %expand_back.1.values_ref.inner_ref), custom_call_target="tpu_custom_call" | custom-call | flops 26575110144 | bytes 43253760 | tf_op jit(solution)/shard_map/hidden_outer/pallas_call | solution.py:517
  648.1 8.1 project.8
  661.2 9.9 attend_back.5
  671.0 15.9 %attend_back.4 = (f32[1,1,16,88,512]{4,3,2,1,0:T(8,128)}, f32[1,1,16,88,384]{4,3,2,1,0:T(8,128)}, f32[1,1,16,88,384]{4,3,2,1,0:T(8,128)}) custom-call(s32[1]{0:T(128)} %get-tuple-element.525.length_ref, bf16[1,1,16,88,512]{4,3,2,1,0:T(8,128)(2,1)} %slice_bitcast_fusion.1.q_ref, bf16[1,1,16,88,384]{4,3,2,1,0:T(8,128)(2,1)} %get-tuple-element.477.k_ref, ...), custom_call_target="tpu_custom_call" | custom-call | flops 8053063680 | bytes 12615680 | tf_op jit(solution)/shard_map/attend_back/pallas_call | solution.py:173
  686.9 7.0 outer.15
  710.0 7.4 outer.17
  730.4 8.5 rebuild.6
  755.6 7.4 fusion.71
  769.1 7.7 project.9
  791.5 7.0 outer.18
  800.6 8.5 outer.19
  814.5 26.0 %attend_back.6 = bf16[2,3,8,88,512]{4,3,2,1,0:T(8,128)(2,1)} custom-call(s32[1]{0:T(128)} %constant.278.clone.1.length_ref, bf16[2,3,8,88,512]{4,3,2,1,0:T(8,128)(2,1)} %all-to-all-done.7.q_ref.k_ref.v_ref, bf16[2,3,8,88,512]{4,3,2,1,0:T(8,128)(2,1)} %all-to-all-done.7.q_ref.k_ref.v_ref, bf16[2,3,8,88,512]{4,3,2,1,0:T(8,128)(2,1)} %all-to-all-done.7.q_ref.k_ref.v_ref, ...), custom_call_target="tpu_custom_call" | custom-call | flops 21474836480 | bytes 14417920 | tf_op jit(solution)/shard_map/attend_back/pallas_call | solution.py:173
  849.1 14.2 %attend_back.7 = bf16[4,3,4,88,256]{4,3,2,1,0:T(8,128)(2,1)} custom-call(s32[1]{0:T(128)} %constant.278.clone.1.length_ref, bf16[4,3,4,88,256]{4,3,2,1,0:T(8,128)(2,1)} %copy-done.39, bf16[4,3,4,88,256]{4,3,2,1,0:T(8,128)(2,1)} %copy-done.39, bf16[4,3,4,88,256]{4,3,2,1,0:T(8,128)(2,1)} %copy-done.39, bf16[4,4,88,256]{3,2,1,0:T(8,128)(2,1)} %get-tuple-element.150.m_ref, ...), custom_call_target="tpu_custom_call" | custom-call | flops 10737418240 | bytes 7208960 | tf_op jit(solution)/shard_map/attend_back/pallas_call | solution.py:173
  871.0 15.2 %collective-permute-done.17 = bf16[1,4,176,384]{3,2,1,0:T(8,128)(2,1)} collective-permute-done((bf16[1,4,176,384]{3,2,1,0:T(8,128)(2,1)}, bf16[1,4,176,384]{3,2,1,0:T(8,128)(2,1)}, u32[]{:S(2)}, u32[]{:S(2)}) %collective-permute-start.17) | collective-permute-done | bytes 540704 | tf_op jit(solution)/shard_map/ppermute | solution.py:747
  905.6 7.0 outer.21
  915.2 10.4 all-to-all-done.14
  936.5 7.7 multiply_reduce_fusion.7
  960.3 22.8 %collective-permute-done.24 = bf16[1,4,2,176,384]{4,3,2,1,0:T(8,128)(2,1)} collective-permute-done((bf16[1,4,2,176,384]{4,3,2,1,0:T(8,128)(2,1)}, bf16[1,4,2,176,384]{4,3,2,1,0:T(8,128)(2,1)}, u32[]{:S(2)}, u32[]{:S(2)}) %collective-permute-start.24) | collective-permute-done | bytes 1081376 | tf_op jit(solution)/shard_map/ppermute | solution.py:747
  983.1 9.3 outer.22
  1005.3 19.0 %rebuild.7 = f32[1408,768]{1,0:T(8,128)} custom-call(bf16[8,4,1408,352]{3,2,1,0:T(8,128)(2,1)} %bitcast.312, bf16[8,4,1408,352]{3,2,1,0:T(8,128)(2,1)} %bitcast.313, bf16[8,4,1408,352]{3,2,1,0:T(8,128)(2,1)} %bitcast.314, bf16[1408,768]{1,0:T(8,128)(2,1)} %bitcast.394, bf16[1408,768]{1,0:T(8,128)(2,1)} %bitcast.397, ...), custom_call_target="tpu_custom_call" | custom-call | flops 9135194112 | bytes 8650752 | tf_op jit(solution)/shard_map/rebuild/pallas_call | solution.py:250
  1030.2 11.5 collective-permute-done.26
  1048.8 10.9 multiply_reduce_fusion.4
  1074.4 9.3 outer.24
  1084.2 10.4 outer.25
  1095.9 7.0 outer.26
  1104.6 13.4 rebuild_blocks.1
  1117.9 11.0 collective-permute-done.33
  1129.0 14.9 %collective-permute-done.32 = bf16[2,2,4,176,384]{4,3,2,1,0:T(8,128)(2,1)S(1)} collective-permute-done((bf16[2,2,4,176,384]{4,3,2,1,0:T(8,128)(2,1)}, bf16[2,2,4,176,384]{4,3,2,1,0:T(8,128)(2,1)S(1)}, u32[]{:S(2)}, u32[]{:S(2)}) %collective-permute-start.32) | collective-permute-done | bytes 2162720 | tf_op jit(solution)/shard_map/ppermute | solution.py:747
  1143.9 10.7 outer.27
  1155.8 20.3 %contract.3 = bf16[1408,768]{1,0:T(8,128)(2,1)} custom-call(bf16[2,4,1408,1536]{3,2,1,0:T(8,128)(2,1)} %bitcast.356, bf16[4,1536,768]{2,1,0:T(8,128)(2,1)} %get-tuple-element.227.values_ref.act_ref, f32[1408,768]{1,0:T(8,128)} %copy-done.3), custom_call_target="tpu_custom_call" | custom-call | flops 13287555072 | bytes 25952256 | tf_op jit(solution)/shard_map/contract/pallas_call | solution.py:484
  1176.1 26.9 %collective-permute-done.34 = bf16[1,2,4,352,384]{4,3,2,1,0:T(8,128)(2,1)} collective-permute-done((bf16[1,2,4,352,384]{4,3,2,1,0:T(8,128)(2,1)}, bf16[1,2,4,352,384]{4,3,2,1,0:T(8,128)(2,1)}, u32[]{:S(2)}, u32[]{:S(2)}) %collective-permute-start.34) | collective-permute-done | bytes 2162720 | tf_op jit(solution)/shard_map/ppermute | solution.py:747
  1219.0 14.1 all-to-all-done.16.got_ref
  1253.5 8.9 collective-permute-done.36
  1262.4 50.1 %collective-permute-done.35 = bf16[2,4,176,384]{3,2,1,0:T(8,128)(2,1)S(1)} collective-permute-done((bf16[2,4,176,384]{3,2,1,0:T(8,128)(2,1)S(1)}, bf16[2,4,176,384]{3,2,1,0:T(8,128)(2,1)S(1)}, u32[]{:S(2)}, u32[]{:S(2)}) %collective-permute-start.35) | collective-permute-done | bytes 1081376 | tf_op jit(solution)/shard_map/ppermute | solution.py:747
  1320.7 6.7 collective-permute-start.42
  1327.3 9.7 collective-permute-done.45
  1346.3 16.9 %collective-permute-done.42 = bf16[2,176,384]{2,1,0:T(8,128)(2,1)S(1)} collective-permute-done((bf16[2,176,384]{2,1,0:T(8,128)(2,1)S(1)}, bf16[2,176,384]{2,1,0:T(8,128)(2,1)S(1)}, u32[]{:S(2)}, u32[]{:S(2)}) %collective-permute-start.42) | collective-permute-done | bytes 270368 | tf_op jit(solution)/shard_map/ppermute | solution.py:747
  1363.3 8.0 undeal.2
  1376.2 9.0 undeal.3
  (679 shorter events, 483.8 us)
Async XLA Ops:
  7.2 279.5 %all-gather.5.cloned.1.call-start = ((), (), s32[]{:S(2)}) async-start(), calls=%async_computation.23 | async-start | bytes 35684352 | tf_op jit(solution)/shard_map/all_gather | solution.py:758
  15.2 507.0 %all-gather.3.cloned.1.call-start = ((), (), s32[]{:S(2)}) async-start(), calls=%async_computation.22 | async-start | bytes 35684352 | tf_op jit(solution)/shard_map/all_gather | solution.py:758
  26.1 97.9 %all-to-all-start = ((bf16[4,704,768]{2,1,0:T(8,128)(2,1)}), bf16[4,704,768]{2,1,0:T(8,128)(2,1)}, u32[]{:S(2)}, u32[]{:S(2)}) async-start(bf16[4,704,768]{2,1,0:T(8,128)(2,1)} %deal.2), calls=%async_computation | async-start | bytes 8650752 | tf_op jit(solution)/shard_map/all_to_all | solution.py:632
  31.4 18.2 %collective-permute-start.2 = (bf16[352,384]{1,0:T(8,128)(2,1)S(1)}, bf16[352,384]{1,0:T(8,128)(2,1)S(1)}, u32[]{:S(2)}, u32[]{:S(2)}) collective-permute-start(bf16[352,384]{1,0:T(8,128)(2,1)S(1)} %get-tuple-element.511), channel_id=1, source_target_pairs={{0,24},{4,28},{8,16},{12,20},{16,8},{20,12},{24,0},{28,4},{1,25},{... | collective-permute-start | bytes 811016 | tf_op jit(solution)/shard_map/ppermute | solution.py:747
  36.5 41.3 %collective-permute-start.1 = (bf16[352,384]{1,0:T(8,128)(2,1)S(1)}, bf16[352,384]{1,0:T(8,128)(2,1)S(1)}, u32[]{:S(2)}, u32[]{:S(2)}) collective-permute-start(bf16[352,384]{1,0:T(8,128)(2,1)S(1)} %get-tuple-element.511), channel_id=1, source_target_pairs={{0,16},{4,20},{8,24},{12,28},{16,0},{20,4},{24,8},{28,12},{1,17},{... | collective-permute-start | bytes 811016 | tf_op jit(solution)/shard_map/ppermute | solution.py:747
  36.5 41.3 %collective-permute-start = (bf16[352,384]{1,0:T(8,128)(2,1)S(1)}, bf16[352,384]{1,0:T(8,128)(2,1)S(1)}, u32[]{:S(2)}, u32[]{:S(2)}) collective-permute-start(bf16[352,384]{1,0:T(8,128)(2,1)S(1)} %get-tuple-element.511), channel_id=1, source_target_pairs={{0,8},{4,12},{8,0},{12,4},{16,24},{20,28},{24,16},{28,20},{1,9},{5... | collective-permute-start | bytes 811016 | tf_op jit(solution)/shard_map/ppermute | solution.py:747
  78.0 44.6 %collective-permute-start.5 = (bf16[4,352,384]{2,1,0:T(8,128)(2,1)S(1)}, bf16[4,352,384]{2,1,0:T(8,128)(2,1)S(1)}, u32[]{:S(2)}, u32[]{:S(2)}) collective-permute-start(bf16[4,352,384]{2,1,0:T(8,128)(2,1)S(1)} %pad_maximum_fusion.12.own_ref), channel_id=1, source_target_pairs={{0,2},{1,3},{2,0},{3,1},{4,6},{5,7},{6,4},{7,5},{8,10},{9,11},{10,... | collective-permute-start | bytes 3244040 | tf_op jit(solution)/shard_map/ppermute | solution.py:747
  79.5 85.8 %collective-permute-start.3 = (bf16[4,352,384]{2,1,0:T(8,128)(2,1)S(1)}, bf16[4,352,384]{2,1,0:T(8,128)(2,1)}, u32[]{:S(2)}, u32[]{:S(2)}) collective-permute-start(bf16[4,352,384]{2,1,0:T(8,128)(2,1)S(1)} %pad_maximum_fusion.12.own_ref), channel_id=1, source_target_pairs={{0,4},{4,0},{8,12},{12,8},{16,20},{20,16},{24,28},{28,24},{1,5},{5... | collective-permute-start | bytes 3244040 | tf_op jit(solution)/shard_map/ppermute | solution.py:747
  122.5 50.2 %collective-permute-start.6 = (bf16[4,352,384]{2,1,0:T(8,128)(2,1)S(1)}, bf16[4,352,384]{2,1,0:T(8,128)(2,1)S(1)}, u32[]{:S(2)}, u32[]{:S(2)}) collective-permute-start(bf16[4,352,384]{2,1,0:T(8,128)(2,1)S(1)} %collective-permute-done.5.own_ref), channel_id=1, source_target_pairs={{0,4},{4,0},{8,12},{12,8},{16,20},{20,16},{24,28},{28,24},{1,5},{5... | collective-permute-start | bytes 3244040 | tf_op jit(solution)/shard_map/ppermute | solution.py:747
  124.7 34.1 %all-to-all-start.3 = ((bf16[8,3,352]{2,1,0:T(4,128)(2,1)}), bf16[8,3,352]{2,1,0:T(4,128)(2,1)S(1)}, u32[]{:S(2)}, u32[]{:S(2)}) async-start(bf16[8,3,352]{2,1,0:T(4,128)(2,1)} %broadcast_in_dim.200), calls=%async_computation.3 | async-start | bytes 49152 | tf_op jit(solution)/shard_map/all_to_all | solution.py:740
  160.7 19.6 %all-to-all-start.4 = ((bf16[4,24,352]{2,1,0:T(8,128)(2,1)}), bf16[4,24,352]{2,1,0:T(8,128)(2,1)}, u32[]{:S(2)}, u32[]{:S(2)}) async-start(bf16[4,24,352]{2,1,0:T(8,128)(2,1)} %broadcast_in_dim.202), calls=%async_computation.4 | async-start | bytes 147456 | tf_op jit(solution)/shard_map/all_to_all | solution.py:740
  172.2 84.2 %collective-permute-start.4 = (bf16[2816,384]{1,0:T(8,128)(2,1)}, bf16[2816,384]{1,0:T(8,128)(2,1)}, u32[]{:S(2)}, u32[]{:S(2)}) collective-permute-start(bf16[2816,384]{1,0:T(8,128)(2,1)} %bitcast.422), channel_id=1, source_target_pairs={{0,1},{1,0},{2,3},{3,2},{4,5},{5,4},{6,7},{7,6},{8,9},{9,8},{10,11... | collective-permute-start | bytes 6488072 | tf_op jit(solution)/shard_map/ppermute | solution.py:747
  180.3 76.2 %collective-permute-start.7 = (bf16[2816,384]{1,0:T(8,128)(2,1)}, bf16[2816,384]{1,0:T(8,128)(2,1)}, u32[]{:S(2)}, u32[]{:S(2)}) collective-permute-start(bf16[2816,384]{1,0:T(8,128)(2,1)} %bitcast.425), channel_id=1, source_target_pairs={{0,1},{1,0},{2,3},{3,2},{4,5},{5,4},{6,7},{7,6},{8,9},{9,8},{10,11... | collective-permute-start | bytes 6488072 | tf_op jit(solution)/shard_map/ppermute | solution.py:747
  205.9 50.6 %all-to-all-start.1 = ((bf16[4,3,384,256]{2,3,1,0:T(8,128)(2,1)}), bf16[4,3,384,256]{2,3,1,0:T(8,128)(2,1)S(1)}, u32[]{:S(2)}, u32[]{:S(2)}) async-start(bf16[4,3,384,256]{2,3,1,0:T(8,128)(2,1)} %broadcast_in_dim.199), calls=%async_computation.1 | async-start | bytes 4718592 | tf_op jit(solution)/shard_map/all_to_all | solution.py:740
  342.3 31.1 %all-to-all-start.9 = ((bf16[4,3,4,88,256]{4,3,2,1,0:T(8,128)(2,1)}), bf16[4,3,4,88,256]{4,3,2,1,0:T(8,128)(2,1)S(1)}, u32[]{:S(2)}, u32[]{:S(2)}) async-start(bf16[4,3,4,88,256]{4,3,2,1,0:T(8,128)(2,1)} %pad_maximum_fusion.3), calls=%async_computation.9 | async-start | bytes 4325376 | tf_op jit(solution)/shard_map/all_to_all | solution.py:632
  387.8 22.6 %all-to-all-start.10 = ((bf16[4,4,88,256]{3,2,1,0:T(8,128)(2,1)}), bf16[4,4,88,256]{3,2,1,0:T(8,128)(2,1)S(1)}, u32[]{:S(2)}, u32[]{:S(2)}) async-start(bf16[4,4,88,256]{3,2,1,0:T(8,128)(2,1)} %get-tuple-element.150.m_ref), calls=%async_computation.10 | async-start | bytes 1441792 | tf_op jit(solution)/shard_map/all_to_all | solution.py:632
  410.3 138.9 %all-to-all-start.2 = ((bf16[4,352,768]{2,1,0:T(8,128)(2,1)}), bf16[4,352,768]{2,1,0:T(8,128)(2,1)S(1)}, u32[]{:S(2)}, u32[]{:S(2)}) async-start(bf16[4,352,768]{2,1,0:T(8,128)(2,1)} %deal.3), calls=%async_computation.2 | async-start | bytes 4325376 | tf_op jit(solution)/shard_map/all_to_all | solution.py:632
  414.0 994.3 %reduce-scatter.2.cloned.1.call-start = ((), (), s32[]{:S(2)}) async-start(), calls=%async_computation.24 | async-start | bytes 35684352 | tf_op jit(solution)/shard_map/reduce_scatter | solution.py:1052
  647.5 39.4 %collective-permute-start.8 = (bf16[1,2,1408,384]{3,2,1,0:T(8,128)(2,1)}, bf16[1,2,1408,384]{3,2,1,0:T(8,128)(2,1)}, u32[]{:S(2)}, u32[]{:S(2)}) collective-permute-start(bf16[1,2,1408,384]{3,2,1,0:T(8,128)(2,1)} %outer.14), channel_id=1, source_target_pairs={{0,1},{1,0},{2,3},{3,2},{4,5},{5,4},{6,7},{7,6},{8,9},{9,8},{10,11... | collective-permute-start | bytes 6488072 | tf_op jit(solution)/shard_map/ppermute | solution.py:747
  693.9 51.7 %collective-permute-start.9 = (bf16[1,2,4,176,384]{4,3,2,1,0:T(8,128)(2,1)}, bf16[1,2,4,176,384]{4,3,2,1,0:T(8,128)(2,1)S(1)}, u32[]{:S(2)}, u32[]{:S(2)}) collective-permute-start(bf16[1,2,4,176,384]{4,3,2,1,0:T(8,128)(2,1)} %get-tuple-element.172), channel_id=1, source_target_pairs={{0,4},{4,0},{8,12},{12,8},{16,20},{20,16},{24,28},{28,24},{1,5},{5... | collective-permute-start | bytes 3244040 | tf_op jit(solution)/shard_map/ppermute | solution.py:747
  717.4 59.4 %collective-permute-start.12 = (bf16[2,2,1024,384]{3,2,1,0:T(8,128)(2,1)}, bf16[2,2,1024,384]{3,2,1,0:T(8,128)(2,1)}, u32[]{:S(2)}, u32[]{:S(2)}) collective-permute-start(bf16[2,2,1024,384]{3,2,1,0:T(8,128)(2,1)} %outer.17), channel_id=1, source_target_pairs={{0,1},{1,0},{2,3},{3,2},{4,5},{5,4},{6,7},{7,6},{8,9},{9,8},{10,11... | collective-permute-start | bytes 9437192 | tf_op jit(solution)/shard_map/ppermute | solution.py:747
  745.3 31.5 %collective-permute-start.11 = (bf16[1,2,1408,384]{3,2,1,0:T(8,128)(2,1)}, bf16[1,2,1408,384]{3,2,1,0:T(8,128)(2,1)}, u32[]{:S(2)}, u32[]{:S(2)}) collective-permute-start(bf16[1,2,1408,384]{3,2,1,0:T(8,128)(2,1)} %outer.16), channel_id=1, source_target_pairs={{0,1},{1,0},{2,3},{3,2},{4,5},{5,4},{6,7},{7,6},{8,9},{9,8},{10,11... | collective-permute-start | bytes 6488072 | tf_op jit(solution)/shard_map/ppermute | solution.py:747
  749.4 27.3 %collective-permute-start.10 = (bf16[1,4,176,384]{3,2,1,0:T(8,128)(2,1)}, bf16[1,4,176,384]{3,2,1,0:T(8,128)(2,1)S(1)}, u32[]{:S(2)}, u32[]{:S(2)}) collective-permute-start(bf16[1,4,176,384]{3,2,1,0:T(8,128)(2,1)} %get-tuple-element.472), channel_id=1, source_target_pairs={{0,2},{1,3},{2,0},{3,1},{4,6},{5,7},{6,4},{7,5},{8,10},{9,11},{10,... | collective-permute-start | bytes 1622024 | tf_op jit(solution)/shard_map/ppermute | solution.py:747
  769.1 102.0 %collective-permute-start.19 = (bf16[1,2,1408,384]{3,2,1,0:T(8,128)(2,1)}, bf16[1,2,1408,384]{3,2,1,0:T(8,128)(2,1)S(1)}, u32[]{:S(2)}, u32[]{:S(2)}) collective-permute-start(bf16[1,2,1408,384]{3,2,1,0:T(8,128)(2,1)} %outer.20), channel_id=1, source_target_pairs={{0,1},{1,0},{2,3},{3,2},{4,5},{5,4},{6,7},{7,6},{8,9},{9,8},{10,11... | collective-permute-start | bytes 6488072 | tf_op jit(solution)/shard_map/ppermute | solution.py:747
  781.6 27.5 %all-to-all-start.11 = ((bf16[2,8,88,512]{3,2,1,0:T(8,128)(2,1)}), bf16[2,8,88,512]{3,2,1,0:T(8,128)(2,1)}, u32[]{:S(2)}, u32[]{:S(2)}) async-start(bf16[2,8,88,512]{3,2,1,0:T(8,128)(2,1)} %bitcast.92), calls=%async_computation.11 | async-start | bytes 2883584 | tf_op jit(solution)/shard_map/all_to_all | solution.py:633
  787.1 26.4 %collective-permute-start.13 = (bf16[1,176,384]{2,1,0:T(8,128)(2,1)S(1)}, bf16[1,176,384]{2,1,0:T(8,128)(2,1)S(1)}, u32[]{:S(2)}, u32[]{:S(2)}) collective-permute-start(bf16[1,176,384]{2,1,0:T(8,128)(2,1)S(1)} %get-tuple-element.504), channel_id=1, source_target_pairs={{0,8},{4,12},{8,0},{12,4},{16,24},{20,28},{24,16},{28,20},{1,9},{5... | collective-permute-start | bytes 405512 | tf_op jit(solution)/shard_map/ppermute | solution.py:747
  787.1 53.5 %collective-permute-start.14 = (bf16[1,176,384]{2,1,0:T(8,128)(2,1)}, bf16[1,176,384]{2,1,0:T(8,128)(2,1)S(1)}, u32[]{:S(2)}, u32[]{:S(2)}) collective-permute-start(bf16[1,176,384]{2,1,0:T(8,128)(2,1)} %get-tuple-element.503), channel_id=1, source_target_pairs={{0,16},{4,20},{8,24},{12,28},{16,0},{20,4},{24,8},{28,12},{1,17},{... | collective-permute-start | bytes 405512 | tf_op jit(solution)/shard_map/ppermute | solution.py:747
  787.8 52.9 %collective-permute-start.15 = (bf16[1,176,384]{2,1,0:T(8,128)(2,1)}, bf16[1,176,384]{2,1,0:T(8,128)(2,1)}, u32[]{:S(2)}, u32[]{:S(2)}) collective-permute-start(bf16[1,176,384]{2,1,0:T(8,128)(2,1)} %get-tuple-element.502), channel_id=1, source_target_pairs={{0,24},{4,28},{8,16},{12,20},{16,8},{20,12},{24,0},{28,4},{1,25},{... | collective-permute-start | bytes 405512 | tf_op jit(solution)/shard_map/ppermute | solution.py:747
  798.5 42.1 %collective-permute-start.16 = (bf16[1,4,2,176,384]{4,3,2,1,0:T(8,128)(2,1)}, bf16[1,4,2,176,384]{4,3,2,1,0:T(8,128)(2,1)}, u32[]{:S(2)}, u32[]{:S(2)}) collective-permute-start(bf16[1,4,2,176,384]{4,3,2,1,0:T(8,128)(2,1)} %get-tuple-element.187), channel_id=1, source_target_pairs={{0,2},{1,3},{2,0},{3,1},{4,6},{5,7},{6,4},{7,5},{8,10},{9,11},{10,... | collective-permute-start | bytes 3244040 | tf_op jit(solution)/shard_map/ppermute | solution.py:747
  809.1 40.0 %all-to-all-start.13 = ((bf16[4,4,88,256]{3,2,1,0:T(8,128)(2,1)}), bf16[4,4,88,256]{3,2,1,0:T(8,128)(2,1)}, u32[]{:S(2)}, u32[]{:S(2)}) async-start(bf16[4,4,88,256]{3,2,1,0:T(8,128)(2,1)} %bitcast.98), calls=%async_computation.13 | async-start | bytes 1441792 | tf_op jit(solution)/shard_map/all_to_all | solution.py:632
  813.5 57.5 %collective-permute-start.18 = (bf16[2,2,4,128,384]{4,3,2,1,0:T(8,128)(2,1)}, bf16[2,2,4,128,384]{4,3,2,1,0:T(8,128)(2,1)}, u32[]{:S(2)}, u32[]{:S(2)}) collective-permute-start(bf16[2,2,4,128,384]{4,3,2,1,0:T(8,128)(2,1)} %get-tuple-element.195), channel_id=1, source_target_pairs={{0,4},{4,0},{8,12},{12,8},{16,20},{20,16},{24,28},{28,24},{1,5},{5... | collective-permute-start | bytes 4718600 | tf_op jit(solution)/shard_map/ppermute | solution.py:747
  842.6 43.6 %collective-permute-start.17 = (bf16[1,4,176,384]{3,2,1,0:T(8,128)(2,1)}, bf16[1,4,176,384]{3,2,1,0:T(8,128)(2,1)}, u32[]{:S(2)}, u32[]{:S(2)}) collective-permute-start(bf16[1,4,176,384]{3,2,1,0:T(8,128)(2,1)} %fusion.28), channel_id=1, source_target_pairs={{0,4},{4,0},{8,12},{12,8},{16,20},{20,16},{24,28},{28,24},{1,5},{5... | collective-permute-start | bytes 1622024 | tf_op jit(solution)/shard_map/ppermute | solution.py:747
  863.3 22.9 %all-to-all-start.12 = ((bf16[2,3,8,88,512]{4,3,2,1,0:T(8,128)(2,1)}), bf16[2,3,8,88,512]{4,3,2,1,0:T(8,128)(2,1)}, u32[]{:S(2)}, u32[]{:S(2)}) async-start(bf16[2,3,8,88,512]{4,3,2,1,0:T(8,128)(2,1)} %attend_back.6), calls=%async_computation.12 | async-start | bytes 8650752 | tf_op jit(solution)/shard_map/all_to_all | solution.py:633
  886.2 39.4 %all-to-all-start.14 = ((bf16[4,3,4,88,256]{4,3,2,1,0:T(8,128)(2,1)}), bf16[4,3,4,88,256]{4,3,2,1,0:T(8,128)(2,1)}, u32[]{:S(2)}, u32[]{:S(2)}) async-start(bf16[4,3,4,88,256]{4,3,2,1,0:T(8,128)(2,1)} %attend_back.7), calls=%async_computation.14 | async-start | bytes 4325376 | tf_op jit(solution)/shard_map/all_to_all | solution.py:632
  897.0 63.3 %collective-permute-start.20 = (bf16[1,176,384]{2,1,0:T(8,128)(2,1)}, bf16[1,176,384]{2,1,0:T(8,128)(2,1)}, u32[]{:S(2)}, u32[]{:S(2)}) collective-permute-start(bf16[1,176,384]{2,1,0:T(8,128)(2,1)} %get-tuple-element.500), channel_id=1, source_target_pairs={{0,8},{4,12},{8,0},{12,4},{16,24},{20,28},{24,16},{28,20},{1,9},{5... | collective-permute-start | bytes 405512 | tf_op jit(solution)/shard_map/ppermute | solution.py:747
  897.0 63.3 %collective-permute-start.21 = (bf16[1,176,384]{2,1,0:T(8,128)(2,1)}, bf16[1,176,384]{2,1,0:T(8,128)(2,1)}, u32[]{:S(2)}, u32[]{:S(2)}) collective-permute-start(bf16[1,176,384]{2,1,0:T(8,128)(2,1)} %get-tuple-element.499), channel_id=1, source_target_pairs={{0,16},{4,20},{8,24},{12,28},{16,0},{20,4},{24,8},{28,12},{1,17},{... | collective-permute-start | bytes 405512 | tf_op jit(solution)/shard_map/ppermute | solution.py:747
  898.6 61.7 %collective-permute-start.22 = (bf16[1,176,384]{2,1,0:T(8,128)(2,1)}, bf16[1,176,384]{2,1,0:T(8,128)(2,1)}, u32[]{:S(2)}, u32[]{:S(2)}) collective-permute-start(bf16[1,176,384]{2,1,0:T(8,128)(2,1)} %get-tuple-element.498), channel_id=1, source_target_pairs={{0,24},{4,28},{8,16},{12,20},{16,8},{20,12},{24,0},{28,4},{1,25},{... | collective-permute-start | bytes 405512 | tf_op jit(solution)/shard_map/ppermute | solution.py:747
  903.6 56.7 %collective-permute-start.23 = (bf16[2,4,128,384]{3,2,1,0:T(8,128)(2,1)}, bf16[2,4,128,384]{3,2,1,0:T(8,128)(2,1)}, u32[]{:S(2)}, u32[]{:S(2)}) collective-permute-start(bf16[2,4,128,384]{3,2,1,0:T(8,128)(2,1)} %fusion.24), channel_id=1, source_target_pairs={{0,2},{1,3},{2,0},{3,1},{4,6},{5,7},{6,4},{7,5},{8,10},{9,11},{10,... | collective-permute-start | bytes 2359304 | tf_op jit(solution)/shard_map/ppermute | solution.py:747
  912.7 70.4 %collective-permute-start.24 = (bf16[1,4,2,176,384]{4,3,2,1,0:T(8,128)(2,1)}, bf16[1,4,2,176,384]{4,3,2,1,0:T(8,128)(2,1)}, u32[]{:S(2)}, u32[]{:S(2)}) collective-permute-start(bf16[1,4,2,176,384]{4,3,2,1,0:T(8,128)(2,1)} %get-tuple-element.203), channel_id=1, source_target_pairs={{0,2},{1,3},{2,0},{3,1},{4,6},{5,7},{6,4},{7,5},{8,10},{9,11},{10,... | collective-permute-start | bytes 3244040 | tf_op jit(solution)/shard_map/ppermute | solution.py:747
  992.4 50.2 %collective-permute-start.29 = (bf16[2,2,1408,384]{3,2,1,0:T(8,128)(2,1)}, bf16[2,2,1408,384]{3,2,1,0:T(8,128)(2,1)}, u32[]{:S(2)}, u32[]{:S(2)}) collective-permute-start(bf16[2,2,1408,384]{3,2,1,0:T(8,128)(2,1)} %outer.22), channel_id=1, source_target_pairs={{0,1},{1,0},{2,3},{3,2},{4,5},{5,4},{6,7},{7,6},{8,9},{9,8},{10,11... | collective-permute-start | bytes 12976136 | tf_op jit(solution)/shard_map/ppermute | solution.py:747
  998.8 43.0 %collective-permute-start.30 = (bf16[1,2,1408,384]{3,2,1,0:T(8,128)(2,1)}, bf16[1,2,1408,384]{3,2,1,0:T(8,128)(2,1)S(1)}, u32[]{:S(2)}, u32[]{:S(2)}) collective-permute-start(bf16[1,2,1408,384]{3,2,1,0:T(8,128)(2,1)} %outer.23), channel_id=1, source_target_pairs={{0,1},{1,0},{2,3},{3,2},{4,5},{5,4},{6,7},{7,6},{8,9},{9,8},{10,11... | collective-permute-start | bytes 6488072 | tf_op jit(solution)/shard_map/ppermute | solution.py:747
  1001.4 25.1 %collective-permute-start.25 = (bf16[2,128,384]{2,1,0:T(8,128)(2,1)S(1)}, bf16[2,128,384]{2,1,0:T(8,128)(2,1)S(1)}, u32[]{:S(2)}, u32[]{:S(2)}) collective-permute-start(bf16[2,128,384]{2,1,0:T(8,128)(2,1)S(1)} %get-tuple-element.488), channel_id=1, source_target_pairs={{0,8},{4,12},{8,0},{12,4},{16,24},{20,28},{24,16},{28,20},{1,9},{5... | collective-permute-start | bytes 589832 | tf_op jit(solution)/shard_map/ppermute | solution.py:747
  1003.6 38.1 %collective-permute-start.28 = (bf16[1,4,176,384]{3,2,1,0:T(8,128)(2,1)}, bf16[1,4,176,384]{3,2,1,0:T(8,128)(2,1)S(1)}, u32[]{:S(2)}, u32[]{:S(2)}) collective-permute-start(bf16[1,4,176,384]{3,2,1,0:T(8,128)(2,1)} %fusion.30), channel_id=1, source_target_pairs={{0,4},{4,0},{8,12},{12,8},{16,20},{20,16},{24,28},{28,24},{1,5},{5... | collective-permute-start | bytes 1622024 | tf_op jit(solution)/shard_map/ppermute | solution.py:747
  1024.3 17.4 %collective-permute-start.26 = (bf16[2,128,384]{2,1,0:T(8,128)(2,1)}, bf16[2,128,384]{2,1,0:T(8,128)(2,1)S(1)}, u32[]{:S(2)}, u32[]{:S(2)}) collective-permute-start(bf16[2,128,384]{2,1,0:T(8,128)(2,1)} %get-tuple-element.487), channel_id=1, source_target_pairs={{0,16},{4,20},{8,24},{12,28},{16,0},{20,4},{24,8},{28,12},{1,17},{... | collective-permute-start | bytes 589832 | tf_op jit(solution)/shard_map/ppermute | solution.py:747
  1026.5 15.2 %collective-permute-start.27 = (bf16[2,128,384]{2,1,0:T(8,128)(2,1)}, bf16[2,128,384]{2,1,0:T(8,128)(2,1)S(1)}, u32[]{:S(2)}, u32[]{:S(2)}) collective-permute-start(bf16[2,128,384]{2,1,0:T(8,128)(2,1)} %get-tuple-element.486), channel_id=1, source_target_pairs={{0,24},{4,28},{8,16},{12,20},{16,8},{20,12},{24,0},{28,4},{1,25},{... | collective-permute-start | bytes 589832 | tf_op jit(solution)/shard_map/ppermute | solution.py:747
  1083.8 60.1 %collective-permute-start.31 = (bf16[1,2,2816,384]{3,2,1,0:T(8,128)(2,1)}, bf16[1,2,2816,384]{3,2,1,0:T(8,128)(2,1)}, u32[]{:S(2)}, u32[]{:S(2)}) collective-permute-start(bf16[1,2,2816,384]{3,2,1,0:T(8,128)(2,1)} %outer.24), channel_id=1, source_target_pairs={{0,1},{1,0},{2,3},{3,2},{4,5},{5,4},{6,7},{7,6},{8,9},{9,8},{10,11... | collective-permute-start | bytes 12976136 | tf_op jit(solution)/shard_map/ppermute | solution.py:747
  1094.7 49.2 %collective-permute-start.32 = (bf16[2,2,4,176,384]{4,3,2,1,0:T(8,128)(2,1)}, bf16[2,2,4,176,384]{4,3,2,1,0:T(8,128)(2,1)S(1)}, u32[]{:S(2)}, u32[]{:S(2)}) collective-permute-start(bf16[2,2,4,176,384]{4,3,2,1,0:T(8,128)(2,1)} %get-tuple-element.215), channel_id=1, source_target_pairs={{0,4},{4,0},{8,12},{12,8},{16,20},{20,16},{24,28},{28,24},{1,5},{5... | collective-permute-start | bytes 6488072 | tf_op jit(solution)/shard_map/ppermute | solution.py:747
  1102.9 26.1 %collective-permute-start.33 = (bf16[1,4,2,176,384]{4,3,2,1,0:T(8,128)(2,1)}, bf16[1,4,2,176,384]{4,3,2,1,0:T(8,128)(2,1)}, u32[]{:S(2)}, u32[]{:S(2)}) collective-permute-start(bf16[1,4,2,176,384]{4,3,2,1,0:T(8,128)(2,1)} %get-tuple-element.218), channel_id=1, source_target_pairs={{0,2},{1,3},{2,0},{3,1},{4,6},{5,7},{6,4},{7,5},{8,10},{9,11},{10,... | collective-permute-start | bytes 3244040 | tf_op jit(solution)/shard_map/ppermute | solution.py:747
  1154.6 48.5 %collective-permute-start.34 = (bf16[1,2,4,352,384]{4,3,2,1,0:T(8,128)(2,1)}, bf16[1,2,4,352,384]{4,3,2,1,0:T(8,128)(2,1)}, u32[]{:S(2)}, u32[]{:S(2)}) collective-permute-start(bf16[1,2,4,352,384]{4,3,2,1,0:T(8,128)(2,1)} %get-tuple-element.229), channel_id=1, source_target_pairs={{0,4},{4,0},{8,12},{12,8},{16,20},{20,16},{24,28},{28,24},{1,5},{5... | collective-permute-start | bytes 6488072 | tf_op jit(solution)/shard_map/ppermute | solution.py:747
  1203.1 30.0 %all-to-all-start.16 = ((bf16[4,352,768]{2,1,0:T(8,128)(2,1)}), bf16[4,352,768]{2,1,0:T(8,128)(2,1)S(1)}, u32[]{:S(2)}, u32[]{:S(2)}) async-start(bf16[4,352,768]{2,1,0:T(8,128)(2,1)} %bitcast.402), calls=%async_computation.16 | async-start | bytes 4325376 | tf_op jit(solution)/shard_map/all_to_all | solution.py:632
  1213.0 32.2 %collective-permute-start.49 = (bf16[1,176,384]{2,1,0:T(8,128)(2,1)}, bf16[1,176,384]{2,1,0:T(8,128)(2,1)}, u32[]{:S(2)}, u32[]{:S(2)}) collective-permute-start(bf16[1,176,384]{2,1,0:T(8,128)(2,1)} %get-tuple-element.491), channel_id=1, source_target_pairs={{0,24},{4,28},{8,16},{12,20},{16,8},{20,12},{24,0},{28,4},{1,25},{... | collective-permute-start | bytes 405512 | tf_op jit(solution)/shard_map/ppermute | solution.py:747
  1214.6 30.7 %collective-permute-start.48 = (bf16[1,176,384]{2,1,0:T(8,128)(2,1)}, bf16[1,176,384]{2,1,0:T(8,128)(2,1)}, u32[]{:S(2)}, u32[]{:S(2)}) collective-permute-start(bf16[1,176,384]{2,1,0:T(8,128)(2,1)} %get-tuple-element.492), channel_id=1, source_target_pairs={{0,16},{4,20},{8,24},{12,28},{16,0},{20,4},{24,8},{28,12},{1,17},{... | collective-permute-start | bytes 405512 | tf_op jit(solution)/shard_map/ppermute | solution.py:747
  1219.0 26.2 %collective-permute-start.47 = (bf16[1,176,384]{2,1,0:T(8,128)(2,1)}, bf16[1,176,384]{2,1,0:T(8,128)(2,1)}, u32[]{:S(2)}, u32[]{:S(2)}) collective-permute-start(bf16[1,176,384]{2,1,0:T(8,128)(2,1)} %get-tuple-element.490), channel_id=1, source_target_pairs={{0,8},{4,12},{8,0},{12,4},{16,24},{20,28},{24,16},{28,20},{1,9},{5... | collective-permute-start | bytes 405512 | tf_op jit(solution)/shard_map/ppermute | solution.py:747
  1234.4 137.5 %all-to-all-start.17 = ((bf16[4,704,768]{2,1,0:T(8,128)(2,1)}), bf16[4,704,768]{2,1,0:T(8,128)(2,1)}, u32[]{:S(2)}, u32[]{:S(2)}) async-start(bf16[4,704,768]{2,1,0:T(8,128)(2,1)} %bitcast.410), calls=%async_computation.17 | async-start | bytes 8650752 | tf_op jit(solution)/shard_map/all_to_all | solution.py:632
  1243.2 69.3 %collective-permute-start.35 = (bf16[2,4,176,384]{3,2,1,0:T(8,128)(2,1)S(1)}, bf16[2,4,176,384]{3,2,1,0:T(8,128)(2,1)S(1)}, u32[]{:S(2)}, u32[]{:S(2)}) collective-permute-start(bf16[2,4,176,384]{3,2,1,0:T(8,128)(2,1)S(1)} %fusion.20), channel_id=1, source_target_pairs={{0,2},{1,3},{2,0},{3,1},{4,6},{5,7},{6,4},{7,5},{8,10},{9,11},{10,... | collective-permute-start | bytes 3244040 | tf_op jit(solution)/shard_map/ppermute | solution.py:747
  1253.2 85.5 %collective-permute-start.37 = (bf16[1,4,352,384]{3,2,1,0:T(8,128)(2,1)S(1)}, bf16[1,4,352,384]{3,2,1,0:T(8,128)(2,1)S(1)}, u32[]{:S(2)}, u32[]{:S(2)}) collective-permute-start(bf16[1,4,352,384]{3,2,1,0:T(8,128)(2,1)S(1)} %get-tuple-element.445), channel_id=1, source_target_pairs={{0,2},{1,3},{2,0},{3,1},{4,6},{5,7},{6,4},{7,5},{8,10},{9,11},{10,... | collective-permute-start | bytes 3244040 | tf_op jit(solution)/shard_map/ppermute | solution.py:747
  1314.3 22.8 %collective-permute-start.45 = (bf16[1,176,384]{2,1,0:T(8,128)(2,1)S(1)}, bf16[1,176,384]{2,1,0:T(8,128)(2,1)S(1)}, u32[]{:S(2)}, u32[]{:S(2)}) collective-permute-start(bf16[1,176,384]{2,1,0:T(8,128)(2,1)S(1)} %get-tuple-element.496), channel_id=1, source_target_pairs={{0,16},{4,20},{8,24},{12,28},{16,0},{20,4},{24,8},{28,12},{1,17},{... | collective-permute-start | bytes 405512 | tf_op jit(solution)/shard_map/ppermute | solution.py:747
  1318.7 20.0 %collective-permute-start.44 = (bf16[1,176,384]{2,1,0:T(8,128)(2,1)S(1)}, bf16[1,176,384]{2,1,0:T(8,128)(2,1)S(1)}, u32[]{:S(2)}, u32[]{:S(2)}) collective-permute-start(bf16[1,176,384]{2,1,0:T(8,128)(2,1)S(1)} %get-tuple-element.494), channel_id=1, source_target_pairs={{0,8},{4,12},{8,0},{12,4},{16,24},{20,28},{24,16},{28,20},{1,9},{5... | collective-permute-start | bytes 405512 | tf_op jit(solution)/shard_map/ppermute | solution.py:747
  1319.1 23.6 %collective-permute-start.43 = (bf16[2,176,384]{2,1,0:T(8,128)(2,1)S(1)}, bf16[2,176,384]{2,1,0:T(8,128)(2,1)S(1)}, u32[]{:S(2)}, u32[]{:S(2)}) collective-permute-start(bf16[2,176,384]{2,1,0:T(8,128)(2,1)S(1)} %get-tuple-element.479), channel_id=1, source_target_pairs={{0,24},{4,28},{8,16},{12,20},{16,8},{20,12},{24,0},{28,4},{1,25},{... | collective-permute-start | bytes 811016 | tf_op jit(solution)/shard_map/ppermute | solution.py:747
  1320.7 42.5 %collective-permute-start.42 = (bf16[2,176,384]{2,1,0:T(8,128)(2,1)S(1)}, bf16[2,176,384]{2,1,0:T(8,128)(2,1)S(1)}, u32[]{:S(2)}, u32[]{:S(2)}) collective-permute-start(bf16[2,176,384]{2,1,0:T(8,128)(2,1)S(1)} %get-tuple-element.480), channel_id=1, source_target_pairs={{0,16},{4,20},{8,24},{12,28},{16,0},{20,4},{24,8},{28,12},{1,17},{... | collective-permute-start | bytes 811016 | tf_op jit(solution)/shard_map/ppermute | solution.py:747
  1337.1 26.1 %collective-permute-start.41 = (bf16[2,176,384]{2,1,0:T(8,128)(2,1)S(1)}, bf16[2,176,384]{2,1,0:T(8,128)(2,1)S(1)}, u32[]{:S(2)}, u32[]{:S(2)}) collective-permute-start(bf16[2,176,384]{2,1,0:T(8,128)(2,1)S(1)} %get-tuple-element.478), channel_id=1, source_target_pairs={{0,8},{4,12},{8,0},{12,4},{16,24},{20,28},{24,16},{28,20},{1,9},{5... | collective-permute-start | bytes 811016 | tf_op jit(solution)/shard_map/ppermute | solution.py:747
  1339.2 50.0 %collective-permute-start.40 = (bf16[1,352,384]{2,1,0:T(8,128)(2,1)S(1)}, bf16[1,352,384]{2,1,0:T(8,128)(2,1)S(1)}, u32[]{:S(2)}, u32[]{:S(2)}) collective-permute-start(bf16[1,352,384]{2,1,0:T(8,128)(2,1)S(1)} %get-tuple-element.483), channel_id=1, source_target_pairs={{0,24},{4,28},{8,16},{12,20},{16,8},{20,12},{24,0},{28,4},{1,25},{... | collective-permute-start | bytes 811016 | tf_op jit(solution)/shard_map/ppermute | solution.py:747
  1342.1 47.1 %collective-permute-start.39 = (bf16[1,352,384]{2,1,0:T(8,128)(2,1)S(1)}, bf16[1,352,384]{2,1,0:T(8,128)(2,1)S(1)}, u32[]{:S(2)}, u32[]{:S(2)}) collective-permute-start(bf16[1,352,384]{2,1,0:T(8,128)(2,1)S(1)} %get-tuple-element.484), channel_id=1, source_target_pairs={{0,16},{4,20},{8,24},{12,28},{16,0},{20,4},{24,8},{28,12},{1,17},{... | collective-permute-start | bytes 811016 | tf_op jit(solution)/shard_map/ppermute | solution.py:747
  1342.8 46.5 %collective-permute-start.38 = (bf16[1,352,384]{2,1,0:T(8,128)(2,1)S(1)}, bf16[1,352,384]{2,1,0:T(8,128)(2,1)S(1)}, u32[]{:S(2)}, u32[]{:S(2)}) collective-permute-start(bf16[1,352,384]{2,1,0:T(8,128)(2,1)S(1)} %get-tuple-element.482), channel_id=1, source_target_pairs={{0,8},{4,12},{8,0},{12,4},{16,24},{20,28},{24,16},{28,20},{1,9},{5... | collective-permute-start | bytes 811016 | tf_op jit(solution)/shard_map/ppermute | solution.py:747
  (158 other events, 3357.9 us)
Sparse Core Ops, SparseCore 0:
  15.3 271.3 all-gather.4
  290.3 231.7 all-gather.2
  633.3 396.3 reduce-scatter.1

commit v7 on v6

--- a/solution.py
+++ b/solution.py
@@ -409,6 +409,43 @@
     )(place, *lefts, *rights, *given)
 
 
+def outer_all(pairs):
+    cols = lax.axis_size("col")
+    if not custom_mesh():
+        return jnp.stack(
+            [einsum("kt,cnt->ckn", a, b.reshape(cols, -1, b.shape[1])).astype(BF) for a, b in pairs]
+        )
+    lefts = []
+    for left, _ in pairs:
+        if not any(left is other for other in lefts):
+            lefts.append(left)
+    which = [next(i for i, l in enumerate(lefts) if l is left) for left, _ in pairs]
+    rights = [right for _, right in pairs]
+    many = len(pairs)
+    rows = lefts[0].shape[0]
+    width = rights[0].shape[0] // cols
+
+    def kernel(*refs):
+        for index in range(many):
+            left = refs[which[index]][...]
+            part = dot(left, refs[len(lefts) + index][...], ((1,), (1,)))
+            refs[-1][index, 0] = part.astype(BF)
+
+    return pl.pallas_call(
+        kernel,
+        grid=(cols,),
+        in_specs=[full(left.shape) for left in lefts]
+        + [pl.BlockSpec((width, right.shape[1]), lambda c: (c, 0)) for right in rights],
+        out_specs=pl.BlockSpec((many, 1, rows, width), lambda c: (0, c, 0, 0)),
+        out_shape=jax.ShapeDtypeStruct((many, cols, rows, width), BF),
+        cost_estimate=work(
+            many * rows, lefts[0].shape[1], cols * width, 3 * many * rows * cols * width
+        ),
+        compiler_params=params(),
+        name="outer_all",
+    )(*lefts, *rights)
+
+
 def expand(weight, kind, values):
     _, many, depth, hidden = weight.shape
     tokens = values.shape[1]
@@ -926,14 +963,9 @@
     block_rows = depth // rows
     both = to_tokens([latents, skip_input], pieces, cols, block_rows)
 
-    weights = gather_weights(
-        [
-            *(self_inputs[:, i] for i in range(3)),
-            self_output.T,
-            cross_query,
-            cross_output.T,
-            *(cross_keyvalue[:, i] for i in range(2)),
-        ]
+    weights_one = gather_weights([*(self_inputs[:, i] for i in range(3)), self_output.T])
+    weights_two = gather_weights(
+        [cross_query, cross_output.T, *(cross_keyvalue[:, i] for i in range(2))]
     )
     skip_block = jnp.concatenate([skip_weight[0], skip_weight[1]], 0)
     skip_block = jnp.pad(skip_block, ((0, 0), (0, lanes(width) - width)))
@@ -978,13 +1010,13 @@
     scaling = 1.0 + per_token(1)
 
     text = shared(jnp.pad(after(text_states, both), ((0, 0), (0, keys - texts), (0, 0))), "col")
-    both, text = lax.optimization_barrier((both, text))
     joined = project_blocks(base, w_skip, width, both)
     skip_normal, skip_inverse = normalize(joined)
     stream = skip_normal * gain_skip + bias_skip
     normal_one, inverse_one = normalize(stream)
     normed_one = (normal_one * scaling + shifting).astype(BF)
-    raw = project(weights, [0, 1, 2], [normed_one], [F32, F32, BF])
+    raw = project(weights_one, [0, 1, 2], [normed_one], [F32, F32, BF])
+    raw, text = lax.optimization_barrier((raw, text))
     raw = [r.reshape(heads, dim, tokens) for r in raw]
     cosine, sine = rope_tables(places, dim)
 
@@ -1011,10 +1043,10 @@
         mixed_parts.append(exchange(kept[0], piece.group, cols).reshape(depth, -1))
     mixed_one = jnp.concatenate(mixed_parts, 1)
     text = after(text, mixed_one)
-    stream = stream + rebuild(weights, [3], [mixed_one], F32)
+    stream = stream + rebuild(weights_one, [3], [mixed_one], F32)
     normal_two, inverse_two = normalize(stream)
     normed_two = (normal_two * gain_cross + bias_cross).astype(BF)
-    raw_cross = project(weights, [4], [normed_two], [F32])[0].reshape(heads, dim, tokens)
+    raw_cross = project(weights_two, [0], [normed_two], [F32])[0].reshape(heads, dim, tokens)
     norm_query, cross_pull = jax.vjp(head_norm, raw_cross, cross_query_gain)
     text = jnp.concatenate(
         [lax.dynamic_index_in_dim(text, p.sequence, 1, False) for p in pieces], 1
@@ -1024,7 +1056,7 @@
     text_wide = jnp.pad(
         text.reshape(rows, text_rows, -1), ((0, 0), (0, block_rows - text_rows), (0, 0))
     ).reshape(depth, -1)
-    raw_text, value_two = project(weights, [6, 7], [text_wide], [F32, BF])
+    raw_text, value_two = project(weights_two, [2, 3], [text_wide], [F32, BF])
     norm_key, text_pull = jax.vjp(head_norm, raw_text.reshape(heads, dim, -1), text_key_gain)
     query_two = norm_query.astype(BF)
     key_two = norm_key.astype(BF)
@@ -1040,15 +1072,16 @@
         saved_cross.append((inputs, kept))
         mixed_parts.append(kept[0].reshape(depth, -1))
     mixed_two = jnp.concatenate(mixed_parts, 1)
-    stream = stream + rebuild(weights, [5], [mixed_two], F32)
+    stream = stream + rebuild(weights_two, [1], [mixed_two], F32)
     normal_three, inverse_three = normalize(stream)
     normed_three = (normal_three * gain_hidden + bias_hidden).astype(BF)
     grad_out = to_tokens([after(out_grad, joined)], pieces, cols, width)
     act, slopes = expand(weights_hidden, 0, normed_three)
 
     g_inner = expand_back(weights_hidden, 1, grad_out, slopes)
+    g_hidden = hidden_outer(grad_out, act, normed_three, g_inner)
+    g_inner, g_hidden = lax.optimization_barrier((g_inner, g_hidden))
     g_normed = contract(weights_hidden, 0, g_inner, None, F32)
-    g_hidden = hidden_outer(grad_out, act, normed_three, g_inner)
     g_hidden = lax.psum_scatter(
         g_hidden.reshape(2, -1, g_hidden.shape[3]), DEVICES, scatter_dimension=1, tiled=True
     ).astype(F32)
@@ -1057,9 +1090,8 @@
     g_stream = grad_out.astype(F32) + norm_back(g_normed * gain_hidden, normal_three, inverse_three)
 
     g_low = g_stream.astype(BF)
-    g_mixed = project(weights, [5], [g_low], [BF])[0].reshape(heads, dim, tokens)
-    r_cross = Reduction(corner, [(g_low, mixed_two)], True)
-    running = [r_cross]
+    g_mixed = project(weights_two, [1], [g_low], [BF])[0].reshape(heads, dim, tokens)
+    pairs = [(g_low, mixed_two)]
     g_queries = []
     g_keys = []
     g_values = []
@@ -1069,7 +1101,6 @@
         g_queries.append(grads[0][0, 0])
         g_keys.append(grads[1][0, 0])
         g_values.append(grads[2][0, 0])
-    g_queries, g_keys, g_values = tick((g_queries, g_keys, g_values), running)
     g_raw_cross, g_cq_gain = cross_pull(jnp.concatenate(g_queries, 2))
     g_raw_text, g_tk_gain = text_pull(jnp.concatenate(g_keys, 2))
     g_craw = g_raw_cross.astype(BF).reshape(depth, tokens)
@@ -1077,19 +1108,19 @@
         g_raw_text.astype(BF).reshape(depth, -1),
         jnp.concatenate(g_values, 2).astype(BF).reshape(depth, -1),
     ]
-    g_normed = rebuild(weights, [4], [g_craw], F32)
-    r_query = Reduction(corner, [(normed_two, g_craw)], False)
-    r_text = Reduction(corner, [(text, g) for g in g_pair], True)
-    g_normed = tick(g_normed, running)
-    running += [r_query, r_text]
+    g_normed = rebuild(weights_two, [0], [g_craw], F32)
+    pairs += [(normed_two, g_craw), *((text_wide, g) for g in g_pair)]
     g_cross_gain = jnp.sum(g_normed * normal_two, 1)
     g_cross_bias = jnp.sum(g_normed, 1)
     g_stream = g_stream + norm_back(g_normed * gain_cross, normal_two, inverse_two)
 
     g_low = g_stream.astype(BF)
-    g_mixed = project(weights, [3], [g_low], [BF])[0].reshape(heads, dim, tokens)
-    g_mixed = tick(g_mixed, running)
-    r_attn = Reduction(corner, [(g_low, mixed_one)], False)
+    g_mixed = project(weights_one, [3], [g_low], [BF])[0].reshape(heads, dim, tokens)
+    pairs.append((g_low, mixed_one))
+    middle = outer_all(pairs)
+    middle = lax.psum_scatter(
+        middle.reshape(len(pairs), -1, width), DEVICES, scatter_dimension=1, tiled=True
+    ).astype(F32)
     g_parts = []
     for index, piece in enumerate(pieces):
         whole, kept = saved_self[index]
@@ -1099,9 +1130,6 @@
         part = attend_back(
             none, whole, whole, whole, (0, 1, 2), kept, grad, False, 2, True
         )
-        part = tick(part, [r_cross, r_query] if index == 0 else running)
-        if index == 0:
-            running.append(r_attn)
         g_parts.append(exchange(part, piece.group, cols))
     g_heads = [
         jnp.concatenate([p[:, i].reshape(heads, dim, -1) for p in g_parts], 2) for i in range(3)
@@ -1111,14 +1139,15 @@
     g_triple = [
         g.reshape(depth, tokens) for g in (g_raw_q.astype(BF), g_raw_k.astype(BF), g_heads[2])
     ]
-    g_triple = tick(g_triple, running)
     r_self = [
         Reduction(corner, [(normed_one, g) for g in g_triple[:2]], True),
         Reduction(corner, [(normed_one, g_triple[2])], False),
     ]
-    g_normed = rebuild(weights, [0, 1, 2], g_triple, F32)
-    running += r_self
-    g_normed = tick(g_normed, running)
+    g_normed = rebuild(weights_one, [0, 1, 2], g_triple, F32)
+    g_normed = tick(g_normed, r_self)
+    g_normed, kept = lax.optimization_barrier((g_normed, [r.state[0] for r in r_self]))
+    for beside, part in zip(r_self, kept):
+        beside.state[0] = part
     crossed = g_normed * normal_one
     sums = jnp.stack(
         [
@@ -1162,8 +1191,7 @@
     else:
         g_latents, g_skip = to_features(g_both, pieces, cols, 2, block_rows)
         output = contract(weights_hidden, 1, act, stream, BF)
-    result = to_features(output, pieces, cols, 1, width)[0]
-    g_modul = shared(after(g_modul, result), "row").reshape(-1, 2, width)
+    g_modul = shared(after(g_modul, g_skip), "row").reshape(-1, 2, width)
     g_modulation = einsum("sd,ske->dke", embed_rows, g_modul)
 
     g_gains = jnp.stack(
@@ -1171,10 +1199,14 @@
     )
     g_gains = g_gains.reshape(6, cols, width).transpose(1, 0, 2)
     g_head = jnp.stack([g_q_gain, g_k_gain, g_cq_gain, g_tk_gain], 0).reshape(1, -1, width)
-    g_gains = after(g_gains, result)
+    g_gains = after(g_gains, g_skip)
     packed = jnp.concatenate([g_gains, jnp.broadcast_to(g_head, (cols, *g_head.shape[1:]))], 1)
     packed = jnp.sum(lax.all_to_all(packed, "col", 0, 0, tiled=True), 0)
     packed = jnp.sum(shared(packed, "row"), 0)
+    output, g_hidden, packed, g_modulation = lax.optimization_barrier(
+        (output, g_hidden, packed, g_modulation)
+    )
+    result = to_features(output, pieces, cols, 1, width)[0]
     g_gains = packed[:6]
     g_head = packed[6:].reshape(4, dim)
     return (
@@ -1184,10 +1216,10 @@
         r_skip.result().reshape(2, block_rows, width),
         g_modulation,
         jnp.concatenate([r.result() for r in r_self], 0).transpose(1, 0, 2),
-        r_attn.result()[0].T,
-        r_query.result()[0],
-        r_text.result().transpose(1, 0, 2),
-        r_cross.result()[0].T,
+        middle[4].T,
+        middle[1],
+        middle[2:4, :text_rows].transpose(1, 0, 2),
+        middle[0].T,
         g_hidden[0],
         g_hidden[1].T,
         *[g_gains[i] for i in range(6)],

time: 1430 us -> 1300 us (0.909)
  waiting for transfers between devices: 429 us -> 365 us
  starting transfers between devices: 158 us -> 121 us
  Pallas kernels: 513 us -> 490 us
    pallas_call x14 -> x6, Pallas kernels: 109 us -> 54 us  [outer(): pl.pallas_call(kernel, grid_spec=pltpu.PrefetchScalarGridSpec(num_scalar_...]
    all_to_all x6, waiting for transfers between devices: 86.9 us -> 42.1 us  [shared(): lax.all_to_all(jnp.broadcast_to(values[None], (size, *values.shape)), axi...]
    ppermute x50 -> x26, starting transfers between devices: 71.7 us -> 31.8 us  [swap(): return lax.ppermute(values, axis, [(i, i ^ bit) for i in range(size)])]
    pallas_call x0 -> x1, Pallas kernels: none -> 31 us  [outer_all(): pl.pallas_call(kernel, grid=(cols,), in_specs=[full(left.shape) for left...]
    ppermute x50 -> x26, waiting for transfers between devices: 270 us -> 251 us  [swap(): return lax.ppermute(values, axis, [(i, i ^ bit) for i in range(size)])]
    all_gather x2 -> x3, waiting for transfers between devices: 10.1 us -> 29 us  [gather_weights(): whole = lax.all_gather(jnp.stack(padded, 0), DEVICES, axis=1, tiled=True)]
    all_to_all x8, waiting for transfers between devices: 50.4 us -> 34.2 us  [exchange(): return lax.all_to_all(values, 'col', 0, 0, tiled=True)]
    convert_element_type x19 -> x8, other arithmetic: 26.7 us -> 12.2 us  [add(): return (left.astype(F32) + right.astype(F32)).astype(BF)]
  transfers between devices with their start and end apart: 74 -> 52, of which waited for: 27 -> 26; matrix products, arithmetic and copies ran while one was open for 19% -> 21% of each run, Pallas kernels for 31% -> 33%
where the time goes in v7:
time: 1300 us; the launch traced here: 1290 us
  Pallas kernels  490 us (38%)
  waiting for transfers between devices  365 us (28%)
  other arithmetic  218 us (17%)
  starting transfers between devices  121 us (9%)
  local copies, waits for them, and re-layouts  76.6 us (6%)
  between operations  16.5 us (1%)
    ppermute x26, waiting for transfers between devices, swap(): return lax.ppermute(values, axis, [(i, i ^ bit) for i in range(size)])  251 us
    pallas_call x4, Pallas kernels, attend_back(): pl.pallas_call(partial(attend_back_kernel, masked), grid=(heads // many,)...  65.8 us
    pallas_call x6, Pallas kernels, outer(): pl.pallas_call(kernel, grid_spec=pltpu.PrefetchScalarGridSpec(num_scalar_...  54 us
    pallas_call x5, Pallas kernels, project(): pl.pallas_call(kernel, grid=(cols,), in_specs=[pl.BlockSpec((1, 1, depth,...  49.8 us
    pallas_call x4, Pallas kernels, attend(): pl.pallas_call(partial(attend_kernel, masked), grid=(heads // many,), in_...  45.5 us
    pallas_call x4, Pallas kernels, rebuild(): pl.pallas_call(kernel, grid=(4,), in_specs=[pl.BlockSpec((1, cols, tile,...  45.4 us
    all_to_all x6, waiting for transfers between devices, shared(): lax.all_to_all(jnp.broadcast_to(values[None], (size, *values.shape)), axi...  42.1 us
    pallas_call x2, Pallas kernels, contract(): pl.pallas_call(kernel, grid=(4,), in_specs=[pl.BlockSpec((1, many, tile,...  41.5 us
  transfers between devices with their start and end apart: 52, of which 26 were waited for; matrix products, arithmetic and copies ran while one was open for 21% of the time, Pallas kernels for 33%

profile of v7, /device:TPU:0, one launch (start us, length us, event | category | flops | bytes accessed | tf_op | source)
XLA Modules:
  0.0 1288.9 jit_solution(14599794351855491674)
XLA Ops:
  14.7 8.7 deal.2
  34.2 16.0 %collective-permute-done = bf16[352,384]{1,0:T(8,128)(2,1)S(1)} collective-permute-done((bf16[352,384]{1,0:T(8,128)(2,1)S(1)}, bf16[352,384]{1,0:T(8,128)(2,1)S(1)}, u32[]{:S(2)}, u32[]{:S(2)}) %collective-permute-start) | collective-permute-done | bytes 270368 | tf_op jit(solution)/shard_map/ppermute | solution.py:784
  50.1 9.0 collective-permute-done.2
  62.4 62.6 %collective-permute-done.5.own_ref = bf16[4,352,384]{2,1,0:T(8,128)(2,1)S(1)} collective-permute-done((bf16[4,352,384]{2,1,0:T(8,128)(2,1)S(1)}, bf16[4,352,384]{2,1,0:T(8,128)(2,1)S(1)}, u32[]{:S(2)}, u32[]{:S(2)}) %collective-permute-start.5) | collective-permute-done | bytes 1081376 | tf_op jit(solution)/shard_map/ppermute | solution.py:784
  128.4 6.7 assemble.2
  135.2 15.4 %collective-permute-done.6.got_ref = bf16[4,352,384]{2,1,0:T(8,128)(2,1)S(1)} collective-permute-done((bf16[4,352,384]{2,1,0:T(8,128)(2,1)S(1)}, bf16[4,352,384]{2,1,0:T(8,128)(2,1)S(1)}, u32[]{:S(2)}, u32[]{:S(2)}) %collective-permute-start.6) | collective-permute-done | bytes 1081376 | tf_op jit(solution)/shard_map/ppermute | solution.py:784
  151.6 6.6 assemble.3
  160.2 8.5 all-to-all-start.2
  168.7 6.6 all-to-all-done.2
  211.6 13.0 %project_blocks.1 = f32[1408,768]{1,0:T(8,128)} custom-call(s32[1]{0:T(128)} %bitcast.4.base_ref, bf16[2816,384]{1,0:T(8,128)(2,1)} %bitcast.362, bf16[2816,384]{1,0:T(8,128)(2,1)} %collective-permute-done.4.refs_1_, bf16[2816,384]{1,0:T(8,128)(2,1)} %bitcast.365, bf16[2816,384]{1,0:T(8,128)(2,1)} %collective-permute-done.7.refs_3_, ...), custom_call_target="tpu_custom_call" | custom-call | flops 6090129408 | bytes 8650752 | tf_op jit(solution)/shard_map/project_blocks/pallas_call | solution.py:283
  238.6 15.1 %project.5 = (f32[1408,768]{1,0:T(8,128)}, f32[1408,768]{1,0:T(8,128)}, bf16[1408,768]{1,0:T(8,128)(2,1)}) custom-call(bf16[4,4,1408,352]{3,2,1,0:T(8,128)(2,1)} %bitcast.248, bf16[4,4,1408,352]{3,2,1,0:T(8,128)(2,1)} %bitcast.249, bf16[4,4,1408,352]{3,2,1,0:T(8,128)(2,1)} %bitcast.250, bf16[1408,768]{1,0:T(8,128)(2,1)} %add_convert_fusion.4.refs_3_.refs_0_), custom_call_target="tpu_custom_call" | custom-call | flops 9135194112 | bytes 8650752 | tf_op jit(solution)/shard_map/project/pallas_call | solution.py:221
  285.3 5.6 all-to-all-start.7
  299.5 16.9 %attend.4 = (bf16[2,8,88,512]{3,2,1,0:T(8,128)(2,1)}, bf16[2,8,88,512]{3,2,1,0:T(8,128)(2,1)}, f32[8,1,1024]{2,1,0:T(1,128)}) custom-call(s32[1]{0:T(128)} %constant.200.clone.1.length_ref, bf16[2,3,8,88,512]{4,3,2,1,0:T(8,128)(2,1)} %all-to-all-done.7.q_ref.k_ref.v_ref, bf16[2,3,8,88,512]{4,3,2,1,0:T(8,128)(2,1)} %all-to-all-done.7.q_ref.k_ref.v_ref, ...), custom_call_target="tpu_custom_call" | custom-call | flops 8589934592 | bytes 5767168 | tf_op jit(solution)/shard_map/attend/pallas_call | solution.py:140
  316.4 17.2 %all-to-all-done.9.q_ref.k_ref.v_ref = bf16[4,3,4,88,256]{4,3,2,1,0:T(8,128)(2,1)S(1)} async-done(((bf16[4,3,4,88,256]{4,3,2,1,0:T(8,128)(2,1)}), bf16[4,3,4,88,256]{4,3,2,1,0:T(8,128)(2,1)S(1)}, u32[]{:S(2)}, u32[]{:S(2)}) %all-to-all-start.9) | async-done | bytes 2162720 | tf_op jit(solution)/shard_map/all_to_all | solution.py:669
  338.9 9.4 attend.5
  352.4 8.0 deal.3
  371.5 8.8 rebuild.4
  388.5 8.1 project.6
  400.5 10.7 project.7
  424.6 7.5 attend.7
  434.7 11.7 attend.6
  449.3 8.9 rebuild.5
  467.4 29.0 %all-gather.4.cloned.1.call-done = bf16[2,5632,1536]{2,1,0:T(8,128)(2,1)} async-done(((bf16[2,176,1536]{2,1,0:T(8,128)(2,1)}), bf16[2,5632,1536]{2,1,0:T(8,128)(2,1)}) %all-gather.4.cloned.1.call-update) | async-done | bytes 34603024 | tf_op jit(solution)/shard_map/all_gather | solution.py:795
  496.3 27.1 %expand.1 = (bf16[4,1536,768]{2,1,0:T(8,128)(2,1)}, bf16[4,1536,768]{2,1,0:T(8,128)(2,1)}) custom-call(bf16[2,4,1408,1536]{3,2,1,0:T(8,128)(2,1)} %bitcast.296, bf16[1408,768]{1,0:T(8,128)(2,1)} %add_convert_fusion.2.values_ref.normed_ref), custom_call_target="tpu_custom_call" | custom-call | flops 13287555072 | bytes 25952256 | tf_op jit(solution)/shard_map/expand/pallas_call | solution.py:466
  524.8 20.5 %expand_back.1.inner_ref.values_ref = bf16[4,1536,768]{2,1,0:T(8,128)(2,1)} custom-call(bf16[2,4,1408,1536]{3,2,1,0:T(8,128)(2,1)} %bitcast.297, bf16[1408,768]{1,0:T(8,128)(2,1)} %bitcast.309, bf16[4,1536,768]{2,1,0:T(8,128)(2,1)} %get-tuple-element.117.slope_ref), custom_call_target="tpu_custom_call" | custom-call | flops 13287555072 | bytes 25952256 | tf_op jit(solution)/shard_map/expand_back/pallas_call | solution.py:491
  545.3 36.3 %hidden_outer.1 = bf16[2,4,1408,1536]{3,2,1,0:T(8,128)(2,1)} custom-call(bf16[1408,768]{1,0:T(8,128)(2,1)} %bitcast.310, bf16[4,1536,768]{2,1,0:T(8,128)(2,1)} %get-tuple-element.148.act_ref.values_ref, bf16[1408,768]{1,0:T(8,128)(2,1)} %add_convert_fusion.2.values_ref.normed_ref, bf16[4,1536,768]{2,1,0:T(8,128)(2,1)} %expand_back.1.inner_ref.values_ref), custom_call_target="tpu_custom_call" | custom-call | flops 26575110144 | bytes 43253760 | tf_op jit(solution)/shard_map/hidden_outer/pallas_call | solution.py:554
  582.4 21.1 %contract.2 = f32[1408,768]{1,0:T(8,128)} custom-call(bf16[2,4,1408,1536]{3,2,1,0:T(8,128)(2,1)} %bitcast.298, bf16[4,1536,768]{2,1,0:T(8,128)(2,1)} %expand_back.1.inner_ref.values_ref), custom_call_target="tpu_custom_call" | custom-call | flops 13287555072 | bytes 25952256 | tf_op jit(solution)/shard_map/contract/pallas_call | solution.py:521
  603.5 7.2 multiply_reduce_fusion.3
  616.0 8.2 project.8
  629.1 9.9 attend_back.5
  639.0 15.7 %attend_back.4 = (f32[1,1,16,88,512]{4,3,2,1,0:T(8,128)}, f32[1,1,16,88,384]{4,3,2,1,0:T(8,128)}, f32[1,1,16,88,384]{4,3,2,1,0:T(8,128)}) custom-call(s32[1]{0:T(128)} %get-tuple-element.428.length_ref, bf16[1,1,16,88,512]{4,3,2,1,0:T(8,128)(2,1)} %slice_bitcast_fusion.1.q_ref, bf16[1,1,16,88,384]{4,3,2,1,0:T(8,128)(2,1)} %get-tuple-element.390.k_ref, ...), custom_call_target="tpu_custom_call" | custom-call | flops 8053063680 | bytes 12615680 | tf_op jit(solution)/shard_map/attend_back/pallas_call | solution.py:173
  666.4 8.5 rebuild.6
  675.0 5.9 multiply_reduce_fusion.4
  680.9 8.2 fusion.62
  689.0 7.7 project.9
  714.0 25.9 %attend_back.6 = bf16[2,3,8,88,512]{4,3,2,1,0:T(8,128)(2,1)} custom-call(s32[1]{0:T(128)} %constant.200.clone.1.length_ref, bf16[2,3,8,88,512]{4,3,2,1,0:T(8,128)(2,1)} %all-to-all-done.7.q_ref.k_ref.v_ref, bf16[2,3,8,88,512]{4,3,2,1,0:T(8,128)(2,1)} %all-to-all-done.7.q_ref.k_ref.v_ref, bf16[2,3,8,88,512]{4,3,2,1,0:T(8,128)(2,1)} %all-to-all-done.7.q_ref.k_ref.v_ref, ...), custom_call_target="tpu_custom_call" | custom-call | flops 21474836480 | bytes 14417920 | tf_op jit(solution)/shard_map/attend_back/pallas_call | solution.py:173
  753.5 5.7 all-to-all-start.12
  759.2 14.2 %attend_back.7 = bf16[4,3,4,88,256]{4,3,2,1,0:T(8,128)(2,1)} custom-call(s32[1]{0:T(128)} %constant.200.clone.1.length_ref, bf16[4,3,4,88,256]{4,3,2,1,0:T(8,128)(2,1)} %copy-done.40, bf16[4,3,4,88,256]{4,3,2,1,0:T(8,128)(2,1)} %copy-done.40, bf16[4,3,4,88,256]{4,3,2,1,0:T(8,128)(2,1)} %copy-done.40, bf16[4,4,88,256]{3,2,1,0:T(8,128)(2,1)} %get-tuple-element.110.m_ref, ...), custom_call_target="tpu_custom_call" | custom-call | flops 10737418240 | bytes 7208960 | tf_op jit(solution)/shard_map/attend_back/pallas_call | solution.py:173
  778.1 31.0 %outer_all.1 = bf16[5,4,1408,352]{3,2,1,0:T(8,128)(2,1)} custom-call(bf16[1408,768]{1,0:T(8,128)(2,1)} %fusion.56.refs_1_.refs_0_, bf16[1408,768]{1,0:T(8,128)(2,1)} %add_convert_fusion.3.refs_1_, bf16[1408,768]{1,0:T(8,128)(2,1)} %bitcast.339, bf16[1408,768]{1,0:T(8,128)(2,1)} %get-tuple-element.349.refs_1_.refs_3_, ...), custom_call_target="tpu_custom_call" | custom-call | flops 15225323520 | bytes 29736960 | tf_op jit(solution)/shard_map/outer_all/pallas_call | solution.py:434
  824.3 7.5 multiply_reduce_fusion.8
  846.9 9.0 outer.6
  857.9 6.1 outer.7
  864.2 19.1 %rebuild.7 = f32[1408,768]{1,0:T(8,128)} custom-call(bf16[4,4,1408,352]{3,2,1,0:T(8,128)(2,1)} %bitcast.253, bf16[4,4,1408,352]{3,2,1,0:T(8,128)(2,1)} %bitcast.254, bf16[4,4,1408,352]{3,2,1,0:T(8,128)(2,1)} %bitcast.255, bf16[1408,768]{1,0:T(8,128)(2,1)} %bitcast.333, bf16[1408,768]{1,0:T(8,128)(2,1)} %bitcast.336, ...), custom_call_target="tpu_custom_call" | custom-call | flops 9135194112 | bytes 8650752 | tf_op jit(solution)/shard_map/rebuild/pallas_call | solution.py:250
  884.7 7.3 outer.9
  892.0 11.0 outer.8
  912.6 10.9 multiply_reduce_fusion.5
  932.0 6.8 multiply_convert_fusion.refs_4_.refs_1_
  939.5 9.8 outer.10
  952.5 13.4 %rebuild_blocks.1 = bf16[2816,768]{1,0:T(8,128)(2,1)} custom-call(s32[1]{0:T(128)} %bitcast.4.base_ref, bf16[2816,384]{1,0:T(8,128)(2,1)} %bitcast.363, bf16[2816,384]{1,0:T(8,128)(2,1)} %collective-permute-done.4.refs_1_, bf16[2816,384]{1,0:T(8,128)(2,1)} %bitcast.366, bf16[2816,384]{1,0:T(8,128)(2,1)} %collective-permute-done.7.refs_3_, ...), custom_call_target="tpu_custom_call" | custom-call | flops 6090129408 | bytes 8650752 | tf_op jit(solution)/shard_map/rebuild_blocks/pallas_call | solution.py:314
  965.9 10.7 collective-permute-done.12
  976.6 32.0 %collective-permute-done.11 = bf16[2,2,4,176,384]{4,3,2,1,0:T(8,128)(2,1)S(1)} collective-permute-done((bf16[2,2,4,176,384]{4,3,2,1,0:T(8,128)(2,1)}, bf16[2,2,4,176,384]{4,3,2,1,0:T(8,128)(2,1)S(1)}, u32[]{:S(2)}, u32[]{:S(2)}) %collective-permute-start.11) | collective-permute-done | bytes 2162720 | tf_op jit(solution)/shard_map/ppermute | solution.py:784
  1008.6 10.7 outer.11
  1032.2 20.4 %contract.3 = bf16[1408,768]{1,0:T(8,128)(2,1)} custom-call(bf16[2,4,1408,1536]{3,2,1,0:T(8,128)(2,1)} %bitcast.299, bf16[4,1536,768]{2,1,0:T(8,128)(2,1)} %get-tuple-element.148.act_ref.values_ref, f32[1408,768]{1,0:T(8,128)} %copy-done.3), custom_call_target="tpu_custom_call" | custom-call | flops 13287555072 | bytes 25952256 | tf_op jit(solution)/shard_map/contract/pallas_call | solution.py:521
  1058.0 36.1 %collective-permute-done.13 = bf16[1,2,4,352,384]{4,3,2,1,0:T(8,128)(2,1)} collective-permute-done((bf16[1,2,4,352,384]{4,3,2,1,0:T(8,128)(2,1)}, bf16[1,2,4,352,384]{4,3,2,1,0:T(8,128)(2,1)}, u32[]{:S(2)}, u32[]{:S(2)}) %collective-permute-start.13) | collective-permute-done | bytes 2162720 | tf_op jit(solution)/shard_map/ppermute | solution.py:784
  1096.3 8.7 collective-permute-done.15
  1105.0 24.4 %collective-permute-done.14 = bf16[2,4,176,384]{3,2,1,0:T(8,128)(2,1)} collective-permute-done((bf16[2,4,176,384]{3,2,1,0:T(8,128)(2,1)}, bf16[2,4,176,384]{3,2,1,0:T(8,128)(2,1)}, u32[]{:S(2)}, u32[]{:S(2)}) %collective-permute-start.14) | collective-permute-done | bytes 1081376 | tf_op jit(solution)/shard_map/ppermute | solution.py:784
  1137.1 8.1 collective-permute-done.23
  1155.6 8.3 collective-permute-done.22
  1163.9 19.0 %collective-permute-done.21 = bf16[2,176,384]{2,1,0:T(8,128)(2,1)} collective-permute-done((bf16[2,176,384]{2,1,0:T(8,128)(2,1)S(1)}, bf16[2,176,384]{2,1,0:T(8,128)(2,1)}, u32[]{:S(2)}, u32[]{:S(2)}) %collective-permute-start.21) | collective-permute-done | bytes 270368 | tf_op jit(solution)/shard_map/ppermute | solution.py:784
  1185.7 9.1 undeal.2
  1208.1 20.8 %all-to-all-done.19 = bf16[8,3,2,352]{3,2,1,0:T(2,128)(2,1)S(1)} async-done(((bf16[8,3,2,352]{3,2,1,0:T(2,128)(2,1)}), bf16[8,3,2,352]{3,2,1,0:T(2,128)(2,1)S(1)}, u32[]{:S(2)}, u32[]{:S(2)}) %all-to-all-start.19) | async-done | bytes 33824 | tf_op jit(solution)/shard_map/all_to_all | solution.py:777
  1233.9 6.0 all-to-all-done.18
  1259.2 13.7 %all-to-all-done.20.got_ref = bf16[4,352,768]{2,1,0:T(8,128)(2,1)S(1)} async-done(((bf16[4,352,768]{2,1,0:T(8,128)(2,1)}), bf16[4,352,768]{2,1,0:T(8,128)(2,1)S(1)}, u32[]{:S(2)}, u32[]{:S(2)}) %all-to-all-start.20) | async-done | bytes 2162720 | tf_op jit(solution)/shard_map/all_to_all | solution.py:669
  1274.2 8.0 undeal.3
  (585 shorter events, 372.7 us)
Async XLA Ops:
  7.2 177.0 %copy-start = (bf16[176,2,352]{2,1,0:T(2,128)(2,1)S(1)}, bf16[176,2,352]{2,1,0:T(2,128)(2,1)}, u32[]{:S(2)}) copy-start(bf16[176,2,352]{2,1,0:T(2,128)(2,1)} %param.34) | copy-start | bytes 743428
  7.2 231.3 %all-gather.6.cloned.1.call-start = ((), (), s32[]{:S(2)}) async-start(), calls=%async_computation.24 | async-start | bytes 17842176 | tf_op jit(solution)/shard_map/all_gather | solution.py:795
  10.3 378.2 %all-gather.8.cloned.1.call-start = ((), (), s32[]{:S(2)}) async-start(), calls=%async_computation.25 | async-start | bytes 17842176 | tf_op jit(solution)/shard_map/all_gather | solution.py:795
  13.5 482.8 %all-gather.4.cloned.1.call-start = ((), (), s32[]{:S(2)}) async-start(), calls=%async_computation.23 | async-start | bytes 35684352 | tf_op jit(solution)/shard_map/all_gather | solution.py:795
  23.4 136.2 %all-to-all-start = ((bf16[4,704,768]{2,1,0:T(8,128)(2,1)}), bf16[4,704,768]{2,1,0:T(8,128)(2,1)}, u32[]{:S(2)}, u32[]{:S(2)}) async-start(bf16[4,704,768]{2,1,0:T(8,128)(2,1)} %deal.2), calls=%async_computation | async-start | bytes 8650752 | tf_op jit(solution)/shard_map/all_to_all | solution.py:669
  28.5 21.7 %collective-permute-start = (bf16[352,384]{1,0:T(8,128)(2,1)S(1)}, bf16[352,384]{1,0:T(8,128)(2,1)S(1)}, u32[]{:S(2)}, u32[]{:S(2)}) collective-permute-start(bf16[352,384]{1,0:T(8,128)(2,1)S(1)} %get-tuple-element.415), channel_id=1, source_target_pairs={{0,8},{4,12},{8,0},{12,4},{16,24},{20,28},{24,16},{28,20},{1,9},{5... | collective-permute-start | bytes 811016 | tf_op jit(solution)/shard_map/ppermute | solution.py:784
  31.6 18.5 %collective-permute-start.1 = (bf16[352,384]{1,0:T(8,128)(2,1)S(1)}, bf16[352,384]{1,0:T(8,128)(2,1)S(1)}, u32[]{:S(2)}, u32[]{:S(2)}) collective-permute-start(bf16[352,384]{1,0:T(8,128)(2,1)S(1)} %get-tuple-element.415), channel_id=1, source_target_pairs={{0,16},{4,20},{8,24},{12,28},{16,0},{20,4},{24,8},{28,12},{1,17},{... | collective-permute-start | bytes 811016 | tf_op jit(solution)/shard_map/ppermute | solution.py:784
  34.2 25.0 %collective-permute-start.2 = (bf16[352,384]{1,0:T(8,128)(2,1)S(1)}, bf16[352,384]{1,0:T(8,128)(2,1)S(1)}, u32[]{:S(2)}, u32[]{:S(2)}) collective-permute-start(bf16[352,384]{1,0:T(8,128)(2,1)S(1)} %get-tuple-element.415), channel_id=1, source_target_pairs={{0,24},{4,28},{8,16},{12,20},{16,8},{20,12},{24,0},{28,4},{1,25},{... | collective-permute-start | bytes 811016 | tf_op jit(solution)/shard_map/ppermute | solution.py:784
  59.3 69.1 %copy-start.34 = (bf16[4,352,384]{2,1,0:T(8,128)(2,1)}, bf16[4,352,384]{2,1,0:T(8,128)(2,1)S(1)}, u32[]{:S(2)}) copy-start(bf16[4,352,384]{2,1,0:T(8,128)(2,1)S(1)} %pad_maximum_fusion.12.own_ref) | copy-start | bytes 3244036
  59.3 65.7 %collective-permute-start.5 = (bf16[4,352,384]{2,1,0:T(8,128)(2,1)S(1)}, bf16[4,352,384]{2,1,0:T(8,128)(2,1)S(1)}, u32[]{:S(2)}, u32[]{:S(2)}) collective-permute-start(bf16[4,352,384]{2,1,0:T(8,128)(2,1)S(1)} %pad_maximum_fusion.12.own_ref), channel_id=1, source_target_pairs={{0,2},{1,3},{2,0},{3,1},{4,6},{5,7},{6,4},{7,5},{8,10},{9,11},{10,... | collective-permute-start | bytes 3244040 | tf_op jit(solution)/shard_map/ppermute | solution.py:784
  60.9 67.5 %collective-permute-start.3 = (bf16[4,352,384]{2,1,0:T(8,128)(2,1)S(1)}, bf16[4,352,384]{2,1,0:T(8,128)(2,1)}, u32[]{:S(2)}, u32[]{:S(2)}) collective-permute-start(bf16[4,352,384]{2,1,0:T(8,128)(2,1)S(1)} %pad_maximum_fusion.12.own_ref), channel_id=1, source_target_pairs={{0,4},{4,0},{8,12},{12,8},{16,20},{20,16},{24,28},{28,24},{1,5},{5... | collective-permute-start | bytes 3244040 | tf_op jit(solution)/shard_map/ppermute | solution.py:784
  125.0 25.6 %collective-permute-start.6 = (bf16[4,352,384]{2,1,0:T(8,128)(2,1)S(1)}, bf16[4,352,384]{2,1,0:T(8,128)(2,1)S(1)}, u32[]{:S(2)}, u32[]{:S(2)}) collective-permute-start(bf16[4,352,384]{2,1,0:T(8,128)(2,1)S(1)} %collective-permute-done.5.own_ref), channel_id=1, source_target_pairs={{0,4},{4,0},{8,12},{12,8},{16,20},{20,16},{24,28},{28,24},{1,5},{5... | collective-permute-start | bytes 3244040 | tf_op jit(solution)/shard_map/ppermute | solution.py:784
  135.1 76.5 %collective-permute-start.4 = (bf16[2816,384]{1,0:T(8,128)(2,1)}, bf16[2816,384]{1,0:T(8,128)(2,1)}, u32[]{:S(2)}, u32[]{:S(2)}) collective-permute-start(bf16[2816,384]{1,0:T(8,128)(2,1)} %bitcast.361), channel_id=1, source_target_pairs={{0,1},{1,0},{2,3},{3,2},{4,5},{5,4},{6,7},{7,6},{8,9},{9,8},{10,11... | collective-permute-start | bytes 6488072 | tf_op jit(solution)/shard_map/ppermute | solution.py:784
  158.1 53.5 %collective-permute-start.7 = (bf16[2816,384]{1,0:T(8,128)(2,1)}, bf16[2816,384]{1,0:T(8,128)(2,1)}, u32[]{:S(2)}, u32[]{:S(2)}) collective-permute-start(bf16[2816,384]{1,0:T(8,128)(2,1)} %bitcast.364), channel_id=1, source_target_pairs={{0,1},{1,0},{2,3},{3,2},{4,5},{5,4},{6,7},{7,6},{8,9},{9,8},{10,11... | collective-permute-start | bytes 6488072 | tf_op jit(solution)/shard_map/ppermute | solution.py:784
  160.2 15.1 %all-to-all-start.2 = ((bf16[8,3,352]{2,1,0:T(4,128)(2,1)}), bf16[8,3,352]{2,1,0:T(4,128)(2,1)S(1)}, u32[]{:S(2)}, u32[]{:S(2)}) async-start(bf16[8,3,352]{2,1,0:T(4,128)(2,1)} %broadcast_in_dim.199), calls=%async_computation.2 | async-start | bytes 49152 | tf_op jit(solution)/shard_map/all_to_all | solution.py:777
  175.9 8.1 all-to-all-start.3
  185.1 10.3 all-to-all-start.4
  190.2 87.1 %copy-start.23 = (f32[88,768]{1,0:T(8,128)}, f32[88,768]{1,0:T(8,128)S(1)}, u32[]{:S(2)}) copy-start(f32[88,768]{1,0:T(8,128)S(1)} %get-tuple-element.420) | copy-start | bytes 811012
  196.2 8.9 all-to-all-start.5
  206.8 46.9 %all-to-all-start.6 = ((bf16[4,3,384,256]{2,3,1,0:T(8,128)(2,1)}), bf16[4,3,384,256]{2,3,1,0:T(8,128)(2,1)S(1)}, u32[]{:S(2)}, u32[]{:S(2)}) async-start(bf16[4,3,384,256]{2,3,1,0:T(8,128)(2,1)} %broadcast_in_dim.212), calls=%async_computation.6 | async-start | bytes 4718592 | tf_op jit(solution)/shard_map/all_to_all | solution.py:777
  211.6 168.8 %copy-start.65 = (f32[1408]{0:T(1024)}, f32[1408]{0:T(1024)S(1)}, u32[]{:S(2)}) copy-start(f32[1408]{0:T(1024)S(1)} %get-tuple-element.339) | copy-start | bytes 16900
  211.6 168.8 %copy-start.73 = (f32[1408]{0:T(1024)}, f32[1408]{0:T(1024)S(1)}, u32[]{:S(2)}) copy-start(f32[1408]{0:T(1024)S(1)} %get-tuple-element.338) | copy-start | bytes 16900
  211.6 173.5 %copy-start.83 = (f32[1408]{0:T(1024)}, f32[1408]{0:T(1024)S(1)}, u32[]{:S(2)}) copy-start(f32[1408]{0:T(1024)S(1)} %get-tuple-element.333) | copy-start | bytes 16900
  227.2 153.2 %copy-start.75 = (f32[768]{0:T(1024)}, f32[768]{0:T(1024)S(1)}, u32[]{:S(2)}) copy-start(f32[768]{0:T(1024)S(1)} %broadcast_multiply_fusion.17) | copy-start | bytes 9220
  230.1 150.3 %copy-start.78 = (f32[768]{0:T(1024)}, f32[768]{0:T(1024)S(1)}, u32[]{:S(2)}) copy-start(f32[768]{0:T(1024)S(1)} %add_rsqrt_fusion.3) | copy-start | bytes 9220
  285.3 10.6 all-to-all-start.7
  295.9 37.7 %all-to-all-start.9 = ((bf16[4,3,4,88,256]{4,3,2,1,0:T(8,128)(2,1)}), bf16[4,3,4,88,256]{4,3,2,1,0:T(8,128)(2,1)S(1)}, u32[]{:S(2)}, u32[]{:S(2)}) async-start(bf16[4,3,4,88,256]{4,3,2,1,0:T(8,128)(2,1)} %pad_maximum_fusion.3), calls=%async_computation.9 | async-start | bytes 4325376 | tf_op jit(solution)/shard_map/all_to_all | solution.py:669
  335.1 13.2 %all-to-all-start.8 = ((bf16[2,8,88,512]{3,2,1,0:T(8,128)(2,1)}), bf16[2,8,88,512]{3,2,1,0:T(8,128)(2,1)S(1)}, u32[]{:S(2)}, u32[]{:S(2)}) async-start(bf16[2,8,88,512]{3,2,1,0:T(8,128)(2,1)} %get-tuple-element.109.m_ref), calls=%async_computation.8 | async-start | bytes 2883584 | tf_op jit(solution)/shard_map/all_to_all | solution.py:670
  348.3 14.7 %all-to-all-start.10 = ((bf16[4,4,88,256]{3,2,1,0:T(8,128)(2,1)}), bf16[4,4,88,256]{3,2,1,0:T(8,128)(2,1)S(1)}, u32[]{:S(2)}, u32[]{:S(2)}) async-start(bf16[4,4,88,256]{3,2,1,0:T(8,128)(2,1)} %get-tuple-element.110.m_ref), calls=%async_computation.10 | async-start | bytes 1441792 | tf_op jit(solution)/shard_map/all_to_all | solution.py:669
  363.0 160.5 %all-to-all-start.1 = ((bf16[4,352,768]{2,1,0:T(8,128)(2,1)}), bf16[4,352,768]{2,1,0:T(8,128)(2,1)S(1)}, u32[]{:S(2)}, u32[]{:S(2)}) async-start(bf16[4,352,768]{2,1,0:T(8,128)(2,1)} %deal.3), calls=%async_computation.1 | async-start | bytes 4325376 | tf_op jit(solution)/shard_map/all_to_all | solution.py:669
  366.6 873.4 %reduce-scatter.3.cloned.1.call-start = ((), (), s32[]{:S(2)}) async-start(), calls=%async_computation.26 | async-start | bytes 35684352 | tf_op jit(solution)/shard_map/reduce_scatter | solution.py:1085
  701.5 8.5 all-to-all-start.11
  710.1 42.6 %all-to-all-start.13 = ((bf16[4,4,88,256]{3,2,1,0:T(8,128)(2,1)}), bf16[4,4,88,256]{3,2,1,0:T(8,128)(2,1)S(1)}, u32[]{:S(2)}, u32[]{:S(2)}) async-start(bf16[4,4,88,256]{3,2,1,0:T(8,128)(2,1)} %bitcast.78), calls=%async_computation.13 | async-start | bytes 1441792 | tf_op jit(solution)/shard_map/all_to_all | solution.py:669
  753.5 19.9 %all-to-all-start.12 = ((bf16[2,3,8,88,512]{4,3,2,1,0:T(8,128)(2,1)}), bf16[2,3,8,88,512]{4,3,2,1,0:T(8,128)(2,1)}, u32[]{:S(2)}, u32[]{:S(2)}) async-start(bf16[2,3,8,88,512]{4,3,2,1,0:T(8,128)(2,1)} %attend_back.6), calls=%async_computation.12 | async-start | bytes 8650752 | tf_op jit(solution)/shard_map/all_to_all | solution.py:670
  773.4 40.2 %all-to-all-start.14 = ((bf16[4,3,4,88,256]{4,3,2,1,0:T(8,128)(2,1)}), bf16[4,3,4,88,256]{4,3,2,1,0:T(8,128)(2,1)}, u32[]{:S(2)}, u32[]{:S(2)}) async-start(bf16[4,3,4,88,256]{4,3,2,1,0:T(8,128)(2,1)} %attend_back.7), calls=%async_computation.14 | async-start | bytes 4325376 | tf_op jit(solution)/shard_map/all_to_all | solution.py:669
  777.9 470.6 %reduce-scatter.5.cloned.1.call-start = ((), (), s32[]{:S(2)}) async-start(), calls=%async_computation.27 | async-start | bytes 22302720 | tf_op jit(solution)/shard_map/reduce_scatter | solution.py:1121
  856.0 27.4 %collective-permute-start.8 = (bf16[2,2,1408,384]{3,2,1,0:T(8,128)(2,1)}, bf16[2,2,1408,384]{3,2,1,0:T(8,128)(2,1)}, u32[]{:S(2)}, u32[]{:S(2)}) collective-permute-start(bf16[2,2,1408,384]{3,2,1,0:T(8,128)(2,1)} %outer.6), channel_id=1, source_target_pairs={{0,1},{1,0},{2,3},{3,2},{4,5},{5,4},{6,7},{7,6},{8,9},{9,8},{10,11... | collective-permute-start | bytes 12976136 | tf_op jit(solution)/shard_map/ppermute | solution.py:784
  864.0 19.3 %collective-permute-start.9 = (bf16[1,2,1408,384]{3,2,1,0:T(8,128)(2,1)}, bf16[1,2,1408,384]{3,2,1,0:T(8,128)(2,1)S(1)}, u32[]{:S(2)}, u32[]{:S(2)}) collective-permute-start(bf16[1,2,1408,384]{3,2,1,0:T(8,128)(2,1)} %outer.7), channel_id=1, source_target_pairs={{0,1},{1,0},{2,3},{3,2},{4,5},{5,4},{6,7},{7,6},{8,9},{9,8},{10,11... | collective-permute-start | bytes 6488072 | tf_op jit(solution)/shard_map/ppermute | solution.py:784
  928.5 10.3 all-to-all-start.15
  949.2 59.3 %collective-permute-start.10 = (bf16[1,2,2816,384]{3,2,1,0:T(8,128)(2,1)}, bf16[1,2,2816,384]{3,2,1,0:T(8,128)(2,1)}, u32[]{:S(2)}, u32[]{:S(2)}) collective-permute-start(bf16[1,2,2816,384]{3,2,1,0:T(8,128)(2,1)} %outer.10), channel_id=1, source_target_pairs={{0,1},{1,0},{2,3},{3,2},{4,5},{5,4},{6,7},{7,6},{8,9},{9,8},{10,11... | collective-permute-start | bytes 12976136 | tf_op jit(solution)/shard_map/ppermute | solution.py:784
  949.8 58.8 %collective-permute-start.11 = (bf16[2,2,4,176,384]{4,3,2,1,0:T(8,128)(2,1)}, bf16[2,2,4,176,384]{4,3,2,1,0:T(8,128)(2,1)S(1)}, u32[]{:S(2)}, u32[]{:S(2)}) collective-permute-start(bf16[2,2,4,176,384]{4,3,2,1,0:T(8,128)(2,1)} %get-tuple-element.138), channel_id=1, source_target_pairs={{0,4},{4,0},{8,12},{12,8},{16,20},{20,16},{24,28},{28,24},{1,5},{5... | collective-permute-start | bytes 6488072 | tf_op jit(solution)/shard_map/ppermute | solution.py:784
  950.6 26.0 %collective-permute-start.12 = (bf16[1,4,2,176,384]{4,3,2,1,0:T(8,128)(2,1)}, bf16[1,4,2,176,384]{4,3,2,1,0:T(8,128)(2,1)S(1)}, u32[]{:S(2)}, u32[]{:S(2)}) collective-permute-start(bf16[1,4,2,176,384]{4,3,2,1,0:T(8,128)(2,1)} %get-tuple-element.140), channel_id=1, source_target_pairs={{0,2},{1,3},{2,0},{3,1},{4,6},{5,7},{6,4},{7,5},{8,10},{9,11},{10,... | collective-permute-start | bytes 3244040 | tf_op jit(solution)/shard_map/ppermute | solution.py:784
  965.8 54.3 %copy-start.98 = (f32[1408]{0:T(1024)S(1)}, f32[1408]{0:T(1024)}, u32[]{:S(2)}) copy-start(f32[1408]{0:T(1024)} %get-tuple-element.325) | copy-start | bytes 16900
  965.8 54.4 %copy-start.102 = (f32[1408]{0:T(1024)S(1)}, f32[1408]{0:T(1024)}, u32[]{:S(2)}) copy-start(f32[1408]{0:T(1024)} %get-tuple-element.357) | copy-start | bytes 16900
  965.9 55.0 %copy-start.101 = (f32[1408]{0:T(1024)S(1)}, f32[1408]{0:T(1024)}, u32[]{:S(2)}) copy-start(f32[1408]{0:T(1024)} %get-tuple-element.316) | copy-start | bytes 16900
  965.9 55.1 %copy-start.100 = (f32[1408]{0:T(1024)S(1)}, f32[1408]{0:T(1024)}, u32[]{:S(2)}) copy-start(f32[1408]{0:T(1024)} %get-tuple-element.326) | copy-start | bytes 16900
  1019.3 74.7 %collective-permute-start.13 = (bf16[1,2,4,352,384]{4,3,2,1,0:T(8,128)(2,1)}, bf16[1,2,4,352,384]{4,3,2,1,0:T(8,128)(2,1)}, u32[]{:S(2)}, u32[]{:S(2)}) collective-permute-start(bf16[1,2,4,352,384]{4,3,2,1,0:T(8,128)(2,1)} %get-tuple-element.150), channel_id=1, source_target_pairs={{0,4},{4,0},{8,12},{12,8},{16,20},{20,16},{24,28},{28,24},{1,5},{5... | collective-permute-start | bytes 6488072 | tf_op jit(solution)/shard_map/ppermute | solution.py:784
  1022.3 163.4 %all-to-all-start.16 = ((bf16[4,704,768]{2,1,0:T(8,128)(2,1)}), bf16[4,704,768]{2,1,0:T(8,128)(2,1)}, u32[]{:S(2)}, u32[]{:S(2)}) async-start(bf16[4,704,768]{2,1,0:T(8,128)(2,1)} %bitcast.351), calls=%async_computation.17 | async-start | bytes 8650752 | tf_op jit(solution)/shard_map/all_to_all | solution.py:669
  1030.3 99.2 %collective-permute-start.14 = (bf16[2,4,176,384]{3,2,1,0:T(8,128)(2,1)}, bf16[2,4,176,384]{3,2,1,0:T(8,128)(2,1)}, u32[]{:S(2)}, u32[]{:S(2)}) collective-permute-start(bf16[2,4,176,384]{3,2,1,0:T(8,128)(2,1)} %fusion.20), channel_id=1, source_target_pairs={{0,2},{1,3},{2,0},{3,1},{4,6},{5,7},{6,4},{7,5},{8,10},{9,11},{10,... | collective-permute-start | bytes 3244040 | tf_op jit(solution)/shard_map/ppermute | solution.py:784
  1054.0 51.0 %collective-permute-start.15 = (bf16[1,4,176,384]{3,2,1,0:T(8,128)(2,1)S(1)}, bf16[1,4,176,384]{3,2,1,0:T(8,128)(2,1)S(1)}, u32[]{:S(2)}, u32[]{:S(2)}) collective-permute-start(bf16[1,4,176,384]{3,2,1,0:T(8,128)(2,1)S(1)} %fusion.24), channel_id=1, source_target_pairs={{0,4},{4,0},{8,12},{12,8},{16,20},{20,16},{24,28},{28,24},{1,5},{5... | collective-permute-start | bytes 1622024 | tf_op jit(solution)/shard_map/ppermute | solution.py:784
  1129.4 54.7 %collective-permute-start.16 = (bf16[1,4,352,384]{3,2,1,0:T(8,128)(2,1)S(1)}, bf16[1,4,352,384]{3,2,1,0:T(8,128)(2,1)}, u32[]{:S(2)}, u32[]{:S(2)}) collective-permute-start(bf16[1,4,352,384]{3,2,1,0:T(8,128)(2,1)S(1)} %get-tuple-element.361), channel_id=1, source_target_pairs={{0,2},{1,3},{2,0},{3,1},{4,6},{5,7},{6,4},{7,5},{8,10},{9,11},{10,... | collective-permute-start | bytes 3244040 | tf_op jit(solution)/shard_map/ppermute | solution.py:784
  1130.0 15.1 %collective-permute-start.23 = (bf16[1,176,384]{2,1,0:T(8,128)(2,1)S(1)}, bf16[1,176,384]{2,1,0:T(8,128)(2,1)S(1)}, u32[]{:S(2)}, u32[]{:S(2)}) collective-permute-start(bf16[1,176,384]{2,1,0:T(8,128)(2,1)S(1)} %get-tuple-element.403), channel_id=1, source_target_pairs={{0,8},{4,12},{8,0},{12,4},{16,24},{20,28},{24,16},{28,20},{1,9},{5... | collective-permute-start | bytes 405512 | tf_op jit(solution)/shard_map/ppermute | solution.py:784
  1130.1 16.3 %collective-permute-start.25 = (bf16[1,176,384]{2,1,0:T(8,128)(2,1)S(1)}, bf16[1,176,384]{2,1,0:T(8,128)(2,1)S(1)}, u32[]{:S(2)}, u32[]{:S(2)}) collective-permute-start(bf16[1,176,384]{2,1,0:T(8,128)(2,1)S(1)} %get-tuple-element.404), channel_id=1, source_target_pairs={{0,24},{4,28},{8,16},{12,20},{16,8},{20,12},{24,0},{28,4},{1,25},{... | collective-permute-start | bytes 405512 | tf_op jit(solution)/shard_map/ppermute | solution.py:784
  1132.7 21.4 %collective-permute-start.24 = (bf16[1,176,384]{2,1,0:T(8,128)(2,1)S(1)}, bf16[1,176,384]{2,1,0:T(8,128)(2,1)}, u32[]{:S(2)}, u32[]{:S(2)}) collective-permute-start(bf16[1,176,384]{2,1,0:T(8,128)(2,1)S(1)} %get-tuple-element.405), channel_id=1, source_target_pairs={{0,16},{4,20},{8,24},{12,28},{16,0},{20,4},{24,8},{28,12},{1,17},{... | collective-permute-start | bytes 405512 | tf_op jit(solution)/shard_map/ppermute | solution.py:784
  1136.1 19.5 %collective-permute-start.20 = (bf16[2,176,384]{2,1,0:T(8,128)(2,1)}, bf16[2,176,384]{2,1,0:T(8,128)(2,1)S(1)}, u32[]{:S(2)}, u32[]{:S(2)}) collective-permute-start(bf16[2,176,384]{2,1,0:T(8,128)(2,1)} %get-tuple-element.395), channel_id=1, source_target_pairs={{0,8},{4,12},{8,0},{12,4},{16,24},{20,28},{24,16},{28,20},{1,9},{5... | collective-permute-start | bytes 811016 | tf_op jit(solution)/shard_map/ppermute | solution.py:784
  1145.1 18.8 %collective-permute-start.22 = (bf16[2,176,384]{2,1,0:T(8,128)(2,1)}, bf16[2,176,384]{2,1,0:T(8,128)(2,1)}, u32[]{:S(2)}, u32[]{:S(2)}) collective-permute-start(bf16[2,176,384]{2,1,0:T(8,128)(2,1)} %get-tuple-element.396), channel_id=1, source_target_pairs={{0,24},{4,28},{8,16},{12,20},{16,8},{20,12},{24,0},{28,4},{1,25},{... | collective-permute-start | bytes 811016 | tf_op jit(solution)/shard_map/ppermute | solution.py:784
  1146.4 36.5 %collective-permute-start.21 = (bf16[2,176,384]{2,1,0:T(8,128)(2,1)S(1)}, bf16[2,176,384]{2,1,0:T(8,128)(2,1)}, u32[]{:S(2)}, u32[]{:S(2)}) collective-permute-start(bf16[2,176,384]{2,1,0:T(8,128)(2,1)S(1)} %get-tuple-element.397), channel_id=1, source_target_pairs={{0,16},{4,20},{8,24},{12,28},{16,0},{20,4},{24,8},{28,12},{1,17},{... | collective-permute-start | bytes 811016 | tf_op jit(solution)/shard_map/ppermute | solution.py:784
  1195.4 7.7 all-to-all-start.17
  1199.7 46.8 %collective-permute-start.17 = (bf16[1,352,384]{2,1,0:T(8,128)(2,1)}, bf16[1,352,384]{2,1,0:T(8,128)(2,1)}, u32[]{:S(2)}, u32[]{:S(2)}) collective-permute-start(bf16[1,352,384]{2,1,0:T(8,128)(2,1)} %get-tuple-element.399), channel_id=1, source_target_pairs={{0,8},{4,12},{8,0},{12,4},{16,24},{20,28},{24,16},{28,20},{1,9},{5... | collective-permute-start | bytes 811016 | tf_op jit(solution)/shard_map/ppermute | solution.py:784
  1199.7 46.8 %collective-permute-start.19 = (bf16[1,352,384]{2,1,0:T(8,128)(2,1)}, bf16[1,352,384]{2,1,0:T(8,128)(2,1)}, u32[]{:S(2)}, u32[]{:S(2)}) collective-permute-start(bf16[1,352,384]{2,1,0:T(8,128)(2,1)} %get-tuple-element.400), channel_id=1, source_target_pairs={{0,24},{4,28},{8,16},{12,20},{16,8},{20,12},{24,0},{28,4},{1,25},{... | collective-permute-start | bytes 811016 | tf_op jit(solution)/shard_map/ppermute | solution.py:784
  1200.7 45.7 %collective-permute-start.18 = (bf16[1,352,384]{2,1,0:T(8,128)(2,1)S(1)}, bf16[1,352,384]{2,1,0:T(8,128)(2,1)}, u32[]{:S(2)}, u32[]{:S(2)}) collective-permute-start(bf16[1,352,384]{2,1,0:T(8,128)(2,1)S(1)} %get-tuple-element.401), channel_id=1, source_target_pairs={{0,16},{4,20},{8,24},{12,28},{16,0},{20,4},{24,8},{28,12},{1,17},{... | collective-permute-start | bytes 811016 | tf_op jit(solution)/shard_map/ppermute | solution.py:784
  1203.8 25.1 %all-to-all-start.19 = ((bf16[8,3,2,352]{3,2,1,0:T(2,128)(2,1)}), bf16[8,3,2,352]{3,2,1,0:T(2,128)(2,1)S(1)}, u32[]{:S(2)}, u32[]{:S(2)}) async-start(bf16[8,3,2,352]{3,2,1,0:T(2,128)(2,1)} %broadcast_in_dim.234), calls=%async_computation.20 | async-start | bytes 73728 | tf_op jit(solution)/shard_map/all_to_all | solution.py:777
  1229.5 10.4 all-to-all-start.18
  1242.8 30.0 %all-to-all-start.20 = ((bf16[4,352,768]{2,1,0:T(8,128)(2,1)}), bf16[4,352,768]{2,1,0:T(8,128)(2,1)S(1)}, u32[]{:S(2)}, u32[]{:S(2)}) async-start(bf16[4,352,768]{2,1,0:T(8,128)(2,1)} %bitcast.103), calls=%async_computation.21 | async-start | bytes 4325376 | tf_op jit(solution)/shard_map/all_to_all | solution.py:669
  (125 other events, 1472.3 us)
Sparse Core Ops, SparseCore 0:
  11.7 152.6 all-gather.5
  168.1 122.0 all-gather.7
  293.9 202.4 all-gather.3
  581.7 332.0 reduce-scatter.2
  921.3 271.3 reduce-scatter.4

commit v8 on v7

--- a/solution.py
+++ b/solution.py
@@ -411,35 +411,36 @@
 
 def outer_all(pairs):
     cols = lax.axis_size("col")
+    parts = lax.axis_size("row")
     if not custom_mesh():
-        return jnp.stack(
-            [einsum("kt,cnt->ckn", a, b.reshape(cols, -1, b.shape[1])).astype(BF) for a, b in pairs]
-        )
+        blocks = [einsum("kt,cnt->ckn", a, b.reshape(cols, -1, b.shape[1])) for a, b in pairs]
+        blocks = [b.reshape(cols, parts, -1, b.shape[2]).astype(BF) for b in blocks]
+        return jnp.concatenate(blocks, 2)
     lefts = []
     for left, _ in pairs:
         if not any(left is other for other in lefts):
             lefts.append(left)
     which = [next(i for i, l in enumerate(lefts) if l is left) for left, _ in pairs]
     rights = [right for _, right in pairs]
-    many = len(pairs)
-    rows = lefts[0].shape[0]
+    sizes = [left.shape[0] // parts for left, _ in pairs]
     width = rights[0].shape[0] // cols
 
     def kernel(*refs):
-        for index in range(many):
+        for index, size in enumerate(sizes):
             left = refs[which[index]][...]
-            part = dot(left, refs[len(lefts) + index][...], ((1,), (1,)))
-            refs[-1][index, 0] = part.astype(BF)
+            part = dot(left, refs[len(lefts) + index][...], ((1,), (1,))).astype(BF)
+            start = sum(sizes[:index])
+            refs[-1][0, :, start : start + size] = part.reshape(parts, size, width)
 
     return pl.pallas_call(
         kernel,
         grid=(cols,),
         in_specs=[full(left.shape) for left in lefts]
         + [pl.BlockSpec((width, right.shape[1]), lambda c: (c, 0)) for right in rights],
-        out_specs=pl.BlockSpec((many, 1, rows, width), lambda c: (0, c, 0, 0)),
-        out_shape=jax.ShapeDtypeStruct((many, cols, rows, width), BF),
+        out_specs=pl.BlockSpec((1, parts, sum(sizes), width), lambda c: (c, 0, 0, 0)),
+        out_shape=jax.ShapeDtypeStruct((cols, parts, sum(sizes), width), BF),
         cost_estimate=work(
-            many * rows, lefts[0].shape[1], cols * width, 3 * many * rows * cols * width
+            parts * sum(sizes), lefts[0].shape[1], cols * width, 3 * parts * sum(sizes) * cols * width
         ),
         compiler_params=params(),
         name="outer_all",
@@ -1109,18 +1110,20 @@
         jnp.concatenate(g_values, 2).astype(BF).reshape(depth, -1),
     ]
     g_normed = rebuild(weights_two, [0], [g_craw], F32)
-    pairs += [(normed_two, g_craw), *((text_wide, g) for g in g_pair)]
+    pairs.append((normed_two, g_craw))
     g_cross_gain = jnp.sum(g_normed * normal_two, 1)
     g_cross_bias = jnp.sum(g_normed, 1)
     g_stream = g_stream + norm_back(g_normed * gain_cross, normal_two, inverse_two)
 
     g_low = g_stream.astype(BF)
     g_mixed = project(weights_one, [3], [g_low], [BF])[0].reshape(heads, dim, tokens)
-    pairs.append((g_low, mixed_one))
+    pairs += [(g_low, mixed_one), *((text, g) for g in g_pair)]
     middle = outer_all(pairs)
     middle = lax.psum_scatter(
-        middle.reshape(len(pairs), -1, width), DEVICES, scatter_dimension=1, tiled=True
+        middle.reshape(-1, width), DEVICES, scatter_dimension=0, tiled=True
     ).astype(F32)
+    ends = [block_rows, 2 * block_rows, 3 * block_rows, 3 * block_rows + text_rows]
+    middle = jnp.split(middle, ends, 0)
     g_parts = []
     for index, piece in enumerate(pieces):
         whole, kept = saved_self[index]
@@ -1170,43 +1173,37 @@
     g_joined, g_modul = lax.optimization_barrier((g_joined, g_modul))
     r_skip = Reduction(corner, [(both, g_joined)], True)
     g_both = rebuild_blocks(base, w_skip, width, g_joined)
+
+    g_gains = jnp.stack(
+        [g_skip_gain, g_skip_bias, g_cross_gain, g_cross_bias, g_hidden_gain, g_hidden_bias], 0
+    )
+    g_gains = g_gains.reshape(6, cols, width).transpose(1, 0, 2)
+    g_head = jnp.stack([g_q_gain, g_k_gain, g_cq_gain, g_tk_gain], 0).reshape(1, -1, width)
+    packed = jnp.concatenate([g_gains, jnp.broadcast_to(g_head, (cols, *g_head.shape[1:]))], 1)
+    packed = jnp.sum(lax.all_to_all(packed, "col", 0, 0, tiled=True), 0)
+    packed = jnp.sum(shared(packed, "row"), 0)
+    g_modul = shared(g_modul, "row").reshape(-1, 2, width)
+
+    g_both, packed, g_modul = lax.optimization_barrier((g_both, packed, g_modul))
+    if custom_mesh():
+        g_both, got = lax.optimization_barrier((g_both, r_skip.state[0]))
+        here, away = outer(corner, r_skip.pairs, True, got)
+        g_both, away, act = lax.optimization_barrier((g_both, away, act))
+        r_skip.stage, r_skip.state = 1, [here, swap(away, "row", 1)]
+    g_latents, g_skip = to_features(g_both, pieces, cols, 2, block_rows)
+    output = contract(weights_hidden, 1, act, stream, BF)
+    output = tick(output, r_self)
+    output = tick(output, [r_skip])
     if custom_mesh():
         states = [r.state for r in r_self]
-        g_both, got, states = lax.optimization_barrier((g_both, r_skip.state[0], states))
-        here, away = outer(corner, r_skip.pairs, True, got)
-        g_both, away, act, states = lax.optimization_barrier((g_both, away, act, states))
-        r_skip.stage, r_skip.state = 1, [here, swap(away, "row", 1)]
+        states, r_skip.state = lax.optimization_barrier((states, r_skip.state))
+        r_skip.advance()
         for beside, state in zip(r_self, states):
             beside.state = state
             beside.advance()
-        g_latents, g_skip = to_features(g_both, pieces, cols, 2, block_rows)
-        output = contract(weights_hidden, 1, act, stream, BF)
-        output = tick(output, [r_skip])
-        states = [r.state for r in r_self]
-        states, here = lax.optimization_barrier((states, r_skip.state[0]))
-        r_skip.state[0] = here
-        for beside, state in zip(r_self, states):
-            beside.state = state
-            beside.advance()
-    else:
-        g_latents, g_skip = to_features(g_both, pieces, cols, 2, block_rows)
-        output = contract(weights_hidden, 1, act, stream, BF)
-    g_modul = shared(after(g_modul, g_skip), "row").reshape(-1, 2, width)
+    output, g_hidden = lax.optimization_barrier((output, g_hidden))
+    result = to_features(after(output, g_skip), pieces, cols, 1, width)[0]
     g_modulation = einsum("sd,ske->dke", embed_rows, g_modul)
-
-    g_gains = jnp.stack(
-        [g_skip_gain, g_skip_bias, g_cross_gain, g_cross_bias, g_hidden_gain, g_hidden_bias], 0
-    )
-    g_gains = g_gains.reshape(6, cols, width).transpose(1, 0, 2)
-    g_head = jnp.stack([g_q_gain, g_k_gain, g_cq_gain, g_tk_gain], 0).reshape(1, -1, width)
-    g_gains = after(g_gains, g_skip)
-    packed = jnp.concatenate([g_gains, jnp.broadcast_to(g_head, (cols, *g_head.shape[1:]))], 1)
-    packed = jnp.sum(lax.all_to_all(packed, "col", 0, 0, tiled=True), 0)
-    packed = jnp.sum(shared(packed, "row"), 0)
-    output, g_hidden, packed, g_modulation = lax.optimization_barrier(
-        (output, g_hidden, packed, g_modulation)
-    )
-    result = to_features(output, pieces, cols, 1, width)[0]
     g_gains = packed[:6]
     g_head = packed[6:].reshape(4, dim)
     return (
@@ -1216,9 +1213,9 @@
         r_skip.result().reshape(2, block_rows, width),
         g_modulation,
         jnp.concatenate([r.result() for r in r_self], 0).transpose(1, 0, 2),
-        middle[4].T,
+        middle[2].T,
         middle[1],
-        middle[2:4, :text_rows].transpose(1, 0, 2),
+        jnp.stack(middle[3:], 1),
         middle[0].T,
         g_hidden[0],
         g_hidden[1].T,

time: 1300 us -> 1290 us (level)
    all_to_all x6, waiting for transfers between devices: 42.1 us -> 58 us  [shared(): lax.all_to_all(jnp.broadcast_to(values[None], (size, *values.shape)), axi...]
  transfers between devices with their start and end apart: 52 -> 51, of which waited for: 26 -> 22; matrix products, arithmetic and copies ran while one was open for 21% -> 20% of each run, Pallas kernels for 33% -> 33%
where the time goes in v8:
time: 1290 us; the launch traced here: 1280 us
  Pallas kernels  487 us (38%)
  waiting for transfers between devices  361 us (28%)
  other arithmetic  207 us (16%)
  starting transfers between devices  123 us (10%)
  local copies, waits for them, and re-layouts  75.7 us (6%)
  between operations  16.4 us (1%)
    ppermute x26, waiting for transfers between devices, swap(): return lax.ppermute(values, axis, [(i, i ^ bit) for i in range(size)])  243 us
    pallas_call x4, Pallas kernels, attend_back(): pl.pallas_call(partial(attend_back_kernel, masked), grid=(heads // many,)...  65.7 us
    all_to_all x6, waiting for transfers between devices, shared(): lax.all_to_all(jnp.broadcast_to(values[None], (size, *values.shape)), axi...  58 us
    pallas_call x6, Pallas kernels, outer(): pl.pallas_call(kernel, grid_spec=pltpu.PrefetchScalarGridSpec(num_scalar_...  53.4 us
    pallas_call x5, Pallas kernels, project(): pl.pallas_call(kernel, grid=(cols,), in_specs=[pl.BlockSpec((1, 1, depth,...  49.9 us
    pallas_call x4, Pallas kernels, attend(): pl.pallas_call(partial(attend_kernel, masked), grid=(heads // many,), in_...  45.4 us
    pallas_call x4, Pallas kernels, rebuild(): pl.pallas_call(kernel, grid=(4,), in_specs=[pl.BlockSpec((1, cols, tile,...  45.3 us
    pallas_call x2, Pallas kernels, contract(): pl.pallas_call(kernel, grid=(4,), in_specs=[pl.BlockSpec((1, many, tile,...  41.8 us
  transfers between devices with their start and end apart: 51, of which 22 were waited for; matrix products, arithmetic and copies ran while one was open for 20% of the time, Pallas kernels for 33%

profile of v8, /device:TPU:0, one launch (start us, length us, event | category | flops | bytes accessed | tf_op | source)
XLA Modules:
  0.0 1277.9 jit_solution(17126531036006865652)
XLA Ops:
  14.7 8.7 deal.2
  34.2 16.0 %collective-permute-done = bf16[352,384]{1,0:T(8,128)(2,1)S(1)} collective-permute-done((bf16[352,384]{1,0:T(8,128)(2,1)S(1)}, bf16[352,384]{1,0:T(8,128)(2,1)S(1)}, u32[]{:S(2)}, u32[]{:S(2)}) %collective-permute-start) | collective-permute-done | bytes 270368 | tf_op jit(solution)/shard_map/ppermute | solution.py:785
  50.1 9.0 collective-permute-done.2
  62.4 62.6 %collective-permute-done.5.own_ref = bf16[4,352,384]{2,1,0:T(8,128)(2,1)S(1)} collective-permute-done((bf16[4,352,384]{2,1,0:T(8,128)(2,1)S(1)}, bf16[4,352,384]{2,1,0:T(8,128)(2,1)S(1)}, u32[]{:S(2)}, u32[]{:S(2)}) %collective-permute-start.5) | collective-permute-done | bytes 1081376 | tf_op jit(solution)/shard_map/ppermute | solution.py:785
  128.4 6.7 assemble.2
  135.1 15.5 %collective-permute-done.6.got_ref = bf16[4,352,384]{2,1,0:T(8,128)(2,1)S(1)} collective-permute-done((bf16[4,352,384]{2,1,0:T(8,128)(2,1)S(1)}, bf16[4,352,384]{2,1,0:T(8,128)(2,1)S(1)}, u32[]{:S(2)}, u32[]{:S(2)}) %collective-permute-start.6) | collective-permute-done | bytes 1081376 | tf_op jit(solution)/shard_map/ppermute | solution.py:785
  151.6 6.6 assemble.3
  160.2 8.5 all-to-all-start.2
  168.7 6.6 all-to-all-done.2
  211.7 13.0 %project_blocks.1 = f32[1408,768]{1,0:T(8,128)} custom-call(s32[1]{0:T(128)} %bitcast.4.base_ref, bf16[2816,384]{1,0:T(8,128)(2,1)} %bitcast.360, bf16[2816,384]{1,0:T(8,128)(2,1)} %collective-permute-done.4.refs_1_, bf16[2816,384]{1,0:T(8,128)(2,1)} %bitcast.363, bf16[2816,384]{1,0:T(8,128)(2,1)} %collective-permute-done.7.refs_3_, ...), custom_call_target="tpu_custom_call" | custom-call | flops 6090129408 | bytes 8650752 | tf_op jit(solution)/shard_map/project_blocks/pallas_call | solution.py:283
  233.0 5.6 add_convert_fusion.4.refs_3_.refs_0_
  238.6 15.1 %project.5 = (f32[1408,768]{1,0:T(8,128)}, f32[1408,768]{1,0:T(8,128)}, bf16[1408,768]{1,0:T(8,128)(2,1)}) custom-call(bf16[4,4,1408,352]{3,2,1,0:T(8,128)(2,1)} %bitcast.246, bf16[4,4,1408,352]{3,2,1,0:T(8,128)(2,1)} %bitcast.247, bf16[4,4,1408,352]{3,2,1,0:T(8,128)(2,1)} %bitcast.248, bf16[1408,768]{1,0:T(8,128)(2,1)} %add_convert_fusion.4.refs_3_.refs_0_), custom_call_target="tpu_custom_call" | custom-call | flops 9135194112 | bytes 8650752 | tf_op jit(solution)/shard_map/project/pallas_call | solution.py:221
  285.4 5.8 all-to-all-start.7
  299.5 16.9 %attend.4 = (bf16[2,8,88,512]{3,2,1,0:T(8,128)(2,1)}, bf16[2,8,88,512]{3,2,1,0:T(8,128)(2,1)}, f32[8,1,1024]{2,1,0:T(1,128)}) custom-call(s32[1]{0:T(128)} %constant.200.clone.1.length_ref, bf16[2,3,8,88,512]{4,3,2,1,0:T(8,128)(2,1)} %all-to-all-done.7.q_ref.k_ref.v_ref, bf16[2,3,8,88,512]{4,3,2,1,0:T(8,128)(2,1)} %all-to-all-done.7.q_ref.k_ref.v_ref, ...), custom_call_target="tpu_custom_call" | custom-call | flops 8589934592 | bytes 5767168 | tf_op jit(solution)/shard_map/attend/pallas_call | solution.py:140
  316.4 17.2 %all-to-all-done.9.q_ref.k_ref.v_ref = bf16[4,3,4,88,256]{4,3,2,1,0:T(8,128)(2,1)S(1)} async-done(((bf16[4,3,4,88,256]{4,3,2,1,0:T(8,128)(2,1)}), bf16[4,3,4,88,256]{4,3,2,1,0:T(8,128)(2,1)S(1)}, u32[]{:S(2)}, u32[]{:S(2)}) %all-to-all-start.9) | async-done | bytes 2162720 | tf_op jit(solution)/shard_map/all_to_all | solution.py:670
  338.9 9.4 attend.5
  352.4 8.1 deal.3
  372.5 8.8 rebuild.4
  389.5 8.1 project.6
  401.5 10.7 project.7
  425.6 7.4 attend.7
  435.6 11.7 attend.6
  450.2 8.8 rebuild.5
  467.7 28.5 %all-gather.4.cloned.1.call-done = bf16[2,5632,1536]{2,1,0:T(8,128)(2,1)} async-done(((bf16[2,176,1536]{2,1,0:T(8,128)(2,1)}), bf16[2,5632,1536]{2,1,0:T(8,128)(2,1)}) %all-gather.4.cloned.1.call-update) | async-done | bytes 34603024 | tf_op jit(solution)/shard_map/all_gather | solution.py:796
  496.2 27.1 %expand.1 = (bf16[4,1536,768]{2,1,0:T(8,128)(2,1)}, bf16[4,1536,768]{2,1,0:T(8,128)(2,1)}) custom-call(bf16[2,4,1408,1536]{3,2,1,0:T(8,128)(2,1)} %bitcast.294, bf16[1408,768]{1,0:T(8,128)(2,1)} %add_convert_fusion.2.values_ref.normed_ref), custom_call_target="tpu_custom_call" | custom-call | flops 13287555072 | bytes 25952256 | tf_op jit(solution)/shard_map/expand/pallas_call | solution.py:467
  524.7 20.5 %expand_back.1.inner_ref.values_ref = bf16[4,1536,768]{2,1,0:T(8,128)(2,1)} custom-call(bf16[2,4,1408,1536]{3,2,1,0:T(8,128)(2,1)} %bitcast.295, bf16[1408,768]{1,0:T(8,128)(2,1)} %bitcast.307, bf16[4,1536,768]{2,1,0:T(8,128)(2,1)} %get-tuple-element.115.slope_ref), custom_call_target="tpu_custom_call" | custom-call | flops 13287555072 | bytes 25952256 | tf_op jit(solution)/shard_map/expand_back/pallas_call | solution.py:492
  545.2 36.2 %hidden_outer.1 = bf16[2,4,1408,1536]{3,2,1,0:T(8,128)(2,1)} custom-call(bf16[1408,768]{1,0:T(8,128)(2,1)} %bitcast.308, bf16[4,1536,768]{2,1,0:T(8,128)(2,1)} %get-tuple-element.142.act_ref.values_ref, bf16[1408,768]{1,0:T(8,128)(2,1)} %add_convert_fusion.2.values_ref.normed_ref, bf16[4,1536,768]{2,1,0:T(8,128)(2,1)} %expand_back.1.inner_ref.values_ref), custom_call_target="tpu_custom_call" | custom-call | flops 26575110144 | bytes 43253760 | tf_op jit(solution)/shard_map/hidden_outer/pallas_call | solution.py:555
  582.2 21.0 %contract.2 = f32[1408,768]{1,0:T(8,128)} custom-call(bf16[2,4,1408,1536]{3,2,1,0:T(8,128)(2,1)} %bitcast.296, bf16[4,1536,768]{2,1,0:T(8,128)(2,1)} %expand_back.1.inner_ref.values_ref), custom_call_target="tpu_custom_call" | custom-call | flops 13287555072 | bytes 25952256 | tf_op jit(solution)/shard_map/contract/pallas_call | solution.py:522
  603.2 7.1 multiply_reduce_fusion.3
  615.7 8.2 project.8
  628.9 9.9 attend_back.5
  638.8 15.7 %attend_back.4 = (f32[1,1,16,88,512]{4,3,2,1,0:T(8,128)}, f32[1,1,16,88,384]{4,3,2,1,0:T(8,128)}, f32[1,1,16,88,384]{4,3,2,1,0:T(8,128)}) custom-call(s32[1]{0:T(128)} %get-tuple-element.425.length_ref, bf16[1,1,16,88,512]{4,3,2,1,0:T(8,128)(2,1)} %slice_bitcast_fusion.1.q_ref, bf16[1,1,16,88,384]{4,3,2,1,0:T(8,128)(2,1)} %get-tuple-element.386.k_ref, ...), custom_call_target="tpu_custom_call" | custom-call | flops 8053063680 | bytes 12615680 | tf_op jit(solution)/shard_map/attend_back/pallas_call | solution.py:173
  666.3 8.5 rebuild.6
  674.8 5.9 multiply_reduce_fusion.4
  680.7 8.1 fusion.62
  688.9 7.7 project.9
  713.8 26.0 %attend_back.6 = bf16[2,3,8,88,512]{4,3,2,1,0:T(8,128)(2,1)} custom-call(s32[1]{0:T(128)} %constant.200.clone.1.length_ref, bf16[2,3,8,88,512]{4,3,2,1,0:T(8,128)(2,1)} %all-to-all-done.7.q_ref.k_ref.v_ref, bf16[2,3,8,88,512]{4,3,2,1,0:T(8,128)(2,1)} %all-to-all-done.7.q_ref.k_ref.v_ref, bf16[2,3,8,88,512]{4,3,2,1,0:T(8,128)(2,1)} %all-to-all-done.7.q_ref.k_ref.v_ref, ...), custom_call_target="tpu_custom_call" | custom-call | flops 21474836480 | bytes 14417920 | tf_op jit(solution)/shard_map/attend_back/pallas_call | solution.py:173
  753.3 5.8 all-to-all-start.12
  759.1 14.2 %attend_back.7 = bf16[4,3,4,88,256]{4,3,2,1,0:T(8,128)(2,1)} custom-call(s32[1]{0:T(128)} %constant.200.clone.1.length_ref, bf16[4,3,4,88,256]{4,3,2,1,0:T(8,128)(2,1)} %copy-done.41, bf16[4,3,4,88,256]{4,3,2,1,0:T(8,128)(2,1)} %copy-done.41, bf16[4,3,4,88,256]{4,3,2,1,0:T(8,128)(2,1)} %copy-done.41, bf16[4,4,88,256]{3,2,1,0:T(8,128)(2,1)} %get-tuple-element.108.m_ref, ...), custom_call_target="tpu_custom_call" | custom-call | flops 10737418240 | bytes 7208960 | tf_op jit(solution)/shard_map/attend_back/pallas_call | solution.py:173
  778.0 27.8 %outer_all.1 = bf16[4,8,784,352]{3,2,1,0:T(8,128)(2,1)} custom-call(bf16[1408,768]{1,0:T(8,128)(2,1)} %fusion.56.refs_1_.refs_0_, bf16[1408,768]{1,0:T(8,128)(2,1)} %add_convert_fusion.3.refs_1_, bf16[1408,768]{1,0:T(8,128)(2,1)} %get-tuple-element.345.refs_1_.refs_2_, bf16[1024,768]{1,0:T(8,128)(2,1)} %bitcast.342, ...), custom_call_target="tpu_custom_call" | custom-call | flops 13564379136 | bytes 26492928 | tf_op jit(solution)/shard_map/outer_all/pallas_call | solution.py:435
  823.6 7.5 multiply_reduce_fusion.8
  845.5 9.1 outer.6
  856.2 6.2 outer.7
  862.6 19.1 %rebuild.7 = f32[1408,768]{1,0:T(8,128)} custom-call(bf16[4,4,1408,352]{3,2,1,0:T(8,128)(2,1)} %bitcast.251, bf16[4,4,1408,352]{3,2,1,0:T(8,128)(2,1)} %bitcast.252, bf16[4,4,1408,352]{3,2,1,0:T(8,128)(2,1)} %bitcast.253, bf16[1408,768]{1,0:T(8,128)(2,1)} %bitcast.331, bf16[1408,768]{1,0:T(8,128)(2,1)} %bitcast.334, ...), custom_call_target="tpu_custom_call" | custom-call | flops 9135194112 | bytes 8650752 | tf_op jit(solution)/shard_map/rebuild/pallas_call | solution.py:250
  883.1 7.0 outer.9
  890.1 10.6 outer.8
  904.9 5.8 fusion.18
  910.7 10.9 multiply_reduce_fusion.5
  929.6 6.7 multiply_convert_fusion.refs_4_.refs_1_
  936.4 9.9 outer.10
  947.6 6.8 all_to_all.105
  969.9 13.8 %rebuild_blocks.1 = bf16[2816,768]{1,0:T(8,128)(2,1)} custom-call(s32[1]{0:T(128)} %bitcast.4.base_ref, bf16[2816,384]{1,0:T(8,128)(2,1)} %bitcast.361, bf16[2816,384]{1,0:T(8,128)(2,1)} %collective-permute-done.4.refs_1_, bf16[2816,384]{1,0:T(8,128)(2,1)} %bitcast.364, bf16[2816,384]{1,0:T(8,128)(2,1)} %collective-permute-done.7.refs_3_, ...), custom_call_target="tpu_custom_call" | custom-call | flops 6090129408 | bytes 8650752 | tf_op jit(solution)/shard_map/rebuild_blocks/pallas_call | solution.py:314
  983.7 37.2 %all-to-all-done.18 = bf16[8,3,2,352]{3,2,1,0:T(2,128)(2,1)S(1)} async-done(((bf16[8,3,2,352]{3,2,1,0:T(2,128)(2,1)}), bf16[8,3,2,352]{3,2,1,0:T(2,128)(2,1)S(1)}, u32[]{:S(2)}, u32[]{:S(2)}) %all-to-all-start.18) | async-done | bytes 33824 | tf_op jit(solution)/shard_map/all_to_all | solution.py:778
  1020.9 10.7 outer.11
  1039.7 20.8 %contract.3 = bf16[1408,768]{1,0:T(8,128)(2,1)} custom-call(bf16[2,4,1408,1536]{3,2,1,0:T(8,128)(2,1)} %bitcast.297, bf16[4,1536,768]{2,1,0:T(8,128)(2,1)} %get-tuple-element.142.act_ref.values_ref, f32[1408,768]{1,0:T(8,128)} %copy-done.3), custom_call_target="tpu_custom_call" | custom-call | flops 13287555072 | bytes 25952256 | tf_op jit(solution)/shard_map/contract/pallas_call | solution.py:522
  1060.5 11.5 collective-permute-done.12
  1076.1 20.4 %collective-permute-done.13 = bf16[1,2,4,352,384]{4,3,2,1,0:T(8,128)(2,1)} collective-permute-done((bf16[1,2,4,352,384]{4,3,2,1,0:T(8,128)(2,1)}, bf16[1,2,4,352,384]{4,3,2,1,0:T(8,128)(2,1)}, u32[]{:S(2)}, u32[]{:S(2)}) %collective-permute-start.13) | collective-permute-done | bytes 2162720 | tf_op jit(solution)/shard_map/ppermute | solution.py:785
  1107.1 9.8 collective-permute-done.15
  1117.0 51.0 %collective-permute-done.14 = bf16[2,4,176,384]{3,2,1,0:T(8,128)(2,1)S(1)} collective-permute-done((bf16[2,4,176,384]{3,2,1,0:T(8,128)(2,1)S(1)}, bf16[2,4,176,384]{3,2,1,0:T(8,128)(2,1)S(1)}, u32[]{:S(2)}, u32[]{:S(2)}) %collective-permute-start.14) | collective-permute-done | bytes 1081376 | tf_op jit(solution)/shard_map/ppermute | solution.py:785
  1168.0 20.1 %collective-permute-done.16 = bf16[1,4,352,384]{3,2,1,0:T(8,128)(2,1)S(1)} collective-permute-done((bf16[1,4,352,384]{3,2,1,0:T(8,128)(2,1)S(1)}, bf16[1,4,352,384]{3,2,1,0:T(8,128)(2,1)S(1)}, u32[]{:S(2)}, u32[]{:S(2)}) %collective-permute-start.16) | collective-permute-done | bytes 1081376 | tf_op jit(solution)/shard_map/ppermute | solution.py:785
  1200.7 9.0 undeal.2
  1220.6 19.4 %collective-permute-done.21 = bf16[2,176,384]{2,1,0:T(8,128)(2,1)} collective-permute-done((bf16[2,176,384]{2,1,0:T(8,128)(2,1)S(1)}, bf16[2,176,384]{2,1,0:T(8,128)(2,1)}, u32[]{:S(2)}, u32[]{:S(2)}) %collective-permute-start.21) | collective-permute-done | bytes 270368 | tf_op jit(solution)/shard_map/ppermute | solution.py:785
  1242.2 7.8 collective-permute-done.18
  1263.2 8.0 undeal.3
  (566 shorter events, 357.4 us)
Async XLA Ops:
  7.2 177.1 %copy-start = (bf16[176,2,352]{2,1,0:T(2,128)(2,1)S(1)}, bf16[176,2,352]{2,1,0:T(2,128)(2,1)}, u32[]{:S(2)}) copy-start(bf16[176,2,352]{2,1,0:T(2,128)(2,1)} %param.34) | copy-start | bytes 743428
  7.2 231.4 %all-gather.6.cloned.1.call-start = ((), (), s32[]{:S(2)}) async-start(), calls=%async_computation.24 | async-start | bytes 17842176 | tf_op jit(solution)/shard_map/all_gather | solution.py:796
  10.3 379.2 %all-gather.8.cloned.1.call-start = ((), (), s32[]{:S(2)}) async-start(), calls=%async_computation.25 | async-start | bytes 17842176 | tf_op jit(solution)/shard_map/all_gather | solution.py:796
  13.5 482.7 %all-gather.4.cloned.1.call-start = ((), (), s32[]{:S(2)}) async-start(), calls=%async_computation.23 | async-start | bytes 35684352 | tf_op jit(solution)/shard_map/all_gather | solution.py:796
  23.4 136.2 %all-to-all-start = ((bf16[4,704,768]{2,1,0:T(8,128)(2,1)}), bf16[4,704,768]{2,1,0:T(8,128)(2,1)}, u32[]{:S(2)}, u32[]{:S(2)}) async-start(bf16[4,704,768]{2,1,0:T(8,128)(2,1)} %deal.2), calls=%async_computation | async-start | bytes 8650752 | tf_op jit(solution)/shard_map/all_to_all | solution.py:670
  28.5 21.7 %collective-permute-start = (bf16[352,384]{1,0:T(8,128)(2,1)S(1)}, bf16[352,384]{1,0:T(8,128)(2,1)S(1)}, u32[]{:S(2)}, u32[]{:S(2)}) collective-permute-start(bf16[352,384]{1,0:T(8,128)(2,1)S(1)} %get-tuple-element.412), channel_id=1, source_target_pairs={{0,8},{4,12},{8,0},{12,4},{16,24},{20,28},{24,16},{28,20},{1,9},{5... | collective-permute-start | bytes 811016 | tf_op jit(solution)/shard_map/ppermute | solution.py:785
  31.6 18.5 %collective-permute-start.1 = (bf16[352,384]{1,0:T(8,128)(2,1)S(1)}, bf16[352,384]{1,0:T(8,128)(2,1)S(1)}, u32[]{:S(2)}, u32[]{:S(2)}) collective-permute-start(bf16[352,384]{1,0:T(8,128)(2,1)S(1)} %get-tuple-element.412), channel_id=1, source_target_pairs={{0,16},{4,20},{8,24},{12,28},{16,0},{20,4},{24,8},{28,12},{1,17},{... | collective-permute-start | bytes 811016 | tf_op jit(solution)/shard_map/ppermute | solution.py:785
  34.2 25.0 %collective-permute-start.2 = (bf16[352,384]{1,0:T(8,128)(2,1)S(1)}, bf16[352,384]{1,0:T(8,128)(2,1)S(1)}, u32[]{:S(2)}, u32[]{:S(2)}) collective-permute-start(bf16[352,384]{1,0:T(8,128)(2,1)S(1)} %get-tuple-element.412), channel_id=1, source_target_pairs={{0,24},{4,28},{8,16},{12,20},{16,8},{20,12},{24,0},{28,4},{1,25},{... | collective-permute-start | bytes 811016 | tf_op jit(solution)/shard_map/ppermute | solution.py:785
  59.3 69.1 %copy-start.34 = (bf16[4,352,384]{2,1,0:T(8,128)(2,1)}, bf16[4,352,384]{2,1,0:T(8,128)(2,1)S(1)}, u32[]{:S(2)}) copy-start(bf16[4,352,384]{2,1,0:T(8,128)(2,1)S(1)} %pad_maximum_fusion.12.own_ref) | copy-start | bytes 3244036
  59.3 65.7 %collective-permute-start.5 = (bf16[4,352,384]{2,1,0:T(8,128)(2,1)S(1)}, bf16[4,352,384]{2,1,0:T(8,128)(2,1)S(1)}, u32[]{:S(2)}, u32[]{:S(2)}) collective-permute-start(bf16[4,352,384]{2,1,0:T(8,128)(2,1)S(1)} %pad_maximum_fusion.12.own_ref), channel_id=1, source_target_pairs={{0,2},{1,3},{2,0},{3,1},{4,6},{5,7},{6,4},{7,5},{8,10},{9,11},{10,... | collective-permute-start | bytes 3244040 | tf_op jit(solution)/shard_map/ppermute | solution.py:785
  60.9 67.5 %collective-permute-start.3 = (bf16[4,352,384]{2,1,0:T(8,128)(2,1)S(1)}, bf16[4,352,384]{2,1,0:T(8,128)(2,1)}, u32[]{:S(2)}, u32[]{:S(2)}) collective-permute-start(bf16[4,352,384]{2,1,0:T(8,128)(2,1)S(1)} %pad_maximum_fusion.12.own_ref), channel_id=1, source_target_pairs={{0,4},{4,0},{8,12},{12,8},{16,20},{20,16},{24,28},{28,24},{1,5},{5... | collective-permute-start | bytes 3244040 | tf_op jit(solution)/shard_map/ppermute | solution.py:785
  125.0 25.6 %collective-permute-start.6 = (bf16[4,352,384]{2,1,0:T(8,128)(2,1)S(1)}, bf16[4,352,384]{2,1,0:T(8,128)(2,1)S(1)}, u32[]{:S(2)}, u32[]{:S(2)}) collective-permute-start(bf16[4,352,384]{2,1,0:T(8,128)(2,1)S(1)} %collective-permute-done.5.own_ref), channel_id=1, source_target_pairs={{0,4},{4,0},{8,12},{12,8},{16,20},{20,16},{24,28},{28,24},{1,5},{5... | collective-permute-start | bytes 3244040 | tf_op jit(solution)/shard_map/ppermute | solution.py:785
  128.4 51.0 %copy-start.109 = (f32[352]{0:T(512)S(1)}, f32[352]{0:T(512)}, u32[]{:S(2)}) copy-start(f32[352]{0:T(512)} %param.43) | copy-start | bytes 4228
  128.4 51.0 %copy-start.110 = (f32[352]{0:T(512)S(1)}, f32[352]{0:T(512)}, u32[]{:S(2)}) copy-start(f32[352]{0:T(512)} %param.44) | copy-start | bytes 4228
  128.4 51.0 %copy-start.111 = (f32[352]{0:T(512)S(1)}, f32[352]{0:T(512)}, u32[]{:S(2)}) copy-start(f32[352]{0:T(512)} %param.45) | copy-start | bytes 4228
  128.4 51.0 %copy-start.112 = (f32[352]{0:T(512)S(1)}, f32[352]{0:T(512)}, u32[]{:S(2)}) copy-start(f32[352]{0:T(512)} %param.46) | copy-start | bytes 4228
  128.4 51.0 %copy-start.113 = (f32[352]{0:T(512)S(1)}, f32[352]{0:T(512)}, u32[]{:S(2)}) copy-start(f32[352]{0:T(512)} %param.47) | copy-start | bytes 4228
  135.1 76.5 %collective-permute-start.4 = (bf16[2816,384]{1,0:T(8,128)(2,1)}, bf16[2816,384]{1,0:T(8,128)(2,1)}, u32[]{:S(2)}, u32[]{:S(2)}) collective-permute-start(bf16[2816,384]{1,0:T(8,128)(2,1)} %bitcast.359), channel_id=1, source_target_pairs={{0,1},{1,0},{2,3},{3,2},{4,5},{5,4},{6,7},{7,6},{8,9},{9,8},{10,11... | collective-permute-start | bytes 6488072 | tf_op jit(solution)/shard_map/ppermute | solution.py:785
  158.1 53.5 %collective-permute-start.7 = (bf16[2816,384]{1,0:T(8,128)(2,1)}, bf16[2816,384]{1,0:T(8,128)(2,1)}, u32[]{:S(2)}, u32[]{:S(2)}) collective-permute-start(bf16[2816,384]{1,0:T(8,128)(2,1)} %bitcast.362), channel_id=1, source_target_pairs={{0,1},{1,0},{2,3},{3,2},{4,5},{5,4},{6,7},{7,6},{8,9},{9,8},{10,11... | collective-permute-start | bytes 6488072 | tf_op jit(solution)/shard_map/ppermute | solution.py:785
  160.2 15.1 %all-to-all-start.2 = ((bf16[8,3,352]{2,1,0:T(4,128)(2,1)}), bf16[8,3,352]{2,1,0:T(4,128)(2,1)S(1)}, u32[]{:S(2)}, u32[]{:S(2)}) async-start(bf16[8,3,352]{2,1,0:T(4,128)(2,1)} %broadcast_in_dim.199), calls=%async_computation.2 | async-start | bytes 49152 | tf_op jit(solution)/shard_map/all_to_all | solution.py:778
  175.9 8.2 all-to-all-start.3
  185.2 10.3 all-to-all-start.4
  190.3 87.1 %copy-start.23 = (f32[88,768]{1,0:T(8,128)}, f32[88,768]{1,0:T(8,128)S(1)}, u32[]{:S(2)}) copy-start(f32[88,768]{1,0:T(8,128)S(1)} %get-tuple-element.417) | copy-start | bytes 811012
  196.3 8.9 all-to-all-start.5
  206.9 46.8 %all-to-all-start.6 = ((bf16[4,3,384,256]{2,3,1,0:T(8,128)(2,1)}), bf16[4,3,384,256]{2,3,1,0:T(8,128)(2,1)S(1)}, u32[]{:S(2)}, u32[]{:S(2)}) async-start(bf16[4,3,384,256]{2,3,1,0:T(8,128)(2,1)} %broadcast_in_dim.212), calls=%async_computation.6 | async-start | bytes 4718592 | tf_op jit(solution)/shard_map/all_to_all | solution.py:778
  211.6 169.7 %copy-start.64 = (f32[1408]{0:T(1024)}, f32[1408]{0:T(1024)S(1)}, u32[]{:S(2)}) copy-start(f32[1408]{0:T(1024)S(1)} %get-tuple-element.335) | copy-start | bytes 16900
  211.6 169.7 %copy-start.72 = (f32[1408]{0:T(1024)}, f32[1408]{0:T(1024)S(1)}, u32[]{:S(2)}) copy-start(f32[1408]{0:T(1024)S(1)} %get-tuple-element.334) | copy-start | bytes 16900
  211.6 174.4 %copy-start.79 = (f32[1408]{0:T(1024)}, f32[1408]{0:T(1024)S(1)}, u32[]{:S(2)}) copy-start(f32[1408]{0:T(1024)S(1)} %get-tuple-element.329) | copy-start | bytes 16900
  227.2 154.1 %copy-start.74 = (f32[768]{0:T(1024)}, f32[768]{0:T(1024)S(1)}, u32[]{:S(2)}) copy-start(f32[768]{0:T(1024)S(1)} %broadcast_multiply_fusion.17) | copy-start | bytes 9220
  230.1 151.2 %copy-start.77 = (f32[768]{0:T(1024)}, f32[768]{0:T(1024)S(1)}, u32[]{:S(2)}) copy-start(f32[768]{0:T(1024)S(1)} %add_rsqrt_fusion.3) | copy-start | bytes 9220
  285.4 10.5 all-to-all-start.7
  295.9 37.7 %all-to-all-start.9 = ((bf16[4,3,4,88,256]{4,3,2,1,0:T(8,128)(2,1)}), bf16[4,3,4,88,256]{4,3,2,1,0:T(8,128)(2,1)S(1)}, u32[]{:S(2)}, u32[]{:S(2)}) async-start(bf16[4,3,4,88,256]{4,3,2,1,0:T(8,128)(2,1)} %pad_maximum_fusion.3), calls=%async_computation.9 | async-start | bytes 4325376 | tf_op jit(solution)/shard_map/all_to_all | solution.py:670
  335.0 13.3 %all-to-all-start.8 = ((bf16[2,8,88,512]{3,2,1,0:T(8,128)(2,1)}), bf16[2,8,88,512]{3,2,1,0:T(8,128)(2,1)S(1)}, u32[]{:S(2)}, u32[]{:S(2)}) async-start(bf16[2,8,88,512]{3,2,1,0:T(8,128)(2,1)} %get-tuple-element.107.m_ref), calls=%async_computation.8 | async-start | bytes 2883584 | tf_op jit(solution)/shard_map/all_to_all | solution.py:671
  348.3 14.6 %all-to-all-start.10 = ((bf16[4,4,88,256]{3,2,1,0:T(8,128)(2,1)}), bf16[4,4,88,256]{3,2,1,0:T(8,128)(2,1)S(1)}, u32[]{:S(2)}, u32[]{:S(2)}) async-start(bf16[4,4,88,256]{3,2,1,0:T(8,128)(2,1)} %get-tuple-element.108.m_ref), calls=%async_computation.10 | async-start | bytes 1441792 | tf_op jit(solution)/shard_map/all_to_all | solution.py:670
  362.9 160.5 %all-to-all-start.1 = ((bf16[4,352,768]{2,1,0:T(8,128)(2,1)}), bf16[4,352,768]{2,1,0:T(8,128)(2,1)S(1)}, u32[]{:S(2)}, u32[]{:S(2)}) async-start(bf16[4,352,768]{2,1,0:T(8,128)(2,1)} %deal.3), calls=%async_computation.1 | async-start | bytes 4325376 | tf_op jit(solution)/shard_map/all_to_all | solution.py:670
  366.5 846.9 %reduce-scatter.3.cloned.1.call-start = ((), (), s32[]{:S(2)}) async-start(), calls=%async_computation.26 | async-start | bytes 35684352 | tf_op jit(solution)/shard_map/reduce_scatter | solution.py:1086
  701.3 8.5 all-to-all-start.11
  709.8 42.6 %all-to-all-start.13 = ((bf16[4,4,88,256]{3,2,1,0:T(8,128)(2,1)}), bf16[4,4,88,256]{3,2,1,0:T(8,128)(2,1)S(1)}, u32[]{:S(2)}, u32[]{:S(2)}) async-start(bf16[4,4,88,256]{3,2,1,0:T(8,128)(2,1)} %bitcast.78), calls=%async_computation.13 | async-start | bytes 1441792 | tf_op jit(solution)/shard_map/all_to_all | solution.py:670
  753.3 20.0 %all-to-all-start.12 = ((bf16[2,3,8,88,512]{4,3,2,1,0:T(8,128)(2,1)}), bf16[2,3,8,88,512]{4,3,2,1,0:T(8,128)(2,1)}, u32[]{:S(2)}, u32[]{:S(2)}) async-start(bf16[2,3,8,88,512]{4,3,2,1,0:T(8,128)(2,1)} %attend_back.6), calls=%async_computation.12 | async-start | bytes 8650752 | tf_op jit(solution)/shard_map/all_to_all | solution.py:671
  773.3 39.6 %all-to-all-start.14 = ((bf16[4,3,4,88,256]{4,3,2,1,0:T(8,128)(2,1)}), bf16[4,3,4,88,256]{4,3,2,1,0:T(8,128)(2,1)}, u32[]{:S(2)}, u32[]{:S(2)}) async-start(bf16[4,3,4,88,256]{4,3,2,1,0:T(8,128)(2,1)} %attend_back.7), calls=%async_computation.14 | async-start | bytes 4325376 | tf_op jit(solution)/shard_map/all_to_all | solution.py:670
  777.8 474.2 %reduce-scatter.5.cloned.1.call-start = ((), (), s32[]{:S(2)}) async-start(), calls=%async_computation.27 | async-start | bytes 19869696 | tf_op jit(solution)/shard_map/reduce_scatter | solution.py:1122
  854.5 27.2 %collective-permute-start.8 = (bf16[2,2,1408,384]{3,2,1,0:T(8,128)(2,1)}, bf16[2,2,1408,384]{3,2,1,0:T(8,128)(2,1)}, u32[]{:S(2)}, u32[]{:S(2)}) collective-permute-start(bf16[2,2,1408,384]{3,2,1,0:T(8,128)(2,1)} %outer.6), channel_id=1, source_target_pairs={{0,1},{1,0},{2,3},{3,2},{4,5},{5,4},{6,7},{7,6},{8,9},{9,8},{10,11... | collective-permute-start | bytes 12976136 | tf_op jit(solution)/shard_map/ppermute | solution.py:785
  862.4 19.3 %collective-permute-start.9 = (bf16[1,2,1408,384]{3,2,1,0:T(8,128)(2,1)}, bf16[1,2,1408,384]{3,2,1,0:T(8,128)(2,1)S(1)}, u32[]{:S(2)}, u32[]{:S(2)}) collective-permute-start(bf16[1,2,1408,384]{3,2,1,0:T(8,128)(2,1)} %outer.7), channel_id=1, source_target_pairs={{0,1},{1,0},{2,3},{3,2},{4,5},{5,4},{6,7},{7,6},{8,9},{9,8},{10,11... | collective-permute-start | bytes 6488072 | tf_op jit(solution)/shard_map/ppermute | solution.py:785
  926.3 10.0 all-to-all-start.15
  946.2 74.6 %collective-permute-start.10 = (bf16[1,2,2816,384]{3,2,1,0:T(8,128)(2,1)}, bf16[1,2,2816,384]{3,2,1,0:T(8,128)(2,1)}, u32[]{:S(2)}, u32[]{:S(2)}) collective-permute-start(bf16[1,2,2816,384]{3,2,1,0:T(8,128)(2,1)} %outer.10), channel_id=1, source_target_pairs={{0,1},{1,0},{2,3},{3,2},{4,5},{5,4},{6,7},{7,6},{8,9},{9,8},{10,11... | collective-permute-start | bytes 12976136 | tf_op jit(solution)/shard_map/ppermute | solution.py:785
  955.1 10.7 all-to-all-start.17
  958.4 113.6 %collective-permute-start.11 = (bf16[2,2,4,176,384]{4,3,2,1,0:T(8,128)(2,1)}, bf16[2,2,4,176,384]{4,3,2,1,0:T(8,128)(2,1)}, u32[]{:S(2)}, u32[]{:S(2)}) collective-permute-start(bf16[2,2,4,176,384]{4,3,2,1,0:T(8,128)(2,1)} %get-tuple-element.144), channel_id=1, source_target_pairs={{0,4},{4,0},{8,12},{12,8},{16,20},{20,16},{24,28},{28,24},{1,5},{5... | collective-permute-start | bytes 6488072 | tf_op jit(solution)/shard_map/ppermute | solution.py:785
  966.4 54.5 %all-to-all-start.18 = ((bf16[8,3,2,352]{3,2,1,0:T(2,128)(2,1)}), bf16[8,3,2,352]{3,2,1,0:T(2,128)(2,1)S(1)}, u32[]{:S(2)}, u32[]{:S(2)}) async-start(bf16[8,3,2,352]{3,2,1,0:T(2,128)(2,1)} %broadcast_in_dim.234), calls=%async_computation.18 | async-start | bytes 73728 | tf_op jit(solution)/shard_map/all_to_all | solution.py:778
  1031.6 64.9 %collective-permute-start.13 = (bf16[1,2,4,352,384]{4,3,2,1,0:T(8,128)(2,1)}, bf16[1,2,4,352,384]{4,3,2,1,0:T(8,128)(2,1)}, u32[]{:S(2)}, u32[]{:S(2)}) collective-permute-start(bf16[1,2,4,352,384]{4,3,2,1,0:T(8,128)(2,1)} %get-tuple-element.149), channel_id=1, source_target_pairs={{0,4},{4,0},{8,12},{12,8},{16,20},{20,16},{24,28},{28,24},{1,5},{5... | collective-permute-start | bytes 6488072 | tf_op jit(solution)/shard_map/ppermute | solution.py:785
  1032.7 39.3 %collective-permute-start.12 = (bf16[1,4,2,176,384]{4,3,2,1,0:T(8,128)(2,1)}, bf16[1,4,2,176,384]{4,3,2,1,0:T(8,128)(2,1)S(1)}, u32[]{:S(2)}, u32[]{:S(2)}) collective-permute-start(bf16[1,4,2,176,384]{4,3,2,1,0:T(8,128)(2,1)} %get-tuple-element.146), channel_id=1, source_target_pairs={{0,2},{1,3},{2,0},{3,1},{4,6},{5,7},{6,4},{7,5},{8,10},{9,11},{10,... | collective-permute-start | bytes 3244040 | tf_op jit(solution)/shard_map/ppermute | solution.py:785
  1034.8 165.9 %all-to-all-start.19 = ((bf16[4,704,768]{2,1,0:T(8,128)(2,1)}), bf16[4,704,768]{2,1,0:T(8,128)(2,1)}, u32[]{:S(2)}, u32[]{:S(2)}) async-start(bf16[4,704,768]{2,1,0:T(8,128)(2,1)} %bitcast.349), calls=%async_computation.20 | async-start | bytes 8650752 | tf_op jit(solution)/shard_map/all_to_all | solution.py:670
  1073.6 94.4 %collective-permute-start.14 = (bf16[2,4,176,384]{3,2,1,0:T(8,128)(2,1)S(1)}, bf16[2,4,176,384]{3,2,1,0:T(8,128)(2,1)S(1)}, u32[]{:S(2)}, u32[]{:S(2)}) collective-permute-start(bf16[2,4,176,384]{3,2,1,0:T(8,128)(2,1)S(1)} %fusion.20), channel_id=1, source_target_pairs={{0,2},{1,3},{2,0},{3,1},{4,6},{5,7},{6,4},{7,5},{8,10},{9,11},{10,... | collective-permute-start | bytes 3244040 | tf_op jit(solution)/shard_map/ppermute | solution.py:785
  1098.6 89.5 %collective-permute-start.16 = (bf16[1,4,352,384]{3,2,1,0:T(8,128)(2,1)S(1)}, bf16[1,4,352,384]{3,2,1,0:T(8,128)(2,1)S(1)}, u32[]{:S(2)}, u32[]{:S(2)}) collective-permute-start(bf16[1,4,352,384]{3,2,1,0:T(8,128)(2,1)S(1)} %get-tuple-element.356), channel_id=1, source_target_pairs={{0,2},{1,3},{2,0},{3,1},{4,6},{5,7},{6,4},{7,5},{8,10},{9,11},{10,... | collective-permute-start | bytes 3244040 | tf_op jit(solution)/shard_map/ppermute | solution.py:785
  1104.9 12.0 collective-permute-start.15
  1188.3 10.5 collective-permute-start.23
  1190.3 19.4 %collective-permute-start.25 = (bf16[1,176,384]{2,1,0:T(8,128)(2,1)S(1)}, bf16[1,176,384]{2,1,0:T(8,128)(2,1)S(1)}, u32[]{:S(2)}, u32[]{:S(2)}) collective-permute-start(bf16[1,176,384]{2,1,0:T(8,128)(2,1)S(1)} %get-tuple-element.401), channel_id=1, source_target_pairs={{0,24},{4,28},{8,16},{12,20},{16,8},{20,12},{24,0},{28,4},{1,25},{... | collective-permute-start | bytes 405512 | tf_op jit(solution)/shard_map/ppermute | solution.py:785
  1193.0 19.5 %collective-permute-start.24 = (bf16[1,176,384]{2,1,0:T(8,128)(2,1)S(1)}, bf16[1,176,384]{2,1,0:T(8,128)(2,1)S(1)}, u32[]{:S(2)}, u32[]{:S(2)}) collective-permute-start(bf16[1,176,384]{2,1,0:T(8,128)(2,1)S(1)} %get-tuple-element.402), channel_id=1, source_target_pairs={{0,16},{4,20},{8,24},{12,28},{16,0},{20,4},{24,8},{28,12},{1,17},{... | collective-permute-start | bytes 405512 | tf_op jit(solution)/shard_map/ppermute | solution.py:785
  1194.7 25.2 %collective-permute-start.20 = (bf16[2,176,384]{2,1,0:T(8,128)(2,1)}, bf16[2,176,384]{2,1,0:T(8,128)(2,1)S(1)}, u32[]{:S(2)}, u32[]{:S(2)}) collective-permute-start(bf16[2,176,384]{2,1,0:T(8,128)(2,1)} %get-tuple-element.392), channel_id=1, source_target_pairs={{0,8},{4,12},{8,0},{12,4},{16,24},{20,28},{24,16},{28,20},{1,9},{5... | collective-permute-start | bytes 811016 | tf_op jit(solution)/shard_map/ppermute | solution.py:785
  1195.9 24.7 %collective-permute-start.22 = (bf16[2,176,384]{2,1,0:T(8,128)(2,1)}, bf16[2,176,384]{2,1,0:T(8,128)(2,1)}, u32[]{:S(2)}, u32[]{:S(2)}) collective-permute-start(bf16[2,176,384]{2,1,0:T(8,128)(2,1)} %get-tuple-element.393), channel_id=1, source_target_pairs={{0,24},{4,28},{8,16},{12,20},{16,8},{20,12},{24,0},{28,4},{1,25},{... | collective-permute-start | bytes 811016 | tf_op jit(solution)/shard_map/ppermute | solution.py:785
  1198.9 41.2 %collective-permute-start.21 = (bf16[2,176,384]{2,1,0:T(8,128)(2,1)S(1)}, bf16[2,176,384]{2,1,0:T(8,128)(2,1)}, u32[]{:S(2)}, u32[]{:S(2)}) collective-permute-start(bf16[2,176,384]{2,1,0:T(8,128)(2,1)S(1)} %get-tuple-element.394), channel_id=1, source_target_pairs={{0,16},{4,20},{8,24},{12,28},{16,0},{20,4},{24,8},{28,12},{1,17},{... | collective-permute-start | bytes 811016 | tf_op jit(solution)/shard_map/ppermute | solution.py:785
  1209.7 32.5 %collective-permute-start.17 = (bf16[1,352,384]{2,1,0:T(8,128)(2,1)}, bf16[1,352,384]{2,1,0:T(8,128)(2,1)}, u32[]{:S(2)}, u32[]{:S(2)}) collective-permute-start(bf16[1,352,384]{2,1,0:T(8,128)(2,1)} %get-tuple-element.396), channel_id=1, source_target_pairs={{0,8},{4,12},{8,0},{12,4},{16,24},{20,28},{24,16},{28,20},{1,9},{5... | collective-permute-start | bytes 811016 | tf_op jit(solution)/shard_map/ppermute | solution.py:785
  1212.5 29.7 %collective-permute-start.19 = (bf16[1,352,384]{2,1,0:T(8,128)(2,1)}, bf16[1,352,384]{2,1,0:T(8,128)(2,1)}, u32[]{:S(2)}, u32[]{:S(2)}) collective-permute-start(bf16[1,352,384]{2,1,0:T(8,128)(2,1)} %get-tuple-element.397), channel_id=1, source_target_pairs={{0,24},{4,28},{8,16},{12,20},{16,8},{20,12},{24,0},{28,4},{1,25},{... | collective-permute-start | bytes 811016 | tf_op jit(solution)/shard_map/ppermute | solution.py:785
  1216.3 45.5 %all-to-all-start.20 = ((bf16[4,352,768]{2,1,0:T(8,128)(2,1)}), bf16[4,352,768]{2,1,0:T(8,128)(2,1)S(1)}, u32[]{:S(2)}, u32[]{:S(2)}) async-start(bf16[4,352,768]{2,1,0:T(8,128)(2,1)} %bitcast.103), calls=%async_computation.21 | async-start | bytes 4325376 | tf_op jit(solution)/shard_map/all_to_all | solution.py:670
  1219.9 30.2 %collective-permute-start.18 = (bf16[1,352,384]{2,1,0:T(8,128)(2,1)}, bf16[1,352,384]{2,1,0:T(8,128)(2,1)S(1)}, u32[]{:S(2)}, u32[]{:S(2)}) collective-permute-start(bf16[1,352,384]{2,1,0:T(8,128)(2,1)} %get-tuple-element.398), channel_id=1, source_target_pairs={{0,16},{4,20},{8,24},{12,28},{16,0},{20,4},{24,8},{28,12},{1,17},{... | collective-permute-start | bytes 811016 | tf_op jit(solution)/shard_map/ppermute | solution.py:785
  (114 other events, 909.8 us)
Sparse Core Ops, SparseCore 0:
  11.7 152.6 all-gather.5
  168.1 122.1 all-gather.7
  293.9 202.2 all-gather.3
  581.5 332.1 reduce-scatter.2
  921.2 253.7 reduce-scatter.4

commit v9 on v8

--- a/solution.py
+++ b/solution.py
@@ -1181,8 +1181,11 @@
     g_head = jnp.stack([g_q_gain, g_k_gain, g_cq_gain, g_tk_gain], 0).reshape(1, -1, width)
     packed = jnp.concatenate([g_gains, jnp.broadcast_to(g_head, (cols, *g_head.shape[1:]))], 1)
     packed = jnp.sum(lax.all_to_all(packed, "col", 0, 0, tiled=True), 0)
-    packed = jnp.sum(shared(packed, "row"), 0)
-    g_modul = shared(g_modul, "row").reshape(-1, 2, width)
+    packed = jnp.concatenate([packed, g_modul.reshape(-1, width).astype(F32)], 0)
+    packed = shared(packed, "row")
+    many = packed.shape[1] - 2 * sequences
+    packed, g_modul = jnp.sum(packed[:, :many], 0), packed[:, many:].astype(BF)
+    g_modul = g_modul.reshape(-1, 2, width)
 
     g_both, packed, g_modul = lax.optimization_barrier((g_both, packed, g_modul))
     if custom_mesh():

time: 1290 us -> 1280 us (level)
    all_to_all x6 -> x5, waiting for transfers between devices: 58 us -> 53.6 us  [shared(): lax.all_to_all(jnp.broadcast_to(values[None], (size, *values.shape)), axi...]
    all_to_all x6 -> x5, starting transfers between devices: 26 us -> 22.7 us  [shared(): lax.all_to_all(jnp.broadcast_to(values[None], (size, *values.shape)), axi...]
  transfers between devices with their start and end apart: 51 -> 51, of which waited for: 22 -> 23; matrix products, arithmetic and copies ran while one was open for 20% -> 20% of each run, Pallas kernels for 33% -> 33%
where the time goes in v9:
time: 1280 us; the launch traced here: 1270 us
  Pallas kernels  487 us (38%)
  waiting for transfers between devices  365 us (29%)
  other arithmetic  207 us (16%)
  starting transfers between devices  118 us (9%)
  local copies, waits for them, and re-layouts  75.2 us (6%)
  between operations  16.4 us (1%)
    ppermute x26, waiting for transfers between devices, swap(): return lax.ppermute(values, axis, [(i, i ^ bit) for i in range(size)])  249 us
    pallas_call x4, Pallas kernels, attend_back(): pl.pallas_call(partial(attend_back_kernel, masked), grid=(heads // many,)...  65.7 us
    all_to_all x5, waiting for transfers between devices, shared(): lax.all_to_all(jnp.broadcast_to(values[None], (size, *values.shape)), axi...  53.6 us
    pallas_call x6, Pallas kernels, outer(): pl.pallas_call(kernel, grid_spec=pltpu.PrefetchScalarGridSpec(num_scalar_...  53.3 us
    pallas_call x5, Pallas kernels, project(): pl.pallas_call(kernel, grid=(cols,), in_specs=[pl.BlockSpec((1, 1, depth,...  49.9 us
    pallas_call x4, Pallas kernels, attend(): pl.pallas_call(partial(attend_kernel, masked), grid=(heads // many,), in_...  45.4 us
    pallas_call x4, Pallas kernels, rebuild(): pl.pallas_call(kernel, grid=(4,), in_specs=[pl.BlockSpec((1, cols, tile,...  45.3 us
    pallas_call x2, Pallas kernels, contract(): pl.pallas_call(kernel, grid=(4,), in_specs=[pl.BlockSpec((1, many, tile,...  41.7 us
  transfers between devices with their start and end apart: 51, of which 23 were waited for; matrix products, arithmetic and copies ran while one was open for 20% of the time, Pallas kernels for 33%

profile of v9, /device:TPU:0, one launch (start us, length us, event | category | flops | bytes accessed | tf_op | source)
XLA Modules:
  0.0 1269.3 jit_solution(18200478341135942269)
XLA Ops:
  14.7 8.7 deal.2
  34.2 16.0 %collective-permute-done = bf16[352,384]{1,0:T(8,128)(2,1)S(1)} collective-permute-done((bf16[352,384]{1,0:T(8,128)(2,1)S(1)}, bf16[352,384]{1,0:T(8,128)(2,1)S(1)}, u32[]{:S(2)}, u32[]{:S(2)}) %collective-permute-start) | collective-permute-done | bytes 270368 | tf_op jit(solution)/shard_map/ppermute | solution.py:785
  50.1 9.0 collective-permute-done.2
  62.4 62.6 %collective-permute-done.5.own_ref = bf16[4,352,384]{2,1,0:T(8,128)(2,1)S(1)} collective-permute-done((bf16[4,352,384]{2,1,0:T(8,128)(2,1)S(1)}, bf16[4,352,384]{2,1,0:T(8,128)(2,1)S(1)}, u32[]{:S(2)}, u32[]{:S(2)}) %collective-permute-start.5) | collective-permute-done | bytes 1081376 | tf_op jit(solution)/shard_map/ppermute | solution.py:785
  128.4 6.7 assemble.2
  135.1 15.5 %collective-permute-done.6.got_ref = bf16[4,352,384]{2,1,0:T(8,128)(2,1)S(1)} collective-permute-done((bf16[4,352,384]{2,1,0:T(8,128)(2,1)S(1)}, bf16[4,352,384]{2,1,0:T(8,128)(2,1)S(1)}, u32[]{:S(2)}, u32[]{:S(2)}) %collective-permute-start.6) | collective-permute-done | bytes 1081376 | tf_op jit(solution)/shard_map/ppermute | solution.py:785
  151.6 6.6 assemble.3
  160.2 8.5 all-to-all-start.2
  168.7 6.6 all-to-all-done.2
  190.3 5.2 all-to-all-done.4
  211.7 13.0 %project_blocks.1 = f32[1408,768]{1,0:T(8,128)} custom-call(s32[1]{0:T(128)} %bitcast.4.base_ref, bf16[2816,384]{1,0:T(8,128)(2,1)} %bitcast.359, bf16[2816,384]{1,0:T(8,128)(2,1)} %collective-permute-done.4.refs_1_, bf16[2816,384]{1,0:T(8,128)(2,1)} %bitcast.362, bf16[2816,384]{1,0:T(8,128)(2,1)} %collective-permute-done.7.refs_3_, ...), custom_call_target="tpu_custom_call" | custom-call | flops 6090129408 | bytes 8650752 | tf_op jit(solution)/shard_map/project_blocks/pallas_call | solution.py:283
  233.0 5.6 add_convert_fusion.4.refs_3_.refs_0_
  238.6 15.1 %project.5 = (f32[1408,768]{1,0:T(8,128)}, f32[1408,768]{1,0:T(8,128)}, bf16[1408,768]{1,0:T(8,128)(2,1)}) custom-call(bf16[4,4,1408,352]{3,2,1,0:T(8,128)(2,1)} %bitcast.245, bf16[4,4,1408,352]{3,2,1,0:T(8,128)(2,1)} %bitcast.246, bf16[4,4,1408,352]{3,2,1,0:T(8,128)(2,1)} %bitcast.247, bf16[1408,768]{1,0:T(8,128)(2,1)} %add_convert_fusion.4.refs_3_.refs_0_), custom_call_target="tpu_custom_call" | custom-call | flops 9135194112 | bytes 8650752 | tf_op jit(solution)/shard_map/project/pallas_call | solution.py:221
  285.4 5.8 all-to-all-start.7
  299.5 16.9 %attend.4 = (bf16[2,8,88,512]{3,2,1,0:T(8,128)(2,1)}, bf16[2,8,88,512]{3,2,1,0:T(8,128)(2,1)}, f32[8,1,1024]{2,1,0:T(1,128)}) custom-call(s32[1]{0:T(128)} %constant.200.clone.1.length_ref, bf16[2,3,8,88,512]{4,3,2,1,0:T(8,128)(2,1)} %all-to-all-done.7.q_ref.k_ref.v_ref, bf16[2,3,8,88,512]{4,3,2,1,0:T(8,128)(2,1)} %all-to-all-done.7.q_ref.k_ref.v_ref, ...), custom_call_target="tpu_custom_call" | custom-call | flops 8589934592 | bytes 5767168 | tf_op jit(solution)/shard_map/attend/pallas_call | solution.py:140
  316.4 17.2 %all-to-all-done.9.q_ref.k_ref.v_ref = bf16[4,3,4,88,256]{4,3,2,1,0:T(8,128)(2,1)S(1)} async-done(((bf16[4,3,4,88,256]{4,3,2,1,0:T(8,128)(2,1)}), bf16[4,3,4,88,256]{4,3,2,1,0:T(8,128)(2,1)S(1)}, u32[]{:S(2)}, u32[]{:S(2)}) %all-to-all-start.9) | async-done | bytes 2162720 | tf_op jit(solution)/shard_map/all_to_all | solution.py:670
  338.9 9.4 attend.5
  352.4 8.1 deal.3
  372.5 8.8 rebuild.4
  389.5 8.1 project.6
  401.5 10.7 project.7
  425.6 7.4 attend.7
  435.6 11.7 attend.6
  450.2 8.8 rebuild.5
  467.7 28.5 %all-gather.4.cloned.1.call-done = bf16[2,5632,1536]{2,1,0:T(8,128)(2,1)} async-done(((bf16[2,176,1536]{2,1,0:T(8,128)(2,1)}), bf16[2,5632,1536]{2,1,0:T(8,128)(2,1)}) %all-gather.4.cloned.1.call-update) | async-done | bytes 34603024 | tf_op jit(solution)/shard_map/all_gather | solution.py:796
  496.2 27.1 %expand.1 = (bf16[4,1536,768]{2,1,0:T(8,128)(2,1)}, bf16[4,1536,768]{2,1,0:T(8,128)(2,1)}) custom-call(bf16[2,4,1408,1536]{3,2,1,0:T(8,128)(2,1)} %bitcast.293, bf16[1408,768]{1,0:T(8,128)(2,1)} %add_convert_fusion.2.values_ref.normed_ref), custom_call_target="tpu_custom_call" | custom-call | flops 13287555072 | bytes 25952256 | tf_op jit(solution)/shard_map/expand/pallas_call | solution.py:467
  524.7 20.5 %expand_back.1.inner_ref.values_ref = bf16[4,1536,768]{2,1,0:T(8,128)(2,1)} custom-call(bf16[2,4,1408,1536]{3,2,1,0:T(8,128)(2,1)} %bitcast.294, bf16[1408,768]{1,0:T(8,128)(2,1)} %bitcast.306, bf16[4,1536,768]{2,1,0:T(8,128)(2,1)} %get-tuple-element.115.slope_ref), custom_call_target="tpu_custom_call" | custom-call | flops 13287555072 | bytes 25952256 | tf_op jit(solution)/shard_map/expand_back/pallas_call | solution.py:492
  545.2 36.2 %hidden_outer.1 = bf16[2,4,1408,1536]{3,2,1,0:T(8,128)(2,1)} custom-call(bf16[1408,768]{1,0:T(8,128)(2,1)} %bitcast.307, bf16[4,1536,768]{2,1,0:T(8,128)(2,1)} %get-tuple-element.142.act_ref.values_ref, bf16[1408,768]{1,0:T(8,128)(2,1)} %add_convert_fusion.2.values_ref.normed_ref, bf16[4,1536,768]{2,1,0:T(8,128)(2,1)} %expand_back.1.inner_ref.values_ref), custom_call_target="tpu_custom_call" | custom-call | flops 26575110144 | bytes 43253760 | tf_op jit(solution)/shard_map/hidden_outer/pallas_call | solution.py:555
  582.2 21.0 %contract.2 = f32[1408,768]{1,0:T(8,128)} custom-call(bf16[2,4,1408,1536]{3,2,1,0:T(8,128)(2,1)} %bitcast.295, bf16[4,1536,768]{2,1,0:T(8,128)(2,1)} %expand_back.1.inner_ref.values_ref), custom_call_target="tpu_custom_call" | custom-call | flops 13287555072 | bytes 25952256 | tf_op jit(solution)/shard_map/contract/pallas_call | solution.py:522
  603.2 7.1 multiply_reduce_fusion.3
  615.7 8.2 project.8
  628.9 9.9 attend_back.5
  638.8 15.7 %attend_back.4 = (f32[1,1,16,88,512]{4,3,2,1,0:T(8,128)}, f32[1,1,16,88,384]{4,3,2,1,0:T(8,128)}, f32[1,1,16,88,384]{4,3,2,1,0:T(8,128)}) custom-call(s32[1]{0:T(128)} %get-tuple-element.403.length_ref, bf16[1,1,16,88,512]{4,3,2,1,0:T(8,128)(2,1)} %slice_bitcast_fusion.1.q_ref, bf16[1,1,16,88,384]{4,3,2,1,0:T(8,128)(2,1)} %get-tuple-element.364.k_ref, ...), custom_call_target="tpu_custom_call" | custom-call | flops 8053063680 | bytes 12615680 | tf_op jit(solution)/shard_map/attend_back/pallas_call | solution.py:173
  666.3 8.5 rebuild.6
  674.8 5.9 multiply_reduce_fusion.4
  680.7 8.1 fusion.62
  688.9 7.7 project.9
  713.8 26.0 %attend_back.6 = bf16[2,3,8,88,512]{4,3,2,1,0:T(8,128)(2,1)} custom-call(s32[1]{0:T(128)} %constant.200.clone.1.length_ref, bf16[2,3,8,88,512]{4,3,2,1,0:T(8,128)(2,1)} %all-to-all-done.7.q_ref.k_ref.v_ref, bf16[2,3,8,88,512]{4,3,2,1,0:T(8,128)(2,1)} %all-to-all-done.7.q_ref.k_ref.v_ref, bf16[2,3,8,88,512]{4,3,2,1,0:T(8,128)(2,1)} %all-to-all-done.7.q_ref.k_ref.v_ref, ...), custom_call_target="tpu_custom_call" | custom-call | flops 21474836480 | bytes 14417920 | tf_op jit(solution)/shard_map/attend_back/pallas_call | solution.py:173
  753.3 5.8 all-to-all-start.12
  759.1 14.2 %attend_back.7 = bf16[4,3,4,88,256]{4,3,2,1,0:T(8,128)(2,1)} custom-call(s32[1]{0:T(128)} %constant.200.clone.1.length_ref, bf16[4,3,4,88,256]{4,3,2,1,0:T(8,128)(2,1)} %copy-done.41, bf16[4,3,4,88,256]{4,3,2,1,0:T(8,128)(2,1)} %copy-done.41, bf16[4,3,4,88,256]{4,3,2,1,0:T(8,128)(2,1)} %copy-done.41, bf16[4,4,88,256]{3,2,1,0:T(8,128)(2,1)} %get-tuple-element.108.m_ref, ...), custom_call_target="tpu_custom_call" | custom-call | flops 10737418240 | bytes 7208960 | tf_op jit(solution)/shard_map/attend_back/pallas_call | solution.py:173
  778.0 27.8 %outer_all.1 = bf16[4,8,784,352]{3,2,1,0:T(8,128)(2,1)} custom-call(bf16[1408,768]{1,0:T(8,128)(2,1)} %fusion.56.refs_1_.refs_0_, bf16[1408,768]{1,0:T(8,128)(2,1)} %add_convert_fusion.3.refs_1_, bf16[1408,768]{1,0:T(8,128)(2,1)} %get-tuple-element.323.refs_1_.refs_2_, bf16[1024,768]{1,0:T(8,128)(2,1)} %bitcast.341, ...), custom_call_target="tpu_custom_call" | custom-call | flops 13564379136 | bytes 26492928 | tf_op jit(solution)/shard_map/outer_all/pallas_call | solution.py:435
  823.6 7.5 multiply_reduce_fusion.8
  845.5 9.1 outer.6
  856.2 6.2 outer.7
  862.6 19.1 %rebuild.7 = f32[1408,768]{1,0:T(8,128)} custom-call(bf16[4,4,1408,352]{3,2,1,0:T(8,128)(2,1)} %bitcast.250, bf16[4,4,1408,352]{3,2,1,0:T(8,128)(2,1)} %bitcast.251, bf16[4,4,1408,352]{3,2,1,0:T(8,128)(2,1)} %bitcast.252, bf16[1408,768]{1,0:T(8,128)(2,1)} %bitcast.330, bf16[1408,768]{1,0:T(8,128)(2,1)} %bitcast.333, ...), custom_call_target="tpu_custom_call" | custom-call | flops 9135194112 | bytes 8650752 | tf_op jit(solution)/shard_map/rebuild/pallas_call | solution.py:250
  883.1 7.0 outer.9
  890.1 10.6 outer.8
  904.9 5.8 fusion.18
  910.7 10.9 multiply_reduce_fusion.5
  929.6 6.7 multiply_convert_fusion.refs_4_.refs_1_
  936.4 9.9 outer.10
  959.8 13.8 %rebuild_blocks.1 = bf16[2816,768]{1,0:T(8,128)(2,1)} custom-call(s32[1]{0:T(128)} %bitcast.4.base_ref, bf16[2816,384]{1,0:T(8,128)(2,1)} %bitcast.360, bf16[2816,384]{1,0:T(8,128)(2,1)} %collective-permute-done.4.refs_1_, bf16[2816,384]{1,0:T(8,128)(2,1)} %bitcast.363, bf16[2816,384]{1,0:T(8,128)(2,1)} %collective-permute-done.7.refs_3_, ...), custom_call_target="tpu_custom_call" | custom-call | flops 6090129408 | bytes 8650752 | tf_op jit(solution)/shard_map/rebuild_blocks/pallas_call | solution.py:314
  973.6 38.2 %all-to-all-done.17 = f32[8,13,352]{2,1,0:T(8,128)S(1)} async-done(((f32[8,13,352]{2,1,0:T(8,128)}), f32[8,13,352]{2,1,0:T(8,128)S(1)}, u32[]{:S(2)}, u32[]{:S(2)}) %all-to-all-start.17) | async-done | bytes 146464 | tf_op jit(solution)/shard_map/all_to_all | solution.py:778
  1012.0 10.6 outer.11
  1030.4 20.6 %contract.3 = bf16[1408,768]{1,0:T(8,128)(2,1)} custom-call(bf16[2,4,1408,1536]{3,2,1,0:T(8,128)(2,1)} %bitcast.296, bf16[4,1536,768]{2,1,0:T(8,128)(2,1)} %get-tuple-element.142.act_ref.values_ref, f32[1408,768]{1,0:T(8,128)} %copy-done.3), custom_call_target="tpu_custom_call" | custom-call | flops 13287555072 | bytes 25952256 | tf_op jit(solution)/shard_map/contract/pallas_call | solution.py:522
  1051.1 8.0 collective-permute-done.12
  1062.7 26.2 %collective-permute-done.13 = bf16[1,2,4,352,384]{4,3,2,1,0:T(8,128)(2,1)} collective-permute-done((bf16[1,2,4,352,384]{4,3,2,1,0:T(8,128)(2,1)}, bf16[1,2,4,352,384]{4,3,2,1,0:T(8,128)(2,1)}, u32[]{:S(2)}, u32[]{:S(2)}) %collective-permute-start.13) | collective-permute-done | bytes 2162720 | tf_op jit(solution)/shard_map/ppermute | solution.py:785
  1098.9 18.1 %collective-permute-done.15 = bf16[1,4,176,384]{3,2,1,0:T(8,128)(2,1)S(1)} collective-permute-done((bf16[1,4,176,384]{3,2,1,0:T(8,128)(2,1)S(1)}, bf16[1,4,176,384]{3,2,1,0:T(8,128)(2,1)S(1)}, u32[]{:S(2)}, u32[]{:S(2)}) %collective-permute-start.15) | collective-permute-done | bytes 540704 | tf_op jit(solution)/shard_map/ppermute | solution.py:785
  1117.0 37.7 %collective-permute-done.14 = bf16[2,4,176,384]{3,2,1,0:T(8,128)(2,1)S(1)} collective-permute-done((bf16[2,4,176,384]{3,2,1,0:T(8,128)(2,1)S(1)}, bf16[2,4,176,384]{3,2,1,0:T(8,128)(2,1)S(1)}, u32[]{:S(2)}, u32[]{:S(2)}) %collective-permute-start.14) | collective-permute-done | bytes 1081376 | tf_op jit(solution)/shard_map/ppermute | solution.py:785
  1154.7 26.0 %collective-permute-done.16 = bf16[1,4,352,384]{3,2,1,0:T(8,128)(2,1)S(1)} collective-permute-done((bf16[1,4,352,384]{3,2,1,0:T(8,128)(2,1)S(1)}, bf16[1,4,352,384]{3,2,1,0:T(8,128)(2,1)S(1)}, u32[]{:S(2)}, u32[]{:S(2)}) %collective-permute-start.16) | collective-permute-done | bytes 1081376 | tf_op jit(solution)/shard_map/ppermute | solution.py:785
  1191.3 9.0 undeal.2
  1211.4 20.3 %collective-permute-done.21 = bf16[2,176,384]{2,1,0:T(8,128)(2,1)} collective-permute-done((bf16[2,176,384]{2,1,0:T(8,128)(2,1)S(1)}, bf16[2,176,384]{2,1,0:T(8,128)(2,1)}, u32[]{:S(2)}, u32[]{:S(2)}) %collective-permute-start.21) | collective-permute-done | bytes 270368 | tf_op jit(solution)/shard_map/ppermute | solution.py:785
  1233.9 7.6 collective-permute-done.18
  1254.6 8.0 undeal.3
  (568 shorter events, 345.9 us)
Async XLA Ops:
  7.2 177.1 %copy-start = (bf16[176,2,352]{2,1,0:T(2,128)(2,1)S(1)}, bf16[176,2,352]{2,1,0:T(2,128)(2,1)}, u32[]{:S(2)}) copy-start(bf16[176,2,352]{2,1,0:T(2,128)(2,1)} %param.34) | copy-start | bytes 743428
  7.2 231.4 %all-gather.6.cloned.1.call-start = ((), (), s32[]{:S(2)}) async-start(), calls=%async_computation.23 | async-start | bytes 17842176 | tf_op jit(solution)/shard_map/all_gather | solution.py:796
  10.3 379.2 %all-gather.8.cloned.1.call-start = ((), (), s32[]{:S(2)}) async-start(), calls=%async_computation.24 | async-start | bytes 17842176 | tf_op jit(solution)/shard_map/all_gather | solution.py:796
  13.5 482.7 %all-gather.4.cloned.1.call-start = ((), (), s32[]{:S(2)}) async-start(), calls=%async_computation.22 | async-start | bytes 35684352 | tf_op jit(solution)/shard_map/all_gather | solution.py:796
  23.4 136.2 %all-to-all-start = ((bf16[4,704,768]{2,1,0:T(8,128)(2,1)}), bf16[4,704,768]{2,1,0:T(8,128)(2,1)}, u32[]{:S(2)}, u32[]{:S(2)}) async-start(bf16[4,704,768]{2,1,0:T(8,128)(2,1)} %deal.2), calls=%async_computation | async-start | bytes 8650752 | tf_op jit(solution)/shard_map/all_to_all | solution.py:670
  28.5 21.7 %collective-permute-start = (bf16[352,384]{1,0:T(8,128)(2,1)S(1)}, bf16[352,384]{1,0:T(8,128)(2,1)S(1)}, u32[]{:S(2)}, u32[]{:S(2)}) collective-permute-start(bf16[352,384]{1,0:T(8,128)(2,1)S(1)} %get-tuple-element.390), channel_id=1, source_target_pairs={{0,8},{4,12},{8,0},{12,4},{16,24},{20,28},{24,16},{28,20},{1,9},{5... | collective-permute-start | bytes 811016 | tf_op jit(solution)/shard_map/ppermute | solution.py:785
  31.6 18.5 %collective-permute-start.1 = (bf16[352,384]{1,0:T(8,128)(2,1)S(1)}, bf16[352,384]{1,0:T(8,128)(2,1)S(1)}, u32[]{:S(2)}, u32[]{:S(2)}) collective-permute-start(bf16[352,384]{1,0:T(8,128)(2,1)S(1)} %get-tuple-element.390), channel_id=1, source_target_pairs={{0,16},{4,20},{8,24},{12,28},{16,0},{20,4},{24,8},{28,12},{1,17},{... | collective-permute-start | bytes 811016 | tf_op jit(solution)/shard_map/ppermute | solution.py:785
  34.2 25.0 %collective-permute-start.2 = (bf16[352,384]{1,0:T(8,128)(2,1)S(1)}, bf16[352,384]{1,0:T(8,128)(2,1)S(1)}, u32[]{:S(2)}, u32[]{:S(2)}) collective-permute-start(bf16[352,384]{1,0:T(8,128)(2,1)S(1)} %get-tuple-element.390), channel_id=1, source_target_pairs={{0,24},{4,28},{8,16},{12,20},{16,8},{20,12},{24,0},{28,4},{1,25},{... | collective-permute-start | bytes 811016 | tf_op jit(solution)/shard_map/ppermute | solution.py:785
  59.3 69.1 %copy-start.34 = (bf16[4,352,384]{2,1,0:T(8,128)(2,1)}, bf16[4,352,384]{2,1,0:T(8,128)(2,1)S(1)}, u32[]{:S(2)}) copy-start(bf16[4,352,384]{2,1,0:T(8,128)(2,1)S(1)} %pad_maximum_fusion.12.own_ref) | copy-start | bytes 3244036
  59.3 65.7 %collective-permute-start.5 = (bf16[4,352,384]{2,1,0:T(8,128)(2,1)S(1)}, bf16[4,352,384]{2,1,0:T(8,128)(2,1)S(1)}, u32[]{:S(2)}, u32[]{:S(2)}) collective-permute-start(bf16[4,352,384]{2,1,0:T(8,128)(2,1)S(1)} %pad_maximum_fusion.12.own_ref), channel_id=1, source_target_pairs={{0,2},{1,3},{2,0},{3,1},{4,6},{5,7},{6,4},{7,5},{8,10},{9,11},{10,... | collective-permute-start | bytes 3244040 | tf_op jit(solution)/shard_map/ppermute | solution.py:785
  60.9 67.5 %collective-permute-start.3 = (bf16[4,352,384]{2,1,0:T(8,128)(2,1)S(1)}, bf16[4,352,384]{2,1,0:T(8,128)(2,1)}, u32[]{:S(2)}, u32[]{:S(2)}) collective-permute-start(bf16[4,352,384]{2,1,0:T(8,128)(2,1)S(1)} %pad_maximum_fusion.12.own_ref), channel_id=1, source_target_pairs={{0,4},{4,0},{8,12},{12,8},{16,20},{20,16},{24,28},{28,24},{1,5},{5... | collective-permute-start | bytes 3244040 | tf_op jit(solution)/shard_map/ppermute | solution.py:785
  125.0 25.6 %collective-permute-start.6 = (bf16[4,352,384]{2,1,0:T(8,128)(2,1)S(1)}, bf16[4,352,384]{2,1,0:T(8,128)(2,1)S(1)}, u32[]{:S(2)}, u32[]{:S(2)}) collective-permute-start(bf16[4,352,384]{2,1,0:T(8,128)(2,1)S(1)} %collective-permute-done.5.own_ref), channel_id=1, source_target_pairs={{0,4},{4,0},{8,12},{12,8},{16,20},{20,16},{24,28},{28,24},{1,5},{5... | collective-permute-start | bytes 3244040 | tf_op jit(solution)/shard_map/ppermute | solution.py:785
  128.4 51.0 %copy-start.109 = (f32[352]{0:T(512)S(1)}, f32[352]{0:T(512)}, u32[]{:S(2)}) copy-start(f32[352]{0:T(512)} %param.43) | copy-start | bytes 4228
  128.4 51.0 %copy-start.110 = (f32[352]{0:T(512)S(1)}, f32[352]{0:T(512)}, u32[]{:S(2)}) copy-start(f32[352]{0:T(512)} %param.44) | copy-start | bytes 4228
  128.4 51.0 %copy-start.111 = (f32[352]{0:T(512)S(1)}, f32[352]{0:T(512)}, u32[]{:S(2)}) copy-start(f32[352]{0:T(512)} %param.45) | copy-start | bytes 4228
  128.4 51.0 %copy-start.112 = (f32[352]{0:T(512)S(1)}, f32[352]{0:T(512)}, u32[]{:S(2)}) copy-start(f32[352]{0:T(512)} %param.46) | copy-start | bytes 4228
  128.4 51.0 %copy-start.113 = (f32[352]{0:T(512)S(1)}, f32[352]{0:T(512)}, u32[]{:S(2)}) copy-start(f32[352]{0:T(512)} %param.47) | copy-start | bytes 4228
  135.1 76.5 %collective-permute-start.4 = (bf16[2816,384]{1,0:T(8,128)(2,1)}, bf16[2816,384]{1,0:T(8,128)(2,1)}, u32[]{:S(2)}, u32[]{:S(2)}) collective-permute-start(bf16[2816,384]{1,0:T(8,128)(2,1)} %bitcast.358), channel_id=1, source_target_pairs={{0,1},{1,0},{2,3},{3,2},{4,5},{5,4},{6,7},{7,6},{8,9},{9,8},{10,11... | collective-permute-start | bytes 6488072 | tf_op jit(solution)/shard_map/ppermute | solution.py:785
  158.1 53.5 %collective-permute-start.7 = (bf16[2816,384]{1,0:T(8,128)(2,1)}, bf16[2816,384]{1,0:T(8,128)(2,1)}, u32[]{:S(2)}, u32[]{:S(2)}) collective-permute-start(bf16[2816,384]{1,0:T(8,128)(2,1)} %bitcast.361), channel_id=1, source_target_pairs={{0,1},{1,0},{2,3},{3,2},{4,5},{5,4},{6,7},{7,6},{8,9},{9,8},{10,11... | collective-permute-start | bytes 6488072 | tf_op jit(solution)/shard_map/ppermute | solution.py:785
  160.2 15.1 %all-to-all-start.2 = ((bf16[8,3,352]{2,1,0:T(4,128)(2,1)}), bf16[8,3,352]{2,1,0:T(4,128)(2,1)S(1)}, u32[]{:S(2)}, u32[]{:S(2)}) async-start(bf16[8,3,352]{2,1,0:T(4,128)(2,1)} %broadcast_in_dim.193), calls=%async_computation.2 | async-start | bytes 49152 | tf_op jit(solution)/shard_map/all_to_all | solution.py:778
  175.9 8.2 all-to-all-start.3
  185.2 10.3 all-to-all-start.4
  190.3 87.1 %copy-start.23 = (f32[88,768]{1,0:T(8,128)}, f32[88,768]{1,0:T(8,128)S(1)}, u32[]{:S(2)}) copy-start(f32[88,768]{1,0:T(8,128)S(1)} %get-tuple-element.395) | copy-start | bytes 811012
  196.3 8.9 all-to-all-start.5
  206.9 46.8 %all-to-all-start.6 = ((bf16[4,3,384,256]{2,3,1,0:T(8,128)(2,1)}), bf16[4,3,384,256]{2,3,1,0:T(8,128)(2,1)S(1)}, u32[]{:S(2)}, u32[]{:S(2)}) async-start(bf16[4,3,384,256]{2,3,1,0:T(8,128)(2,1)} %broadcast_in_dim.206), calls=%async_computation.6 | async-start | bytes 4718592 | tf_op jit(solution)/shard_map/all_to_all | solution.py:778
  211.6 169.7 %copy-start.64 = (f32[1408]{0:T(1024)}, f32[1408]{0:T(1024)S(1)}, u32[]{:S(2)}) copy-start(f32[1408]{0:T(1024)S(1)} %get-tuple-element.313) | copy-start | bytes 16900
  211.6 169.7 %copy-start.72 = (f32[1408]{0:T(1024)}, f32[1408]{0:T(1024)S(1)}, u32[]{:S(2)}) copy-start(f32[1408]{0:T(1024)S(1)} %get-tuple-element.312) | copy-start | bytes 16900
  211.6 174.4 %copy-start.79 = (f32[1408]{0:T(1024)}, f32[1408]{0:T(1024)S(1)}, u32[]{:S(2)}) copy-start(f32[1408]{0:T(1024)S(1)} %get-tuple-element.307) | copy-start | bytes 16900
  227.2 154.1 %copy-start.74 = (f32[768]{0:T(1024)}, f32[768]{0:T(1024)S(1)}, u32[]{:S(2)}) copy-start(f32[768]{0:T(1024)S(1)} %broadcast_multiply_fusion.17) | copy-start | bytes 9220
  230.1 151.2 %copy-start.77 = (f32[768]{0:T(1024)}, f32[768]{0:T(1024)S(1)}, u32[]{:S(2)}) copy-start(f32[768]{0:T(1024)S(1)} %add_rsqrt_fusion.3) | copy-start | bytes 9220
  285.4 10.5 all-to-all-start.7
  295.9 37.7 %all-to-all-start.9 = ((bf16[4,3,4,88,256]{4,3,2,1,0:T(8,128)(2,1)}), bf16[4,3,4,88,256]{4,3,2,1,0:T(8,128)(2,1)S(1)}, u32[]{:S(2)}, u32[]{:S(2)}) async-start(bf16[4,3,4,88,256]{4,3,2,1,0:T(8,128)(2,1)} %pad_maximum_fusion.3), calls=%async_computation.9 | async-start | bytes 4325376 | tf_op jit(solution)/shard_map/all_to_all | solution.py:670
  335.0 13.3 %all-to-all-start.8 = ((bf16[2,8,88,512]{3,2,1,0:T(8,128)(2,1)}), bf16[2,8,88,512]{3,2,1,0:T(8,128)(2,1)S(1)}, u32[]{:S(2)}, u32[]{:S(2)}) async-start(bf16[2,8,88,512]{3,2,1,0:T(8,128)(2,1)} %get-tuple-element.107.m_ref), calls=%async_computation.8 | async-start | bytes 2883584 | tf_op jit(solution)/shard_map/all_to_all | solution.py:671
  348.3 14.6 %all-to-all-start.10 = ((bf16[4,4,88,256]{3,2,1,0:T(8,128)(2,1)}), bf16[4,4,88,256]{3,2,1,0:T(8,128)(2,1)S(1)}, u32[]{:S(2)}, u32[]{:S(2)}) async-start(bf16[4,4,88,256]{3,2,1,0:T(8,128)(2,1)} %get-tuple-element.108.m_ref), calls=%async_computation.10 | async-start | bytes 1441792 | tf_op jit(solution)/shard_map/all_to_all | solution.py:670
  362.9 160.5 %all-to-all-start.1 = ((bf16[4,352,768]{2,1,0:T(8,128)(2,1)}), bf16[4,352,768]{2,1,0:T(8,128)(2,1)S(1)}, u32[]{:S(2)}, u32[]{:S(2)}) async-start(bf16[4,352,768]{2,1,0:T(8,128)(2,1)} %deal.3), calls=%async_computation.1 | async-start | bytes 4325376 | tf_op jit(solution)/shard_map/all_to_all | solution.py:670
  366.5 838.4 %reduce-scatter.3.cloned.1.call-start = ((), (), s32[]{:S(2)}) async-start(), calls=%async_computation.25 | async-start | bytes 35684352 | tf_op jit(solution)/shard_map/reduce_scatter | solution.py:1086
  701.3 8.5 all-to-all-start.11
  709.8 42.6 %all-to-all-start.13 = ((bf16[4,4,88,256]{3,2,1,0:T(8,128)(2,1)}), bf16[4,4,88,256]{3,2,1,0:T(8,128)(2,1)S(1)}, u32[]{:S(2)}, u32[]{:S(2)}) async-start(bf16[4,4,88,256]{3,2,1,0:T(8,128)(2,1)} %bitcast.78), calls=%async_computation.13 | async-start | bytes 1441792 | tf_op jit(solution)/shard_map/all_to_all | solution.py:670
  753.3 20.0 %all-to-all-start.12 = ((bf16[2,3,8,88,512]{4,3,2,1,0:T(8,128)(2,1)}), bf16[2,3,8,88,512]{4,3,2,1,0:T(8,128)(2,1)}, u32[]{:S(2)}, u32[]{:S(2)}) async-start(bf16[2,3,8,88,512]{4,3,2,1,0:T(8,128)(2,1)} %attend_back.6), calls=%async_computation.12 | async-start | bytes 8650752 | tf_op jit(solution)/shard_map/all_to_all | solution.py:671
  773.3 39.6 %all-to-all-start.14 = ((bf16[4,3,4,88,256]{4,3,2,1,0:T(8,128)(2,1)}), bf16[4,3,4,88,256]{4,3,2,1,0:T(8,128)(2,1)}, u32[]{:S(2)}, u32[]{:S(2)}) async-start(bf16[4,3,4,88,256]{4,3,2,1,0:T(8,128)(2,1)} %attend_back.7), calls=%async_computation.14 | async-start | bytes 4325376 | tf_op jit(solution)/shard_map/all_to_all | solution.py:670
  777.8 465.7 %reduce-scatter.5.cloned.1.call-start = ((), (), s32[]{:S(2)}) async-start(), calls=%async_computation.26 | async-start | bytes 19869696 | tf_op jit(solution)/shard_map/reduce_scatter | solution.py:1122
  854.5 27.2 %collective-permute-start.8 = (bf16[2,2,1408,384]{3,2,1,0:T(8,128)(2,1)}, bf16[2,2,1408,384]{3,2,1,0:T(8,128)(2,1)}, u32[]{:S(2)}, u32[]{:S(2)}) collective-permute-start(bf16[2,2,1408,384]{3,2,1,0:T(8,128)(2,1)} %outer.6), channel_id=1, source_target_pairs={{0,1},{1,0},{2,3},{3,2},{4,5},{5,4},{6,7},{7,6},{8,9},{9,8},{10,11... | collective-permute-start | bytes 12976136 | tf_op jit(solution)/shard_map/ppermute | solution.py:785
  862.4 19.3 %collective-permute-start.9 = (bf16[1,2,1408,384]{3,2,1,0:T(8,128)(2,1)}, bf16[1,2,1408,384]{3,2,1,0:T(8,128)(2,1)S(1)}, u32[]{:S(2)}, u32[]{:S(2)}) collective-permute-start(bf16[1,2,1408,384]{3,2,1,0:T(8,128)(2,1)} %outer.7), channel_id=1, source_target_pairs={{0,1},{1,0},{2,3},{3,2},{4,5},{5,4},{6,7},{7,6},{8,9},{9,8},{10,11... | collective-permute-start | bytes 6488072 | tf_op jit(solution)/shard_map/ppermute | solution.py:785
  926.3 10.0 all-to-all-start.15
  946.2 65.7 %collective-permute-start.10 = (bf16[1,2,2816,384]{3,2,1,0:T(8,128)(2,1)}, bf16[1,2,2816,384]{3,2,1,0:T(8,128)(2,1)}, u32[]{:S(2)}, u32[]{:S(2)}) collective-permute-start(bf16[1,2,2816,384]{3,2,1,0:T(8,128)(2,1)} %outer.10), channel_id=1, source_target_pairs={{0,1},{1,0},{2,3},{3,2},{4,5},{5,4},{6,7},{7,6},{8,9},{9,8},{10,11... | collective-permute-start | bytes 12976136 | tf_op jit(solution)/shard_map/ppermute | solution.py:785
  948.2 7.3 all-to-all-start.16
  951.5 107.5 %collective-permute-start.11 = (bf16[2,2,4,176,384]{4,3,2,1,0:T(8,128)(2,1)}, bf16[2,2,4,176,384]{4,3,2,1,0:T(8,128)(2,1)}, u32[]{:S(2)}, u32[]{:S(2)}) collective-permute-start(bf16[2,2,4,176,384]{4,3,2,1,0:T(8,128)(2,1)} %get-tuple-element.144), channel_id=1, source_target_pairs={{0,4},{4,0},{8,12},{12,8},{16,20},{20,16},{24,28},{28,24},{1,5},{5... | collective-permute-start | bytes 6488072 | tf_op jit(solution)/shard_map/ppermute | solution.py:785
  956.2 55.6 %all-to-all-start.17 = ((f32[8,13,352]{2,1,0:T(8,128)}), f32[8,13,352]{2,1,0:T(8,128)S(1)}, u32[]{:S(2)}, u32[]{:S(2)}) async-start(f32[8,13,352]{2,1,0:T(8,128)} %broadcast_in_dim.227), calls=%async_computation.17 | async-start | bytes 393216 | tf_op jit(solution)/shard_map/all_to_all | solution.py:778
  1022.5 66.4 %collective-permute-start.13 = (bf16[1,2,4,352,384]{4,3,2,1,0:T(8,128)(2,1)}, bf16[1,2,4,352,384]{4,3,2,1,0:T(8,128)(2,1)}, u32[]{:S(2)}, u32[]{:S(2)}) collective-permute-start(bf16[1,2,4,352,384]{4,3,2,1,0:T(8,128)(2,1)} %get-tuple-element.149), channel_id=1, source_target_pairs={{0,4},{4,0},{8,12},{12,8},{16,20},{20,16},{24,28},{28,24},{1,5},{5... | collective-permute-start | bytes 6488072 | tf_op jit(solution)/shard_map/ppermute | solution.py:785
  1023.8 35.3 %collective-permute-start.12 = (bf16[1,4,2,176,384]{4,3,2,1,0:T(8,128)(2,1)}, bf16[1,4,2,176,384]{4,3,2,1,0:T(8,128)(2,1)S(1)}, u32[]{:S(2)}, u32[]{:S(2)}) collective-permute-start(bf16[1,4,2,176,384]{4,3,2,1,0:T(8,128)(2,1)} %get-tuple-element.146), channel_id=1, source_target_pairs={{0,2},{1,3},{2,0},{3,1},{4,6},{5,7},{6,4},{7,5},{8,10},{9,11},{10,... | collective-permute-start | bytes 3244040 | tf_op jit(solution)/shard_map/ppermute | solution.py:785
  1025.5 165.9 %all-to-all-start.18 = ((bf16[4,704,768]{2,1,0:T(8,128)(2,1)}), bf16[4,704,768]{2,1,0:T(8,128)(2,1)}, u32[]{:S(2)}, u32[]{:S(2)}) async-start(bf16[4,704,768]{2,1,0:T(8,128)(2,1)} %bitcast.348), calls=%async_computation.19 | async-start | bytes 8650752 | tf_op jit(solution)/shard_map/all_to_all | solution.py:670
  1060.6 94.0 %collective-permute-start.14 = (bf16[2,4,176,384]{3,2,1,0:T(8,128)(2,1)S(1)}, bf16[2,4,176,384]{3,2,1,0:T(8,128)(2,1)S(1)}, u32[]{:S(2)}, u32[]{:S(2)}) collective-permute-start(bf16[2,4,176,384]{3,2,1,0:T(8,128)(2,1)S(1)} %fusion.20), channel_id=1, source_target_pairs={{0,2},{1,3},{2,0},{3,1},{4,6},{5,7},{6,4},{7,5},{8,10},{9,11},{10,... | collective-permute-start | bytes 3244040 | tf_op jit(solution)/shard_map/ppermute | solution.py:785
  1091.1 89.6 %collective-permute-start.16 = (bf16[1,4,352,384]{3,2,1,0:T(8,128)(2,1)S(1)}, bf16[1,4,352,384]{3,2,1,0:T(8,128)(2,1)S(1)}, u32[]{:S(2)}, u32[]{:S(2)}) collective-permute-start(bf16[1,4,352,384]{3,2,1,0:T(8,128)(2,1)S(1)} %get-tuple-element.334), channel_id=1, source_target_pairs={{0,2},{1,3},{2,0},{3,1},{4,6},{5,7},{6,4},{7,5},{8,10},{9,11},{10,... | collective-permute-start | bytes 3244040 | tf_op jit(solution)/shard_map/ppermute | solution.py:785
  1095.9 21.0 %collective-permute-start.15 = (bf16[1,4,176,384]{3,2,1,0:T(8,128)(2,1)S(1)}, bf16[1,4,176,384]{3,2,1,0:T(8,128)(2,1)S(1)}, u32[]{:S(2)}, u32[]{:S(2)}) collective-permute-start(bf16[1,4,176,384]{3,2,1,0:T(8,128)(2,1)S(1)} %fusion.24), channel_id=1, source_target_pairs={{0,4},{4,0},{8,12},{12,8},{16,20},{20,16},{24,28},{28,24},{1,5},{5... | collective-permute-start | bytes 1622024 | tf_op jit(solution)/shard_map/ppermute | solution.py:785
  1180.9 9.5 collective-permute-start.23
  1181.0 19.4 %collective-permute-start.25 = (bf16[1,176,384]{2,1,0:T(8,128)(2,1)S(1)}, bf16[1,176,384]{2,1,0:T(8,128)(2,1)S(1)}, u32[]{:S(2)}, u32[]{:S(2)}) collective-permute-start(bf16[1,176,384]{2,1,0:T(8,128)(2,1)S(1)} %get-tuple-element.379), channel_id=1, source_target_pairs={{0,24},{4,28},{8,16},{12,20},{16,8},{20,12},{24,0},{28,4},{1,25},{... | collective-permute-start | bytes 405512 | tf_op jit(solution)/shard_map/ppermute | solution.py:785
  1182.9 18.5 %collective-permute-start.24 = (bf16[1,176,384]{2,1,0:T(8,128)(2,1)S(1)}, bf16[1,176,384]{2,1,0:T(8,128)(2,1)S(1)}, u32[]{:S(2)}, u32[]{:S(2)}) collective-permute-start(bf16[1,176,384]{2,1,0:T(8,128)(2,1)S(1)} %get-tuple-element.380), channel_id=1, source_target_pairs={{0,16},{4,20},{8,24},{12,28},{16,0},{20,4},{24,8},{28,12},{1,17},{... | collective-permute-start | bytes 405512 | tf_op jit(solution)/shard_map/ppermute | solution.py:785
  1185.7 25.6 %collective-permute-start.20 = (bf16[2,176,384]{2,1,0:T(8,128)(2,1)}, bf16[2,176,384]{2,1,0:T(8,128)(2,1)S(1)}, u32[]{:S(2)}, u32[]{:S(2)}) collective-permute-start(bf16[2,176,384]{2,1,0:T(8,128)(2,1)} %get-tuple-element.370), channel_id=1, source_target_pairs={{0,8},{4,12},{8,0},{12,4},{16,24},{20,28},{24,16},{28,20},{1,9},{5... | collective-permute-start | bytes 811016 | tf_op jit(solution)/shard_map/ppermute | solution.py:785
  1186.7 24.7 %collective-permute-start.22 = (bf16[2,176,384]{2,1,0:T(8,128)(2,1)}, bf16[2,176,384]{2,1,0:T(8,128)(2,1)}, u32[]{:S(2)}, u32[]{:S(2)}) collective-permute-start(bf16[2,176,384]{2,1,0:T(8,128)(2,1)} %get-tuple-element.371), channel_id=1, source_target_pairs={{0,24},{4,28},{8,16},{12,20},{16,8},{20,12},{24,0},{28,4},{1,25},{... | collective-permute-start | bytes 811016 | tf_op jit(solution)/shard_map/ppermute | solution.py:785
  1190.4 41.3 %collective-permute-start.21 = (bf16[2,176,384]{2,1,0:T(8,128)(2,1)S(1)}, bf16[2,176,384]{2,1,0:T(8,128)(2,1)}, u32[]{:S(2)}, u32[]{:S(2)}) collective-permute-start(bf16[2,176,384]{2,1,0:T(8,128)(2,1)S(1)} %get-tuple-element.372), channel_id=1, source_target_pairs={{0,16},{4,20},{8,24},{12,28},{16,0},{20,4},{24,8},{28,12},{1,17},{... | collective-permute-start | bytes 811016 | tf_op jit(solution)/shard_map/ppermute | solution.py:785
  1200.4 33.5 %collective-permute-start.17 = (bf16[1,352,384]{2,1,0:T(8,128)(2,1)}, bf16[1,352,384]{2,1,0:T(8,128)(2,1)}, u32[]{:S(2)}, u32[]{:S(2)}) collective-permute-start(bf16[1,352,384]{2,1,0:T(8,128)(2,1)} %get-tuple-element.374), channel_id=1, source_target_pairs={{0,8},{4,12},{8,0},{12,4},{16,24},{20,28},{24,16},{28,20},{1,9},{5... | collective-permute-start | bytes 811016 | tf_op jit(solution)/shard_map/ppermute | solution.py:785
  1201.5 32.4 %collective-permute-start.19 = (bf16[1,352,384]{2,1,0:T(8,128)(2,1)}, bf16[1,352,384]{2,1,0:T(8,128)(2,1)}, u32[]{:S(2)}, u32[]{:S(2)}) collective-permute-start(bf16[1,352,384]{2,1,0:T(8,128)(2,1)} %get-tuple-element.375), channel_id=1, source_target_pairs={{0,24},{4,28},{8,16},{12,20},{16,8},{20,12},{24,0},{28,4},{1,25},{... | collective-permute-start | bytes 811016 | tf_op jit(solution)/shard_map/ppermute | solution.py:785
  1207.7 45.5 %all-to-all-start.19 = ((bf16[4,352,768]{2,1,0:T(8,128)(2,1)}), bf16[4,352,768]{2,1,0:T(8,128)(2,1)S(1)}, u32[]{:S(2)}, u32[]{:S(2)}) async-start(bf16[4,352,768]{2,1,0:T(8,128)(2,1)} %bitcast.102), calls=%async_computation.20 | async-start | bytes 4325376 | tf_op jit(solution)/shard_map/all_to_all | solution.py:670
  1211.3 30.1 %collective-permute-start.18 = (bf16[1,352,384]{2,1,0:T(8,128)(2,1)}, bf16[1,352,384]{2,1,0:T(8,128)(2,1)S(1)}, u32[]{:S(2)}, u32[]{:S(2)}) collective-permute-start(bf16[1,352,384]{2,1,0:T(8,128)(2,1)} %get-tuple-element.376), channel_id=1, source_target_pairs={{0,16},{4,20},{8,24},{12,28},{16,0},{20,4},{24,8},{28,12},{1,17},{... | collective-permute-start | bytes 811016 | tf_op jit(solution)/shard_map/ppermute | solution.py:785
  (114 other events, 912.0 us)
Sparse Core Ops, SparseCore 0:
  11.7 152.6 all-gather.5
  168.1 122.1 all-gather.7
  293.9 202.2 all-gather.3
  581.5 332.1 reduce-scatter.2
  921.2 253.6 reduce-scatter.4

commit v10 on v9

--- a/solution.py
+++ b/solution.py
@@ -1199,7 +1199,9 @@
     output = tick(output, [r_skip])
     if custom_mesh():
         states = [r.state for r in r_self]
-        states, r_skip.state = lax.optimization_barrier((states, r_skip.state))
+        states, r_skip.state, g_latents, g_skip = lax.optimization_barrier(
+            (states, r_skip.state, g_latents, g_skip)
+        )
         r_skip.advance()
         for beside, state in zip(r_self, states):
             beside.state = state

time: 1280 us -> 1280 us (level)
  transfers between devices with their start and end apart: 51 -> 51, of which waited for: 23 -> 22; matrix products, arithmetic and copies ran while one was open for 20% -> 21% of each run, Pallas kernels for 33% -> 33%
where the time goes in v10:
time: 1280 us
  Pallas kernels  487 us (38%)
  waiting for transfers between devices  367 us (29%)
  other arithmetic  214 us (17%)
  starting transfers between devices  114 us (9%)
  local copies, waits for them, and re-layouts  75.3 us (6%)
  between operations  16.5 us (1%)
    ppermute x26, waiting for transfers between devices, swap(): return lax.ppermute(values, axis, [(i, i ^ bit) for i in range(size)])  251 us
    pallas_call x4, Pallas kernels, attend_back(): pl.pallas_call(partial(attend_back_kernel, masked), grid=(heads // many,)...  65.7 us
    all_to_all x5, waiting for transfers between devices, shared(): lax.all_to_all(jnp.broadcast_to(values[None], (size, *values.shape)), axi...  53.6 us
    pallas_call x6, Pallas kernels, outer(): pl.pallas_call(kernel, grid_spec=pltpu.PrefetchScalarGridSpec(num_scalar_...  53.3 us
    pallas_call x5, Pallas kernels, project(): pl.pallas_call(kernel, grid=(cols,), in_specs=[pl.BlockSpec((1, 1, depth,...  49.8 us
    pallas_call x4, Pallas kernels, attend(): pl.pallas_call(partial(attend_kernel, masked), grid=(heads // many,), in_...  45.4 us
    pallas_call x4, Pallas kernels, rebuild(): pl.pallas_call(kernel, grid=(4,), in_specs=[pl.BlockSpec((1, cols, tile,...  45.3 us
    pallas_call x2, Pallas kernels, contract(): pl.pallas_call(kernel, grid=(4,), in_specs=[pl.BlockSpec((1, many, tile,...  41.6 us
  transfers between devices with their start and end apart: 51, of which 22 were waited for; matrix products, arithmetic and copies ran while one was open for 21% of the time, Pallas kernels for 33%

profile of v10, /device:TPU:0, one launch (start us, length us, event | category | flops | bytes accessed | tf_op | source)
XLA Modules:
  0.0 1275.4 jit_solution(2391864397596481200)
XLA Ops:
  14.7 8.7 deal.2
  23.4 5.0 all-to-all-start
  34.2 15.9 %collective-permute-done = bf16[352,384]{1,0:T(8,128)(2,1)S(1)} collective-permute-done((bf16[352,384]{1,0:T(8,128)(2,1)S(1)}, bf16[352,384]{1,0:T(8,128)(2,1)S(1)}, u32[]{:S(2)}, u32[]{:S(2)}) %collective-permute-start) | collective-permute-done | bytes 270368 | tf_op jit(solution)/shard_map/ppermute | solution.py:785
  50.1 9.0 collective-permute-done.2
  62.4 62.6 %collective-permute-done.5.own_ref = bf16[4,352,384]{2,1,0:T(8,128)(2,1)S(1)} collective-permute-done((bf16[4,352,384]{2,1,0:T(8,128)(2,1)S(1)}, bf16[4,352,384]{2,1,0:T(8,128)(2,1)S(1)}, u32[]{:S(2)}, u32[]{:S(2)}) %collective-permute-start.5) | collective-permute-done | bytes 1081376 | tf_op jit(solution)/shard_map/ppermute | solution.py:785
  128.5 6.7 assemble.2
  135.2 15.5 %collective-permute-done.6.got_ref = bf16[4,352,384]{2,1,0:T(8,128)(2,1)S(1)} collective-permute-done((bf16[4,352,384]{2,1,0:T(8,128)(2,1)S(1)}, bf16[4,352,384]{2,1,0:T(8,128)(2,1)S(1)}, u32[]{:S(2)}, u32[]{:S(2)}) %collective-permute-start.6) | collective-permute-done | bytes 1081376 | tf_op jit(solution)/shard_map/ppermute | solution.py:785
  151.6 6.6 assemble.3
  160.2 8.4 all-to-all-start.2
  168.6 6.6 all-to-all-done.2
  190.2 5.2 all-to-all-done.4
  211.5 13.0 %project_blocks.1 = f32[1408,768]{1,0:T(8,128)} custom-call(s32[1]{0:T(128)} %bitcast.4.base_ref, bf16[2816,384]{1,0:T(8,128)(2,1)} %bitcast.359, bf16[2816,384]{1,0:T(8,128)(2,1)} %collective-permute-done.4.refs_1_, bf16[2816,384]{1,0:T(8,128)(2,1)} %bitcast.362, bf16[2816,384]{1,0:T(8,128)(2,1)} %collective-permute-done.7.refs_3_, ...), custom_call_target="tpu_custom_call" | custom-call | flops 6090129408 | bytes 8650752 | tf_op jit(solution)/shard_map/project_blocks/pallas_call | solution.py:283
  232.9 5.6 add_convert_fusion.4.refs_3_.refs_0_
  238.5 15.1 %project.5 = (f32[1408,768]{1,0:T(8,128)}, f32[1408,768]{1,0:T(8,128)}, bf16[1408,768]{1,0:T(8,128)(2,1)}) custom-call(bf16[4,4,1408,352]{3,2,1,0:T(8,128)(2,1)} %bitcast.245, bf16[4,4,1408,352]{3,2,1,0:T(8,128)(2,1)} %bitcast.246, bf16[4,4,1408,352]{3,2,1,0:T(8,128)(2,1)} %bitcast.247, bf16[1408,768]{1,0:T(8,128)(2,1)} %add_convert_fusion.4.refs_3_.refs_0_), custom_call_target="tpu_custom_call" | custom-call | flops 9135194112 | bytes 8650752 | tf_op jit(solution)/shard_map/project/pallas_call | solution.py:221
  285.2 5.7 all-to-all-start.7
  299.4 16.9 %attend.4 = (bf16[2,8,88,512]{3,2,1,0:T(8,128)(2,1)}, bf16[2,8,88,512]{3,2,1,0:T(8,128)(2,1)}, f32[8,1,1024]{2,1,0:T(1,128)}) custom-call(s32[1]{0:T(128)} %constant.200.clone.1.length_ref, bf16[2,3,8,88,512]{4,3,2,1,0:T(8,128)(2,1)} %all-to-all-done.7.q_ref.k_ref.v_ref, bf16[2,3,8,88,512]{4,3,2,1,0:T(8,128)(2,1)} %all-to-all-done.7.q_ref.k_ref.v_ref, ...), custom_call_target="tpu_custom_call" | custom-call | flops 8589934592 | bytes 5767168 | tf_op jit(solution)/shard_map/attend/pallas_call | solution.py:140
  316.3 17.2 %all-to-all-done.9.q_ref.k_ref.v_ref = bf16[4,3,4,88,256]{4,3,2,1,0:T(8,128)(2,1)S(1)} async-done(((bf16[4,3,4,88,256]{4,3,2,1,0:T(8,128)(2,1)}), bf16[4,3,4,88,256]{4,3,2,1,0:T(8,128)(2,1)S(1)}, u32[]{:S(2)}, u32[]{:S(2)}) %all-to-all-start.9) | async-done | bytes 2162720 | tf_op jit(solution)/shard_map/all_to_all | solution.py:670
  338.8 9.4 attend.5
  352.3 8.0 deal.3
  372.5 8.8 rebuild.4
  389.5 8.1 project.6
  401.5 10.7 project.7
  425.6 7.4 attend.7
  435.6 11.7 attend.6
  450.1 8.9 rebuild.5
  467.7 28.5 %all-gather.4.cloned.1.call-done = bf16[2,5632,1536]{2,1,0:T(8,128)(2,1)} async-done(((bf16[2,176,1536]{2,1,0:T(8,128)(2,1)}), bf16[2,5632,1536]{2,1,0:T(8,128)(2,1)}) %all-gather.4.cloned.1.call-update) | async-done | bytes 34603024 | tf_op jit(solution)/shard_map/all_gather | solution.py:796
  496.2 27.2 %expand.1 = (bf16[4,1536,768]{2,1,0:T(8,128)(2,1)}, bf16[4,1536,768]{2,1,0:T(8,128)(2,1)}) custom-call(bf16[2,4,1408,1536]{3,2,1,0:T(8,128)(2,1)} %bitcast.293, bf16[1408,768]{1,0:T(8,128)(2,1)} %add_convert_fusion.2.values_ref.normed_ref), custom_call_target="tpu_custom_call" | custom-call | flops 13287555072 | bytes 25952256 | tf_op jit(solution)/shard_map/expand/pallas_call | solution.py:467
  524.7 20.6 %expand_back.1.inner_ref.values_ref = bf16[4,1536,768]{2,1,0:T(8,128)(2,1)} custom-call(bf16[2,4,1408,1536]{3,2,1,0:T(8,128)(2,1)} %bitcast.294, bf16[1408,768]{1,0:T(8,128)(2,1)} %bitcast.306, bf16[4,1536,768]{2,1,0:T(8,128)(2,1)} %get-tuple-element.117.slope_ref), custom_call_target="tpu_custom_call" | custom-call | flops 13287555072 | bytes 25952256 | tf_op jit(solution)/shard_map/expand_back/pallas_call | solution.py:492
  545.3 36.3 %hidden_outer.1 = bf16[2,4,1408,1536]{3,2,1,0:T(8,128)(2,1)} custom-call(bf16[1408,768]{1,0:T(8,128)(2,1)} %bitcast.307, bf16[4,1536,768]{2,1,0:T(8,128)(2,1)} %get-tuple-element.144.act_ref.values_ref, bf16[1408,768]{1,0:T(8,128)(2,1)} %add_convert_fusion.2.values_ref.normed_ref, bf16[4,1536,768]{2,1,0:T(8,128)(2,1)} %expand_back.1.inner_ref.values_ref), custom_call_target="tpu_custom_call" | custom-call | flops 26575110144 | bytes 43253760 | tf_op jit(solution)/shard_map/hidden_outer/pallas_call | solution.py:555
  582.4 21.1 %contract.2 = f32[1408,768]{1,0:T(8,128)} custom-call(bf16[2,4,1408,1536]{3,2,1,0:T(8,128)(2,1)} %bitcast.295, bf16[4,1536,768]{2,1,0:T(8,128)(2,1)} %expand_back.1.inner_ref.values_ref), custom_call_target="tpu_custom_call" | custom-call | flops 13287555072 | bytes 25952256 | tf_op jit(solution)/shard_map/contract/pallas_call | solution.py:522
  603.5 7.2 multiply_reduce_fusion.3
  616.0 8.2 project.8
  629.1 9.8 attend_back.5
  638.9 15.7 %attend_back.4 = (f32[1,1,16,88,512]{4,3,2,1,0:T(8,128)}, f32[1,1,16,88,384]{4,3,2,1,0:T(8,128)}, f32[1,1,16,88,384]{4,3,2,1,0:T(8,128)}) custom-call(s32[1]{0:T(128)} %get-tuple-element.407.length_ref, bf16[1,1,16,88,512]{4,3,2,1,0:T(8,128)(2,1)} %slice_bitcast_fusion.1.q_ref, bf16[1,1,16,88,384]{4,3,2,1,0:T(8,128)(2,1)} %get-tuple-element.368.k_ref, ...), custom_call_target="tpu_custom_call" | custom-call | flops 8053063680 | bytes 12615680 | tf_op jit(solution)/shard_map/attend_back/pallas_call | solution.py:173
  666.4 8.5 rebuild.6
  674.9 5.9 multiply_reduce_fusion.4
  680.8 8.2 fusion.62
  689.0 7.7 project.9
  714.0 26.0 %attend_back.6 = bf16[2,3,8,88,512]{4,3,2,1,0:T(8,128)(2,1)} custom-call(s32[1]{0:T(128)} %constant.200.clone.1.length_ref, bf16[2,3,8,88,512]{4,3,2,1,0:T(8,128)(2,1)} %all-to-all-done.7.q_ref.k_ref.v_ref, bf16[2,3,8,88,512]{4,3,2,1,0:T(8,128)(2,1)} %all-to-all-done.7.q_ref.k_ref.v_ref, bf16[2,3,8,88,512]{4,3,2,1,0:T(8,128)(2,1)} %all-to-all-done.7.q_ref.k_ref.v_ref, ...), custom_call_target="tpu_custom_call" | custom-call | flops 21474836480 | bytes 14417920 | tf_op jit(solution)/shard_map/attend_back/pallas_call | solution.py:173
  753.4 5.8 all-to-all-start.12
  759.3 14.2 %attend_back.7 = bf16[4,3,4,88,256]{4,3,2,1,0:T(8,128)(2,1)} custom-call(s32[1]{0:T(128)} %constant.200.clone.1.length_ref, bf16[4,3,4,88,256]{4,3,2,1,0:T(8,128)(2,1)} %copy-done.41, bf16[4,3,4,88,256]{4,3,2,1,0:T(8,128)(2,1)} %copy-done.41, bf16[4,3,4,88,256]{4,3,2,1,0:T(8,128)(2,1)} %copy-done.41, bf16[4,4,88,256]{3,2,1,0:T(8,128)(2,1)} %get-tuple-element.110.m_ref, ...), custom_call_target="tpu_custom_call" | custom-call | flops 10737418240 | bytes 7208960 | tf_op jit(solution)/shard_map/attend_back/pallas_call | solution.py:173
  778.1 27.9 %outer_all.1 = bf16[4,8,784,352]{3,2,1,0:T(8,128)(2,1)} custom-call(bf16[1408,768]{1,0:T(8,128)(2,1)} %fusion.56.refs_1_.refs_0_, bf16[1408,768]{1,0:T(8,128)(2,1)} %add_convert_fusion.3.refs_1_, bf16[1408,768]{1,0:T(8,128)(2,1)} %get-tuple-element.327.refs_1_.refs_2_, bf16[1024,768]{1,0:T(8,128)(2,1)} %bitcast.341, ...), custom_call_target="tpu_custom_call" | custom-call | flops 13564379136 | bytes 26492928 | tf_op jit(solution)/shard_map/outer_all/pallas_call | solution.py:435
  823.8 7.5 multiply_reduce_fusion.8
  845.6 9.1 outer.6
  856.4 6.2 outer.7
  862.8 19.1 %rebuild.7 = f32[1408,768]{1,0:T(8,128)} custom-call(bf16[4,4,1408,352]{3,2,1,0:T(8,128)(2,1)} %bitcast.250, bf16[4,4,1408,352]{3,2,1,0:T(8,128)(2,1)} %bitcast.251, bf16[4,4,1408,352]{3,2,1,0:T(8,128)(2,1)} %bitcast.252, bf16[1408,768]{1,0:T(8,128)(2,1)} %bitcast.330, bf16[1408,768]{1,0:T(8,128)(2,1)} %bitcast.333, ...), custom_call_target="tpu_custom_call" | custom-call | flops 9135194112 | bytes 8650752 | tf_op jit(solution)/shard_map/rebuild/pallas_call | solution.py:250
  883.3 7.0 outer.9
  890.3 10.6 outer.8
  905.1 5.8 fusion.18
  910.9 10.9 multiply_reduce_fusion.5
  929.8 6.7 multiply_convert_fusion.refs_4_.refs_1_
  936.6 9.8 outer.10
  960.1 13.8 %rebuild_blocks.1 = bf16[2816,768]{1,0:T(8,128)(2,1)} custom-call(s32[1]{0:T(128)} %bitcast.4.base_ref, bf16[2816,384]{1,0:T(8,128)(2,1)} %bitcast.360, bf16[2816,384]{1,0:T(8,128)(2,1)} %collective-permute-done.4.refs_1_, bf16[2816,384]{1,0:T(8,128)(2,1)} %bitcast.363, bf16[2816,384]{1,0:T(8,128)(2,1)} %collective-permute-done.7.refs_3_, ...), custom_call_target="tpu_custom_call" | custom-call | flops 6090129408 | bytes 8650752 | tf_op jit(solution)/shard_map/rebuild_blocks/pallas_call | solution.py:314
  973.9 38.2 %all-to-all-done.17 = f32[8,13,352]{2,1,0:T(8,128)S(1)} async-done(((f32[8,13,352]{2,1,0:T(8,128)}), f32[8,13,352]{2,1,0:T(8,128)S(1)}, u32[]{:S(2)}, u32[]{:S(2)}) %all-to-all-start.17) | async-done | bytes 146464 | tf_op jit(solution)/shard_map/all_to_all | solution.py:778
  1012.2 10.6 outer.11
  1031.2 20.5 %contract.3 = bf16[1408,768]{1,0:T(8,128)(2,1)} custom-call(bf16[2,4,1408,1536]{3,2,1,0:T(8,128)(2,1)} %bitcast.296, bf16[4,1536,768]{2,1,0:T(8,128)(2,1)} %get-tuple-element.144.act_ref.values_ref, f32[1408,768]{1,0:T(8,128)} %copy-done.3), custom_call_target="tpu_custom_call" | custom-call | flops 13287555072 | bytes 25952256 | tf_op jit(solution)/shard_map/contract/pallas_call | solution.py:522
  1051.7 79.5 %collective-permute-done.12 = bf16[1,4,2,176,384]{4,3,2,1,0:T(8,128)(2,1)S(1)} collective-permute-done((bf16[1,4,2,176,384]{4,3,2,1,0:T(8,128)(2,1)}, bf16[1,4,2,176,384]{4,3,2,1,0:T(8,128)(2,1)S(1)}, u32[]{:S(2)}, u32[]{:S(2)}) %collective-permute-start.12) | collective-permute-done | bytes 1081376 | tf_op jit(solution)/shard_map/ppermute | solution.py:785
  1146.5 9.1 undeal.2
  1155.7 5.0 collective-permute-done.15
  1165.6 21.5 %collective-permute-done.16 = bf16[1,4,352,384]{3,2,1,0:T(8,128)(2,1)} collective-permute-done((bf16[1,4,352,384]{3,2,1,0:T(8,128)(2,1)}, bf16[1,4,352,384]{3,2,1,0:T(8,128)(2,1)}, u32[]{:S(2)}, u32[]{:S(2)}) %collective-permute-start.16) | collective-permute-done | bytes 1081376 | tf_op jit(solution)/shard_map/ppermute | solution.py:785
  1201.3 10.6 collective-permute-done.24
  1218.6 18.7 %collective-permute-done.21 = bf16[2,176,384]{2,1,0:T(8,128)(2,1)} collective-permute-done((bf16[2,176,384]{2,1,0:T(8,128)(2,1)S(1)}, bf16[2,176,384]{2,1,0:T(8,128)(2,1)}, u32[]{:S(2)}, u32[]{:S(2)}) %collective-permute-start.21) | collective-permute-done | bytes 270368 | tf_op jit(solution)/shard_map/ppermute | solution.py:785
  1239.4 8.1 collective-permute-done.18
  1260.7 8.0 undeal.3
  (572 shorter events, 347.2 us)
Async XLA Ops:
  7.2 177.0 %copy-start = (bf16[176,2,352]{2,1,0:T(2,128)(2,1)S(1)}, bf16[176,2,352]{2,1,0:T(2,128)(2,1)}, u32[]{:S(2)}) copy-start(bf16[176,2,352]{2,1,0:T(2,128)(2,1)} %param.34) | copy-start | bytes 743428
  7.2 231.3 %all-gather.6.cloned.1.call-start = ((), (), s32[]{:S(2)}) async-start(), calls=%async_computation.23 | async-start | bytes 17842176 | tf_op jit(solution)/shard_map/all_gather | solution.py:796
  10.3 379.2 %all-gather.8.cloned.1.call-start = ((), (), s32[]{:S(2)}) async-start(), calls=%async_computation.24 | async-start | bytes 17842176 | tf_op jit(solution)/shard_map/all_gather | solution.py:796
  13.5 482.7 %all-gather.4.cloned.1.call-start = ((), (), s32[]{:S(2)}) async-start(), calls=%async_computation.22 | async-start | bytes 35684352 | tf_op jit(solution)/shard_map/all_gather | solution.py:796
  23.4 136.2 %all-to-all-start = ((bf16[4,704,768]{2,1,0:T(8,128)(2,1)}), bf16[4,704,768]{2,1,0:T(8,128)(2,1)}, u32[]{:S(2)}, u32[]{:S(2)}) async-start(bf16[4,704,768]{2,1,0:T(8,128)(2,1)} %deal.2), calls=%async_computation | async-start | bytes 8650752 | tf_op jit(solution)/shard_map/all_to_all | solution.py:670
  28.5 21.7 %collective-permute-start = (bf16[352,384]{1,0:T(8,128)(2,1)S(1)}, bf16[352,384]{1,0:T(8,128)(2,1)S(1)}, u32[]{:S(2)}, u32[]{:S(2)}) collective-permute-start(bf16[352,384]{1,0:T(8,128)(2,1)S(1)} %get-tuple-element.394), channel_id=1, source_target_pairs={{0,8},{4,12},{8,0},{12,4},{16,24},{20,28},{24,16},{28,20},{1,9},{5... | collective-permute-start | bytes 811016 | tf_op jit(solution)/shard_map/ppermute | solution.py:785
  31.6 18.5 %collective-permute-start.1 = (bf16[352,384]{1,0:T(8,128)(2,1)S(1)}, bf16[352,384]{1,0:T(8,128)(2,1)S(1)}, u32[]{:S(2)}, u32[]{:S(2)}) collective-permute-start(bf16[352,384]{1,0:T(8,128)(2,1)S(1)} %get-tuple-element.394), channel_id=1, source_target_pairs={{0,16},{4,20},{8,24},{12,28},{16,0},{20,4},{24,8},{28,12},{1,17},{... | collective-permute-start | bytes 811016 | tf_op jit(solution)/shard_map/ppermute | solution.py:785
  34.2 24.9 %collective-permute-start.2 = (bf16[352,384]{1,0:T(8,128)(2,1)S(1)}, bf16[352,384]{1,0:T(8,128)(2,1)S(1)}, u32[]{:S(2)}, u32[]{:S(2)}) collective-permute-start(bf16[352,384]{1,0:T(8,128)(2,1)S(1)} %get-tuple-element.394), channel_id=1, source_target_pairs={{0,24},{4,28},{8,16},{12,20},{16,8},{20,12},{24,0},{28,4},{1,25},{... | collective-permute-start | bytes 811016 | tf_op jit(solution)/shard_map/ppermute | solution.py:785
  59.3 69.1 %copy-start.34 = (bf16[4,352,384]{2,1,0:T(8,128)(2,1)}, bf16[4,352,384]{2,1,0:T(8,128)(2,1)S(1)}, u32[]{:S(2)}) copy-start(bf16[4,352,384]{2,1,0:T(8,128)(2,1)S(1)} %pad_maximum_fusion.12.own_ref) | copy-start | bytes 3244036
  59.3 65.7 %collective-permute-start.5 = (bf16[4,352,384]{2,1,0:T(8,128)(2,1)S(1)}, bf16[4,352,384]{2,1,0:T(8,128)(2,1)S(1)}, u32[]{:S(2)}, u32[]{:S(2)}) collective-permute-start(bf16[4,352,384]{2,1,0:T(8,128)(2,1)S(1)} %pad_maximum_fusion.12.own_ref), channel_id=1, source_target_pairs={{0,2},{1,3},{2,0},{3,1},{4,6},{5,7},{6,4},{7,5},{8,10},{9,11},{10,... | collective-permute-start | bytes 3244040 | tf_op jit(solution)/shard_map/ppermute | solution.py:785
  60.9 67.5 %collective-permute-start.3 = (bf16[4,352,384]{2,1,0:T(8,128)(2,1)S(1)}, bf16[4,352,384]{2,1,0:T(8,128)(2,1)}, u32[]{:S(2)}, u32[]{:S(2)}) collective-permute-start(bf16[4,352,384]{2,1,0:T(8,128)(2,1)S(1)} %pad_maximum_fusion.12.own_ref), channel_id=1, source_target_pairs={{0,4},{4,0},{8,12},{12,8},{16,20},{20,16},{24,28},{28,24},{1,5},{5... | collective-permute-start | bytes 3244040 | tf_op jit(solution)/shard_map/ppermute | solution.py:785
  125.0 25.6 %collective-permute-start.6 = (bf16[4,352,384]{2,1,0:T(8,128)(2,1)S(1)}, bf16[4,352,384]{2,1,0:T(8,128)(2,1)S(1)}, u32[]{:S(2)}, u32[]{:S(2)}) collective-permute-start(bf16[4,352,384]{2,1,0:T(8,128)(2,1)S(1)} %collective-permute-done.5.own_ref), channel_id=1, source_target_pairs={{0,4},{4,0},{8,12},{12,8},{16,20},{20,16},{24,28},{28,24},{1,5},{5... | collective-permute-start | bytes 3244040 | tf_op jit(solution)/shard_map/ppermute | solution.py:785
  128.4 51.0 %copy-start.113 = (f32[352]{0:T(512)S(1)}, f32[352]{0:T(512)}, u32[]{:S(2)}) copy-start(f32[352]{0:T(512)} %param.45) | copy-start | bytes 4228
  128.4 51.0 %copy-start.114 = (f32[352]{0:T(512)S(1)}, f32[352]{0:T(512)}, u32[]{:S(2)}) copy-start(f32[352]{0:T(512)} %param.46) | copy-start | bytes 4228
  128.4 51.0 %copy-start.115 = (f32[352]{0:T(512)S(1)}, f32[352]{0:T(512)}, u32[]{:S(2)}) copy-start(f32[352]{0:T(512)} %param.47) | copy-start | bytes 4228
  135.2 76.4 %collective-permute-start.4 = (bf16[2816,384]{1,0:T(8,128)(2,1)}, bf16[2816,384]{1,0:T(8,128)(2,1)}, u32[]{:S(2)}, u32[]{:S(2)}) collective-permute-start(bf16[2816,384]{1,0:T(8,128)(2,1)} %bitcast.358), channel_id=1, source_target_pairs={{0,1},{1,0},{2,3},{3,2},{4,5},{5,4},{6,7},{7,6},{8,9},{9,8},{10,11... | collective-permute-start | bytes 6488072 | tf_op jit(solution)/shard_map/ppermute | solution.py:785
  158.2 53.4 %collective-permute-start.7 = (bf16[2816,384]{1,0:T(8,128)(2,1)}, bf16[2816,384]{1,0:T(8,128)(2,1)}, u32[]{:S(2)}, u32[]{:S(2)}) collective-permute-start(bf16[2816,384]{1,0:T(8,128)(2,1)} %bitcast.361), channel_id=1, source_target_pairs={{0,1},{1,0},{2,3},{3,2},{4,5},{5,4},{6,7},{7,6},{8,9},{9,8},{10,11... | collective-permute-start | bytes 6488072 | tf_op jit(solution)/shard_map/ppermute | solution.py:785
  160.2 15.0 %all-to-all-start.2 = ((bf16[8,3,352]{2,1,0:T(4,128)(2,1)}), bf16[8,3,352]{2,1,0:T(4,128)(2,1)S(1)}, u32[]{:S(2)}, u32[]{:S(2)}) async-start(bf16[8,3,352]{2,1,0:T(4,128)(2,1)} %broadcast_in_dim.193), calls=%async_computation.2 | async-start | bytes 49152 | tf_op jit(solution)/shard_map/all_to_all | solution.py:778
  175.9 8.1 all-to-all-start.3
  185.1 10.3 all-to-all-start.4
  190.2 87.0 %copy-start.23 = (f32[88,768]{1,0:T(8,128)}, f32[88,768]{1,0:T(8,128)S(1)}, u32[]{:S(2)}) copy-start(f32[88,768]{1,0:T(8,128)S(1)} %get-tuple-element.399) | copy-start | bytes 811012
  196.2 8.9 all-to-all-start.5
  206.8 46.8 %all-to-all-start.6 = ((bf16[4,3,384,256]{2,3,1,0:T(8,128)(2,1)}), bf16[4,3,384,256]{2,3,1,0:T(8,128)(2,1)S(1)}, u32[]{:S(2)}, u32[]{:S(2)}) async-start(bf16[4,3,384,256]{2,3,1,0:T(8,128)(2,1)} %broadcast_in_dim.206), calls=%async_computation.6 | async-start | bytes 4718592 | tf_op jit(solution)/shard_map/all_to_all | solution.py:778
  211.5 169.8 %copy-start.66 = (f32[1408]{0:T(1024)}, f32[1408]{0:T(1024)S(1)}, u32[]{:S(2)}) copy-start(f32[1408]{0:T(1024)S(1)} %get-tuple-element.317) | copy-start | bytes 16900
  211.5 169.8 %copy-start.74 = (f32[1408]{0:T(1024)}, f32[1408]{0:T(1024)S(1)}, u32[]{:S(2)}) copy-start(f32[1408]{0:T(1024)S(1)} %get-tuple-element.316) | copy-start | bytes 16900
  211.5 174.5 %copy-start.81 = (f32[1408]{0:T(1024)}, f32[1408]{0:T(1024)S(1)}, u32[]{:S(2)}) copy-start(f32[1408]{0:T(1024)S(1)} %get-tuple-element.311) | copy-start | bytes 16900
  227.1 154.2 %copy-start.76 = (f32[768]{0:T(1024)}, f32[768]{0:T(1024)S(1)}, u32[]{:S(2)}) copy-start(f32[768]{0:T(1024)S(1)} %broadcast_multiply_fusion.17) | copy-start | bytes 9220
  230.0 151.4 %copy-start.79 = (f32[768]{0:T(1024)}, f32[768]{0:T(1024)S(1)}, u32[]{:S(2)}) copy-start(f32[768]{0:T(1024)S(1)} %add_rsqrt_fusion.3) | copy-start | bytes 9220
  285.2 10.7 all-to-all-start.7
  295.8 37.7 %all-to-all-start.9 = ((bf16[4,3,4,88,256]{4,3,2,1,0:T(8,128)(2,1)}), bf16[4,3,4,88,256]{4,3,2,1,0:T(8,128)(2,1)S(1)}, u32[]{:S(2)}, u32[]{:S(2)}) async-start(bf16[4,3,4,88,256]{4,3,2,1,0:T(8,128)(2,1)} %pad_maximum_fusion.3), calls=%async_computation.9 | async-start | bytes 4325376 | tf_op jit(solution)/shard_map/all_to_all | solution.py:670
  334.9 13.3 %all-to-all-start.8 = ((bf16[2,8,88,512]{3,2,1,0:T(8,128)(2,1)}), bf16[2,8,88,512]{3,2,1,0:T(8,128)(2,1)S(1)}, u32[]{:S(2)}, u32[]{:S(2)}) async-start(bf16[2,8,88,512]{3,2,1,0:T(8,128)(2,1)} %get-tuple-element.109.m_ref), calls=%async_computation.8 | async-start | bytes 2883584 | tf_op jit(solution)/shard_map/all_to_all | solution.py:671
  348.2 14.6 %all-to-all-start.10 = ((bf16[4,4,88,256]{3,2,1,0:T(8,128)(2,1)}), bf16[4,4,88,256]{3,2,1,0:T(8,128)(2,1)S(1)}, u32[]{:S(2)}, u32[]{:S(2)}) async-start(bf16[4,4,88,256]{3,2,1,0:T(8,128)(2,1)} %get-tuple-element.110.m_ref), calls=%async_computation.10 | async-start | bytes 1441792 | tf_op jit(solution)/shard_map/all_to_all | solution.py:670
  362.8 160.5 %all-to-all-start.1 = ((bf16[4,352,768]{2,1,0:T(8,128)(2,1)}), bf16[4,352,768]{2,1,0:T(8,128)(2,1)S(1)}, u32[]{:S(2)}, u32[]{:S(2)}) async-start(bf16[4,352,768]{2,1,0:T(8,128)(2,1)} %deal.3), calls=%async_computation.1 | async-start | bytes 4325376 | tf_op jit(solution)/shard_map/all_to_all | solution.py:670
  366.4 845.5 %reduce-scatter.3.cloned.1.call-start = ((), (), s32[]{:S(2)}) async-start(), calls=%async_computation.25 | async-start | bytes 35684352 | tf_op jit(solution)/shard_map/reduce_scatter | solution.py:1086
  701.5 8.5 all-to-all-start.11
  710.0 42.5 %all-to-all-start.13 = ((bf16[4,4,88,256]{3,2,1,0:T(8,128)(2,1)}), bf16[4,4,88,256]{3,2,1,0:T(8,128)(2,1)S(1)}, u32[]{:S(2)}, u32[]{:S(2)}) async-start(bf16[4,4,88,256]{3,2,1,0:T(8,128)(2,1)} %bitcast.78), calls=%async_computation.13 | async-start | bytes 1441792 | tf_op jit(solution)/shard_map/all_to_all | solution.py:670
  753.4 20.0 %all-to-all-start.12 = ((bf16[2,3,8,88,512]{4,3,2,1,0:T(8,128)(2,1)}), bf16[2,3,8,88,512]{4,3,2,1,0:T(8,128)(2,1)}, u32[]{:S(2)}, u32[]{:S(2)}) async-start(bf16[2,3,8,88,512]{4,3,2,1,0:T(8,128)(2,1)} %attend_back.6), calls=%async_computation.12 | async-start | bytes 8650752 | tf_op jit(solution)/shard_map/all_to_all | solution.py:671
  773.4 39.7 %all-to-all-start.14 = ((bf16[4,3,4,88,256]{4,3,2,1,0:T(8,128)(2,1)}), bf16[4,3,4,88,256]{4,3,2,1,0:T(8,128)(2,1)}, u32[]{:S(2)}, u32[]{:S(2)}) async-start(bf16[4,3,4,88,256]{4,3,2,1,0:T(8,128)(2,1)} %attend_back.7), calls=%async_computation.14 | async-start | bytes 4325376 | tf_op jit(solution)/shard_map/all_to_all | solution.py:670
  777.9 471.6 %reduce-scatter.5.cloned.1.call-start = ((), (), s32[]{:S(2)}) async-start(), calls=%async_computation.26 | async-start | bytes 19869696 | tf_op jit(solution)/shard_map/reduce_scatter | solution.py:1122
  854.7 27.2 %collective-permute-start.8 = (bf16[2,2,1408,384]{3,2,1,0:T(8,128)(2,1)}, bf16[2,2,1408,384]{3,2,1,0:T(8,128)(2,1)}, u32[]{:S(2)}, u32[]{:S(2)}) collective-permute-start(bf16[2,2,1408,384]{3,2,1,0:T(8,128)(2,1)} %outer.6), channel_id=1, source_target_pairs={{0,1},{1,0},{2,3},{3,2},{4,5},{5,4},{6,7},{7,6},{8,9},{9,8},{10,11... | collective-permute-start | bytes 12976136 | tf_op jit(solution)/shard_map/ppermute | solution.py:785
  862.6 19.4 %collective-permute-start.9 = (bf16[1,2,1408,384]{3,2,1,0:T(8,128)(2,1)}, bf16[1,2,1408,384]{3,2,1,0:T(8,128)(2,1)S(1)}, u32[]{:S(2)}, u32[]{:S(2)}) collective-permute-start(bf16[1,2,1408,384]{3,2,1,0:T(8,128)(2,1)} %outer.7), channel_id=1, source_target_pairs={{0,1},{1,0},{2,3},{3,2},{4,5},{5,4},{6,7},{7,6},{8,9},{9,8},{10,11... | collective-permute-start | bytes 6488072 | tf_op jit(solution)/shard_map/ppermute | solution.py:785
  926.5 10.0 all-to-all-start.15
  946.4 65.8 %collective-permute-start.10 = (bf16[1,2,2816,384]{3,2,1,0:T(8,128)(2,1)}, bf16[1,2,2816,384]{3,2,1,0:T(8,128)(2,1)}, u32[]{:S(2)}, u32[]{:S(2)}) collective-permute-start(bf16[1,2,2816,384]{3,2,1,0:T(8,128)(2,1)} %outer.10), channel_id=1, source_target_pairs={{0,1},{1,0},{2,3},{3,2},{4,5},{5,4},{6,7},{7,6},{8,9},{9,8},{10,11... | collective-permute-start | bytes 12976136 | tf_op jit(solution)/shard_map/ppermute | solution.py:785
  948.5 7.3 all-to-all-start.16
  951.8 179.4 %collective-permute-start.11 = (bf16[2,2,4,176,384]{4,3,2,1,0:T(8,128)(2,1)}, bf16[2,2,4,176,384]{4,3,2,1,0:T(8,128)(2,1)}, u32[]{:S(2)}, u32[]{:S(2)}) collective-permute-start(bf16[2,2,4,176,384]{4,3,2,1,0:T(8,128)(2,1)} %get-tuple-element.146), channel_id=1, source_target_pairs={{0,4},{4,0},{8,12},{12,8},{16,20},{20,16},{24,28},{28,24},{1,5},{5... | collective-permute-start | bytes 6488072 | tf_op jit(solution)/shard_map/ppermute | solution.py:785
  956.5 55.6 %all-to-all-start.17 = ((f32[8,13,352]{2,1,0:T(8,128)}), f32[8,13,352]{2,1,0:T(8,128)S(1)}, u32[]{:S(2)}, u32[]{:S(2)}) async-start(f32[8,13,352]{2,1,0:T(8,128)} %broadcast_in_dim.227), calls=%async_computation.17 | async-start | bytes 393216 | tf_op jit(solution)/shard_map/all_to_all | solution.py:778
  1022.8 111.3 %collective-permute-start.13 = (bf16[1,2,4,352,384]{4,3,2,1,0:T(8,128)(2,1)}, bf16[1,2,4,352,384]{4,3,2,1,0:T(8,128)(2,1)}, u32[]{:S(2)}, u32[]{:S(2)}) collective-permute-start(bf16[1,2,4,352,384]{4,3,2,1,0:T(8,128)(2,1)} %get-tuple-element.151), channel_id=1, source_target_pairs={{0,4},{4,0},{8,12},{12,8},{16,20},{20,16},{24,28},{28,24},{1,5},{5... | collective-permute-start | bytes 6488072 | tf_op jit(solution)/shard_map/ppermute | solution.py:785
  1024.3 122.3 %all-to-all-start.18 = ((bf16[4,704,768]{2,1,0:T(8,128)(2,1)}), bf16[4,704,768]{2,1,0:T(8,128)(2,1)}, u32[]{:S(2)}, u32[]{:S(2)}) async-start(bf16[4,704,768]{2,1,0:T(8,128)(2,1)} %bitcast.348), calls=%async_computation.19 | async-start | bytes 8650752 | tf_op jit(solution)/shard_map/all_to_all | solution.py:670
  1029.3 101.9 %copy-start.43 = (bf16[2,2,4,176,384]{4,3,2,1,0:T(8,128)(2,1)S(1)}, bf16[2,2,4,176,384]{4,3,2,1,0:T(8,128)(2,1)}, u32[]{:S(2)}) copy-start(bf16[2,2,4,176,384]{4,3,2,1,0:T(8,128)(2,1)} %get-tuple-element.155) | copy-start | bytes 6488068
  1029.3 101.9 %collective-permute-start.12 = (bf16[1,4,2,176,384]{4,3,2,1,0:T(8,128)(2,1)}, bf16[1,4,2,176,384]{4,3,2,1,0:T(8,128)(2,1)S(1)}, u32[]{:S(2)}, u32[]{:S(2)}) collective-permute-start(bf16[1,4,2,176,384]{4,3,2,1,0:T(8,128)(2,1)} %get-tuple-element.148), channel_id=1, source_target_pairs={{0,2},{1,3},{2,0},{3,1},{4,6},{5,7},{6,4},{7,5},{8,10},{9,11},{10,... | collective-permute-start | bytes 3244040 | tf_op jit(solution)/shard_map/ppermute | solution.py:785
  1051.7 82.5 %copy-start.45 = (bf16[1,2,4,352,384]{4,3,2,1,0:T(8,128)(2,1)S(1)}, bf16[1,2,4,352,384]{4,3,2,1,0:T(8,128)(2,1)}, u32[]{:S(2)}) copy-start(bf16[1,2,4,352,384]{4,3,2,1,0:T(8,128)(2,1)} %get-tuple-element.159) | copy-start | bytes 6488068
  1134.2 31.4 %collective-permute-start.14 = (bf16[2,4,176,384]{3,2,1,0:T(8,128)(2,1)}, bf16[2,4,176,384]{3,2,1,0:T(8,128)(2,1)}, u32[]{:S(2)}, u32[]{:S(2)}) collective-permute-start(bf16[2,4,176,384]{3,2,1,0:T(8,128)(2,1)} %fusion.20), channel_id=1, source_target_pairs={{0,2},{1,3},{2,0},{3,1},{4,6},{5,7},{6,4},{7,5},{8,10},{9,11},{10,... | collective-permute-start | bytes 3244040 | tf_op jit(solution)/shard_map/ppermute | solution.py:785
  1137.5 49.6 %collective-permute-start.16 = (bf16[1,4,352,384]{3,2,1,0:T(8,128)(2,1)}, bf16[1,4,352,384]{3,2,1,0:T(8,128)(2,1)}, u32[]{:S(2)}, u32[]{:S(2)}) collective-permute-start(bf16[1,4,352,384]{3,2,1,0:T(8,128)(2,1)} %get-tuple-element.338), channel_id=1, source_target_pairs={{0,2},{1,3},{2,0},{3,1},{4,6},{5,7},{6,4},{7,5},{8,10},{9,11},{10,... | collective-permute-start | bytes 3244040 | tf_op jit(solution)/shard_map/ppermute | solution.py:785
  1143.8 16.9 %collective-permute-start.15 = (bf16[1,4,176,384]{3,2,1,0:T(8,128)(2,1)}, bf16[1,4,176,384]{3,2,1,0:T(8,128)(2,1)S(1)}, u32[]{:S(2)}, u32[]{:S(2)}) collective-permute-start(bf16[1,4,176,384]{3,2,1,0:T(8,128)(2,1)} %fusion.24), channel_id=1, source_target_pairs={{0,4},{4,0},{8,12},{12,8},{16,20},{20,16},{24,28},{28,24},{1,5},{5... | collective-permute-start | bytes 1622024 | tf_op jit(solution)/shard_map/ppermute | solution.py:785
  1187.3 9.0 collective-permute-start.23
  1187.4 12.0 collective-permute-start.25
  1187.6 24.3 %collective-permute-start.24 = (bf16[1,176,384]{2,1,0:T(8,128)(2,1)S(1)}, bf16[1,176,384]{2,1,0:T(8,128)(2,1)S(1)}, u32[]{:S(2)}, u32[]{:S(2)}) collective-permute-start(bf16[1,176,384]{2,1,0:T(8,128)(2,1)S(1)} %get-tuple-element.384), channel_id=1, source_target_pairs={{0,16},{4,20},{8,24},{12,28},{16,0},{20,4},{24,8},{28,12},{1,17},{... | collective-permute-start | bytes 405512 | tf_op jit(solution)/shard_map/ppermute | solution.py:785
  1193.4 25.1 %collective-permute-start.20 = (bf16[2,176,384]{2,1,0:T(8,128)(2,1)}, bf16[2,176,384]{2,1,0:T(8,128)(2,1)S(1)}, u32[]{:S(2)}, u32[]{:S(2)}) collective-permute-start(bf16[2,176,384]{2,1,0:T(8,128)(2,1)} %get-tuple-element.374), channel_id=1, source_target_pairs={{0,8},{4,12},{8,0},{12,4},{16,24},{20,28},{24,16},{28,20},{1,9},{5... | collective-permute-start | bytes 811016 | tf_op jit(solution)/shard_map/ppermute | solution.py:785
  1194.4 24.2 %collective-permute-start.22 = (bf16[2,176,384]{2,1,0:T(8,128)(2,1)}, bf16[2,176,384]{2,1,0:T(8,128)(2,1)}, u32[]{:S(2)}, u32[]{:S(2)}) collective-permute-start(bf16[2,176,384]{2,1,0:T(8,128)(2,1)} %get-tuple-element.375), channel_id=1, source_target_pairs={{0,24},{4,28},{8,16},{12,20},{16,8},{20,12},{24,0},{28,4},{1,25},{... | collective-permute-start | bytes 811016 | tf_op jit(solution)/shard_map/ppermute | solution.py:785
  1196.4 40.9 %collective-permute-start.21 = (bf16[2,176,384]{2,1,0:T(8,128)(2,1)S(1)}, bf16[2,176,384]{2,1,0:T(8,128)(2,1)}, u32[]{:S(2)}, u32[]{:S(2)}) collective-permute-start(bf16[2,176,384]{2,1,0:T(8,128)(2,1)S(1)} %get-tuple-element.376), channel_id=1, source_target_pairs={{0,16},{4,20},{8,24},{12,28},{16,0},{20,4},{24,8},{28,12},{1,17},{... | collective-permute-start | bytes 811016 | tf_op jit(solution)/shard_map/ppermute | solution.py:785
  1199.4 40.0 %collective-permute-start.17 = (bf16[1,352,384]{2,1,0:T(8,128)(2,1)}, bf16[1,352,384]{2,1,0:T(8,128)(2,1)}, u32[]{:S(2)}, u32[]{:S(2)}) collective-permute-start(bf16[1,352,384]{2,1,0:T(8,128)(2,1)} %get-tuple-element.378), channel_id=1, source_target_pairs={{0,8},{4,12},{8,0},{12,4},{16,24},{20,28},{24,16},{28,20},{1,9},{5... | collective-permute-start | bytes 811016 | tf_op jit(solution)/shard_map/ppermute | solution.py:785
  1211.9 27.5 %collective-permute-start.19 = (bf16[1,352,384]{2,1,0:T(8,128)(2,1)}, bf16[1,352,384]{2,1,0:T(8,128)(2,1)}, u32[]{:S(2)}, u32[]{:S(2)}) collective-permute-start(bf16[1,352,384]{2,1,0:T(8,128)(2,1)} %get-tuple-element.379), channel_id=1, source_target_pairs={{0,24},{4,28},{8,16},{12,20},{16,8},{20,12},{24,0},{28,4},{1,25},{... | collective-permute-start | bytes 811016 | tf_op jit(solution)/shard_map/ppermute | solution.py:785
  1214.8 44.5 %all-to-all-start.19 = ((bf16[4,352,768]{2,1,0:T(8,128)(2,1)}), bf16[4,352,768]{2,1,0:T(8,128)(2,1)S(1)}, u32[]{:S(2)}, u32[]{:S(2)}) async-start(bf16[4,352,768]{2,1,0:T(8,128)(2,1)} %bitcast.108), calls=%async_computation.20 | async-start | bytes 4325376 | tf_op jit(solution)/shard_map/all_to_all | solution.py:670
  1218.5 29.1 %collective-permute-start.18 = (bf16[1,352,384]{2,1,0:T(8,128)(2,1)}, bf16[1,352,384]{2,1,0:T(8,128)(2,1)S(1)}, u32[]{:S(2)}, u32[]{:S(2)}) collective-permute-start(bf16[1,352,384]{2,1,0:T(8,128)(2,1)} %get-tuple-element.380), channel_id=1, source_target_pairs={{0,16},{4,20},{8,24},{12,28},{16,0},{20,4},{24,8},{28,12},{1,17},{... | collective-permute-start | bytes 811016 | tf_op jit(solution)/shard_map/ppermute | solution.py:785
  (116 other events, 943.2 us)
Sparse Core Ops, SparseCore 0:
  11.7 152.6 all-gather.5
  168.1 122.0 all-gather.7
  293.8 202.3 all-gather.3
  581.7 332.0 reduce-scatter.2
  921.3 250.0 reduce-scatter.4
